TPU v7x, 32 devices: a whole 2x2x4 slice. The times are simulated.
32 devices in a mesh: groups: 2 (over y), frame: 4 (over z), tensor: 4 (over x, core).
Axes of the slice: x: 2, y: 2, z: 4, core: 2. Of those that a mesh axis runs over, the one named last changes fastest.
Arguments:
- latent: bfloat16 [6, 1024, 1024], P(None, ('groups', 'frame')), parts along dimension 1, may hold values from -17 to 17
- norm1_gain: float32 [1024], replicated, may hold values from 0.1 to 1.9
- conv1_weight: bfloat16 [3, 1024, 1024], P(None, None, 'tensor'), may hold values from -0.109375 to 0.109375
- time_bias: float32 [1024], P('tensor'), may hold values from -4 to 4
- norm2_gain: float32 [1024], P('tensor'), may hold values from 0.1 to 1.9
- conv2_weight: bfloat16 [3, 1024, 1024], P(None, 'tensor'), may hold values from -0.375 to 0.375
- attn_gain: float32 [1024], replicated, may hold values from 0.1 to 1.9
- qkv_weight: bfloat16 [1024, 3, 1024], P(None, None, 'tensor'), may hold values from -2 to 2
- out_weight: bfloat16 [1024, 1024], P('tensor'), may hold values from -0.1875 to 0.1875
Outputs:
- velocity: bfloat16 [6, 1024, 1024], P(None, ('groups', 'frame'), 'tensor'), parts along dimension 1
There are 2 independent parts, one for each index of `groups`. A program takes and returns all parts, laid end to end along the dimension named above; an argument that names none is the same for every part. Nothing has to cross between parts.
All inputs are finite; a program needn't handle non-finite values.
Results may differ from a plain program's by a relative error of at most 0.014.
Values may be sent and summed in bfloat16 or wider, within the bound.
No kernel may reach another device: no remote copies, remote signals or barrier semaphores. Data moves between devices by JAX's collectives and lax.ppermute only.
A program may use at most 64 MiB of HBM per device.

v0:
```python
import math

import jax
import jax.numpy as jnp
from jax import lax
from jax.sharding import PartitionSpec as P

GROUPS = 32
HEAD_DIM = 64
WINDOW = 64


norm_eps = 1e-05
rms_eps = 1e-06


def extended(block, sides, width):
    for axis, dim in sides:
        count = lax.axis_size(axis)
        forward = [(i, i + 1) for i in range(count - 1)]
        backward = [(target, source) for source, target in forward]
        low = lax.ppermute(
            lax.slice_in_dim(block, block.shape[dim] - width, None, axis=dim), axis, forward
        )
        high = lax.ppermute(lax.slice_in_dim(block, 0, width, axis=dim), axis, backward)
        block = jnp.concatenate([low, block, high], axis=dim)
    return block


def group_sums(hidden, group_count):
    stem_count, frame_count, channels = hidden.shape
    grouped = hidden.reshape(stem_count, frame_count, group_count, channels // group_count)
    return (jnp.sum(grouped, axis=(1, 3)), jnp.sum(grouped * grouped, axis=(1, 3)))


def apply_group(hidden, totals, squares, entries, gain_vec):
    stem_count, frame_count, channels = hidden.shape
    group_count = totals.shape[1]
    centre = totals / entries
    spread = squares / entries - centre * centre
    grouped = hidden.reshape(stem_count, frame_count, group_count, channels // group_count)
    scaled = (grouped - centre[:, None, :, None]) * lax.rsqrt(spread + norm_eps)[:, None, :, None]
    return scaled.reshape(stem_count, frame_count, channels) * gain_vec


def conv_padded(padded, kernel, frame_count):
    stem_count = padded.shape[0]
    channels = padded.shape[2]
    result = jnp.zeros((stem_count * frame_count, kernel.shape[2]), jnp.float32)
    for tap_index in range(3):
        tap_rows = padded[:, tap_index : tap_index + frame_count].reshape(
            stem_count * frame_count, channels
        )
        result = result + jnp.dot(tap_rows, kernel[tap_index], preferred_element_type=jnp.float32)
    return result.reshape(stem_count, frame_count, kernel.shape[2])


def attend(queries, keys_all, values):
    stem_count, frame_count, head_count, head_dim = queries.shape
    window_count = frame_count // WINDOW

    def arrange(source):
        shaped = source.reshape(stem_count, window_count, WINDOW, head_count, head_dim)
        return shaped.transpose(1, 3, 0, 2, 4).reshape(
            window_count, head_count, stem_count * WINDOW, head_dim
        )

    scores = jnp.einsum(
        "nhqd,nhkd->nhqk",
        arrange(queries),
        arrange(keys_all),
        precision=lax.Precision.HIGHEST,
        preferred_element_type=jnp.float32,
    ) / math.sqrt(head_dim)
    scores = scores - jnp.max(scores, axis=3, keepdims=True)
    exp_scores = jnp.exp(scores)
    attn_probs = (exp_scores / jnp.sum(exp_scores, axis=3, keepdims=True)).astype(jnp.bfloat16)
    context = jnp.einsum(
        "nhqk,nhkd->nhqd", attn_probs, arrange(values), preferred_element_type=jnp.float32
    ).astype(jnp.bfloat16)
    context = context.reshape(window_count, head_count, stem_count, WINDOW, head_dim).transpose(
        2, 0, 3, 1, 4
    )
    return context.reshape(stem_count * frame_count, head_count * head_dim)


def local(
    latent,
    norm1_gain,
    conv1_weight,
    time_bias,
    norm2_gain,
    conv2_weight,
    attn_gain,
    qkv_weight,
    out_weight,
):
    stem_count, frame_count, channels = latent.shape
    tensor_size = lax.axis_size("tensor")
    shard_width = channels // tensor_size
    row_count = stem_count * frame_count
    group_entries = frame_count * lax.axis_size("frame") * (channels // GROUPS)
    latent_f = latent.astype(jnp.float32)
    sums_one, squares_one = group_sums(latent_f, GROUPS)
    sums_one, squares_one = lax.psum((sums_one, squares_one), "frame")
    act_one = jax.nn.silu(
        apply_group(latent_f, sums_one, squares_one, group_entries, norm1_gain)
    ).astype(jnp.bfloat16)
    padded_one = extended(act_one, (("frame", 1),), 1)
    hid_one = conv_padded(padded_one, conv1_weight, frame_count)
    hid_one = hid_one + time_bias
    local_groups = GROUPS // tensor_size
    sums_two, squares_two = group_sums(hid_one, local_groups)
    sums_two, squares_two = lax.psum((sums_two, squares_two), "frame")
    act_two = jax.nn.silu(
        apply_group(hid_one, sums_two, squares_two, group_entries, norm2_gain)
    ).astype(jnp.bfloat16)
    padded_two = extended(act_two, (("frame", 1),), 1)
    conv_term = conv_padded(padded_two, conv2_weight, frame_count)
    own_start = lax.axis_index("tensor") * shard_width
    qkv_flat = qkv_weight.reshape(channels, 3 * shard_width)
    conv_total = lax.psum(conv_term.astype(jnp.bfloat16), "tensor").astype(jnp.float32)
    residual = (latent_f + conv_total).astype(jnp.bfloat16)
    res_f = residual.astype(jnp.float32)
    mean_sq = jnp.mean(res_f * res_f, axis=2, keepdims=True)
    normed = (res_f * lax.rsqrt(mean_sq + rms_eps) * attn_gain).astype(jnp.bfloat16)
    projected = jnp.dot(
        normed.reshape(row_count, channels), qkv_flat, preferred_element_type=jnp.float32
    )
    res_own = lax.dynamic_slice_in_dim(res_f, own_start, shard_width, 2)
    head_local = shard_width // HEAD_DIM
    projected = projected.reshape(stem_count, frame_count, 3, head_local, HEAD_DIM)
    values = projected[:, :, 2].astype(jnp.bfloat16)
    context = attend(projected[:, :, 0], projected[:, :, 1], values)
    out_term = jnp.dot(context, out_weight, preferred_element_type=jnp.float32).reshape(
        stem_count, frame_count, channels
    )
    attn_share = lax.psum_scatter(
        out_term.astype(jnp.bfloat16), "tensor", scatter_dimension=2, tiled=True
    ).astype(jnp.float32)
    velocity = (res_own + attn_share).astype(jnp.bfloat16)
    return velocity


def solution(mesh):
    return jax.shard_map(
        local,
        mesh=mesh,
        in_specs=(
            P(None, ("groups", "frame"), None),
            P(),
            P(None, None, "tensor"),
            P("tensor"),
            P("tensor"),
            P(None, "tensor", None),
            P(),
            P(None, None, "tensor"),
            P("tensor", None),
        ),
        out_specs=P(None, ("groups", "frame"), "tensor"),
        check_vma=False,
    )
```

profile of v0, /device:TPU:0, one launch (start us, length us, event | category | flops | bytes accessed | tf_op | source)
XLA Modules:
  0.0 182.4 jit_solution(185818736089615130)
XLA Ops:
  6.5 2.0 %convert_reduce_fusion = (f32[6,1024]{1,0:T(8,128)S(1)}, f32[6,1024]{1,0:T(8,128)S(1)}) fusion(bf16[6,128,1024]{2,1,0:T(8,128)(2,1)} %param.9), kind=kLoop, calls=%fused_computation.4 | loop fusion | flops 3133440 | bytes 1622016 | tf_op jit(solution)/shard_map/reduce_sum | solution.py:33
  9.0 13.7 %all-reduce.1 = (f32[6,32]{1,0:T(8,128)S(1)}, f32[6,32]{1,0:T(8,128)S(1)}) all-reduce(f32[6,32]{1,0:T(8,128)S(1)} %reduce_sum.73, f32[6,32]{1,0:T(8,128)S(1)} %reduce_sum.70), channel_id=1, replica_groups=mesh['groups'=2,'frame'=4,'tensor'=4] {'frame'}, use_global_device_ids=true, to_apply=%region_5.6 | all-reduce | flops 384 | bytes 3072 | tf_op jit(solution)/shard_map/psum | solution.py:105
  23.1 2.8 %fusion.11 = bf16[6,128,1024]{2,1,0:T(8,128)(2,1)} fusion(bf16[6,128,1024]{2,1,0:T(8,128)(2,1)S(1)} %copy-done.1, f32[1024]{0:T(1024)} %param.10, f32[6,1024]{1,0:T(8,128)S(1)} %mul.101, f32[6,1024]{1,0:T(8,128)S(1)} %sub.46), kind=kLoop, calls=%fused_computation.16 | loop fusion | flops 7077888 | bytes 3198976 | tf_op jit(solution)/shard_map/convert_element_type | solution.py:108
  26.0 1.0 fusion.55
  27.0 1.3 collective-permute-start
  28.3 1.3 collective-permute-start.1
  29.6 3.0 %fusion.36 = f32[768,256]{1,0:T(8,128)} fusion(bf16[768,1024]{1,0:T(8,128)(2,1)} %bitcast.2, bf16[3,1024,256]{2,1,0:T(8,128)(2,1)} %param.11), kind=kOutput, calls=%fused_computation.56 | convolution fusion | flops 402653184 | bytes 2883584 | tf_op jit(solution)/shard_map/dot_general | solution.py:54
  32.6 1.3 collective-permute-done.1
  34.0 3.0 %pad_maximum_fusion.1 = (bf16[6,128,1024]{2,1,0:T(8,128)(2,1)S(1)}, bf16[6,128,1024]{2,1,0:T(8,128)(2,1)S(1)}) fusion(bf16[6,128,1024]{2,1,0:T(8,128)(2,1)} %fusion.11, bf16[6,1,1024]{2,1,0:T(2,128)(2,1)S(1)} %collective-permute-done, bf16[6,1,1024]{2,1,0:T(2,128)(2,1)S(1)} %collective-permute-done.1), kind=kLoop, calls=%fused_computation.31 | loop fusion | flops 6291456 | bytes 4743168 | tf_op jit(solution)/shard_map/concatenate | solution.py:26
  37.0 0.6 fusion.34
  37.6 0.6 fusion.22
  38.2 1.2 copy.37
  39.4 2.2 %reshape.92 = f32[6,128,8,32]{1,0,3,2:T(8,128)} reshape(f32[768,256]{0,1:T(8,128)} %copy.37) | data formatting | bytes 1572864 | tf_op jit(solution)/shard_map/reshape | solution.py:55
  41.7 1.6 add_reduce_fusion
  43.3 10.4 %all-reduce = (f32[6,8]{0,1:T(8,128)S(1)}, f32[6,8]{0,1:T(8,128)S(1)}) all-reduce(f32[6,8]{0,1:T(8,128)S(1)} %get-tuple-element.8, f32[6,8]{0,1:T(8,128)S(1)} %get-tuple-element.7), channel_id=1, replica_groups=mesh['groups'=2,'frame'=4,'tensor'=4] {'frame'}, use_global_device_ids=true, to_apply=%region_9.10 | all-reduce | flops 96 | bytes 768 | tf_op jit(solution)/shard_map/psum | solution.py:114
  54.2 0.3 multiply_convert_fusion.1
  54.5 0.3 multiply_convert_fusion.2
  54.7 1.4 collective-permute-start.3
  56.2 4.5 %collective-permute-start.2 = (bf16[6,1,256]{2,1,0:T(2,128)(2,1)S(1)}, bf16[6,1,256]{2,1,0:T(2,128)(2,1)S(1)}, u32[]{:S(2)}, u32[]{:S(2)}) collective-permute-start(bf16[6,1,256]{2,1,0:T(2,128)(2,1)S(1)} %get-tuple-element.24), channel_id=1, source_target_pairs={{0,4},{4,8},{8,12},{1,5},{5,9},{9,13},{2,6},{6,10},{10,14},{3,7},{... | collective-permute-start | bytes 9224 | tf_op jit(solution)/shard_map/ppermute | solution.py:22
  60.7 1.6 fusion.30
  62.4 0.2 pad_maximum_fusion.2
  62.6 0.6 fusion.32
  63.1 1.7 add_convert_fusion
  64.9 0.2 reduce-scatter.2.cloned.1.call-start
  65.1 2.6 %copy.40 = bf16[1024,3,256]{0,2,1:T(8,128)(2,1)} copy(bf16[1024,3,256]{2,0,1:T(8,128)(2,1)} %param.16) | data formatting | bytes 3145728 | tf_op args[7]
  67.7 39.7 %all-reduce.4.cloned.1.call-done = bf16[6,128,1024]{2,1,0:T(8,128)(2,1)} async-done(((bf16[6,128,1024]{2,1,0:T(8,128)(2,1)}), bf16[6,128,1024]{2,1,0:T(8,128)(2,1)}) %all-reduce.4.cloned.1.call-update) | async-done | bytes 1572880 | tf_op jit(solution)/shard_map/psum | solution.py:122
  107.5 3.7 %fusion.19 = (f32[6,128,1024]{2,1,0:T(8,128)}, f32[6,128]{1,0:T(8,128)S(1)}) fusion(bf16[6,128,1024]{2,1,0:T(8,128)(2,1)} %all-reduce.4.cloned.1.call-done, bf16[6,128,1024]{2,1,0:T(8,128)(2,1)S(1)} %copy-done.1), kind=kLoop, calls=%fused_computation.29 | loop fusion | flops 5504256 | bytes 6294528 | tf_op jit(solution)/shard_map/convert_element_type | solution.py:124
  111.2 1.6 fusion.17
  112.8 1.0 fusion.54
  113.8 0.3 convert_element_type.61
  114.2 0.5 copy.53
  114.7 1.4 reshape.98
  116.1 2.0 %reshape_squeeze.6 = f32[6,2,64,4,64]{2,1,4,3,0:T(2,128)} reshape(f32[6,128,1,4,64]{1,4,3,2,0:T(8,128)S(1)} %get-tuple-element.16) | data formatting | bytes 1572864 | tf_op jit(solution)/shard_map/reshape;squeeze | solution.py:63
  118.1 2.4 %copy.52 = f32[6,2,64,4,64]{2,0,4,3,1:T(8,128)S(1)} copy(f32[6,2,64,4,64]{2,1,4,3,0:T(2,128)} %reshape_squeeze.6) | data formatting | bytes 1572864 | tf_op jit(solution)/shard_map/reshape;squeeze | solution.py:63
  120.5 0.5 reshape.96
  120.9 3.2 %reshape_squeeze.7 = f32[6,2,64,4,64]{2,1,4,3,0:T(2,128)} reshape(f32[6,128,1,4,64]{1,4,3,2,0:T(8,128)} %get-tuple-element.15) | data formatting | bytes 1572864 | tf_op jit(solution)/shard_map/reshape;squeeze | solution.py:63
  124.1 2.4 %copy.51 = f32[6,2,64,4,64]{2,0,4,3,1:T(8,128)S(1)} copy(f32[6,2,64,4,64]{2,1,4,3,0:T(2,128)} %reshape_squeeze.7) | data formatting | bytes 1572864 | tf_op jit(solution)/shard_map/reshape;squeeze | solution.py:63
  126.5 1.4 reshape.97
  127.8 5.0 %fusion.58 = f32[2,4,384,384]{2,3,1,0:T(8,128)S(1)} fusion(f32[2,4,384,64]{2,3,1,0:T(8,128)S(1)} %reshape.96, f32[2,4,384,64]{2,3,1,0:T(8,128)} %reshape.97), kind=kOutput, calls=%fused_computation.79 | convolution fusion | flops 905969664 | bytes 6291456 | tf_op jit(solution)/shard_map/nhqd,nhkd->nhqk/dot_general | solution.py:68
  132.9 2.1 %copy-done.2 = f32[2,4,384,384]{2,3,1,0:T(8,128)} copy-done((f32[2,4,384,384]{2,3,1,0:T(8,128)}, f32[2,4,384,384]{2,3,1,0:T(8,128)S(1)}, u32[]{:S(2)}) %copy-start.2) | copy-done | bytes 4718616
  135.0 1.2 fusion.57
  136.2 5.3 %fusion.23 = bf16[2,4,384,64]{2,3,1,0:T(8,128)(2,1)S(1)} fusion(bf16[2,4,384,64]{2,3,1,0:T(8,128)(2,1)S(1)} %copy-done.7, f32[2,4,384]{2,1,0:T(4,128)S(1)} %fusion.57, f32[2,4,384,384]{2,3,1,0:T(8,128)} %copy-done.2), kind=kOutput, calls=%fused_computation.36 | convolution fusion | flops 157093248 | bytes 5517312 | tf_op jit(solution)/shard_map/nhqk,nhkd->nhqd/dot_general | solution.py:78
  141.5 0.6 reshape.99
  142.1 0.8 copy.45
  142.9 0.5 dot_general.47
  143.4 1.7 convolution_convert_fusion
  145.2 28.3 %reduce-scatter.2.cloned.1.call-done = bf16[6,128,256]{2,1,0:T(8,128)(2,1)} async-done(((bf16[6,128,1024]{2,1,0:T(8,128)(2,1)}), bf16[6,128,256]{2,1,0:T(8,128)(2,1)}) %reduce-scatter.2.cloned.1.call-update) | async-done | bytes 393232 | tf_op jit(solution)/shard_map/reduce_scatter | solution.py:138
  173.4 2.1 %add_convert_fusion.1 = bf16[6,128,256]{2,1,0:T(8,128)(2,1)} fusion(bf16[6,128,256]{2,1,0:T(8,128)(2,1)} %reduce-scatter.2.cloned.1.call-done, f32[6,128,1024]{2,1,0:T(8,128)} %get-tuple-element.13, s32[]{:T(128)S(6)} %select_n.3), kind=kLoop, calls=%fused_computation.44 | loop fusion | flops 589824 | bytes 1572868 | tf_op jit(solution)/shard_map/convert_element_type | solution.py:141
  (49 shorter events, 1.5 us)
Async XLA Ops:
  6.5 136.9 %copy-start = (bf16[256,1024]{1,0:T(8,128)(2,1)S(1)}, bf16[256,1024]{1,0:T(8,128)(2,1)}, u32[]{:S(2)}) copy-start(bf16[256,1024]{1,0:T(8,128)(2,1)} %param.17) | copy-start | bytes 1572868
  6.5 16.6 %copy-start.1 = (bf16[6,128,1024]{2,1,0:T(8,128)(2,1)S(1)}, bf16[6,128,1024]{2,1,0:T(8,128)(2,1)}, u32[]{:S(2)}) copy-start(bf16[6,128,1024]{2,1,0:T(8,128)(2,1)} %param.9) | copy-start | bytes 4718596
  6.5 100.9 %all-reduce.4.cloned.1.call-start = ((), (), s32[]{:S(2)}) async-start(), calls=%async_computation.1 | async-start | bytes 3145728 | tf_op jit(solution)/shard_map/psum | solution.py:122
  23.1 9.4 %copy-start.9 = (f32[256]{0:T(256)S(1)}, f32[256]{0:T(256)}, u32[]{:S(2)}) copy-start(f32[256]{0:T(256)} %param.12) | copy-start | bytes 3076
  27.0 5.7 %collective-permute-start = (bf16[6,1,1024]{2,1,0:T(2,128)(2,1)S(1)}, bf16[6,1,1024]{2,1,0:T(2,128)(2,1)S(1)}, u32[]{:S(2)}, u32[]{:S(2)}) collective-permute-start(bf16[6,1,1024]{2,1,0:T(2,128)(2,1)S(1)} %get-tuple-element.19), channel_id=1, source_target_pairs={{0,4},{4,8},{8,12},{1,5},{5,9},{9,13},{2,6},{6,10},{10,14},{3,7},{... | collective-permute-start | bytes 36872 | tf_op jit(solution)/shard_map/ppermute | solution.py:22
  28.3 5.7 %collective-permute-start.1 = (bf16[6,1,1024]{2,1,0:T(2,128)(2,1)S(1)}, bf16[6,1,1024]{2,1,0:T(2,128)(2,1)S(1)}, u32[]{:S(2)}, u32[]{:S(2)}) collective-permute-start(bf16[6,1,1024]{2,1,0:T(2,128)(2,1)S(1)} %get-tuple-element.20), channel_id=1, source_target_pairs={{4,0},{8,4},{12,8},{5,1},{9,5},{13,9},{6,2},{10,6},{14,10},{7,3},{... | collective-permute-start | bytes 36872 | tf_op jit(solution)/shard_map/ppermute | solution.py:25
  32.6 4.4 %copy-start.8 = (bf16[3,1024,256]{2,1,0:T(8,128)(2,1)S(1)}, bf16[3,1024,256]{2,1,0:T(8,128)(2,1)}, u32[]{:S(2)}) copy-start(bf16[3,1024,256]{2,1,0:T(8,128)(2,1)} %param.11) | copy-start | bytes 4718596
  32.6 5.0 %copy-start.6 = (f32[768,256]{1,0:T(8,128)S(1)}, f32[768,256]{1,0:T(8,128)}, u32[]{:S(2)}) copy-start(f32[768,256]{1,0:T(8,128)} %fusion.36) | copy-start | bytes 2359300
  38.2 16.0 %copy-start.10 = (f32[256]{0:T(256)S(1)}, f32[256]{0:T(256)}, u32[]{:S(2)}) copy-start(f32[256]{0:T(256)} %param.13) | copy-start | bytes 3076
  54.4 8.1 %copy-start.5 = (bf16[3,256,1024]{2,1,0:T(8,128)(2,1)S(1)}, bf16[3,256,1024]{2,1,0:T(8,128)(2,1)}, u32[]{:S(2)}) copy-start(bf16[3,256,1024]{2,1,0:T(8,128)(2,1)} %param.14) | copy-start | bytes 4718596
  54.7 7.6 %collective-permute-start.3 = (bf16[6,1,256]{2,1,0:T(2,128)(2,1)S(1)}, bf16[6,1,256]{2,1,0:T(2,128)(2,1)S(1)}, u32[]{:S(2)}, u32[]{:S(2)}) collective-permute-start(bf16[6,1,256]{2,1,0:T(2,128)(2,1)S(1)} %get-tuple-element.23), channel_id=1, source_target_pairs={{4,0},{8,4},{12,8},{5,1},{9,5},{13,9},{6,2},{10,6},{14,10},{7,3},{... | collective-permute-start | bytes 9224 | tf_op jit(solution)/shard_map/ppermute | solution.py:25
  56.2 6.2 %collective-permute-start.2 = (bf16[6,1,256]{2,1,0:T(2,128)(2,1)S(1)}, bf16[6,1,256]{2,1,0:T(2,128)(2,1)S(1)}, u32[]{:S(2)}, u32[]{:S(2)}) collective-permute-start(bf16[6,1,256]{2,1,0:T(2,128)(2,1)S(1)} %get-tuple-element.24), channel_id=1, source_target_pairs={{0,4},{4,8},{8,12},{1,5},{5,9},{9,13},{2,6},{6,10},{10,14},{3,7},{... | collective-permute-start | bytes 9224 | tf_op jit(solution)/shard_map/ppermute | solution.py:22
  64.9 108.5 %reduce-scatter.2.cloned.1.call-start = ((), (), s32[]{:S(2)}) async-start(), calls=%async_computation.2 | async-start | bytes 1966080 | tf_op jit(solution)/shard_map/reduce_scatter | solution.py:138
  67.7 43.5 %copy-start.11 = (f32[1024]{0:T(1024)S(1)}, f32[1024]{0:T(1024)}, u32[]{:S(2)}) copy-start(f32[1024]{0:T(1024)} %param.15) | copy-start | bytes 12292
  107.4 3.7 %copy-start.3 = (bf16[1024,3,256]{0,2,1:T(8,128)(2,1)S(1)}, bf16[1024,3,256]{0,2,1:T(8,128)(2,1)}, u32[]{:S(2)}) copy-start(bf16[1024,3,256]{0,2,1:T(8,128)(2,1)} %copy.40) | copy-start | bytes 4718596
  107.4 3.7 %copy-start.4 = (bf16[6,128,1024]{2,1,0:T(8,128)(2,1)S(1)}, bf16[6,128,1024]{2,1,0:T(8,128)(2,1)}, u32[]{:S(2)}) copy-start(bf16[6,128,1024]{2,1,0:T(8,128)(2,1)} %all-reduce.4.cloned.1.call-done) | copy-start | bytes 4718596
  132.9 2.1 %copy-start.2 = (f32[2,4,384,384]{2,3,1,0:T(8,128)}, f32[2,4,384,384]{2,3,1,0:T(8,128)S(1)}, u32[]{:S(2)}) copy-start(f32[2,4,384,384]{2,3,1,0:T(8,128)S(1)} %fusion.58) | copy-start | bytes 14155780
  135.0 1.2 copy-start.7
Sparse Core Ops, SparseCore 0:
  65.0 42.3 all-reduce.3
  145.3 28.0 reduce-scatter.1
where the time goes:
time: 183 us; the launch traced here: 182 us
  waiting for transfers between devices  69.4 us (38%)
  local copies, waits for them, and re-layouts  27.2 us (15%)
  blocking collectives  24.1 us (13%)
  matrix products  21.7 us (12%)
  other arithmetic  17.4 us (10%)
  between operations  13.8 us (8%)
  starting transfers between devices  8.78 us (5%)
    psum x1, waiting for transfers between devices, local(): lax.psum(conv_term.astype(jnp.bfloat16), 'tensor').astype(jnp.float32)  39.7 us
    reduce_scatter x1, waiting for transfers between devices, local(): lax.psum_scatter(out_term.astype(jnp.bfloat16), 'tensor', scatter_dimensi...  28.3 us
    psum x1, blocking collectives, local(): sums_one, squares_one = lax.psum((sums_one, squares_one), 'frame')  13.7 us
    psum x1, blocking collectives, local(): sums_two, squares_two = lax.psum((sums_two, squares_two), 'frame')  10.4 us
    another operation x4, local copies, waits for them, and re-layouts, arrange(): source.reshape(stem_count, window_count, WINDOW, head_count, head_dim)  9.92 us
    dot_general x6, matrix products, conv_padded(): jnp.dot(tap_rows, kernel[tap_index], preferred_element_type=jnp.float32)  8.07 us
    ppermute x2, starting transfers between devices, extended(): lax.ppermute(lax.slice_in_dim(block, block.shape[dim] - width, None, axis...  5.84 us
    dot_general x1, matrix products, attend(): jnp.einsum('nhqk,nhkd->nhqd', attn_probs, arrange(values), preferred_elem...  5.34 us
  transfers between devices with their start and end apart: 6, of which 3 were waited for; matrix products, arithmetic and copies ran while one was open for 4% of the time, Pallas kernels for 0%

commit v1 on v0

--- a/solution.py
+++ b/solution.py
@@ -1,17 +1,24 @@
+import functools
 import math
 
 import jax
 import jax.numpy as jnp
 from jax import lax
+from jax.experimental import pallas as pl
+from jax.experimental.pallas import tpu as pltpu
 from jax.sharding import PartitionSpec as P
 
 GROUPS = 32
 HEAD_DIM = 64
 WINDOW = 64
-
+LANES = 128
 
 norm_eps = 1e-05
 rms_eps = 1e-06
+HIGHEST = lax.Precision.HIGHEST
+VMEM = pltpu.VMEM
+bf16 = jnp.bfloat16
+f32 = jnp.float32
 
 
 def extended(block, sides, width):
@@ -84,7 +91,7 @@
     return context.reshape(stem_count * frame_count, head_count * head_dim)
 
 
-def local(
+def generic(
     latent,
     norm1_gain,
     conv1_weight,
@@ -142,6 +149,342 @@
     return velocity
 
 
+def silu(v):
+    half = 0.5 * v
+    return half + half * jnp.tanh(half)
+
+
+def one_hot(rows, columns, width, by_row):
+    row = lax.broadcasted_iota(jnp.int32, (rows, columns), 0)
+    column = lax.broadcasted_iota(jnp.int32, (rows, columns), 1)
+    if by_row:
+        return (row // width == column).astype(f32)
+    return (row == column // width).astype(f32)
+
+
+def f32_dot(a, b):
+    return jnp.dot(a, b, precision=HIGHEST, preferred_element_type=f32)
+
+
+def group_totals(sums, squares, width):
+    hot = one_hot(sums.shape[1], LANES, width, True)
+    return f32_dot(sums, hot), f32_dot(squares, hot)
+
+
+def channel_scale(refs, entries, channels, width):
+    total = refs[0]
+    for other in refs[1:]:
+        total = total + other
+    centre = total[:, :LANES] / entries
+    spread = total[:, LANES:] / entries - centre * centre
+    hot = one_hot(LANES, channels, width, False)
+    return f32_dot(centre, hot), f32_dot(lax.rsqrt(spread + norm_eps), hot)
+
+
+def stats_kernel(width, lat_ref, up_ref, down_ref, own_ref, sum_ref, square_ref):
+    stems, frames, channels = lat_ref.shape
+    for stem in range(stems):
+        block = lat_ref[stem].astype(f32)
+        sum_ref[stem : stem + 1, :] = jnp.sum(block, axis=0, keepdims=True)
+        square_ref[stem : stem + 1, :] = jnp.sum(block * block, axis=0, keepdims=True)
+        down_ref[stem : stem + 1, :channels] = block[:1]
+        up_ref[stem : stem + 1, :channels] = block[frames - 1 :]
+    sums, squares = group_totals(sum_ref[...], square_ref[...], width)
+    for ref, start in ((up_ref, channels), (down_ref, channels), (own_ref, 0)):
+        ref[:, start : start + LANES] = sums
+        ref[:, start + LANES : start + 2 * LANES] = squares
+
+
+def first_kernel(
+    entries, width, frame_size,
+    lat_ref, low_ref, high_ref, far_ref, own_ref, gain_ref, weight_ref, bias_ref,
+    hid_ref, up_ref, down_ref, tot_ref, act_ref, edge_ref, sum_ref, square_ref,
+):
+    stems, frames, channels = lat_ref.shape
+    shard = weight_ref.shape[2]
+    place = lax.axis_index("frame")
+    centre, scale = channel_scale(
+        [own_ref[...], low_ref[:, channels:], high_ref[:, channels:], far_ref[...]],
+        entries, channels, width,
+    )
+    scale = scale * gain_ref[...]
+    edge_ref[...] = jnp.zeros_like(edge_ref)
+    low = silu((low_ref[:, :channels] - centre) * scale)
+    high = silu((high_ref[:, :channels] - centre) * scale)
+    edge_ref[0:stems, :] = jnp.where(place > 0, low, 0.0)
+    edge_ref[8 : 8 + stems, :] = jnp.where(place < frame_size - 1, high, 0.0)
+    edge = edge_ref[...].astype(bf16)
+    edge_low = jnp.dot(edge, weight_ref[0], preferred_element_type=f32)
+    edge_high = jnp.dot(edge, weight_ref[2], preferred_element_type=f32)
+    row = lax.broadcasted_iota(jnp.int32, (frames, shard), 0)
+    bias = bias_ref[...]
+    step = stems // 2
+    for first in range(0, stems, step):
+        for stem in range(first, first + step):
+            block = lat_ref[stem].astype(f32)
+            block = (block - centre[stem : stem + 1]) * scale[stem : stem + 1]
+            act_ref[stem * frames : (stem + 1) * frames, :] = silu(block).astype(bf16)
+        rows = act_ref[first * frames : (first + step) * frames, :]
+        taps = [jnp.dot(rows, weight_ref[tap], preferred_element_type=f32) for tap in range(3)]
+        for stem in range(first, first + step):
+            lo = (stem - first) * frames
+            before = pltpu.roll(taps[0][lo : lo + frames], 1, 0)
+            after = pltpu.roll(taps[2][lo : lo + frames], frames - 1, 0)
+            before = jnp.where(row == 0, edge_low[stem : stem + 1], before)
+            after = jnp.where(row == frames - 1, edge_high[8 + stem : 9 + stem], after)
+            hid = taps[1][lo : lo + frames] + before + after + bias
+            hid_ref[stem] = hid
+            sum_ref[stem : stem + 1, :] = jnp.sum(hid, axis=0, keepdims=True)
+            square_ref[stem : stem + 1, :] = jnp.sum(hid * hid, axis=0, keepdims=True)
+            down_ref[stem : stem + 1, :shard] = hid[:1]
+            up_ref[stem : stem + 1, :shard] = hid[frames - 1 :]
+    sums, squares = group_totals(sum_ref[...], square_ref[...], width)
+    for ref, start in ((up_ref, shard), (down_ref, shard), (tot_ref, 0)):
+        ref[:, start : start + LANES] = sums
+        ref[:, start + LANES : start + 2 * LANES] = squares
+
+
+def second_kernel(
+    entries, width, frame_size, other,
+    hid_ref, low_ref, high_ref, far_ref, own_ref, gain_ref, weight_ref,
+    send_ref, keep_ref, act_ref,
+):
+    stems, frames, shard = hid_ref.shape
+    place = lax.axis_index("frame")
+    index = lax.axis_index("tensor")
+    chip, core = index // 2, index % 2
+    window = 1 - chip if other else chip
+    centre, scale = channel_scale(
+        [own_ref[...], low_ref[:, shard:], high_ref[:, shard:], far_ref[...]],
+        entries, shard, width,
+    )
+    scale = scale * gain_ref[...]
+    low = jnp.where(place > 0, silu((low_ref[:, :shard] - centre) * scale), 0.0)
+    high = jnp.where(
+        place < frame_size - 1, silu((high_ref[:, :shard] - centre) * scale), 0.0
+    )
+    row = lax.broadcasted_iota(jnp.int32, (WINDOW, shard), 0)
+    half = stems // 2
+    for stem in range(stems):
+        start = pl.multiple_of(window * WINDOW, WINDOW)
+        mean, factor = centre[stem : stem + 1], scale[stem : stem + 1]
+        act = silu((hid_ref[stem, pl.ds(start, WINDOW), :] - mean) * factor)
+        inner = silu((hid_ref[stem, WINDOW - 8 : WINDOW + 8, :] - mean) * factor)
+        before = jnp.where(window == 0, low[stem : stem + 1], inner[7:8])
+        after = jnp.where(window == 0, inner[8:9], high[stem : stem + 1])
+        before = jnp.where(row == 0, before, pltpu.roll(act, 1, 0))
+        after = jnp.where(row == WINDOW - 1, after, pltpu.roll(act, WINDOW - 1, 0))
+        mine = core if stem < half else 1 - core
+        base = jnp.where(mine == 0, half * WINDOW, 0) + (stem % half) * WINDOW
+        at = pl.ds(pl.multiple_of(base, WINDOW), WINDOW)
+        act_ref[at, 0:shard] = before.astype(bf16)
+        act_ref[at, shard : 2 * shard] = act.astype(bf16)
+        act_ref[at, 2 * shard : 3 * shard] = after.astype(bf16)
+    total = jnp.dot(act_ref[...], weight_ref[...], preferred_element_type=f32)
+    send_ref[...] = total[: half * WINDOW].astype(bf16)
+    keep_ref[...] = total[half * WINDOW :].astype(bf16)
+
+
+def split3(value):
+    high = value.astype(bf16)
+    rest = value - high.astype(f32)
+    middle = rest.astype(bf16)
+    return high, middle, (rest - middle.astype(f32)).astype(bf16)
+
+
+def attention_kernel(
+    mine_ref, theirs_ref, gain_ref, qkv_ref, qkv_far_ref, out_ref, out_far_ref,
+    send_ref, keep_ref, res_ref, normed_ref, context_ref,
+):
+    rows, channels = mine_ref.shape
+    shard = qkv_ref.shape[2]
+    index = lax.axis_index("tensor")
+    chip, core = index // 2, index % 2
+    for first, ref in ((0, mine_ref), (rows, theirs_ref)):
+        res = ref[...].astype(f32)
+        res_ref[first : first + rows, :] = res
+        mean_sq = jnp.mean(res * res, axis=1, keepdims=True)
+        normed_ref[first : first + rows, :] = (
+            res * lax.rsqrt(mean_sq + rms_eps) * gain_ref[...]
+        ).astype(bf16)
+    normed = normed_ref[...]
+    lane = lax.broadcasted_iota(jnp.int32, (2 * rows, LANES), 1)
+    per_tile = LANES // HEAD_DIM
+    nt = (((1,), (1,)), ((), ()))
+    for side, ref in enumerate((qkv_ref, qkv_far_ref)):
+        queries, keys, values = [
+            jnp.dot(normed, ref[which], preferred_element_type=f32) for which in range(3)
+        ]
+        queries = queries * (1.0 / math.sqrt(HEAD_DIM))
+        values = values.astype(bf16)
+        for tile in range(shard // LANES):
+            at = slice(tile * LANES, (tile + 1) * LANES)
+            q_high, q_mid, q_low = split3(queries[:, at])
+            left = jnp.concatenate([q_high, q_mid, q_high, q_mid, q_high, q_low], axis=1)
+            result = None
+            for head in range(per_tile):
+                inside = lane // HEAD_DIM == head
+                k_high, k_mid, k_low = split3(jnp.where(inside, keys[:, at], 0.0))
+                right = jnp.concatenate([k_high, k_high, k_mid, k_mid, k_low, k_high], axis=1)
+                scores = lax.dot_general(left, right, nt, preferred_element_type=f32)
+                scores = jnp.exp(scores - jnp.max(scores, axis=1, keepdims=True))
+                total = jnp.sum(scores, axis=1, keepdims=True)
+                probs = (scores / total).astype(bf16)
+                part = jnp.dot(probs, values[:, at], preferred_element_type=f32)
+                result = part if result is None else jnp.where(inside, part, result)
+            base = side * shard + tile * LANES
+            context_ref[:, base : base + LANES] = result.astype(bf16)
+    context = context_ref[...]
+
+    def term(block):
+        at = pl.ds(pl.multiple_of(block * shard, shard), shard)
+        near = jnp.dot(context[:, :shard], out_ref[:, at], preferred_element_type=f32)
+        return near + jnp.dot(context[:, shard:], out_far_ref[:, at], preferred_element_type=f32)
+
+    for place, goal in enumerate((1 - chip, chip)):
+        at = slice(place * shard, (place + 1) * shard)
+        value = term(2 * goal + 1 - core).astype(bf16)
+        send_ref[:rows, at] = value[rows:]
+        send_ref[rows:, at] = value[:rows]
+        block = 2 * goal + core
+        kept = term(block)
+        keep_ref[:, at] = kept + res_ref[:, pl.ds(pl.multiple_of(block * shard, shard), shard)]
+
+
+def place_kernel(own_ref, far_ref, out_ref):
+    stems, frames, shard = out_ref.shape
+    index = lax.axis_index("tensor")
+    chip, core = index // 2, index % 2
+    half = stems // 2
+    for stem in range(stems):
+        goal = (core if stem < half else 1 - core) * half + stem % half
+        rows = slice(stem * WINDOW, (stem + 1) * WINDOW)
+        near = pl.multiple_of(chip * WINDOW, WINDOW)
+        away = pl.multiple_of((1 - chip) * WINDOW, WINDOW)
+        out_ref[goal, pl.ds(near, WINDOW), :] = own_ref[rows, :]
+        out_ref[goal, pl.ds(away, WINDOW), :] = far_ref[rows, :]
+
+
+def call(kernel, name, outs, scratch, args, flops=0, moved=0):
+    return pl.pallas_call(
+        kernel,
+        name=name,
+        out_shape=[jax.ShapeDtypeStruct(shape, dtype) for shape, dtype in outs],
+        in_specs=[pl.BlockSpec(memory_space=VMEM)] * len(args),
+        out_specs=[pl.BlockSpec(memory_space=VMEM)] * len(outs),
+        scratch_shapes=[VMEM(shape, dtype) for shape, dtype in scratch],
+        compiler_params=pltpu.CompilerParams(vmem_limit_bytes=40 * 2**20),
+        cost_estimate=pl.CostEstimate(flops=flops, bytes_accessed=moved, transcendentals=0),
+    )(*args)
+
+
+def swap_cores(value):
+    return lax.ppermute(value, "tensor", [(0, 1), (1, 0), (2, 3), (3, 2)])
+
+
+def swap_chips(value):
+    return lax.ppermute(value, "tensor", [(0, 2), (2, 0), (1, 3), (3, 1)])
+
+
+def shift_frames(value, by):
+    count = lax.axis_size("frame")
+    return lax.ppermute(value, "frame", [(i, (i + by) % count) for i in range(count)])
+
+
+def exchange(up, down, own):
+    return shift_frames(up, 1), shift_frames(down, -1), shift_frames(own, 2)
+
+
+def fast(
+    latent, norm1_gain, conv1_weight, time_bias, norm2_gain, conv2_weight,
+    attn_gain, qkv_weight, out_weight,
+):
+    stems, frames, channels = latent.shape
+    frame_size = lax.axis_size("frame")
+    shard = conv1_weight.shape[2]
+    width = channels // GROUPS
+    entries = frames * frame_size * width
+    half_rows = stems // 2 * WINDOW
+    qkv = jnp.transpose(qkv_weight, (1, 0, 2))
+    qkv_far = swap_chips(qkv)
+    out_far = swap_chips(out_weight)
+    wide = channels + 2 * LANES
+    up, down, own = call(
+        functools.partial(stats_kernel, width), "stats",
+        [((stems, wide), f32), ((stems, wide), f32), ((stems, 2 * LANES), f32)],
+        [((stems, channels), f32)] * 2,
+        [latent],
+    )
+    low, high, far = exchange(up, down, own)
+    narrow = shard + 2 * LANES
+    hid, up2, down2, own2 = call(
+        functools.partial(first_kernel, entries, width, frame_size), "first",
+        [((stems, frames, shard), f32), ((stems, narrow), f32), ((stems, narrow), f32),
+         ((stems, 2 * LANES), f32)],
+        [((stems * frames, channels), bf16), ((16, channels), f32)] + [((stems, shard), f32)] * 2,
+        [latent, low, high, far, own, norm1_gain[None], conv1_weight, time_bias[None]],
+        flops=6 * stems * frames * channels * shard,
+    )
+    low2, high2, far2 = exchange(up2, down2, own2)
+    weight2 = conv2_weight.reshape(3 * shard, channels)
+
+    def second(other):
+        return call(
+            functools.partial(second_kernel, entries, width, frame_size, other),
+            "second_other" if other else "second_own",
+            [((half_rows, channels), bf16)] * 2,
+            [((2 * half_rows, 3 * shard), bf16)],
+            [hid, low2, high2, far2, own2, norm2_gain[None], weight2],
+            flops=12 * half_rows * channels * shard,
+        )
+
+    send, keep = second(True)
+    summed = (swap_cores(send).astype(f32) + keep.astype(f32)).astype(bf16)
+    summed = swap_chips(summed)
+    send_own, keep_own = second(False)
+    got_own = swap_cores(send_own)
+    index = lax.axis_index("tensor")
+    chip, core = index // 2, index % 2
+    latent_own = lax.dynamic_slice(
+        latent, (core * (stems // 2), chip * WINDOW, 0), (stems // 2, WINDOW, channels)
+    ).reshape(half_rows, channels)
+    mine = (
+        latent_own.astype(f32) + keep_own.astype(f32) + got_own.astype(f32) + summed.astype(f32)
+    ).astype(bf16)
+    theirs = swap_cores(mine)
+    out_send, out_keep = call(
+        attention_kernel, "attention",
+        [((2 * half_rows, 2 * shard), bf16), ((2 * half_rows, 2 * shard), f32)],
+        [((2 * half_rows, channels), f32), ((2 * half_rows, channels), bf16),
+         ((2 * half_rows, 2 * shard), bf16)],
+        [mine, theirs, attn_gain[None], qkv, qkv_far, out_weight, out_far],
+        flops=24 * half_rows * channels * shard,
+    )
+    out_got = swap_cores(out_send)
+    away = (out_keep[:, :shard] + out_got[:, :shard].astype(f32)).astype(bf16)
+    stay = (out_keep[:, shard:] + out_got[:, shard:].astype(f32)).astype(bf16)
+    arrived = swap_chips(away)
+    return call(
+        place_kernel, "place", [((stems, frames, shard), bf16)], [], [stay, arrived]
+    )[0]
+
+
+def local(*args):
+    latent = args[0]
+    stems, frames, channels = latent.shape
+    tensor_size, frame_size = lax.axis_size("tensor"), lax.axis_size("frame")
+    shard = channels // tensor_size
+    suits = (
+        tensor_size == 4
+        and frame_size == 4
+        and frames == 2 * WINDOW
+        and stems % 2 == 0
+        and stems <= 8
+        and shard % (2 * LANES) == 0
+    )
+    return fast(*args) if suits else generic(*args)
+
+
 def solution(mesh):
     return jax.shard_map(
         local,

time: 183 us -> 99.7 us (0.54)
  local copies, waits for them, and re-layouts: 27.2 us -> 2.46 us
  blocking collectives: 24.1 us -> 0 us
  matrix products: 21.7 us -> 0 us
  Pallas kernels: 0 us -> 16.1 us
  other arithmetic: 17.4 us -> 2.36 us
  between operations: 13.8 us -> 0.14 us
  starting transfers between devices: 8.78 us -> 15.8 us
  waiting for transfers between devices: 69.4 us -> 62.6 us
    ppermute x4 -> x14, waiting for transfers between devices: 1.35 us -> 62.6 us  [the longest x4 52.7 us: swap_chips(): return lax.ppermute(value, 'tensor', [(0, 2), (2, 0), (1, 3), (3, 1)])]
    psum x1 -> x0, waiting for transfers between devices: 39.7 us -> none  [local(): lax.psum(conv_term.astype(jnp.bfloat16), 'tensor').astype(jnp.float32)]
    reduce_scatter x1 -> x0, waiting for transfers between devices: 28.3 us -> none  [local(): lax.psum_scatter(out_term.astype(jnp.bfloat16), 'tensor', scatter_dimensi...]
    psum x2 -> x0, blocking collectives: 24.1 us -> none  [the longest x1 13.7 us: local(): sums_one, squares_one = lax.psum((sums_one, squares_one), 'frame')]
    dot_general x10 -> x0, matrix products: 21.7 us -> none  [the longest x6 8.07 us: conv_padded(): jnp.dot(tap_rows, kernel[tap_index], preferred_element_type=jnp.float32)]
    pallas_call x0 -> x6, Pallas kernels: none -> 16.1 us  [call(): pl.pallas_call(kernel, name=name, out_shape=[jax.ShapeDtypeStruct(shape,...]
    another operation x4 -> x0, local copies, waits for them, and re-layouts: 9.92 us -> none  [arrange(): source.reshape(stem_count, window_count, WINDOW, head_count, head_dim)]
    ppermute x4 -> x14, starting transfers between devices: 8.55 us -> 15.8 us  [the longest x6 10 us: shift_frames(): lax.ppermute(value, 'frame', [(i, (i + by) % count) for i in range(count)])]
  transfers between devices with their start and end apart: 6 -> 14, of which waited for: 3 -> 6; matrix products, arithmetic and copies ran while one was open for 4% -> 3% of each run, Pallas kernels for 0% -> 2%
where the time goes in v1:
time: 99.7 us; the launch traced here: 99.5 us
  waiting for transfers between devices  62.6 us (63%)
  Pallas kernels  16.1 us (16%)
  starting transfers between devices  15.8 us (16%)
  local copies, waits for them, and re-layouts  2.46 us (2%)
  other arithmetic  2.36 us (2%)
    ppermute x4, waiting for transfers between devices, swap_chips(): return lax.ppermute(value, 'tensor', [(0, 2), (2, 0), (1, 3), (3, 1)])  52.7 us
    pallas_call x6, Pallas kernels, call(): pl.pallas_call(kernel, name=name, out_shape=[jax.ShapeDtypeStruct(shape,...  16.1 us
    ppermute x6, starting transfers between devices, shift_frames(): lax.ppermute(value, 'frame', [(i, (i + by) % count) for i in range(count)])  10 us
    ppermute x6, waiting for transfers between devices, shift_frames(): lax.ppermute(value, 'frame', [(i, (i + by) % count) for i in range(count)])  8.16 us
    ppermute x4, starting transfers between devices, swap_chips(): return lax.ppermute(value, 'tensor', [(0, 2), (2, 0), (1, 3), (3, 1)])  5.45 us
  transfers between devices with their start and end apart: 14, of which 6 were waited for; matrix products, arithmetic and copies ran while one was open for 3% of the time, Pallas kernels for 2%

profile of v1, /device:TPU:0, one launch (start us, length us, event | category | flops | bytes accessed | tf_op | source)
XLA Modules:
  0.0 99.5 jit_solution(12614695654895618752)
XLA Ops:
  0.0 1.4 %copy-done.1 = bf16[6,128,1024]{2,1,0:T(8,128)(2,1)S(1)} copy-done((bf16[6,128,1024]{2,1,0:T(8,128)(2,1)S(1)}, bf16[6,128,1024]{2,1,0:T(8,128)(2,1)}, u32[]{:S(2)}) %copy-start.1) | copy-done | bytes 1572888
  1.4 0.9 stats.1
  2.4 3.1 %collective-permute-start = (f32[6,1280]{1,0:T(8,128)S(1)}, f32[6,1280]{1,0:T(8,128)S(1)}, u32[]{:S(2)}, u32[]{:S(2)}) collective-permute-start(f32[6,1280]{1,0:T(8,128)S(1)} %get-tuple-element.18), channel_id=1, source_target_pairs={{0,4},{4,8},{8,12},{12,0},{1,5},{5,9},{9,13},{13,1},{2,6},{6,10},{... | collective-permute-start | bytes 92168 | tf_op jit(solution)/shard_map/ppermute | solution.py:391
  5.5 2.1 %collective-permute-start.1 = (f32[6,1280]{1,0:T(8,128)S(1)}, f32[6,1280]{1,0:T(8,128)S(1)}, u32[]{:S(2)}, u32[]{:S(2)}) collective-permute-start(f32[6,1280]{1,0:T(8,128)S(1)} %get-tuple-element.19), channel_id=1, source_target_pairs={{0,12},{4,0},{8,4},{12,8},{1,13},{5,1},{9,5},{13,9},{2,14},{6,2},{... | collective-permute-start | bytes 92168 | tf_op jit(solution)/shard_map/ppermute | solution.py:391
  7.5 0.9 collective-permute-start.2
  8.5 3.6 %collective-permute-done.2.far_ref = f32[6,256]{1,0:T(8,128)S(1)} collective-permute-done((f32[6,256]{1,0:T(8,128)S(1)}, f32[6,256]{1,0:T(8,128)S(1)}, u32[]{:S(2)}, u32[]{:S(2)}) %collective-permute-start.2) | collective-permute-done | bytes 6176 | tf_op jit(solution)/shard_map/ppermute | solution.py:391
  12.1 0.0 collective-permute-done.low_ref
  12.1 0.0 collective-permute-done.1.high_ref
  12.1 0.0 copy-done.5
  12.1 0.0 copy-done.6
  12.1 0.0 copy-done.7
  12.1 0.0 copy-start
  12.1 0.0 copy-start.3
  12.2 2.4 %first.1 = (f32[6,128,256]{2,1,0:T(8,128)S(1)}, f32[6,512]{1,0:T(8,128)S(1)}, f32[6,512]{1,0:T(8,128)S(1)}, f32[6,256]{1,0:T(8,128)S(1)}) custom-call(bf16[6,128,1024]{2,1,0:T(8,128)(2,1)S(1)} %copy-done.1, f32[6,1280]{1,0:T(8,128)S(1)} %collective-permute-done.low_ref, f32[6,1280]{1,0:T(8,128)S(1)} %collective-permute-done.1.high_ref, ...), custom_call_target="tpu_custom_call" | custom-call | flops 1207959552 | tf_op jit(solution)/shard_map/first/pallas_call | solution.py:369
  14.5 0.0 copy-start.2
  14.5 0.1 collective-permute-start.3
  14.6 3.8 %collective-permute-start.4 = (f32[6,512]{1,0:T(8,128)S(1)}, f32[6,512]{1,0:T(8,128)S(1)}, u32[]{:S(2)}, u32[]{:S(2)}) collective-permute-start(f32[6,512]{1,0:T(8,128)S(1)} %get-tuple-element.23), channel_id=1, source_target_pairs={{0,12},{4,0},{8,4},{12,8},{1,13},{5,1},{9,5},{13,9},{2,14},{6,2},{... | collective-permute-start | bytes 36872 | tf_op jit(solution)/shard_map/ppermute | solution.py:391
  18.4 0.0 collective-permute-start.5
  18.4 4.5 %collective-permute-done.5.far_ref = f32[6,256]{1,0:T(8,128)S(1)} collective-permute-done((f32[6,256]{1,0:T(8,128)S(1)}, f32[6,256]{1,0:T(8,128)S(1)}, u32[]{:S(2)}, u32[]{:S(2)}) %collective-permute-start.5) | collective-permute-done | bytes 6176 | tf_op jit(solution)/shard_map/ppermute | solution.py:391
  23.0 0.0 collective-permute-done.3.low_ref
  23.0 0.0 collective-permute-done.4.high_ref
  23.0 0.0 copy-done
  23.0 0.0 copy-done.3
  23.0 1.1 %second_other.1 = (bf16[192,1024]{1,0:T(8,128)(2,1)S(1)}, bf16[192,1024]{1,0:T(8,128)(2,1)S(1)}) custom-call(f32[6,128,256]{2,1,0:T(8,128)S(1)} %get-tuple-element.21.hid_ref, f32[6,512]{1,0:T(8,128)S(1)} %collective-permute-done.3.low_ref, f32[6,512]{1,0:T(8,128)S(1)} %collective-permute-done.4.high_ref, f32[6,256]{1,0:T(8,128)S(1)} %collective-permute-done.5.far_ref, ...), custom_call_target="tpu_custom_call" | custom-call | flops 603979776 | tf_op jit(solution)/shard_map/second_other/pallas_call | solution.py:369
  24.1 0.1 collective-permute-start.7
  24.2 0.0 copy-done.2
  24.2 1.7 %collective-permute-start.10 = (bf16[3,1024,256]{2,1,0:T(8,128)(2,1)S(1)}, bf16[3,1024,256]{2,1,0:T(8,128)(2,1)S(1)}, u32[]{:S(2)}, u32[]{:S(2)}) collective-permute-start(bf16[3,1024,256]{2,1,0:T(8,128)(2,1)S(1)} %bitcast.11), channel_id=1, source_target_pairs={{0,2},{2,0},{1,3},{3,1},{4,6},{6,4},{5,7},{7,5},{8,10},{10,8},{9,1... | collective-permute-start | bytes 4718600 | tf_op jit(solution)/shard_map/ppermute | solution.py:386
  26.0 1.9 %second_own.1 = (bf16[192,1024]{1,0:T(8,128)(2,1)}, bf16[192,1024]{1,0:T(8,128)(2,1)S(1)}) custom-call(f32[6,128,256]{2,1,0:T(8,128)S(1)} %get-tuple-element.21.hid_ref, f32[6,512]{1,0:T(8,128)S(1)} %collective-permute-done.3.low_ref, f32[6,512]{1,0:T(8,128)S(1)} %collective-permute-done.4.high_ref, f32[6,256]{1,0:T(8,128)S(1)} %collective-permute-done.5.far_ref, ...), custom_call_target="tpu_custom_call" | custom-call | flops 603979776 | tf_op jit(solution)/shard_map/second_own/pallas_call | solution.py:369
  27.8 0.1 collective-permute-start.6
  28.0 0.0 collective-permute-done.7
  28.0 0.9 add_convert_fusion
  28.9 0.4 collective-permute-start.8
  29.2 1.7 %collective-permute-start.11 = (bf16[256,1024]{1,0:T(8,128)(2,1)}, bf16[256,1024]{1,0:T(8,128)(2,1)}, u32[]{:S(2)}, u32[]{:S(2)}) collective-permute-start(bf16[256,1024]{1,0:T(8,128)(2,1)} %out_ref.1), channel_id=1, source_target_pairs={{0,2},{2,0},{1,3},{3,1},{4,6},{6,4},{5,7},{7,5},{8,10},{10,8},{9,1... | collective-permute-start | bytes 1572872 | tf_op jit(solution)/shard_map/ppermute | solution.py:386
  30.9 1.0 %constant_dynamic-slice_fusion = bf16[3,64,1024]{2,1,0:T(8,128)(2,1)S(1)} fusion(bf16[6,128,1024]{2,1,0:T(8,128)(2,1)} %lat_ref.3, s32[]{:T(128)S(6)} %select_n.18, s32[]{:T(128)S(6)} %select_n.20), kind=kLoop, calls=%fused_computation.7 | loop fusion | bytes 786440 | tf_op jit(solution)/shard_map/dynamic_slice | solution.py:448
  31.9 0.0 collective-permute-done.6
  31.9 38.2 %collective-permute-done.8 = bf16[192,1024]{1,0:T(8,128)(2,1)} collective-permute-done((bf16[192,1024]{1,0:T(8,128)(2,1)}, bf16[192,1024]{1,0:T(8,128)(2,1)}, u32[]{:S(2)}, u32[]{:S(2)}) %collective-permute-start.8) | collective-permute-done | bytes 393248 | tf_op jit(solution)/shard_map/ppermute | solution.py:386
  70.1 1.4 %fusion.2.mine_ref = bf16[192,1024]{1,0:T(8,128)(2,1)S(1)} fusion(bf16[192,1024]{1,0:T(8,128)(2,1)} %collective-permute-done.8, bf16[192,1024]{1,0:T(8,128)(2,1)} %collective-permute-done.6, bf16[192,1024]{1,0:T(8,128)(2,1)S(1)} %get-tuple-element.25, bf16[3,64,1024]{2,1,0:T(8,128)(2,1)S(1)} %constant_dynamic-slice_fusion), kind=kLoop, calls=%fused_computation.3 | loop fusion | flops 1572864 | bytes 1966080 | tf_op jit(solution)/shard_map/convert_element_type | solution.py:453
  71.5 0.1 collective-permute-start.9
  71.6 9.2 %collective-permute-done.11.out_far_ref = bf16[256,1024]{1,0:T(8,128)(2,1)} collective-permute-done((bf16[256,1024]{1,0:T(8,128)(2,1)}, bf16[256,1024]{1,0:T(8,128)(2,1)}, u32[]{:S(2)}, u32[]{:S(2)}) %collective-permute-start.11) | collective-permute-done | bytes 524320 | tf_op jit(solution)/shard_map/ppermute | solution.py:386
  80.8 0.0 collective-permute-done.9.theirs_ref
  80.8 0.0 collective-permute-done.10.qkv_far_ref
  80.8 9.0 %attention.1 = (bf16[384,512]{1,0:T(8,128)(2,1)S(1)}, f32[384,512]{1,0:T(8,128)S(1)}) custom-call(bf16[192,1024]{1,0:T(8,128)(2,1)S(1)} %fusion.2.mine_ref, bf16[192,1024]{1,0:T(8,128)(2,1)S(1)} %collective-permute-done.9.theirs_ref, f32[1,1024]{1,0:T(1,128)S(1)} %bitcast.15, bf16[3,1024,256]{2,1,0:T(8,128)(2,1)S(1)} %bitcast.12, ...), custom_call_target="tpu_custom_call" | custom-call | flops 1207959552 | tf_op jit(solution)/shard_map/attention/pallas_call | solution.py:369
  89.8 0.1 collective-permute-start.12
  89.9 1.7 %collective-permute-done.12 = bf16[384,512]{1,0:T(8,128)(2,1)S(1)} collective-permute-done((bf16[384,512]{1,0:T(8,128)(2,1)S(1)}, bf16[384,512]{1,0:T(8,128)(2,1)S(1)}, u32[]{:S(2)}, u32[]{:S(2)}) %collective-permute-start.12) | collective-permute-done | bytes 393248 | tf_op jit(solution)/shard_map/ppermute | solution.py:382
  91.6 0.1 add_convert_fusion.1
  91.7 1.7 %collective-permute-start.13 = (bf16[384,256]{1,0:T(8,128)(2,1)S(1)}, bf16[384,256]{1,0:T(8,128)(2,1)S(1)}, u32[]{:S(2)}, u32[]{:S(2)}) collective-permute-start(bf16[384,256]{1,0:T(8,128)(2,1)S(1)} %get-tuple-element.31), channel_id=1, source_target_pairs={{0,2},{2,0},{1,3},{3,1},{4,6},{6,4},{5,7},{7,5},{8,10},{10,8},{9,1... | collective-permute-start | bytes 589832 | tf_op jit(solution)/shard_map/ppermute | solution.py:386
  93.4 5.3 %collective-permute-done.13.far_ref = bf16[384,256]{1,0:T(8,128)(2,1)S(1)} collective-permute-done((bf16[384,256]{1,0:T(8,128)(2,1)S(1)}, bf16[384,256]{1,0:T(8,128)(2,1)S(1)}, u32[]{:S(2)}, u32[]{:S(2)}) %collective-permute-start.13) | collective-permute-done | bytes 196640 | tf_op jit(solution)/shard_map/ppermute | solution.py:386
  98.7 0.8 place.1
  (6 shorter events, 0.0 us)
Async XLA Ops:
  0.0 1.4 %copy-start.1 = (bf16[6,128,1024]{2,1,0:T(8,128)(2,1)S(1)}, bf16[6,128,1024]{2,1,0:T(8,128)(2,1)}, u32[]{:S(2)}) copy-start(bf16[6,128,1024]{2,1,0:T(8,128)(2,1)} %lat_ref.3) | copy-start | bytes 4718596
  1.4 10.7 %copy-start.5 = (bf16[3,1024,256]{2,1,0:T(8,128)(2,1)S(1)}, bf16[3,1024,256]{2,1,0:T(8,128)(2,1)}, u32[]{:S(2)}) copy-start(bf16[3,1024,256]{2,1,0:T(8,128)(2,1)} %weight_ref.1) | copy-start | bytes 4718596
  1.4 10.7 %copy-start.6 = (f32[1024]{0:T(1024)S(1)}, f32[1024]{0:T(1024)}, u32[]{:S(2)}) copy-start(f32[1024]{0:T(1024)} %param.10) | copy-start | bytes 12292
  1.4 10.7 %copy-start.7 = (f32[256]{0:T(256)S(1)}, f32[256]{0:T(256)}, u32[]{:S(2)}) copy-start(f32[256]{0:T(256)} %param.12) | copy-start | bytes 3076
  2.4 9.7 %collective-permute-start = (f32[6,1280]{1,0:T(8,128)S(1)}, f32[6,1280]{1,0:T(8,128)S(1)}, u32[]{:S(2)}, u32[]{:S(2)}) collective-permute-start(f32[6,1280]{1,0:T(8,128)S(1)} %get-tuple-element.18), channel_id=1, source_target_pairs={{0,4},{4,8},{8,12},{12,0},{1,5},{5,9},{9,13},{13,1},{2,6},{6,10},{... | collective-permute-start | bytes 92168 | tf_op jit(solution)/shard_map/ppermute | solution.py:391
  5.5 6.6 %collective-permute-start.1 = (f32[6,1280]{1,0:T(8,128)S(1)}, f32[6,1280]{1,0:T(8,128)S(1)}, u32[]{:S(2)}, u32[]{:S(2)}) collective-permute-start(f32[6,1280]{1,0:T(8,128)S(1)} %get-tuple-element.19), channel_id=1, source_target_pairs={{0,12},{4,0},{8,4},{12,8},{1,13},{5,1},{9,5},{13,9},{2,14},{6,2},{... | collective-permute-start | bytes 92168 | tf_op jit(solution)/shard_map/ppermute | solution.py:391
  7.5 4.5 %collective-permute-start.2 = (f32[6,256]{1,0:T(8,128)S(1)}, f32[6,256]{1,0:T(8,128)S(1)}, u32[]{:S(2)}, u32[]{:S(2)}) collective-permute-start(f32[6,256]{1,0:T(8,128)S(1)} %get-tuple-element.20.own_ref), channel_id=1, source_target_pairs={{0,8},{4,12},{8,0},{12,4},{1,9},{5,13},{9,1},{13,5},{2,10},{6,14},... | collective-permute-start | bytes 18440 | tf_op jit(solution)/shard_map/ppermute | solution.py:391
  12.1 10.8 %copy-start = (bf16[3,256,1024]{2,1,0:T(8,128)(2,1)S(1)}, bf16[3,256,1024]{2,1,0:T(8,128)(2,1)}, u32[]{:S(2)}) copy-start(bf16[3,256,1024]{2,1,0:T(8,128)(2,1)} %param.14) | copy-start | bytes 4718596
  12.1 10.8 %copy-start.3 = (f32[256]{0:T(256)S(1)}, f32[256]{0:T(256)}, u32[]{:S(2)}) copy-start(f32[256]{0:T(256)} %param.13) | copy-start | bytes 3076
  14.5 9.7 %copy-start.2 = (bf16[1024,3,256]{2,0,1:T(8,128)(2,1)S(1)}, bf16[1024,3,256]{2,0,1:T(8,128)(2,1)}, u32[]{:S(2)}) copy-start(bf16[1024,3,256]{2,0,1:T(8,128)(2,1)} %param.16) | copy-start | bytes 4718596
  14.5 8.4 %collective-permute-start.3 = (f32[6,512]{1,0:T(8,128)S(1)}, f32[6,512]{1,0:T(8,128)S(1)}, u32[]{:S(2)}, u32[]{:S(2)}) collective-permute-start(f32[6,512]{1,0:T(8,128)S(1)} %get-tuple-element.22), channel_id=1, source_target_pairs={{0,4},{4,8},{8,12},{12,0},{1,5},{5,9},{9,13},{13,1},{2,6},{6,10},{... | collective-permute-start | bytes 36872 | tf_op jit(solution)/shard_map/ppermute | solution.py:391
  14.6 8.3 %collective-permute-start.4 = (f32[6,512]{1,0:T(8,128)S(1)}, f32[6,512]{1,0:T(8,128)S(1)}, u32[]{:S(2)}, u32[]{:S(2)}) collective-permute-start(f32[6,512]{1,0:T(8,128)S(1)} %get-tuple-element.23), channel_id=1, source_target_pairs={{0,12},{4,0},{8,4},{12,8},{1,13},{5,1},{9,5},{13,9},{2,14},{6,2},{... | collective-permute-start | bytes 36872 | tf_op jit(solution)/shard_map/ppermute | solution.py:391
  18.4 4.5 %collective-permute-start.5 = (f32[6,256]{1,0:T(8,128)S(1)}, f32[6,256]{1,0:T(8,128)S(1)}, u32[]{:S(2)}, u32[]{:S(2)}) collective-permute-start(f32[6,256]{1,0:T(8,128)S(1)} %get-tuple-element.24.own_ref), channel_id=1, source_target_pairs={{0,8},{4,12},{8,0},{12,4},{1,9},{5,13},{9,1},{13,5},{2,10},{6,14},... | collective-permute-start | bytes 18440 | tf_op jit(solution)/shard_map/ppermute | solution.py:391
  24.1 3.8 %collective-permute-start.7 = (bf16[192,1024]{1,0:T(8,128)(2,1)S(1)}, bf16[192,1024]{1,0:T(8,128)(2,1)S(1)}, u32[]{:S(2)}, u32[]{:S(2)}) collective-permute-start(bf16[192,1024]{1,0:T(8,128)(2,1)S(1)} %get-tuple-element.27), channel_id=1, source_target_pairs={{0,1},{1,0},{2,3},{3,2},{4,5},{5,4},{6,7},{7,6},{8,9},{9,8},{10,11... | collective-permute-start | bytes 1179656 | tf_op jit(solution)/shard_map/ppermute | solution.py:382
  24.2 56.6 %collective-permute-start.10 = (bf16[3,1024,256]{2,1,0:T(8,128)(2,1)S(1)}, bf16[3,1024,256]{2,1,0:T(8,128)(2,1)S(1)}, u32[]{:S(2)}, u32[]{:S(2)}) collective-permute-start(bf16[3,1024,256]{2,1,0:T(8,128)(2,1)S(1)} %bitcast.11), channel_id=1, source_target_pairs={{0,2},{2,0},{1,3},{3,1},{4,6},{6,4},{5,7},{7,5},{8,10},{10,8},{9,1... | collective-permute-start | bytes 4718600 | tf_op jit(solution)/shard_map/ppermute | solution.py:386
  27.8 4.1 %collective-permute-start.6 = (bf16[192,1024]{1,0:T(8,128)(2,1)}, bf16[192,1024]{1,0:T(8,128)(2,1)}, u32[]{:S(2)}, u32[]{:S(2)}) collective-permute-start(bf16[192,1024]{1,0:T(8,128)(2,1)} %get-tuple-element.26), channel_id=1, source_target_pairs={{0,1},{1,0},{2,3},{3,2},{4,5},{5,4},{6,7},{7,6},{8,9},{9,8},{10,11... | collective-permute-start | bytes 1179656 | tf_op jit(solution)/shard_map/ppermute | solution.py:382
  28.9 51.9 %copy-start.4 = (f32[1024]{0:T(1024)S(1)}, f32[1024]{0:T(1024)}, u32[]{:S(2)}) copy-start(f32[1024]{0:T(1024)} %param.15) | copy-start | bytes 12292
  28.9 41.2 %collective-permute-start.8 = (bf16[192,1024]{1,0:T(8,128)(2,1)}, bf16[192,1024]{1,0:T(8,128)(2,1)}, u32[]{:S(2)}, u32[]{:S(2)}) collective-permute-start(bf16[192,1024]{1,0:T(8,128)(2,1)} %add_convert_fusion), channel_id=1, source_target_pairs={{0,2},{2,0},{1,3},{3,1},{4,6},{6,4},{5,7},{7,5},{8,10},{10,8},{9,1... | collective-permute-start | bytes 1179656 | tf_op jit(solution)/shard_map/ppermute | solution.py:386
  29.2 51.5 %collective-permute-start.11 = (bf16[256,1024]{1,0:T(8,128)(2,1)}, bf16[256,1024]{1,0:T(8,128)(2,1)}, u32[]{:S(2)}, u32[]{:S(2)}) collective-permute-start(bf16[256,1024]{1,0:T(8,128)(2,1)} %out_ref.1), channel_id=1, source_target_pairs={{0,2},{2,0},{1,3},{3,1},{4,6},{6,4},{5,7},{7,5},{8,10},{10,8},{9,1... | collective-permute-start | bytes 1572872 | tf_op jit(solution)/shard_map/ppermute | solution.py:386
  71.5 9.3 %collective-permute-start.9 = (bf16[192,1024]{1,0:T(8,128)(2,1)S(1)}, bf16[192,1024]{1,0:T(8,128)(2,1)S(1)}, u32[]{:S(2)}, u32[]{:S(2)}) collective-permute-start(bf16[192,1024]{1,0:T(8,128)(2,1)S(1)} %fusion.2.mine_ref), channel_id=1, source_target_pairs={{0,1},{1,0},{2,3},{3,2},{4,5},{5,4},{6,7},{7,6},{8,9},{9,8},{10,11... | collective-permute-start | bytes 1179656 | tf_op jit(solution)/shard_map/ppermute | solution.py:382
  89.8 1.8 %collective-permute-start.12 = (bf16[384,512]{1,0:T(8,128)(2,1)S(1)}, bf16[384,512]{1,0:T(8,128)(2,1)S(1)}, u32[]{:S(2)}, u32[]{:S(2)}) collective-permute-start(bf16[384,512]{1,0:T(8,128)(2,1)S(1)} %get-tuple-element.30), channel_id=1, source_target_pairs={{0,1},{1,0},{2,3},{3,2},{4,5},{5,4},{6,7},{7,6},{8,9},{9,8},{10,11... | collective-permute-start | bytes 1179656 | tf_op jit(solution)/shard_map/ppermute | solution.py:382
  91.7 7.0 %collective-permute-start.13 = (bf16[384,256]{1,0:T(8,128)(2,1)S(1)}, bf16[384,256]{1,0:T(8,128)(2,1)S(1)}, u32[]{:S(2)}, u32[]{:S(2)}) collective-permute-start(bf16[384,256]{1,0:T(8,128)(2,1)S(1)} %get-tuple-element.31), channel_id=1, source_target_pairs={{0,2},{2,0},{1,3},{3,1},{4,6},{6,4},{5,7},{7,5},{8,10},{10,8},{9,1... | collective-permute-start | bytes 589832 | tf_op jit(solution)/shard_map/ppermute | solution.py:386

commit v2 on v1

--- a/solution.py
+++ b/solution.py
@@ -7,6 +7,7 @@
 from jax.experimental import pallas as pl
 from jax.experimental.pallas import tpu as pltpu
 from jax.sharding import PartitionSpec as P
+
 
 GROUPS = 32
 HEAD_DIM = 64
@@ -249,7 +250,7 @@
     hid_ref, low_ref, high_ref, far_ref, own_ref, gain_ref, weight_ref,
     send_ref, keep_ref, act_ref,
 ):
-    stems, frames, shard = hid_ref.shape
+    stems, _, shard = hid_ref.shape
     place = lax.axis_index("frame")
     index = lax.axis_index("tensor")
     chip, core = index // 2, index % 2
@@ -293,11 +294,15 @@
 
 
 def attention_kernel(
-    mine_ref, theirs_ref, gain_ref, qkv_ref, qkv_far_ref, out_ref, out_far_ref,
+    mine_ref, theirs_ref, gain_ref, qkv_ref, out_ref,
+    heads_x_ref, rest_x_ref, heads_y_ref, rest_y_ref,
     send_ref, keep_ref, res_ref, normed_ref, context_ref,
 ):
     rows, channels = mine_ref.shape
     shard = qkv_ref.shape[2]
+    depth = channels // 2
+    part = shard // 2
+    group = lax.axis_index("groups")
     index = lax.axis_index("tensor")
     chip, core = index // 2, index % 2
     for first, ref in ((0, mine_ref), (rows, theirs_ref)):
@@ -311,10 +316,19 @@
     lane = lax.broadcasted_iota(jnp.int32, (2 * rows, LANES), 1)
     per_tile = LANES // HEAD_DIM
     nt = (((1,), (1,)), ((), ()))
-    for side, ref in enumerate((qkv_ref, qkv_far_ref)):
-        queries, keys, values = [
-            jnp.dot(normed, ref[which], preferred_element_type=f32) for which in range(3)
-        ]
+    near_at = pl.ds(pl.multiple_of(group * depth, depth), depth)
+    away_at = pl.ds(pl.multiple_of((1 - group) * depth, depth), depth)
+
+    def project(side, which):
+        if side == 0:
+            return jnp.dot(normed, qkv_ref[which], preferred_element_type=f32)
+        from_x = heads_x_ref[which] if which < 2 else rest_x_ref[0]
+        from_y = heads_y_ref[which] if which < 2 else rest_y_ref[0]
+        near = jnp.dot(normed_ref[:, near_at], from_x, preferred_element_type=f32)
+        return near + jnp.dot(normed_ref[:, away_at], from_y, preferred_element_type=f32)
+
+    for side in range(2):
+        queries, keys, values = [project(side, which) for which in range(3)]
         queries = queries * (1.0 / math.sqrt(HEAD_DIM))
         values = values.astype(bf16)
         for tile in range(shard // LANES):
@@ -330,16 +344,20 @@
                 scores = jnp.exp(scores - jnp.max(scores, axis=1, keepdims=True))
                 total = jnp.sum(scores, axis=1, keepdims=True)
                 probs = (scores / total).astype(bf16)
-                part = jnp.dot(probs, values[:, at], preferred_element_type=f32)
-                result = part if result is None else jnp.where(inside, part, result)
+                mixed = jnp.dot(probs, values[:, at], preferred_element_type=f32)
+                result = mixed if result is None else jnp.where(inside, mixed, result)
             base = side * shard + tile * LANES
             context_ref[:, base : base + LANES] = result.astype(bf16)
-    context = context_ref[...]
+    context = context_ref[:, :shard]
+    from_x = context_ref[:, pl.ds(pl.multiple_of(shard + group * part, part), part)]
+    from_y = context_ref[:, pl.ds(pl.multiple_of(shard + (1 - group) * part, part), part)]
 
     def term(block):
         at = pl.ds(pl.multiple_of(block * shard, shard), shard)
-        near = jnp.dot(context[:, :shard], out_ref[:, at], preferred_element_type=f32)
-        return near + jnp.dot(context[:, shard:], out_far_ref[:, at], preferred_element_type=f32)
+        rows_at = pl.ds(pl.multiple_of(block * part, part), part)
+        value = jnp.dot(context, out_ref[:, at], preferred_element_type=f32)
+        value = value + jnp.dot(from_x, rest_x_ref[1, rows_at, :], preferred_element_type=f32)
+        return value + jnp.dot(from_y, rest_y_ref[1, rows_at, :], preferred_element_type=f32)
 
     for place, goal in enumerate((1 - chip, chip)):
         at = slice(place * shard, (place + 1) * shard)
@@ -351,8 +369,48 @@
         keep_ref[:, at] = kept + res_ref[:, pl.ds(pl.multiple_of(block * shard, shard), shard)]
 
 
+def pack_heads_kernel(qkv_ref, send_ref, sem):
+    depth = send_ref.shape[1]
+    start = pl.multiple_of(lax.axis_index("groups") * depth, depth)
+    copy = pltpu.make_async_copy(qkv_ref.at[pl.ds(0, 2), pl.ds(start, depth), :], send_ref, sem)
+    copy.start()
+    copy.wait()
+
+
+def pack_rest_kernel(qkv_ref, out_ref, send_ref, sems):
+    depth, shard = send_ref.shape[1:]
+    part = shard // 2
+    group = lax.axis_index("groups")
+    at = pl.ds(pl.multiple_of(group * depth, depth), depth)
+    copies = [pltpu.make_async_copy(qkv_ref.at[2, at, :], send_ref.at[0], sems.at[0])]
+    rows = pl.ds(pl.multiple_of(group * part, part), part)
+    for block in range(depth // part):
+        copies.append(
+            pltpu.make_async_copy(
+                out_ref.at[rows, pl.ds(block * shard, shard)],
+                send_ref.at[1, pl.ds(block * part, part), :],
+                sems.at[1 + block],
+            )
+        )
+    for copy in copies:
+        copy.start()
+    for copy in copies:
+        copy.wait()
+
+
+def pack(kernel, shape, copies, args):
+    return pl.pallas_call(
+        kernel,
+        out_shape=jax.ShapeDtypeStruct(shape, bf16),
+        in_specs=[pl.BlockSpec(memory_space=pl.ANY)] * len(args),
+        out_specs=pl.BlockSpec(memory_space=VMEM),
+        scratch_shapes=[pltpu.SemaphoreType.DMA(copies)],
+        cost_estimate=pl.CostEstimate(flops=0, bytes_accessed=2**20, transcendentals=0),
+    )(*args)
+
+
 def place_kernel(own_ref, far_ref, out_ref):
-    stems, frames, shard = out_ref.shape
+    stems, _, _ = out_ref.shape
     index = lax.axis_index("tensor")
     chip, core = index // 2, index % 2
     half = stems // 2
@@ -365,10 +423,9 @@
         out_ref[goal, pl.ds(away, WINDOW), :] = far_ref[rows, :]
 
 
-def call(kernel, name, outs, scratch, args, flops=0, moved=0):
+def call(kernel, outs, scratch, args, flops=0, moved=0):
     return pl.pallas_call(
         kernel,
-        name=name,
         out_shape=[jax.ShapeDtypeStruct(shape, dtype) for shape, dtype in outs],
         in_specs=[pl.BlockSpec(memory_space=VMEM)] * len(args),
         out_specs=[pl.BlockSpec(memory_space=VMEM)] * len(outs),
@@ -386,13 +443,17 @@
     return lax.ppermute(value, "tensor", [(0, 2), (2, 0), (1, 3), (3, 1)])
 
 
+def swap_groups(value):
+    return lax.ppermute(value, "groups", [(0, 1), (1, 0)])
+
+
 def shift_frames(value, by):
     count = lax.axis_size("frame")
     return lax.ppermute(value, "frame", [(i, (i + by) % count) for i in range(count)])
 
 
 def exchange(up, down, own):
-    return shift_frames(up, 1), shift_frames(down, -1), shift_frames(own, 2)
+    return (shift_frames(up, 1), shift_frames(down, -1), shift_frames(own, 2))
 
 
 def fast(
@@ -406,11 +467,16 @@
     entries = frames * frame_size * width
     half_rows = stems // 2 * WINDOW
     qkv = jnp.transpose(qkv_weight, (1, 0, 2))
-    qkv_far = swap_chips(qkv)
-    out_far = swap_chips(out_weight)
+    depth, part = channels // 2, shard // 2
+    heads = pack(pack_heads_kernel, (2, depth, shard), (), [qkv])
+    rest = pack(pack_rest_kernel, (2, depth, shard), (1 + depth // part,), [qkv, out_weight])
+    heads_x = swap_chips(heads)
+    rest_x = swap_chips(rest)
+    heads_y = swap_groups(heads_x)
+    rest_y = swap_groups(rest_x)
     wide = channels + 2 * LANES
     up, down, own = call(
-        functools.partial(stats_kernel, width), "stats",
+        functools.partial(stats_kernel, width),
         [((stems, wide), f32), ((stems, wide), f32), ((stems, 2 * LANES), f32)],
         [((stems, channels), f32)] * 2,
         [latent],
@@ -418,7 +484,7 @@
     low, high, far = exchange(up, down, own)
     narrow = shard + 2 * LANES
     hid, up2, down2, own2 = call(
-        functools.partial(first_kernel, entries, width, frame_size), "first",
+        functools.partial(first_kernel, entries, width, frame_size),
         [((stems, frames, shard), f32), ((stems, narrow), f32), ((stems, narrow), f32),
          ((stems, 2 * LANES), f32)],
         [((stems * frames, channels), bf16), ((16, channels), f32)] + [((stems, shard), f32)] * 2,
@@ -431,7 +497,6 @@
     def second(other):
         return call(
             functools.partial(second_kernel, entries, width, frame_size, other),
-            "second_other" if other else "second_own",
             [((half_rows, channels), bf16)] * 2,
             [((2 * half_rows, 3 * shard), bf16)],
             [hid, low2, high2, far2, own2, norm2_gain[None], weight2],
@@ -439,7 +504,8 @@
         )
 
     send, keep = second(True)
-    summed = (swap_cores(send).astype(f32) + keep.astype(f32)).astype(bf16)
+    got = swap_cores(send)
+    summed = (got.astype(f32) + keep.astype(f32)).astype(bf16)
     summed = swap_chips(summed)
     send_own, keep_own = second(False)
     got_own = swap_cores(send_own)
@@ -453,20 +519,18 @@
     ).astype(bf16)
     theirs = swap_cores(mine)
     out_send, out_keep = call(
-        attention_kernel, "attention",
+        attention_kernel,
         [((2 * half_rows, 2 * shard), bf16), ((2 * half_rows, 2 * shard), f32)],
         [((2 * half_rows, channels), f32), ((2 * half_rows, channels), bf16),
          ((2 * half_rows, 2 * shard), bf16)],
-        [mine, theirs, attn_gain[None], qkv, qkv_far, out_weight, out_far],
+        [mine, theirs, attn_gain[None], qkv, out_weight, heads_x, rest_x, heads_y, rest_y],
         flops=24 * half_rows * channels * shard,
     )
     out_got = swap_cores(out_send)
     away = (out_keep[:, :shard] + out_got[:, :shard].astype(f32)).astype(bf16)
     stay = (out_keep[:, shard:] + out_got[:, shard:].astype(f32)).astype(bf16)
     arrived = swap_chips(away)
-    return call(
-        place_kernel, "place", [((stems, frames, shard), bf16)], [], [stay, arrived]
-    )[0]
+    return call(place_kernel, [((stems, frames, shard), bf16)], [], [stay, arrived])[0]
 
 
 def local(*args):
@@ -477,12 +541,15 @@
     suits = (
         tensor_size == 4
         and frame_size == 4
+        and lax.axis_size("groups") == 2
         and frames == 2 * WINDOW
         and stems % 2 == 0
         and stems <= 8
         and shard % (2 * LANES) == 0
     )
-    return fast(*args) if suits else generic(*args)
+    if not suits:
+        return generic(*args)
+    return fast(*args)
 
 
 def solution(mesh):

time: 99.7 us -> 86.2 us (0.86)
  waiting for transfers between devices: 62.6 us -> 39.6 us
  Pallas kernels: 16.1 us -> 19.6 us
  starting transfers between devices: 15.8 us -> 19.1 us
  local copies, waits for them, and re-layouts: 2.46 us -> 4.64 us
    ppermute x4, waiting for transfers between devices: 52.7 us -> 26.3 us  [swap_chips(): return lax.ppermute(value, 'tensor', [(0, 2), (2, 0), (1, 3), (3, 1)])]
    pallas_call x6 -> x8, Pallas kernels: 16.1 us -> 19.6 us  [the longest x6 15.9 us: call(): pl.pallas_call(kernel, out_shape=[jax.ShapeDtypeStruct(shape, dtype) for...]
    ppermute x0 -> x2, waiting for transfers between devices: none -> 3.36 us  [swap_groups(): return lax.ppermute(value, 'groups', [(0, 1), (1, 0)])]
    ppermute x0 -> x2, starting transfers between devices: none -> 3.35 us  [swap_groups(): return lax.ppermute(value, 'groups', [(0, 1), (1, 0)])]
    unnamed x16 -> x26, local copies, waits for them, and re-layouts: 1.44 us -> 3.61 us
  transfers between devices with their start and end apart: 14 -> 16, of which waited for: 6 -> 8; matrix products, arithmetic and copies ran while one was open for 3% -> 4% of each run, Pallas kernels for 2% -> 6%
where the time goes in v2:
time: 86.2 us; the launch traced here: 85.9 us
  waiting for transfers between devices  39.6 us (46%)
  Pallas kernels  19.6 us (23%)
  starting transfers between devices  19.1 us (22%)
  local copies, waits for them, and re-layouts  4.64 us (5%)
  other arithmetic  2.85 us (3%)
    ppermute x4, waiting for transfers between devices, swap_chips(): return lax.ppermute(value, 'tensor', [(0, 2), (2, 0), (1, 3), (3, 1)])  26.3 us
    pallas_call x6, Pallas kernels, call(): pl.pallas_call(kernel, out_shape=[jax.ShapeDtypeStruct(shape, dtype) for...  15.9 us
    ppermute x6, starting transfers between devices, shift_frames(): lax.ppermute(value, 'frame', [(i, (i + by) % count) for i in range(count)])  10 us
    ppermute x6, waiting for transfers between devices, shift_frames(): lax.ppermute(value, 'frame', [(i, (i + by) % count) for i in range(count)])  8.16 us
    ppermute x4, starting transfers between devices, swap_chips(): return lax.ppermute(value, 'tensor', [(0, 2), (2, 0), (1, 3), (3, 1)])  5.58 us
    pallas_call x2, Pallas kernels, pack(): pl.pallas_call(kernel, out_shape=jax.ShapeDtypeStruct(shape, bf16), in_sp...  3.7 us
    unnamed x26, local copies, waits for them, and re-layouts  3.61 us
    ppermute x2, waiting for transfers between devices, swap_groups(): return lax.ppermute(value, 'groups', [(0, 1), (1, 0)])  3.36 us
  transfers between devices with their start and end apart: 16, of which 8 were waited for; matrix products, arithmetic and copies ran while one was open for 4% of the time, Pallas kernels for 6%

profile of v2, /device:TPU:0, one launch (start us, length us, event | category | flops | bytes accessed | tf_op | source)
XLA Modules:
  0.0 85.9 jit_solution(1929894075378723981)
XLA Ops:
  0.0 1.4 %copy-done.2 = bf16[6,128,1024]{2,1,0:T(8,128)(2,1)S(1)} copy-done((bf16[6,128,1024]{2,1,0:T(8,128)(2,1)S(1)}, bf16[6,128,1024]{2,1,0:T(8,128)(2,1)}, u32[]{:S(2)}) %copy-start.2) | copy-done | bytes 1572888
  1.4 0.9 %shard_map.91 = (f32[6,1280]{1,0:T(8,128)S(1)}, f32[6,1280]{1,0:T(8,128)S(1)}, f32[6,256]{1,0:T(8,128)S(1)}) custom-call(bf16[6,128,1024]{2,1,0:T(8,128)(2,1)S(1)} %copy-done.2), custom_call_target="tpu_custom_call" | custom-call | tf_op jit(solution)/shard_map/pallas_call | solution.py:427
  2.4 3.1 %collective-permute-start = (f32[6,1280]{1,0:T(8,128)S(1)}, f32[6,1280]{1,0:T(8,128)S(1)}, u32[]{:S(2)}, u32[]{:S(2)}) collective-permute-start(f32[6,1280]{1,0:T(8,128)S(1)} %get-tuple-element.18), channel_id=1, source_target_pairs={{0,4},{4,8},{8,12},{12,0},{1,5},{5,9},{9,13},{13,1},{2,6},{6,10},{... | collective-permute-start | bytes 92168 | tf_op jit(solution)/shard_map/ppermute | solution.py:452
  5.5 2.1 %collective-permute-start.1 = (f32[6,1280]{1,0:T(8,128)S(1)}, f32[6,1280]{1,0:T(8,128)S(1)}, u32[]{:S(2)}, u32[]{:S(2)}) collective-permute-start(f32[6,1280]{1,0:T(8,128)S(1)} %get-tuple-element.19), channel_id=1, source_target_pairs={{0,12},{4,0},{8,4},{12,8},{1,13},{5,1},{9,5},{13,9},{2,14},{6,2},{... | collective-permute-start | bytes 92168 | tf_op jit(solution)/shard_map/ppermute | solution.py:452
  7.5 0.9 %collective-permute-start.2 = (f32[6,256]{1,0:T(8,128)S(1)}, f32[6,256]{1,0:T(8,128)S(1)}, u32[]{:S(2)}, u32[]{:S(2)}) collective-permute-start(f32[6,256]{1,0:T(8,128)S(1)} %get-tuple-element.20.own_ref), channel_id=1, source_target_pairs={{0,8},{4,12},{8,0},{12,4},{1,9},{5,13},{9,1},{13,5},{2,10},{6,14},... | collective-permute-start | bytes 18440 | tf_op jit(solution)/shard_map/ppermute | solution.py:452
  8.5 3.6 %collective-permute-done.2.far_ref = f32[6,256]{1,0:T(8,128)S(1)} collective-permute-done((f32[6,256]{1,0:T(8,128)S(1)}, f32[6,256]{1,0:T(8,128)S(1)}, u32[]{:S(2)}, u32[]{:S(2)}) %collective-permute-start.2) | collective-permute-done | bytes 6176 | tf_op jit(solution)/shard_map/ppermute | solution.py:452
  12.1 0.0 collective-permute-done.low_ref
  12.1 0.0 copy-start.10
  12.1 1.4 %copy-done.10 = bf16[3,1024,256]{2,1,0:T(8,128)(2,1)S(1)} copy-done((bf16[3,1024,256]{2,1,0:T(8,128)(2,1)S(1)}, bf16[3,1024,256]{2,1,0:T(8,128)(2,1)}, u32[]{:S(2)}) %copy-start.10) | copy-done | bytes 1572888
  13.5 2.4 %shard_map.92 = (f32[6,128,256]{2,1,0:T(8,128)S(1)}, f32[6,512]{1,0:T(8,128)S(1)}, f32[6,512]{1,0:T(8,128)S(1)}, f32[6,256]{1,0:T(8,128)S(1)}) custom-call(bf16[6,128,1024]{2,1,0:T(8,128)(2,1)S(1)} %copy-done.3, f32[6,1280]{1,0:T(8,128)S(1)} %collective-permute-done.low_ref, f32[6,1280]{1,0:T(8,128)S(1)} %collective-permute-done.1.high_ref, ...), custom_call_target="tpu_custom_call" | custom-call | flops 1207959552 | tf_op jit(solution)/shard_map/pallas_call | solution.py:427
  16.0 0.1 collective-permute-start.3
  16.1 3.8 %collective-permute-start.4 = (f32[6,512]{1,0:T(8,128)S(1)}, f32[6,512]{1,0:T(8,128)S(1)}, u32[]{:S(2)}, u32[]{:S(2)}) collective-permute-start(f32[6,512]{1,0:T(8,128)S(1)} %get-tuple-element.23), channel_id=1, source_target_pairs={{0,12},{4,0},{8,4},{12,8},{1,13},{5,1},{9,5},{13,9},{2,14},{6,2},{... | collective-permute-start | bytes 36872 | tf_op jit(solution)/shard_map/ppermute | solution.py:452
  19.9 0.0 collective-permute-start.5
  19.9 4.5 %collective-permute-done.5.far_ref = f32[6,256]{1,0:T(8,128)S(1)} collective-permute-done((f32[6,256]{1,0:T(8,128)S(1)}, f32[6,256]{1,0:T(8,128)S(1)}, u32[]{:S(2)}, u32[]{:S(2)}) %collective-permute-start.5) | collective-permute-done | bytes 6176 | tf_op jit(solution)/shard_map/ppermute | solution.py:452
  24.4 0.0 collective-permute-done.3.low_ref
  24.4 0.0 collective-permute-done.4.high_ref
  24.4 1.9 %shard_map.94 = (bf16[192,1024]{1,0:T(8,128)(2,1)}, bf16[192,1024]{1,0:T(8,128)(2,1)S(1)}) custom-call(f32[6,128,256]{2,1,0:T(8,128)S(1)} %get-tuple-element.21.hid_ref, f32[6,512]{1,0:T(8,128)S(1)} %collective-permute-done.3.low_ref, f32[6,512]{1,0:T(8,128)S(1)} %collective-permute-done.4.high_ref, f32[6,256]{1,0:T(8,128)S(1)} %collective-permute-done.5.far_ref, ...), custom_call_target="tpu_custom_call" | custom-call | flops 603979776 | tf_op jit(solution)/shard_map/pallas_call | solution.py:427
  26.3 0.8 copy-done.5
  27.1 0.0 collective-permute-start.7
  27.1 1.8 %shard_map.95 = bf16[2,512,256]{2,1,0:T(8,128)(2,1)} custom-call(bf16[3,1024,256]{2,1,0:T(8,128)(2,1)} %bitcast.9), custom_call_target="tpu_custom_call" | custom-call | bytes 1048576 | tf_op jit(solution)/shard_map/pallas_call | solution.py:402
  28.9 1.7 %collective-permute-start.10 = (bf16[2,512,256]{2,1,0:T(8,128)(2,1)}, bf16[2,512,256]{2,1,0:T(8,128)(2,1)S(1)}, u32[]{:S(2)}, u32[]{:S(2)}) collective-permute-start(bf16[2,512,256]{2,1,0:T(8,128)(2,1)} %shard_map.95), channel_id=1, source_target_pairs={{0,2},{2,0},{1,3},{3,1},{4,6},{6,4},{5,7},{7,5},{8,10},{10,8},{9,1... | collective-permute-start | bytes 1572872 | tf_op jit(solution)/shard_map/ppermute | solution.py:443
  30.6 1.9 %shard_map.96 = bf16[2,512,256]{2,1,0:T(8,128)(2,1)} custom-call(bf16[3,1024,256]{2,1,0:T(8,128)(2,1)} %bitcast.10, bf16[256,1024]{1,0:T(8,128)(2,1)} %out_ref.3), custom_call_target="tpu_custom_call" | custom-call | bytes 1048576 | tf_op jit(solution)/shard_map/pallas_call | solution.py:402
  32.5 0.4 collective-permute-start.11
  33.0 1.9 %shard_map.93 = (bf16[192,1024]{1,0:T(8,128)(2,1)}, bf16[192,1024]{1,0:T(8,128)(2,1)S(1)}) custom-call(f32[6,128,256]{2,1,0:T(8,128)S(1)} %get-tuple-element.21.hid_ref, f32[6,512]{1,0:T(8,128)S(1)} %collective-permute-done.3.low_ref, f32[6,512]{1,0:T(8,128)S(1)} %collective-permute-done.4.high_ref, f32[6,256]{1,0:T(8,128)S(1)} %collective-permute-done.5.far_ref, ...), custom_call_target="tpu_custom_call" | custom-call | flops 603979776 | tf_op jit(solution)/shard_map/pallas_call | solution.py:427
  34.8 0.0 collective-permute-start.6
  34.8 0.0 collective-permute-done.7
  34.9 1.3 %add_convert_fusion = bf16[192,1024]{1,0:T(8,128)(2,1)S(1)} fusion(bf16[192,1024]{1,0:T(8,128)(2,1)S(1)} %copy-done.6, bf16[192,1024]{1,0:T(8,128)(2,1)} %collective-permute-done.7), kind=kLoop, calls=%fused_computation.4 | loop fusion | flops 786432 | bytes 1179648 | tf_op jit(solution)/shard_map/convert_element_type | solution.py:508
  36.1 0.0 copy-start
  36.2 0.0 copy-start.4
  36.2 0.0 copy-start.9
  36.2 1.7 %collective-permute-start.8 = (bf16[192,1024]{1,0:T(8,128)(2,1)S(1)}, bf16[192,1024]{1,0:T(8,128)(2,1)}, u32[]{:S(2)}, u32[]{:S(2)}) collective-permute-start(bf16[192,1024]{1,0:T(8,128)(2,1)S(1)} %add_convert_fusion), channel_id=1, source_target_pairs={{0,2},{2,0},{1,3},{3,1},{4,6},{6,4},{5,7},{7,5},{8,10},{10,8},{9,1... | collective-permute-start | bytes 1179656 | tf_op jit(solution)/shard_map/ppermute | solution.py:443
  37.9 1.0 %constant_dynamic-slice_fusion = bf16[3,64,1024]{2,1,0:T(8,128)(2,1)S(1)} fusion(bf16[6,128,1024]{2,1,0:T(8,128)(2,1)} %lat_ref.3, s32[]{:T(128)S(6)} %select_n.18, s32[]{:T(128)S(6)} %select_n.20), kind=kLoop, calls=%fused_computation.7 | loop fusion | bytes 786440 | tf_op jit(solution)/shard_map/dynamic_slice | solution.py:514
  38.9 5.1 %collective-permute-done.10.heads_x_ref = bf16[2,512,256]{2,1,0:T(8,128)(2,1)S(1)} collective-permute-done((bf16[2,512,256]{2,1,0:T(8,128)(2,1)}, bf16[2,512,256]{2,1,0:T(8,128)(2,1)S(1)}, u32[]{:S(2)}, u32[]{:S(2)}) %collective-permute-start.10) | collective-permute-done | bytes 524320 | tf_op jit(solution)/shard_map/ppermute | solution.py:443
  44.0 1.7 %collective-permute-start.12 = (bf16[2,512,256]{2,1,0:T(8,128)(2,1)S(1)}, bf16[2,512,256]{2,1,0:T(8,128)(2,1)S(1)}, u32[]{:S(2)}, u32[]{:S(2)}) collective-permute-start(bf16[2,512,256]{2,1,0:T(8,128)(2,1)S(1)} %collective-permute-done.10.heads_x_ref), channel_id=1, source_target_pairs={{0,16},{16,0},{1,17},{17,1},{2,18},{18,2},{3,19},{19,3},{4,20},{20... | collective-permute-start | bytes 1572872 | tf_op jit(solution)/shard_map/ppermute | solution.py:447
  45.7 9.6 %collective-permute-done.11.rest_x_ref = bf16[2,512,256]{2,1,0:T(8,128)(2,1)S(1)} collective-permute-done((bf16[2,512,256]{2,1,0:T(8,128)(2,1)}, bf16[2,512,256]{2,1,0:T(8,128)(2,1)S(1)}, u32[]{:S(2)}, u32[]{:S(2)}) %collective-permute-start.11) | collective-permute-done | bytes 524320 | tf_op jit(solution)/shard_map/ppermute | solution.py:443
  55.2 1.7 %collective-permute-start.13 = (bf16[2,512,256]{2,1,0:T(8,128)(2,1)S(1)}, bf16[2,512,256]{2,1,0:T(8,128)(2,1)S(1)}, u32[]{:S(2)}, u32[]{:S(2)}) collective-permute-start(bf16[2,512,256]{2,1,0:T(8,128)(2,1)S(1)} %collective-permute-done.11.rest_x_ref), channel_id=1, source_target_pairs={{0,16},{16,0},{1,17},{17,1},{2,18},{18,2},{3,19},{19,3},{4,20},{20... | collective-permute-start | bytes 1572872 | tf_op jit(solution)/shard_map/ppermute | solution.py:447
  56.9 6.4 %collective-permute-done.8 = bf16[192,1024]{1,0:T(8,128)(2,1)} collective-permute-done((bf16[192,1024]{1,0:T(8,128)(2,1)S(1)}, bf16[192,1024]{1,0:T(8,128)(2,1)}, u32[]{:S(2)}, u32[]{:S(2)}) %collective-permute-start.8) | collective-permute-done | bytes 393248 | tf_op jit(solution)/shard_map/ppermute | solution.py:443
  63.3 1.5 %fusion.2.mine_ref = bf16[192,1024]{1,0:T(8,128)(2,1)S(1)} fusion(bf16[192,1024]{1,0:T(8,128)(2,1)} %collective-permute-done.8, bf16[192,1024]{1,0:T(8,128)(2,1)} %collective-permute-done.6, bf16[192,1024]{1,0:T(8,128)(2,1)} %copy-done.7, bf16[3,64,1024]{2,1,0:T(8,128)(2,1)S(1)} %constant_dynamic-slice_fusion), kind=kLoop, calls=%fused_computation.3 | loop fusion | flops 1572864 | bytes 1966080 | tf_op jit(solution)/shard_map/convert_element_type | solution.py:519
  64.8 0.1 collective-permute-start.9
  64.9 3.4 %collective-permute-done.13.rest_y_ref = bf16[2,512,256]{2,1,0:T(8,128)(2,1)S(1)} collective-permute-done((bf16[2,512,256]{2,1,0:T(8,128)(2,1)S(1)}, bf16[2,512,256]{2,1,0:T(8,128)(2,1)S(1)}, u32[]{:S(2)}, u32[]{:S(2)}) %collective-permute-start.13) | collective-permute-done | bytes 524320 | tf_op jit(solution)/shard_map/ppermute | solution.py:447
  68.2 0.0 collective-permute-done.9.theirs_ref
  68.3 8.0 %shard_map.97 = (bf16[384,512]{1,0:T(8,128)(2,1)S(1)}, f32[384,512]{1,0:T(8,128)S(1)}) custom-call(bf16[192,1024]{1,0:T(8,128)(2,1)S(1)} %fusion.2.mine_ref, bf16[192,1024]{1,0:T(8,128)(2,1)S(1)} %collective-permute-done.9.theirs_ref, f32[1,1024]{1,0:T(1,128)S(1)} %bitcast.16, bf16[3,1024,256]{2,1,0:T(8,128)(2,1)S(1)} %bitcast.11, ...), custom_call_target="tpu_custom_call" | custom-call | flops 1207959552 | tf_op jit(solution)/shard_map/pallas_call | solution.py:427
  76.2 0.1 collective-permute-start.14
  76.3 1.7 %collective-permute-done.14 = bf16[384,512]{1,0:T(8,128)(2,1)S(1)} collective-permute-done((bf16[384,512]{1,0:T(8,128)(2,1)S(1)}, bf16[384,512]{1,0:T(8,128)(2,1)S(1)}, u32[]{:S(2)}, u32[]{:S(2)}) %collective-permute-start.14) | collective-permute-done | bytes 393248 | tf_op jit(solution)/shard_map/ppermute | solution.py:439
  78.0 0.1 add_convert_fusion.1
  78.1 1.7 %collective-permute-start.15 = (bf16[384,256]{1,0:T(8,128)(2,1)S(1)}, bf16[384,256]{1,0:T(8,128)(2,1)S(1)}, u32[]{:S(2)}, u32[]{:S(2)}) collective-permute-start(bf16[384,256]{1,0:T(8,128)(2,1)S(1)} %get-tuple-element.31), channel_id=1, source_target_pairs={{0,2},{2,0},{1,3},{3,1},{4,6},{6,4},{5,7},{7,5},{8,10},{10,8},{9,1... | collective-permute-start | bytes 589832 | tf_op jit(solution)/shard_map/ppermute | solution.py:443
  79.8 5.3 %collective-permute-done.15.far_ref = bf16[384,256]{1,0:T(8,128)(2,1)S(1)} collective-permute-done((bf16[384,256]{1,0:T(8,128)(2,1)S(1)}, bf16[384,256]{1,0:T(8,128)(2,1)S(1)}, u32[]{:S(2)}, u32[]{:S(2)}) %collective-permute-start.15) | collective-permute-done | bytes 196640 | tf_op jit(solution)/shard_map/ppermute | solution.py:443
  85.1 0.8 shard_map.98
  (22 shorter events, 0.0 us)
Async XLA Ops:
  0.0 1.4 %copy-start.2 = (bf16[6,128,1024]{2,1,0:T(8,128)(2,1)S(1)}, bf16[6,128,1024]{2,1,0:T(8,128)(2,1)}, u32[]{:S(2)}) copy-start(bf16[6,128,1024]{2,1,0:T(8,128)(2,1)} %lat_ref.3) | copy-start | bytes 4718596
  1.4 10.7 %copy-start.3 = (bf16[6,128,1024]{2,1,0:T(8,128)(2,1)S(1)}, bf16[6,128,1024]{2,1,0:T(8,128)(2,1)}, u32[]{:S(2)}) copy-start(bf16[6,128,1024]{2,1,0:T(8,128)(2,1)} %lat_ref.3) | copy-start | bytes 4718596
  1.4 10.7 %copy-start.11 = (f32[1024]{0:T(1024)S(1)}, f32[1024]{0:T(1024)}, u32[]{:S(2)}) copy-start(f32[1024]{0:T(1024)} %param.10) | copy-start | bytes 12292
  1.4 10.7 %copy-start.12 = (f32[256]{0:T(256)S(1)}, f32[256]{0:T(256)}, u32[]{:S(2)}) copy-start(f32[256]{0:T(256)} %param.12) | copy-start | bytes 3076
  2.4 9.7 %collective-permute-start = (f32[6,1280]{1,0:T(8,128)S(1)}, f32[6,1280]{1,0:T(8,128)S(1)}, u32[]{:S(2)}, u32[]{:S(2)}) collective-permute-start(f32[6,1280]{1,0:T(8,128)S(1)} %get-tuple-element.18), channel_id=1, source_target_pairs={{0,4},{4,8},{8,12},{12,0},{1,5},{5,9},{9,13},{13,1},{2,6},{6,10},{... | collective-permute-start | bytes 92168 | tf_op jit(solution)/shard_map/ppermute | solution.py:452
  5.5 6.6 %collective-permute-start.1 = (f32[6,1280]{1,0:T(8,128)S(1)}, f32[6,1280]{1,0:T(8,128)S(1)}, u32[]{:S(2)}, u32[]{:S(2)}) collective-permute-start(f32[6,1280]{1,0:T(8,128)S(1)} %get-tuple-element.19), channel_id=1, source_target_pairs={{0,12},{4,0},{8,4},{12,8},{1,13},{5,1},{9,5},{13,9},{2,14},{6,2},{... | collective-permute-start | bytes 92168 | tf_op jit(solution)/shard_map/ppermute | solution.py:452
  7.5 4.5 %collective-permute-start.2 = (f32[6,256]{1,0:T(8,128)S(1)}, f32[6,256]{1,0:T(8,128)S(1)}, u32[]{:S(2)}, u32[]{:S(2)}) collective-permute-start(f32[6,256]{1,0:T(8,128)S(1)} %get-tuple-element.20.own_ref), channel_id=1, source_target_pairs={{0,8},{4,12},{8,0},{12,4},{1,9},{5,13},{9,1},{13,5},{2,10},{6,14},... | collective-permute-start | bytes 18440 | tf_op jit(solution)/shard_map/ppermute | solution.py:452
  12.1 1.4 %copy-start.10 = (bf16[3,1024,256]{2,1,0:T(8,128)(2,1)S(1)}, bf16[3,1024,256]{2,1,0:T(8,128)(2,1)}, u32[]{:S(2)}) copy-start(bf16[3,1024,256]{2,1,0:T(8,128)(2,1)} %weight_ref.1) | copy-start | bytes 4718596
  13.5 10.9 %copy-start.1 = (bf16[3,256,1024]{2,1,0:T(8,128)(2,1)S(1)}, bf16[3,256,1024]{2,1,0:T(8,128)(2,1)}, u32[]{:S(2)}) copy-start(bf16[3,256,1024]{2,1,0:T(8,128)(2,1)} %param.14) | copy-start | bytes 4718596
  13.5 10.9 %copy-start.8 = (f32[256]{0:T(256)S(1)}, f32[256]{0:T(256)}, u32[]{:S(2)}) copy-start(f32[256]{0:T(256)} %param.13) | copy-start | bytes 3076
  16.0 8.4 %collective-permute-start.3 = (f32[6,512]{1,0:T(8,128)S(1)}, f32[6,512]{1,0:T(8,128)S(1)}, u32[]{:S(2)}, u32[]{:S(2)}) collective-permute-start(f32[6,512]{1,0:T(8,128)S(1)} %get-tuple-element.22), channel_id=1, source_target_pairs={{0,4},{4,8},{8,12},{12,0},{1,5},{5,9},{9,13},{13,1},{2,6},{6,10},{... | collective-permute-start | bytes 36872 | tf_op jit(solution)/shard_map/ppermute | solution.py:452
  16.1 8.3 %collective-permute-start.4 = (f32[6,512]{1,0:T(8,128)S(1)}, f32[6,512]{1,0:T(8,128)S(1)}, u32[]{:S(2)}, u32[]{:S(2)}) collective-permute-start(f32[6,512]{1,0:T(8,128)S(1)} %get-tuple-element.23), channel_id=1, source_target_pairs={{0,12},{4,0},{8,4},{12,8},{1,13},{5,1},{9,5},{13,9},{2,14},{6,2},{... | collective-permute-start | bytes 36872 | tf_op jit(solution)/shard_map/ppermute | solution.py:452
  19.9 4.5 %collective-permute-start.5 = (f32[6,256]{1,0:T(8,128)S(1)}, f32[6,256]{1,0:T(8,128)S(1)}, u32[]{:S(2)}, u32[]{:S(2)}) collective-permute-start(f32[6,256]{1,0:T(8,128)S(1)} %get-tuple-element.24.own_ref), channel_id=1, source_target_pairs={{0,8},{4,12},{8,0},{12,4},{1,9},{5,13},{9,1},{13,5},{2,10},{6,14},... | collective-permute-start | bytes 18440 | tf_op jit(solution)/shard_map/ppermute | solution.py:452
  26.3 0.8 copy-start.5
  27.1 7.8 %collective-permute-start.7 = (bf16[192,1024]{1,0:T(8,128)(2,1)}, bf16[192,1024]{1,0:T(8,128)(2,1)}, u32[]{:S(2)}, u32[]{:S(2)}) collective-permute-start(bf16[192,1024]{1,0:T(8,128)(2,1)} %get-tuple-element.27), channel_id=1, source_target_pairs={{0,1},{1,0},{2,3},{3,2},{4,5},{5,4},{6,7},{7,6},{8,9},{9,8},{10,11... | collective-permute-start | bytes 1179656 | tf_op jit(solution)/shard_map/ppermute | solution.py:439
  28.9 15.1 %collective-permute-start.10 = (bf16[2,512,256]{2,1,0:T(8,128)(2,1)}, bf16[2,512,256]{2,1,0:T(8,128)(2,1)S(1)}, u32[]{:S(2)}, u32[]{:S(2)}) collective-permute-start(bf16[2,512,256]{2,1,0:T(8,128)(2,1)} %shard_map.95), channel_id=1, source_target_pairs={{0,2},{2,0},{1,3},{3,1},{4,6},{6,4},{5,7},{7,5},{8,10},{10,8},{9,1... | collective-permute-start | bytes 1572872 | tf_op jit(solution)/shard_map/ppermute | solution.py:443
  32.5 2.4 %copy-start.6 = (bf16[192,1024]{1,0:T(8,128)(2,1)S(1)}, bf16[192,1024]{1,0:T(8,128)(2,1)}, u32[]{:S(2)}) copy-start(bf16[192,1024]{1,0:T(8,128)(2,1)} %copy-done.5) | copy-start | bytes 1179652
  32.5 22.7 %collective-permute-start.11 = (bf16[2,512,256]{2,1,0:T(8,128)(2,1)}, bf16[2,512,256]{2,1,0:T(8,128)(2,1)S(1)}, u32[]{:S(2)}, u32[]{:S(2)}) collective-permute-start(bf16[2,512,256]{2,1,0:T(8,128)(2,1)} %shard_map.96), channel_id=1, source_target_pairs={{0,2},{2,0},{1,3},{3,1},{4,6},{6,4},{5,7},{7,5},{8,10},{10,8},{9,1... | collective-permute-start | bytes 1572872 | tf_op jit(solution)/shard_map/ppermute | solution.py:443
  34.8 1.3 %copy-start.7 = (bf16[192,1024]{1,0:T(8,128)(2,1)}, bf16[192,1024]{1,0:T(8,128)(2,1)S(1)}, u32[]{:S(2)}) copy-start(bf16[192,1024]{1,0:T(8,128)(2,1)S(1)} %get-tuple-element.25) | copy-start | bytes 1179652
  34.8 22.1 %collective-permute-start.6 = (bf16[192,1024]{1,0:T(8,128)(2,1)}, bf16[192,1024]{1,0:T(8,128)(2,1)}, u32[]{:S(2)}, u32[]{:S(2)}) collective-permute-start(bf16[192,1024]{1,0:T(8,128)(2,1)} %get-tuple-element.26), channel_id=1, source_target_pairs={{0,1},{1,0},{2,3},{3,2},{4,5},{5,4},{6,7},{7,6},{8,9},{9,8},{10,11... | collective-permute-start | bytes 1179656 | tf_op jit(solution)/shard_map/ppermute | solution.py:439
  36.1 32.1 %copy-start = (bf16[1024,3,256]{2,0,1:T(8,128)(2,1)S(1)}, bf16[1024,3,256]{2,0,1:T(8,128)(2,1)}, u32[]{:S(2)}) copy-start(bf16[1024,3,256]{2,0,1:T(8,128)(2,1)} %param.16) | copy-start | bytes 4718596
  36.2 32.1 %copy-start.4 = (bf16[256,1024]{1,0:T(8,128)(2,1)S(1)}, bf16[256,1024]{1,0:T(8,128)(2,1)}, u32[]{:S(2)}) copy-start(bf16[256,1024]{1,0:T(8,128)(2,1)} %out_ref.3) | copy-start | bytes 1572868
  36.2 32.1 %copy-start.9 = (f32[1024]{0:T(1024)S(1)}, f32[1024]{0:T(1024)}, u32[]{:S(2)}) copy-start(f32[1024]{0:T(1024)} %param.15) | copy-start | bytes 12292
  36.2 27.1 %collective-permute-start.8 = (bf16[192,1024]{1,0:T(8,128)(2,1)S(1)}, bf16[192,1024]{1,0:T(8,128)(2,1)}, u32[]{:S(2)}, u32[]{:S(2)}) collective-permute-start(bf16[192,1024]{1,0:T(8,128)(2,1)S(1)} %add_convert_fusion), channel_id=1, source_target_pairs={{0,2},{2,0},{1,3},{3,1},{4,6},{6,4},{5,7},{7,5},{8,10},{10,8},{9,1... | collective-permute-start | bytes 1179656 | tf_op jit(solution)/shard_map/ppermute | solution.py:443
  44.0 20.9 %collective-permute-start.12 = (bf16[2,512,256]{2,1,0:T(8,128)(2,1)S(1)}, bf16[2,512,256]{2,1,0:T(8,128)(2,1)S(1)}, u32[]{:S(2)}, u32[]{:S(2)}) collective-permute-start(bf16[2,512,256]{2,1,0:T(8,128)(2,1)S(1)} %collective-permute-done.10.heads_x_ref), channel_id=1, source_target_pairs={{0,16},{16,0},{1,17},{17,1},{2,18},{18,2},{3,19},{19,3},{4,20},{20... | collective-permute-start | bytes 1572872 | tf_op jit(solution)/shard_map/ppermute | solution.py:447
  55.2 13.0 %collective-permute-start.13 = (bf16[2,512,256]{2,1,0:T(8,128)(2,1)S(1)}, bf16[2,512,256]{2,1,0:T(8,128)(2,1)S(1)}, u32[]{:S(2)}, u32[]{:S(2)}) collective-permute-start(bf16[2,512,256]{2,1,0:T(8,128)(2,1)S(1)} %collective-permute-done.11.rest_x_ref), channel_id=1, source_target_pairs={{0,16},{16,0},{1,17},{17,1},{2,18},{18,2},{3,19},{19,3},{4,20},{20... | collective-permute-start | bytes 1572872 | tf_op jit(solution)/shard_map/ppermute | solution.py:447
  64.8 3.5 %collective-permute-start.9 = (bf16[192,1024]{1,0:T(8,128)(2,1)S(1)}, bf16[192,1024]{1,0:T(8,128)(2,1)S(1)}, u32[]{:S(2)}, u32[]{:S(2)}) collective-permute-start(bf16[192,1024]{1,0:T(8,128)(2,1)S(1)} %fusion.2.mine_ref), channel_id=1, source_target_pairs={{0,1},{1,0},{2,3},{3,2},{4,5},{5,4},{6,7},{7,6},{8,9},{9,8},{10,11... | collective-permute-start | bytes 1179656 | tf_op jit(solution)/shard_map/ppermute | solution.py:439
  76.2 1.8 %collective-permute-start.14 = (bf16[384,512]{1,0:T(8,128)(2,1)S(1)}, bf16[384,512]{1,0:T(8,128)(2,1)S(1)}, u32[]{:S(2)}, u32[]{:S(2)}) collective-permute-start(bf16[384,512]{1,0:T(8,128)(2,1)S(1)} %get-tuple-element.30), channel_id=1, source_target_pairs={{0,1},{1,0},{2,3},{3,2},{4,5},{5,4},{6,7},{7,6},{8,9},{9,8},{10,11... | collective-permute-start | bytes 1179656 | tf_op jit(solution)/shard_map/ppermute | solution.py:439
  78.1 7.0 %collective-permute-start.15 = (bf16[384,256]{1,0:T(8,128)(2,1)S(1)}, bf16[384,256]{1,0:T(8,128)(2,1)S(1)}, u32[]{:S(2)}, u32[]{:S(2)}) collective-permute-start(bf16[384,256]{1,0:T(8,128)(2,1)S(1)} %get-tuple-element.31), channel_id=1, source_target_pairs={{0,2},{2,0},{1,3},{3,1},{4,6},{6,4},{5,7},{7,5},{8,10},{10,8},{9,1... | collective-permute-start | bytes 589832 | tf_op jit(solution)/shard_map/ppermute | solution.py:443

commit v3 on v2

--- a/solution.py
+++ b/solution.py
@@ -13,6 +13,7 @@
 HEAD_DIM = 64
 WINDOW = 64
 LANES = 128
+PIECES = 4
 
 norm_eps = 1e-05
 rms_eps = 1e-06
@@ -286,16 +287,14 @@
     keep_ref[...] = total[half * WINDOW :].astype(bf16)
 
 
-def split3(value):
+def split2(value):
     high = value.astype(bf16)
-    rest = value - high.astype(f32)
-    middle = rest.astype(bf16)
-    return high, middle, (rest - middle.astype(f32)).astype(bf16)
+    return high, (value - high.astype(f32)).astype(bf16)
 
 
 def attention_kernel(
     mine_ref, theirs_ref, gain_ref, qkv_ref, out_ref,
-    heads_x_ref, rest_x_ref, heads_y_ref, rest_y_ref,
+    heads_x_ref, values_x_ref, outs_x_ref, heads_y_ref, values_y_ref, outs_z_ref,
     send_ref, keep_ref, res_ref, normed_ref, context_ref,
 ):
     rows, channels = mine_ref.shape
@@ -315,6 +314,8 @@
     normed = normed_ref[...]
     lane = lax.broadcasted_iota(jnp.int32, (2 * rows, LANES), 1)
     per_tile = LANES // HEAD_DIM
+    ones = jnp.ones((2 * rows, LANES), bf16)
+    zero = jnp.zeros((), bf16)
     nt = (((1,), (1,)), ((), ()))
     near_at = pl.ds(pl.multiple_of(group * depth, depth), depth)
     away_at = pl.ds(pl.multiple_of((1 - group) * depth, depth), depth)
@@ -322,8 +323,8 @@
     def project(side, which):
         if side == 0:
             return jnp.dot(normed, qkv_ref[which], preferred_element_type=f32)
-        from_x = heads_x_ref[which] if which < 2 else rest_x_ref[0]
-        from_y = heads_y_ref[which] if which < 2 else rest_y_ref[0]
+        from_x = heads_x_ref[which] if which < 2 else values_x_ref[...]
+        from_y = heads_y_ref[which] if which < 2 else values_y_ref[...]
         near = jnp.dot(normed_ref[:, near_at], from_x, preferred_element_type=f32)
         return near + jnp.dot(normed_ref[:, away_at], from_y, preferred_element_type=f32)
 
@@ -333,31 +334,34 @@
         values = values.astype(bf16)
         for tile in range(shard // LANES):
             at = slice(tile * LANES, (tile + 1) * LANES)
-            q_high, q_mid, q_low = split3(queries[:, at])
-            left = jnp.concatenate([q_high, q_mid, q_high, q_mid, q_high, q_low], axis=1)
+            q_high, q_low = split2(queries[:, at])
+            left = jnp.concatenate([q_high, q_low, q_high, q_low], axis=1)
+            k_high, k_low = split2(keys[:, at])
+            mixing = jnp.concatenate([values[:, at], ones], axis=1)
             result = None
             for head in range(per_tile):
                 inside = lane // HEAD_DIM == head
-                k_high, k_mid, k_low = split3(jnp.where(inside, keys[:, at], 0.0))
-                right = jnp.concatenate([k_high, k_high, k_mid, k_mid, k_low, k_high], axis=1)
+                own_high = jnp.where(inside, k_high, zero)
+                own_low = jnp.where(inside, k_low, zero)
+                right = jnp.concatenate([own_high, own_high, own_low, own_low], axis=1)
                 scores = lax.dot_general(left, right, nt, preferred_element_type=f32)
-                scores = jnp.exp(scores - jnp.max(scores, axis=1, keepdims=True))
-                total = jnp.sum(scores, axis=1, keepdims=True)
-                probs = (scores / total).astype(bf16)
-                mixed = jnp.dot(probs, values[:, at], preferred_element_type=f32)
+                scores = jnp.exp(scores - jnp.max(scores, axis=1, keepdims=True)).astype(bf16)
+                mixed = jnp.dot(scores, mixing, preferred_element_type=f32)
+                mixed = mixed[:, :LANES] / mixed[:, LANES:]
                 result = mixed if result is None else jnp.where(inside, mixed, result)
             base = side * shard + tile * LANES
             context_ref[:, base : base + LANES] = result.astype(bf16)
     context = context_ref[:, :shard]
-    from_x = context_ref[:, pl.ds(pl.multiple_of(shard + group * part, part), part)]
-    from_y = context_ref[:, pl.ds(pl.multiple_of(shard + (1 - group) * part, part), part)]
+    parity = lax.axis_index("frame") % 2
+    from_x = context_ref[:, pl.ds(pl.multiple_of(shard + parity * part, part), part)]
+    from_z = context_ref[:, pl.ds(pl.multiple_of(shard + (1 - parity) * part, part), part)]
 
     def term(block):
         at = pl.ds(pl.multiple_of(block * shard, shard), shard)
         rows_at = pl.ds(pl.multiple_of(block * part, part), part)
         value = jnp.dot(context, out_ref[:, at], preferred_element_type=f32)
-        value = value + jnp.dot(from_x, rest_x_ref[1, rows_at, :], preferred_element_type=f32)
-        return value + jnp.dot(from_y, rest_y_ref[1, rows_at, :], preferred_element_type=f32)
+        value = value + jnp.dot(from_x, outs_x_ref[rows_at, :], preferred_element_type=f32)
+        return value + jnp.dot(from_z, outs_z_ref[rows_at, :], preferred_element_type=f32)
 
     for place, goal in enumerate((1 - chip, chip)):
         at = slice(place * shard, (place + 1) * shard)
@@ -369,44 +373,69 @@
         keep_ref[:, at] = kept + res_ref[:, pl.ds(pl.multiple_of(block * shard, shard), shard)]
 
 
-def pack_heads_kernel(qkv_ref, send_ref, sem):
-    depth = send_ref.shape[1]
-    start = pl.multiple_of(lax.axis_index("groups") * depth, depth)
-    copy = pltpu.make_async_copy(qkv_ref.at[pl.ds(0, 2), pl.ds(start, depth), :], send_ref, sem)
-    copy.start()
-    copy.wait()
-
-
-def pack_rest_kernel(qkv_ref, out_ref, send_ref, sems):
-    depth, shard = send_ref.shape[1:]
-    part = shard // 2
-    group = lax.axis_index("groups")
-    at = pl.ds(pl.multiple_of(group * depth, depth), depth)
-    copies = [pltpu.make_async_copy(qkv_ref.at[2, at, :], send_ref.at[0], sems.at[0])]
-    rows = pl.ds(pl.multiple_of(group * part, part), part)
-    for block in range(depth // part):
-        copies.append(
-            pltpu.make_async_copy(
-                out_ref.at[rows, pl.ds(block * shard, shard)],
-                send_ref.at[1, pl.ds(block * part, part), :],
-                sems.at[1 + block],
-            )
-        )
+def run_copies(pairs, sems):
+    copies = [
+        pltpu.make_async_copy(source, goal, sems.at[place])
+        for place, (source, goal) in enumerate(pairs)
+    ]
     for copy in copies:
         copy.start()
     for copy in copies:
         copy.wait()
 
 
+def pack_heads_kernel(qkv_ref, send_ref, sems):
+    depth = send_ref.shape[1]
+    step = depth // PIECES
+    start = lax.axis_index("groups") * depth
+    pairs = []
+    for which in range(2):
+        for piece in range(PIECES):
+            rows = pl.ds(pl.multiple_of(start + piece * step, step), step)
+            goal = send_ref.at[which, pl.ds(piece * step, step), :]
+            pairs.append((qkv_ref.at[which, rows, :], goal))
+    run_copies(pairs, sems)
+
+
+def pack_rest_kernel(qkv_ref, out_ref, send_ref, sems):
+    depth, shard = send_ref.shape[1:]
+    part = shard // 2
+    step = depth // PIECES
+    start = lax.axis_index("groups") * depth
+    pairs = []
+    for piece in range(PIECES):
+        rows = pl.ds(pl.multiple_of(start + piece * step, step), step)
+        pairs.append((qkv_ref.at[2, rows, :], send_ref.at[0, pl.ds(piece * step, step), :]))
+    rows = pl.ds(pl.multiple_of(lax.axis_index("frame") % 2 * part, part), part)
+    for block in range(depth // part):
+        goal = send_ref.at[1, pl.ds(block * part, part), :]
+        pairs.append((out_ref.at[rows, pl.ds(block * shard, shard)], goal))
+    run_copies(pairs, sems)
+
+
 def pack(kernel, shape, copies, args):
     return pl.pallas_call(
         kernel,
         out_shape=jax.ShapeDtypeStruct(shape, bf16),
-        in_specs=[pl.BlockSpec(memory_space=pl.ANY)] * len(args),
+        in_specs=[pl.BlockSpec(memory_space=pltpu.HBM)] * len(args),
         out_specs=pl.BlockSpec(memory_space=VMEM),
-        scratch_shapes=[pltpu.SemaphoreType.DMA(copies)],
+        scratch_shapes=[pltpu.SemaphoreType.DMA((copies,))],
+        compiler_params=pltpu.CompilerParams(vmem_limit_bytes=4 * 2**20),
         cost_estimate=pl.CostEstimate(flops=0, bytes_accessed=2**20, transcendentals=0),
-    )(*args)
+    )(*[pltpu.with_memory_space_constraint(arg, pltpu.HBM) for arg in args])
+
+
+def residual_kernel(latent_ref, keep_ref, got_ref, far_ref, out_ref):
+    stems = latent_ref.shape[0]
+    index = lax.axis_index("tensor")
+    chip, core = index // 2, index % 2
+    start = pl.multiple_of(chip * WINDOW, WINDOW)
+    for stem in range(stems // 2):
+        rows = slice(stem * WINDOW, (stem + 1) * WINDOW)
+        total = keep_ref[rows, :].astype(f32) + got_ref[rows, :].astype(f32)
+        total = total + far_ref[rows, :].astype(f32)
+        latent = latent_ref[core * (stems // 2) + stem, pl.ds(start, WINDOW), :]
+        out_ref[rows, :] = (latent.astype(f32) + total).astype(bf16)
 
 
 def place_kernel(own_ref, far_ref, out_ref):
@@ -423,14 +452,14 @@
         out_ref[goal, pl.ds(away, WINDOW), :] = far_ref[rows, :]
 
 
-def call(kernel, outs, scratch, args, flops=0, moved=0):
+def call(kernel, outs, scratch, args, flops=0, moved=0, limit=16):
     return pl.pallas_call(
         kernel,
         out_shape=[jax.ShapeDtypeStruct(shape, dtype) for shape, dtype in outs],
         in_specs=[pl.BlockSpec(memory_space=VMEM)] * len(args),
         out_specs=[pl.BlockSpec(memory_space=VMEM)] * len(outs),
         scratch_shapes=[VMEM(shape, dtype) for shape, dtype in scratch],
-        compiler_params=pltpu.CompilerParams(vmem_limit_bytes=40 * 2**20),
+        compiler_params=pltpu.CompilerParams(vmem_limit_bytes=limit * 2**20),
         cost_estimate=pl.CostEstimate(flops=flops, bytes_accessed=moved, transcendentals=0),
     )(*args)
 
@@ -445,6 +474,10 @@
 
 def swap_groups(value):
     return lax.ppermute(value, "groups", [(0, 1), (1, 0)])
+
+
+def swap_frames(value):
+    return lax.ppermute(value, "frame", [(0, 1), (1, 0), (2, 3), (3, 2)])
 
 
 def shift_frames(value, by):
@@ -468,12 +501,17 @@
     half_rows = stems // 2 * WINDOW
     qkv = jnp.transpose(qkv_weight, (1, 0, 2))
     depth, part = channels // 2, shard // 2
-    heads = pack(pack_heads_kernel, (2, depth, shard), (), [qkv])
-    rest = pack(pack_rest_kernel, (2, depth, shard), (1 + depth // part,), [qkv, out_weight])
+    heads = pack(pack_heads_kernel, (2, depth, shard), 2 * PIECES, [qkv])
+    rest = pack(
+        pack_rest_kernel, (2, depth, shard), PIECES + depth // part,
+        [qkv, out_weight],
+    )
     heads_x = swap_chips(heads)
     rest_x = swap_chips(rest)
     heads_y = swap_groups(heads_x)
-    rest_y = swap_groups(rest_x)
+    values_x, outs_x = rest_x[0], rest_x[1]
+    values_y = swap_groups(values_x)
+    outs_z = swap_frames(outs_x)
     wide = channels + 2 * LANES
     up, down, own = call(
         functools.partial(stats_kernel, width),
@@ -509,22 +547,19 @@
     summed = swap_chips(summed)
     send_own, keep_own = second(False)
     got_own = swap_cores(send_own)
-    index = lax.axis_index("tensor")
-    chip, core = index // 2, index % 2
-    latent_own = lax.dynamic_slice(
-        latent, (core * (stems // 2), chip * WINDOW, 0), (stems // 2, WINDOW, channels)
-    ).reshape(half_rows, channels)
-    mine = (
-        latent_own.astype(f32) + keep_own.astype(f32) + got_own.astype(f32) + summed.astype(f32)
-    ).astype(bf16)
+    mine = call(
+        residual_kernel, [((half_rows, channels), bf16)], [],
+        [latent, keep_own, got_own, summed],
+    )[0]
     theirs = swap_cores(mine)
     out_send, out_keep = call(
         attention_kernel,
         [((2 * half_rows, 2 * shard), bf16), ((2 * half_rows, 2 * shard), f32)],
         [((2 * half_rows, channels), f32), ((2 * half_rows, channels), bf16),
          ((2 * half_rows, 2 * shard), bf16)],
-        [mine, theirs, attn_gain[None], qkv, out_weight, heads_x, rest_x, heads_y, rest_y],
-        flops=24 * half_rows * channels * shard,
+        [mine, theirs, attn_gain[None], qkv, out_weight, heads_x, values_x, outs_x,
+         heads_y, values_y, outs_z],
+        flops=24 * half_rows * channels * shard, limit=24,
     )
     out_got = swap_cores(out_send)
     away = (out_keep[:, :shard] + out_got[:, :shard].astype(f32)).astype(bf16)

time: 86.2 us -> 86.5 us (level)
  waiting for transfers between devices: 39.6 us -> 49.7 us
  Pallas kernels: 19.6 us -> 15.3 us
  local copies, waits for them, and re-layouts: 4.64 us -> 1.48 us
  other arithmetic: 2.85 us -> 0.23 us
    ppermute x2, waiting for transfers between devices: 3.36 us -> 8.55 us  [swap_groups(): return lax.ppermute(value, 'groups', [(0, 1), (1, 0)])]
    ppermute x4, waiting for transfers between devices: 26.3 us -> 31.3 us  [swap_chips(): return lax.ppermute(value, 'tensor', [(0, 2), (2, 0), (1, 3), (3, 1)])]
    pallas_call x6 -> x7, Pallas kernels: 15.9 us -> 13.1 us  [call(): pl.pallas_call(kernel, out_shape=[jax.ShapeDtypeStruct(shape, dtype) for...]
    unnamed x26 -> x20, local copies, waits for them, and re-layouts: 3.61 us -> 1.45 us
    convert_element_type x1 -> x0, other arithmetic: 1.49 us -> none  [fast(): mine = (latent_own.astype(f32) + keep_own.astype(f32) + got_own.astype(f3...]
    pallas_call x2, Pallas kernels: 3.7 us -> 2.27 us  [pack(): pl.pallas_call(kernel, out_shape=jax.ShapeDtypeStruct(shape, bf16), in_sp...]
    convert_element_type x1, other arithmetic: 1.27 us -> 0.13 us  [fast(): summed = (got.astype(f32) + keep.astype(f32)).astype(bf16)]
    dynamic_slice x1 -> x0, local copies, waits for them, and re-layouts: 1.02 us -> none  [fast(): lax.dynamic_slice(latent, (core * (stems // 2), chip * WINDOW, 0), (stems...]
  transfers between devices with their start and end apart: 16 -> 17, of which waited for: 8 -> 7; matrix products, arithmetic and copies ran while one was open for 4% -> 0% of each run, Pallas kernels for 6% -> 4%
where the time goes in v3:
time: 86.5 us; the launch traced here: 86.3 us
  waiting for transfers between devices  49.7 us (57%)
  starting transfers between devices  19.3 us (22%)
  Pallas kernels  15.3 us (18%)
  local copies, waits for them, and re-layouts  1.48 us (2%)
    ppermute x4, waiting for transfers between devices, swap_chips(): return lax.ppermute(value, 'tensor', [(0, 2), (2, 0), (1, 3), (3, 1)])  31.3 us
    pallas_call x7, Pallas kernels, call(): pl.pallas_call(kernel, out_shape=[jax.ShapeDtypeStruct(shape, dtype) for...  13.1 us
    ppermute x6, starting transfers between devices, shift_frames(): lax.ppermute(value, 'frame', [(i, (i + by) % count) for i in range(count)])  10 us
    ppermute x2, waiting for transfers between devices, swap_groups(): return lax.ppermute(value, 'groups', [(0, 1), (1, 0)])  8.55 us
    ppermute x6, waiting for transfers between devices, shift_frames(): lax.ppermute(value, 'frame', [(i, (i + by) % count) for i in range(count)])  8.16 us
    ppermute x4, starting transfers between devices, swap_chips(): return lax.ppermute(value, 'tensor', [(0, 2), (2, 0), (1, 3), (3, 1)])  5.58 us
    ppermute x2, starting transfers between devices, swap_groups(): return lax.ppermute(value, 'groups', [(0, 1), (1, 0)])  3.41 us
    pallas_call x2, Pallas kernels, pack(): pl.pallas_call(kernel, out_shape=jax.ShapeDtypeStruct(shape, bf16), in_sp...  2.27 us
  transfers between devices with their start and end apart: 17, of which 7 were waited for; matrix products, arithmetic and copies ran while one was open for 0% of the time, Pallas kernels for 4%

profile of v3, /device:TPU:0, one launch (start us, length us, event | category | flops | bytes accessed | tf_op | source)
XLA Modules:
  0.0 86.3 jit_solution(107122754820042880)
XLA Ops:
  0.0 1.4 %copy-done.1 = bf16[6,128,1024]{2,1,0:T(8,128)(2,1)S(1)} copy-done((bf16[6,128,1024]{2,1,0:T(8,128)(2,1)S(1)}, bf16[6,128,1024]{2,1,0:T(8,128)(2,1)}, u32[]{:S(2)}) %copy-start.1) | copy-done | bytes 1572888
  1.4 0.9 %shard_map.91 = (f32[6,1280]{1,0:T(8,128)S(1)}, f32[6,1280]{1,0:T(8,128)S(1)}, f32[6,256]{1,0:T(8,128)S(1)}) custom-call(bf16[6,128,1024]{2,1,0:T(8,128)(2,1)S(1)} %copy-done.1), custom_call_target="tpu_custom_call" | custom-call | tf_op jit(solution)/shard_map/pallas_call | solution.py:456
  2.4 3.1 %collective-permute-start = (f32[6,1280]{1,0:T(8,128)S(1)}, f32[6,1280]{1,0:T(8,128)S(1)}, u32[]{:S(2)}, u32[]{:S(2)}) collective-permute-start(f32[6,1280]{1,0:T(8,128)S(1)} %get-tuple-element.18), channel_id=1, source_target_pairs={{0,4},{4,8},{8,12},{12,0},{1,5},{5,9},{9,13},{13,1},{2,6},{6,10},{... | collective-permute-start | bytes 92168 | tf_op jit(solution)/shard_map/ppermute | solution.py:485
  5.5 2.1 %collective-permute-start.1 = (f32[6,1280]{1,0:T(8,128)S(1)}, f32[6,1280]{1,0:T(8,128)S(1)}, u32[]{:S(2)}, u32[]{:S(2)}) collective-permute-start(f32[6,1280]{1,0:T(8,128)S(1)} %get-tuple-element.19), channel_id=1, source_target_pairs={{0,12},{4,0},{8,4},{12,8},{1,13},{5,1},{9,5},{13,9},{2,14},{6,2},{... | collective-permute-start | bytes 92168 | tf_op jit(solution)/shard_map/ppermute | solution.py:485
  7.5 0.9 %collective-permute-start.2 = (f32[6,256]{1,0:T(8,128)S(1)}, f32[6,256]{1,0:T(8,128)S(1)}, u32[]{:S(2)}, u32[]{:S(2)}) collective-permute-start(f32[6,256]{1,0:T(8,128)S(1)} %get-tuple-element.20.own_ref), channel_id=1, source_target_pairs={{0,8},{4,12},{8,0},{12,4},{1,9},{5,13},{9,1},{13,5},{2,10},{6,14},... | collective-permute-start | bytes 18440 | tf_op jit(solution)/shard_map/ppermute | solution.py:485
  8.5 3.6 %collective-permute-done.2.far_ref = f32[6,256]{1,0:T(8,128)S(1)} collective-permute-done((f32[6,256]{1,0:T(8,128)S(1)}, f32[6,256]{1,0:T(8,128)S(1)}, u32[]{:S(2)}, u32[]{:S(2)}) %collective-permute-start.2) | collective-permute-done | bytes 6176 | tf_op jit(solution)/shard_map/ppermute | solution.py:485
  12.1 0.0 collective-permute-done.low_ref
  12.1 0.0 collective-permute-done.1.high_ref
  12.1 0.0 copy-start.3
  12.1 0.0 copy-start.5
  12.2 2.4 %shard_map.92 = (f32[6,128,256]{2,1,0:T(8,128)S(1)}, f32[6,512]{1,0:T(8,128)S(1)}, f32[6,512]{1,0:T(8,128)S(1)}, f32[6,256]{1,0:T(8,128)S(1)}) custom-call(bf16[6,128,1024]{2,1,0:T(8,128)(2,1)S(1)} %copy-done.1, f32[6,1280]{1,0:T(8,128)S(1)} %collective-permute-done.low_ref, f32[6,1280]{1,0:T(8,128)S(1)} %collective-permute-done.1.high_ref, ...), custom_call_target="tpu_custom_call" | custom-call | flops 1207959552 | tf_op jit(solution)/shard_map/pallas_call | solution.py:456
  14.5 0.1 collective-permute-start.3
  14.6 3.8 %collective-permute-start.4 = (f32[6,512]{1,0:T(8,128)S(1)}, f32[6,512]{1,0:T(8,128)S(1)}, u32[]{:S(2)}, u32[]{:S(2)}) collective-permute-start(f32[6,512]{1,0:T(8,128)S(1)} %get-tuple-element.23), channel_id=1, source_target_pairs={{0,12},{4,0},{8,4},{12,8},{1,13},{5,1},{9,5},{13,9},{2,14},{6,2},{... | collective-permute-start | bytes 36872 | tf_op jit(solution)/shard_map/ppermute | solution.py:485
  18.4 0.0 collective-permute-start.5
  18.4 4.5 %collective-permute-done.5.far_ref = f32[6,256]{1,0:T(8,128)S(1)} collective-permute-done((f32[6,256]{1,0:T(8,128)S(1)}, f32[6,256]{1,0:T(8,128)S(1)}, u32[]{:S(2)}, u32[]{:S(2)}) %collective-permute-start.5) | collective-permute-done | bytes 6176 | tf_op jit(solution)/shard_map/ppermute | solution.py:485
  23.0 0.0 collective-permute-done.3.low_ref
  23.0 0.0 collective-permute-done.4.high_ref
  23.0 1.2 %shard_map.94 = (bf16[192,1024]{1,0:T(8,128)(2,1)S(1)}, bf16[192,1024]{1,0:T(8,128)(2,1)S(1)}) custom-call(f32[6,128,256]{2,1,0:T(8,128)S(1)} %get-tuple-element.21.hid_ref, f32[6,512]{1,0:T(8,128)S(1)} %collective-permute-done.3.low_ref, f32[6,512]{1,0:T(8,128)S(1)} %collective-permute-done.4.high_ref, f32[6,256]{1,0:T(8,128)S(1)} %collective-permute-done.5.far_ref, ...), custom_call_target="tpu_custom_call" | custom-call | flops 603979776 | tf_op jit(solution)/shard_map/pallas_call | solution.py:456
  24.1 0.1 collective-permute-start.7
  24.2 1.1 %shard_map.97 = bf16[2,512,256]{2,1,0:T(8,128)(2,1)S(1)} custom-call(bf16[3,1024,256]{2,1,0:T(8,128)(2,1)} %bitcast.10, bf16[256,1024]{1,0:T(8,128)(2,1)} %out_ref.3), custom_call_target="tpu_custom_call" | custom-call | bytes 1048576 | tf_op jit(solution)/shard_map/pallas_call | solution.py:417
  25.4 1.7 %collective-permute-start.11 = (bf16[2,512,256]{2,1,0:T(8,128)(2,1)S(1)}, bf16[2,512,256]{2,1,0:T(8,128)(2,1)S(1)}, u32[]{:S(2)}, u32[]{:S(2)}) collective-permute-start(bf16[2,512,256]{2,1,0:T(8,128)(2,1)S(1)} %shard_map.97), channel_id=1, source_target_pairs={{0,2},{2,0},{1,3},{3,1},{4,6},{6,4},{5,7},{7,5},{8,10},{10,8},{9,1... | collective-permute-start | bytes 1572872 | tf_op jit(solution)/shard_map/ppermute | solution.py:472
  27.1 1.1 %shard_map.96 = bf16[2,512,256]{2,1,0:T(8,128)(2,1)S(1)} custom-call(bf16[3,1024,256]{2,1,0:T(8,128)(2,1)} %bitcast.11), custom_call_target="tpu_custom_call" | custom-call | bytes 1048576 | tf_op jit(solution)/shard_map/pallas_call | solution.py:417
  28.2 0.0 copy-start.2
  28.2 0.4 collective-permute-start.10
  28.7 1.2 %shard_map.93 = (bf16[192,1024]{1,0:T(8,128)(2,1)S(1)}, bf16[192,1024]{1,0:T(8,128)(2,1)S(1)}) custom-call(f32[6,128,256]{2,1,0:T(8,128)S(1)} %get-tuple-element.21.hid_ref, f32[6,512]{1,0:T(8,128)S(1)} %collective-permute-done.3.low_ref, f32[6,512]{1,0:T(8,128)S(1)} %collective-permute-done.4.high_ref, f32[6,256]{1,0:T(8,128)S(1)} %collective-permute-done.5.far_ref, ...), custom_call_target="tpu_custom_call" | custom-call | flops 603979776 | tf_op jit(solution)/shard_map/pallas_call | solution.py:456
  29.8 0.1 collective-permute-start.6
  29.9 0.0 collective-permute-done.7
  29.9 0.1 add_convert_fusion
  30.1 1.7 %collective-permute-start.8 = (bf16[192,1024]{1,0:T(8,128)(2,1)S(1)}, bf16[192,1024]{1,0:T(8,128)(2,1)S(1)}, u32[]{:S(2)}, u32[]{:S(2)}) collective-permute-start(bf16[192,1024]{1,0:T(8,128)(2,1)S(1)} %add_convert_fusion), channel_id=1, source_target_pairs={{0,2},{2,0},{1,3},{3,1},{4,6},{6,4},{5,7},{7,5},{8,10},{10,8},{9,1... | collective-permute-start | bytes 1179656 | tf_op jit(solution)/shard_map/ppermute | solution.py:472
  31.8 19.7 %collective-permute-done.10.heads_x_ref = bf16[2,512,256]{2,1,0:T(8,128)(2,1)S(1)} collective-permute-done((bf16[2,512,256]{2,1,0:T(8,128)(2,1)S(1)}, bf16[2,512,256]{2,1,0:T(8,128)(2,1)S(1)}, u32[]{:S(2)}, u32[]{:S(2)}) %collective-permute-start.10) | collective-permute-done | bytes 524320 | tf_op jit(solution)/shard_map/ppermute | solution.py:472
  51.5 1.7 %collective-permute-start.12 = (bf16[2,512,256]{2,1,0:T(8,128)(2,1)S(1)}, bf16[2,512,256]{2,1,0:T(8,128)(2,1)S(1)}, u32[]{:S(2)}, u32[]{:S(2)}) collective-permute-start(bf16[2,512,256]{2,1,0:T(8,128)(2,1)S(1)} %collective-permute-done.10.heads_x_ref), channel_id=1, source_target_pairs={{0,16},{16,0},{1,17},{17,1},{2,18},{18,2},{3,19},{19,3},{4,20},{20... | collective-permute-start | bytes 1572872 | tf_op jit(solution)/shard_map/ppermute | solution.py:476
  53.1 0.0 collective-permute-done.6.got_ref
  53.2 6.3 %collective-permute-done.8.far_ref = bf16[192,1024]{1,0:T(8,128)(2,1)S(1)} collective-permute-done((bf16[192,1024]{1,0:T(8,128)(2,1)S(1)}, bf16[192,1024]{1,0:T(8,128)(2,1)S(1)}, u32[]{:S(2)}, u32[]{:S(2)}) %collective-permute-start.8) | collective-permute-done | bytes 393248 | tf_op jit(solution)/shard_map/ppermute | solution.py:472
  59.4 0.2 shard_map.95.mine_ref
  59.6 0.1 collective-permute-start.9
  59.7 0.0 collective-permute-done.11
  59.8 1.7 %collective-permute-start.13 = (bf16[512,256]{1,0:T(8,128)(2,1)S(1)}, bf16[512,256]{1,0:T(8,128)(2,1)S(1)}, u32[]{:S(2)}, u32[]{:S(2)}) collective-permute-start(bf16[512,256]{1,0:T(8,128)(2,1)S(1)} %get-tuple-element.34.values_x_ref), channel_id=1, source_target_pairs={{0,16},{16,0},{1,17},{17,1},{2,18},{18,2},{3,19},{19,3},{4,20},{20... | collective-permute-start | bytes 786440 | tf_op jit(solution)/shard_map/ppermute | solution.py:476
  61.5 0.0 collective-permute-start.14
  61.5 8.5 %collective-permute-done.13.values_y_ref = bf16[512,256]{1,0:T(8,128)(2,1)S(1)} collective-permute-done((bf16[512,256]{1,0:T(8,128)(2,1)S(1)}, bf16[512,256]{1,0:T(8,128)(2,1)S(1)}, u32[]{:S(2)}, u32[]{:S(2)}) %collective-permute-start.13) | collective-permute-done | bytes 262176 | tf_op jit(solution)/shard_map/ppermute | solution.py:476
  70.1 0.0 collective-permute-done.12.heads_y_ref
  70.1 0.0 collective-permute-done.9.theirs_ref
  70.1 6.5 %shard_map.98 = (bf16[384,512]{1,0:T(8,128)(2,1)S(1)}, f32[384,512]{1,0:T(8,128)S(1)}) custom-call(bf16[192,1024]{1,0:T(8,128)(2,1)S(1)} %shard_map.95.mine_ref, bf16[192,1024]{1,0:T(8,128)(2,1)S(1)} %collective-permute-done.9.theirs_ref, f32[1,1024]{1,0:T(1,128)S(1)} %bitcast.17, bf16[3,1024,256]{2,1,0:T(8,128)(2,1)S(1)} %bitcast.12, ...), custom_call_target="tpu_custom_call" | custom-call | flops 1207959552 | tf_op jit(solution)/shard_map/pallas_call | solution.py:456
  76.6 0.1 collective-permute-start.15
  76.7 1.7 %collective-permute-done.15 = bf16[384,512]{1,0:T(8,128)(2,1)S(1)} collective-permute-done((bf16[384,512]{1,0:T(8,128)(2,1)S(1)}, bf16[384,512]{1,0:T(8,128)(2,1)S(1)}, u32[]{:S(2)}, u32[]{:S(2)}) %collective-permute-start.15) | collective-permute-done | bytes 393248 | tf_op jit(solution)/shard_map/ppermute | solution.py:468
  78.4 0.1 add_convert_fusion.1
  78.5 1.7 %collective-permute-start.16 = (bf16[384,256]{1,0:T(8,128)(2,1)S(1)}, bf16[384,256]{1,0:T(8,128)(2,1)S(1)}, u32[]{:S(2)}, u32[]{:S(2)}) collective-permute-start(bf16[384,256]{1,0:T(8,128)(2,1)S(1)} %get-tuple-element.31), channel_id=1, source_target_pairs={{0,2},{2,0},{1,3},{3,1},{4,6},{6,4},{5,7},{7,5},{8,10},{10,8},{9,1... | collective-permute-start | bytes 589832 | tf_op jit(solution)/shard_map/ppermute | solution.py:472
  80.2 5.3 %collective-permute-done.16.far_ref = bf16[384,256]{1,0:T(8,128)(2,1)S(1)} collective-permute-done((bf16[384,256]{1,0:T(8,128)(2,1)S(1)}, bf16[384,256]{1,0:T(8,128)(2,1)S(1)}, u32[]{:S(2)}, u32[]{:S(2)}) %collective-permute-start.16) | collective-permute-done | bytes 196640 | tf_op jit(solution)/shard_map/ppermute | solution.py:472
  85.5 0.8 shard_map.99
  (18 shorter events, 0.1 us)
Async XLA Ops:
  0.0 1.4 %copy-start.1 = (bf16[6,128,1024]{2,1,0:T(8,128)(2,1)S(1)}, bf16[6,128,1024]{2,1,0:T(8,128)(2,1)}, u32[]{:S(2)}) copy-start(bf16[6,128,1024]{2,1,0:T(8,128)(2,1)} %latent_ref.1) | copy-start | bytes 4718596
  1.4 10.7 %copy-start.7 = (bf16[3,1024,256]{2,1,0:T(8,128)(2,1)S(1)}, bf16[3,1024,256]{2,1,0:T(8,128)(2,1)}, u32[]{:S(2)}) copy-start(bf16[3,1024,256]{2,1,0:T(8,128)(2,1)} %weight_ref.1) | copy-start | bytes 4718596
  1.4 10.7 %copy-start.8 = (f32[1024]{0:T(1024)S(1)}, f32[1024]{0:T(1024)}, u32[]{:S(2)}) copy-start(f32[1024]{0:T(1024)} %param.10) | copy-start | bytes 12292
  1.4 10.7 %copy-start.9 = (f32[256]{0:T(256)S(1)}, f32[256]{0:T(256)}, u32[]{:S(2)}) copy-start(f32[256]{0:T(256)} %param.12) | copy-start | bytes 3076
  2.4 9.7 %collective-permute-start = (f32[6,1280]{1,0:T(8,128)S(1)}, f32[6,1280]{1,0:T(8,128)S(1)}, u32[]{:S(2)}, u32[]{:S(2)}) collective-permute-start(f32[6,1280]{1,0:T(8,128)S(1)} %get-tuple-element.18), channel_id=1, source_target_pairs={{0,4},{4,8},{8,12},{12,0},{1,5},{5,9},{9,13},{13,1},{2,6},{6,10},{... | collective-permute-start | bytes 92168 | tf_op jit(solution)/shard_map/ppermute | solution.py:485
  5.5 6.6 %collective-permute-start.1 = (f32[6,1280]{1,0:T(8,128)S(1)}, f32[6,1280]{1,0:T(8,128)S(1)}, u32[]{:S(2)}, u32[]{:S(2)}) collective-permute-start(f32[6,1280]{1,0:T(8,128)S(1)} %get-tuple-element.19), channel_id=1, source_target_pairs={{0,12},{4,0},{8,4},{12,8},{1,13},{5,1},{9,5},{13,9},{2,14},{6,2},{... | collective-permute-start | bytes 92168 | tf_op jit(solution)/shard_map/ppermute | solution.py:485
  7.5 4.5 %collective-permute-start.2 = (f32[6,256]{1,0:T(8,128)S(1)}, f32[6,256]{1,0:T(8,128)S(1)}, u32[]{:S(2)}, u32[]{:S(2)}) collective-permute-start(f32[6,256]{1,0:T(8,128)S(1)} %get-tuple-element.20.own_ref), channel_id=1, source_target_pairs={{0,8},{4,12},{8,0},{12,4},{1,9},{5,13},{9,1},{13,5},{2,10},{6,14},... | collective-permute-start | bytes 18440 | tf_op jit(solution)/shard_map/ppermute | solution.py:485
  12.1 10.8 %copy-start.3 = (bf16[3,256,1024]{2,1,0:T(8,128)(2,1)S(1)}, bf16[3,256,1024]{2,1,0:T(8,128)(2,1)}, u32[]{:S(2)}) copy-start(bf16[3,256,1024]{2,1,0:T(8,128)(2,1)} %param.14) | copy-start | bytes 4718596
  12.1 10.8 %copy-start.5 = (f32[256]{0:T(256)S(1)}, f32[256]{0:T(256)}, u32[]{:S(2)}) copy-start(f32[256]{0:T(256)} %param.13) | copy-start | bytes 3076
  14.5 8.4 %collective-permute-start.3 = (f32[6,512]{1,0:T(8,128)S(1)}, f32[6,512]{1,0:T(8,128)S(1)}, u32[]{:S(2)}, u32[]{:S(2)}) collective-permute-start(f32[6,512]{1,0:T(8,128)S(1)} %get-tuple-element.22), channel_id=1, source_target_pairs={{0,4},{4,8},{8,12},{12,0},{1,5},{5,9},{9,13},{13,1},{2,6},{6,10},{... | collective-permute-start | bytes 36872 | tf_op jit(solution)/shard_map/ppermute | solution.py:485
  14.6 8.3 %collective-permute-start.4 = (f32[6,512]{1,0:T(8,128)S(1)}, f32[6,512]{1,0:T(8,128)S(1)}, u32[]{:S(2)}, u32[]{:S(2)}) collective-permute-start(f32[6,512]{1,0:T(8,128)S(1)} %get-tuple-element.23), channel_id=1, source_target_pairs={{0,12},{4,0},{8,4},{12,8},{1,13},{5,1},{9,5},{13,9},{2,14},{6,2},{... | collective-permute-start | bytes 36872 | tf_op jit(solution)/shard_map/ppermute | solution.py:485
  18.4 4.5 %collective-permute-start.5 = (f32[6,256]{1,0:T(8,128)S(1)}, f32[6,256]{1,0:T(8,128)S(1)}, u32[]{:S(2)}, u32[]{:S(2)}) collective-permute-start(f32[6,256]{1,0:T(8,128)S(1)} %get-tuple-element.24.own_ref), channel_id=1, source_target_pairs={{0,8},{4,12},{8,0},{12,4},{1,9},{5,13},{9,1},{13,5},{2,10},{6,14},... | collective-permute-start | bytes 18440 | tf_op jit(solution)/shard_map/ppermute | solution.py:485
  24.1 5.8 %collective-permute-start.7 = (bf16[192,1024]{1,0:T(8,128)(2,1)S(1)}, bf16[192,1024]{1,0:T(8,128)(2,1)S(1)}, u32[]{:S(2)}, u32[]{:S(2)}) collective-permute-start(bf16[192,1024]{1,0:T(8,128)(2,1)S(1)} %get-tuple-element.27), channel_id=1, source_target_pairs={{0,1},{1,0},{2,3},{3,2},{4,5},{5,4},{6,7},{7,6},{8,9},{9,8},{10,11... | collective-permute-start | bytes 1179656 | tf_op jit(solution)/shard_map/ppermute | solution.py:468
  25.4 34.3 %collective-permute-start.11 = (bf16[2,512,256]{2,1,0:T(8,128)(2,1)S(1)}, bf16[2,512,256]{2,1,0:T(8,128)(2,1)S(1)}, u32[]{:S(2)}, u32[]{:S(2)}) collective-permute-start(bf16[2,512,256]{2,1,0:T(8,128)(2,1)S(1)} %shard_map.97), channel_id=1, source_target_pairs={{0,2},{2,0},{1,3},{3,1},{4,6},{6,4},{5,7},{7,5},{8,10},{10,8},{9,1... | collective-permute-start | bytes 1572872 | tf_op jit(solution)/shard_map/ppermute | solution.py:472
  28.2 31.2 %copy-start.2 = (bf16[6,128,1024]{2,1,0:T(8,128)(2,1)S(1)}, bf16[6,128,1024]{2,1,0:T(8,128)(2,1)}, u32[]{:S(2)}) copy-start(bf16[6,128,1024]{2,1,0:T(8,128)(2,1)} %latent_ref.1) | copy-start | bytes 4718596
  28.2 23.2 %collective-permute-start.10 = (bf16[2,512,256]{2,1,0:T(8,128)(2,1)S(1)}, bf16[2,512,256]{2,1,0:T(8,128)(2,1)S(1)}, u32[]{:S(2)}, u32[]{:S(2)}) collective-permute-start(bf16[2,512,256]{2,1,0:T(8,128)(2,1)S(1)} %shard_map.96), channel_id=1, source_target_pairs={{0,2},{2,0},{1,3},{3,1},{4,6},{6,4},{5,7},{7,5},{8,10},{10,8},{9,1... | collective-permute-start | bytes 1572872 | tf_op jit(solution)/shard_map/ppermute | solution.py:472
  29.8 23.3 %collective-permute-start.6 = (bf16[192,1024]{1,0:T(8,128)(2,1)S(1)}, bf16[192,1024]{1,0:T(8,128)(2,1)S(1)}, u32[]{:S(2)}, u32[]{:S(2)}) collective-permute-start(bf16[192,1024]{1,0:T(8,128)(2,1)S(1)} %get-tuple-element.26), channel_id=1, source_target_pairs={{0,1},{1,0},{2,3},{3,2},{4,5},{5,4},{6,7},{7,6},{8,9},{9,8},{10,11... | collective-permute-start | bytes 1179656 | tf_op jit(solution)/shard_map/ppermute | solution.py:468
  30.1 29.3 %collective-permute-start.8 = (bf16[192,1024]{1,0:T(8,128)(2,1)S(1)}, bf16[192,1024]{1,0:T(8,128)(2,1)S(1)}, u32[]{:S(2)}, u32[]{:S(2)}) collective-permute-start(bf16[192,1024]{1,0:T(8,128)(2,1)S(1)} %add_convert_fusion), channel_id=1, source_target_pairs={{0,2},{2,0},{1,3},{3,1},{4,6},{6,4},{5,7},{7,5},{8,10},{10,8},{9,1... | collective-permute-start | bytes 1179656 | tf_op jit(solution)/shard_map/ppermute | solution.py:472
  51.5 18.6 %collective-permute-start.12 = (bf16[2,512,256]{2,1,0:T(8,128)(2,1)S(1)}, bf16[2,512,256]{2,1,0:T(8,128)(2,1)S(1)}, u32[]{:S(2)}, u32[]{:S(2)}) collective-permute-start(bf16[2,512,256]{2,1,0:T(8,128)(2,1)S(1)} %collective-permute-done.10.heads_x_ref), channel_id=1, source_target_pairs={{0,16},{16,0},{1,17},{17,1},{2,18},{18,2},{3,19},{19,3},{4,20},{20... | collective-permute-start | bytes 1572872 | tf_op jit(solution)/shard_map/ppermute | solution.py:476
  59.4 10.7 %copy-start = (bf16[1024,3,256]{2,0,1:T(8,128)(2,1)S(1)}, bf16[1024,3,256]{2,0,1:T(8,128)(2,1)}, u32[]{:S(2)}) copy-start(bf16[1024,3,256]{2,0,1:T(8,128)(2,1)} %param.16) | copy-start | bytes 4718596
  59.4 10.7 %copy-start.4 = (bf16[256,1024]{1,0:T(8,128)(2,1)S(1)}, bf16[256,1024]{1,0:T(8,128)(2,1)}, u32[]{:S(2)}) copy-start(bf16[256,1024]{1,0:T(8,128)(2,1)} %out_ref.3) | copy-start | bytes 1572868
  59.4 10.7 %copy-start.6 = (f32[1024]{0:T(1024)S(1)}, f32[1024]{0:T(1024)}, u32[]{:S(2)}) copy-start(f32[1024]{0:T(1024)} %param.15) | copy-start | bytes 12292
  59.6 10.4 %collective-permute-start.9 = (bf16[192,1024]{1,0:T(8,128)(2,1)S(1)}, bf16[192,1024]{1,0:T(8,128)(2,1)S(1)}, u32[]{:S(2)}, u32[]{:S(2)}) collective-permute-start(bf16[192,1024]{1,0:T(8,128)(2,1)S(1)} %shard_map.95.mine_ref), channel_id=1, source_target_pairs={{0,1},{1,0},{2,3},{3,2},{4,5},{5,4},{6,7},{7,6},{8,9},{9,8},{10,11... | collective-permute-start | bytes 1179656 | tf_op jit(solution)/shard_map/ppermute | solution.py:468
  59.8 10.3 %collective-permute-start.13 = (bf16[512,256]{1,0:T(8,128)(2,1)S(1)}, bf16[512,256]{1,0:T(8,128)(2,1)S(1)}, u32[]{:S(2)}, u32[]{:S(2)}) collective-permute-start(bf16[512,256]{1,0:T(8,128)(2,1)S(1)} %get-tuple-element.34.values_x_ref), channel_id=1, source_target_pairs={{0,16},{16,0},{1,17},{17,1},{2,18},{18,2},{3,19},{19,3},{4,20},{20... | collective-permute-start | bytes 786440 | tf_op jit(solution)/shard_map/ppermute | solution.py:476
  61.5 8.6 %collective-permute-start.14 = (bf16[512,256]{1,0:T(8,128)(2,1)S(1)}, bf16[512,256]{1,0:T(8,128)(2,1)S(1)}, u32[]{:S(2)}, u32[]{:S(2)}) collective-permute-start(bf16[512,256]{1,0:T(8,128)(2,1)S(1)} %get-tuple-element.33.outs_x_ref), channel_id=1, source_target_pairs={{0,4},{4,0},{8,12},{12,8},{1,5},{5,1},{9,13},{13,9},{2,6},{6,2},{1... | collective-permute-start | bytes 786440 | tf_op jit(solution)/shard_map/ppermute | solution.py:480
  76.6 1.8 %collective-permute-start.15 = (bf16[384,512]{1,0:T(8,128)(2,1)S(1)}, bf16[384,512]{1,0:T(8,128)(2,1)S(1)}, u32[]{:S(2)}, u32[]{:S(2)}) collective-permute-start(bf16[384,512]{1,0:T(8,128)(2,1)S(1)} %get-tuple-element.30), channel_id=1, source_target_pairs={{0,1},{1,0},{2,3},{3,2},{4,5},{5,4},{6,7},{7,6},{8,9},{9,8},{10,11... | collective-permute-start | bytes 1179656 | tf_op jit(solution)/shard_map/ppermute | solution.py:468
  78.5 7.0 %collective-permute-start.16 = (bf16[384,256]{1,0:T(8,128)(2,1)S(1)}, bf16[384,256]{1,0:T(8,128)(2,1)S(1)}, u32[]{:S(2)}, u32[]{:S(2)}) collective-permute-start(bf16[384,256]{1,0:T(8,128)(2,1)S(1)} %get-tuple-element.31), channel_id=1, source_target_pairs={{0,2},{2,0},{1,3},{3,1},{4,6},{6,4},{5,7},{7,5},{8,10},{10,8},{9,1... | collective-permute-start | bytes 589832 | tf_op jit(solution)/shard_map/ppermute | solution.py:472

commit v4 on v3

--- a/solution.py
+++ b/solution.py
@@ -151,8 +151,7 @@
     return velocity
 
 
-def silu(v):
-    half = 0.5 * v
+def silu_of_half(half):
     return half + half * jnp.tanh(half)
 
 
@@ -209,10 +208,10 @@
         [own_ref[...], low_ref[:, channels:], high_ref[:, channels:], far_ref[...]],
         entries, channels, width,
     )
-    scale = scale * gain_ref[...]
+    scale = scale * (0.5 * gain_ref[...])
     edge_ref[...] = jnp.zeros_like(edge_ref)
-    low = silu((low_ref[:, :channels] - centre) * scale)
-    high = silu((high_ref[:, :channels] - centre) * scale)
+    low = silu_of_half((low_ref[:, :channels] - centre) * scale)
+    high = silu_of_half((high_ref[:, :channels] - centre) * scale)
     edge_ref[0:stems, :] = jnp.where(place > 0, low, 0.0)
     edge_ref[8 : 8 + stems, :] = jnp.where(place < frame_size - 1, high, 0.0)
     edge = edge_ref[...].astype(bf16)
@@ -225,7 +224,7 @@
         for stem in range(first, first + step):
             block = lat_ref[stem].astype(f32)
             block = (block - centre[stem : stem + 1]) * scale[stem : stem + 1]
-            act_ref[stem * frames : (stem + 1) * frames, :] = silu(block).astype(bf16)
+            act_ref[stem * frames : (stem + 1) * frames, :] = silu_of_half(block).astype(bf16)
         rows = act_ref[first * frames : (first + step) * frames, :]
         taps = [jnp.dot(rows, weight_ref[tap], preferred_element_type=f32) for tap in range(3)]
         for stem in range(first, first + step):
@@ -260,18 +259,18 @@
         [own_ref[...], low_ref[:, shard:], high_ref[:, shard:], far_ref[...]],
         entries, shard, width,
     )
-    scale = scale * gain_ref[...]
-    low = jnp.where(place > 0, silu((low_ref[:, :shard] - centre) * scale), 0.0)
+    scale = scale * (0.5 * gain_ref[...])
+    low = jnp.where(place > 0, silu_of_half((low_ref[:, :shard] - centre) * scale), 0.0)
     high = jnp.where(
-        place < frame_size - 1, silu((high_ref[:, :shard] - centre) * scale), 0.0
+        place < frame_size - 1, silu_of_half((high_ref[:, :shard] - centre) * scale), 0.0
     )
     row = lax.broadcasted_iota(jnp.int32, (WINDOW, shard), 0)
     half = stems // 2
     for stem in range(stems):
         start = pl.multiple_of(window * WINDOW, WINDOW)
         mean, factor = centre[stem : stem + 1], scale[stem : stem + 1]
-        act = silu((hid_ref[stem, pl.ds(start, WINDOW), :] - mean) * factor)
-        inner = silu((hid_ref[stem, WINDOW - 8 : WINDOW + 8, :] - mean) * factor)
+        act = silu_of_half((hid_ref[stem, pl.ds(start, WINDOW), :] - mean) * factor)
+        inner = silu_of_half((hid_ref[stem, WINDOW - 8 : WINDOW + 8, :] - mean) * factor)
         before = jnp.where(window == 0, low[stem : stem + 1], inner[7:8])
         after = jnp.where(window == 0, inner[8:9], high[stem : stem + 1])
         before = jnp.where(row == 0, before, pltpu.roll(act, 1, 0))
@@ -295,7 +294,8 @@
 def attention_kernel(
     mine_ref, theirs_ref, gain_ref, qkv_ref, out_ref,
     heads_x_ref, values_x_ref, outs_x_ref, heads_y_ref, values_y_ref, outs_z_ref,
-    send_ref, keep_ref, res_ref, normed_ref, context_ref,
+    send_far_ref, keep_far_ref, send_near_ref, keep_near_ref,
+    res_ref, normed_ref, context_ref,
 ):
     rows, channels = mine_ref.shape
     shard = qkv_ref.shape[2]
@@ -313,9 +313,6 @@
         ).astype(bf16)
     normed = normed_ref[...]
     lane = lax.broadcasted_iota(jnp.int32, (2 * rows, LANES), 1)
-    per_tile = LANES // HEAD_DIM
-    ones = jnp.ones((2 * rows, LANES), bf16)
-    zero = jnp.zeros((), bf16)
     nt = (((1,), (1,)), ((), ()))
     near_at = pl.ds(pl.multiple_of(group * depth, depth), depth)
     away_at = pl.ds(pl.multiple_of((1 - group) * depth, depth), depth)
@@ -331,26 +328,36 @@
     for side in range(2):
         queries, keys, values = [project(side, which) for which in range(3)]
         queries = queries * (1.0 / math.sqrt(HEAD_DIM))
-        values = values.astype(bf16)
         for tile in range(shard // LANES):
             at = slice(tile * LANES, (tile + 1) * LANES)
             q_high, q_low = split2(queries[:, at])
-            left = jnp.concatenate([q_high, q_low, q_high, q_low], axis=1)
+            q_low = pltpu.roll(q_low.astype(f32), HEAD_DIM, 1).astype(bf16)
             k_high, k_low = split2(keys[:, at])
-            mixing = jnp.concatenate([values[:, at], ones], axis=1)
-            result = None
-            for head in range(per_tile):
+            k_rolled = split2(pltpu.roll(keys[:, at], HEAD_DIM, 1))
+            terms, mixing = [], []
+            for head in range(LANES // HEAD_DIM):
                 inside = lane // HEAD_DIM == head
-                own_high = jnp.where(inside, k_high, zero)
-                own_low = jnp.where(inside, k_low, zero)
-                right = jnp.concatenate([own_high, own_high, own_low, own_low], axis=1)
+                left = jnp.where(inside, q_high, q_low)
+                left = jnp.concatenate([left, left], axis=1)
+                right = [
+                    jnp.where(inside, own, rolled)
+                    for own, rolled in zip((k_high, k_low), k_rolled)
+                ]
+                right = jnp.concatenate(right, axis=1)
                 scores = lax.dot_general(left, right, nt, preferred_element_type=f32)
-                scores = jnp.exp(scores - jnp.max(scores, axis=1, keepdims=True)).astype(bf16)
-                mixed = jnp.dot(scores, mixing, preferred_element_type=f32)
-                mixed = mixed[:, :LANES] / mixed[:, LANES:]
-                result = mixed if result is None else jnp.where(inside, mixed, result)
+                scores = jnp.exp(scores - jnp.max(scores, axis=1, keepdims=True))
+                terms.append(scores.astype(bf16))
+                mixing.append(
+                    jnp.concatenate(
+                        [jnp.where(inside, values[:, at], 0.0), jnp.where(inside, 1.0, 0.0)], axis=1
+                    ).astype(bf16)
+                )
+            mixed = jnp.dot(
+                jnp.concatenate(terms, axis=1), jnp.concatenate(mixing, axis=0),
+                preferred_element_type=f32,
+            )
             base = side * shard + tile * LANES
-            context_ref[:, base : base + LANES] = result.astype(bf16)
+            context_ref[:, base : base + LANES] = (mixed[:, :LANES] / mixed[:, LANES:]).astype(bf16)
     context = context_ref[:, :shard]
     parity = lax.axis_index("frame") % 2
     from_x = context_ref[:, pl.ds(pl.multiple_of(shard + parity * part, part), part)]
@@ -363,14 +370,14 @@
         value = value + jnp.dot(from_x, outs_x_ref[rows_at, :], preferred_element_type=f32)
         return value + jnp.dot(from_z, outs_z_ref[rows_at, :], preferred_element_type=f32)
 
-    for place, goal in enumerate((1 - chip, chip)):
-        at = slice(place * shard, (place + 1) * shard)
+    sides = ((1 - chip, send_far_ref, keep_far_ref), (chip, send_near_ref, keep_near_ref))
+    for goal, send_ref, keep_ref in sides:
         value = term(2 * goal + 1 - core).astype(bf16)
-        send_ref[:rows, at] = value[rows:]
-        send_ref[rows:, at] = value[:rows]
+        send_ref[:rows, :] = value[rows:]
+        send_ref[rows:, :] = value[:rows]
         block = 2 * goal + core
-        kept = term(block)
-        keep_ref[:, at] = kept + res_ref[:, pl.ds(pl.multiple_of(block * shard, shard), shard)]
+        at = pl.ds(pl.multiple_of(block * shard, shard), shard)
+        keep_ref[...] = term(block) + res_ref[:, at]
 
 
 def run_copies(pairs, sems):
@@ -438,18 +445,27 @@
         out_ref[rows, :] = (latent.astype(f32) + total).astype(bf16)
 
 
-def place_kernel(own_ref, far_ref, out_ref):
-    stems, _, _ = out_ref.shape
-    index = lax.axis_index("tensor")
-    chip, core = index // 2, index % 2
+def place(value_ref, out_ref, window, sems):
+    stems = out_ref.shape[0]
+    core = lax.axis_index("tensor") % 2
     half = stems // 2
+    at = pl.ds(pl.multiple_of(window * WINDOW, WINDOW), WINDOW)
+    pairs = []
     for stem in range(stems):
         goal = (core if stem < half else 1 - core) * half + stem % half
-        rows = slice(stem * WINDOW, (stem + 1) * WINDOW)
-        near = pl.multiple_of(chip * WINDOW, WINDOW)
-        away = pl.multiple_of((1 - chip) * WINDOW, WINDOW)
-        out_ref[goal, pl.ds(near, WINDOW), :] = own_ref[rows, :]
-        out_ref[goal, pl.ds(away, WINDOW), :] = far_ref[rows, :]
+        source = value_ref.at[pl.ds(stem * WINDOW, WINDOW), :]
+        pairs.append((source, out_ref.at[goal, at, :]))
+    run_copies(pairs, sems)
+
+
+def place_near_kernel(keep_ref, got_ref, out_ref, value_ref, sems):
+    value_ref[...] = (keep_ref[...] + got_ref[...].astype(f32)).astype(bf16)
+    place(value_ref, out_ref, lax.axis_index("tensor") // 2, sems)
+
+
+def place_far_kernel(value_ref, near_ref, out_ref, sems):
+    del near_ref
+    place(value_ref, out_ref, 1 - lax.axis_index("tensor") // 2, sems)
 
 
 def call(kernel, outs, scratch, args, flops=0, moved=0, limit=16):
@@ -552,20 +568,33 @@
         [latent, keep_own, got_own, summed],
     )[0]
     theirs = swap_cores(mine)
-    out_send, out_keep = call(
+    send_far, keep_far, send_near, keep_near = call(
         attention_kernel,
-        [((2 * half_rows, 2 * shard), bf16), ((2 * half_rows, 2 * shard), f32)],
+        [((2 * half_rows, shard), bf16), ((2 * half_rows, shard), f32)] * 2,
         [((2 * half_rows, channels), f32), ((2 * half_rows, channels), bf16),
          ((2 * half_rows, 2 * shard), bf16)],
         [mine, theirs, attn_gain[None], qkv, out_weight, heads_x, values_x, outs_x,
          heads_y, values_y, outs_z],
         flops=24 * half_rows * channels * shard, limit=24,
     )
-    out_got = swap_cores(out_send)
-    away = (out_keep[:, :shard] + out_got[:, :shard].astype(f32)).astype(bf16)
-    stay = (out_keep[:, shard:] + out_got[:, shard:].astype(f32)).astype(bf16)
+    got_far = swap_cores(send_far)
+    got_near = swap_cores(send_near)
+    away = (keep_far + got_far.astype(f32)).astype(bf16)
     arrived = swap_chips(away)
-    return call(place_kernel, [((stems, frames, shard), bf16)], [], [stay, arrived])[0]
+    vmem, anywhere = pl.BlockSpec(memory_space=VMEM), pl.BlockSpec(memory_space=pl.ANY)
+    shape = jax.ShapeDtypeStruct((stems, frames, shard), bf16)
+    sems = pltpu.SemaphoreType.DMA((stems,))
+    params = pltpu.CompilerParams(vmem_limit_bytes=4 * 2**20)
+    near = pl.pallas_call(
+        place_near_kernel, name="place_near", out_shape=shape,
+        in_specs=[vmem, vmem], out_specs=anywhere, compiler_params=params,
+        scratch_shapes=[VMEM((2 * half_rows, shard), bf16), sems],
+    )(keep_near, got_near)
+    return pl.pallas_call(
+        place_far_kernel, name="place_far", out_shape=shape,
+        in_specs=[vmem, anywhere], out_specs=anywhere, compiler_params=params,
+        scratch_shapes=[sems], input_output_aliases={1: 0},
+    )(arrived, near)
 
 
 def local(*args):

time: 86.5 us -> 84 us (0.971)
  waiting for transfers between devices: 49.7 us -> 48.1 us
  Pallas kernels: 15.3 us -> 13.9 us
    pallas_call x7 -> x6, Pallas kernels: 13.1 us -> 10.1 us  [call(): pl.pallas_call(kernel, out_shape=[jax.ShapeDtypeStruct(shape, dtype) for...]
    pallas_call x0 -> x2, Pallas kernels: none -> 1.48 us  [the longest x1 0.76 us: fast(): pl.pallas_call(place_near_kernel, name='place_near', out_shape=shape, in_...]
  transfers between devices with their start and end apart: 17 -> 18, of which waited for: 7 -> 7; matrix products, arithmetic and copies ran while one was open for 0% -> 0% of each run, Pallas kernels for 4% -> 5%
where the time goes in v4:
time: 84 us; the launch traced here: 83.7 us
  waiting for transfers between devices  48.1 us (57%)
  starting transfers between devices  19.8 us (24%)
  Pallas kernels  13.9 us (17%)
  local copies, waits for them, and re-layouts  1.48 us (2%)
    ppermute x4, waiting for transfers between devices, swap_chips(): return lax.ppermute(value, 'tensor', [(0, 2), (2, 0), (1, 3), (3, 1)])  30.5 us
    pallas_call x6, Pallas kernels, call(): pl.pallas_call(kernel, out_shape=[jax.ShapeDtypeStruct(shape, dtype) for...  10.1 us
    ppermute x6, starting transfers between devices, shift_frames(): lax.ppermute(value, 'frame', [(i, (i + by) % count) for i in range(count)])  10 us
    ppermute x2, waiting for transfers between devices, swap_groups(): return lax.ppermute(value, 'groups', [(0, 1), (1, 0)])  8.54 us
    ppermute x6, waiting for transfers between devices, shift_frames(): lax.ppermute(value, 'frame', [(i, (i + by) % count) for i in range(count)])  8.16 us
    ppermute x4, starting transfers between devices, swap_chips(): return lax.ppermute(value, 'tensor', [(0, 2), (2, 0), (1, 3), (3, 1)])  5.59 us
    ppermute x2, starting transfers between devices, swap_groups(): return lax.ppermute(value, 'groups', [(0, 1), (1, 0)])  3.43 us
    pallas_call x2, Pallas kernels, pack(): pl.pallas_call(kernel, out_shape=jax.ShapeDtypeStruct(shape, bf16), in_sp...  2.27 us
  transfers between devices with their start and end apart: 18, of which 7 were waited for; matrix products, arithmetic and copies ran while one was open for 0% of the time, Pallas kernels for 5%

profile of v4, /device:TPU:0, one launch (start us, length us, event | category | flops | bytes accessed | tf_op | source)
XLA Modules:
  0.0 83.7 jit_solution(5283772977768224394)
XLA Ops:
  0.0 1.4 %copy-done.1 = bf16[6,128,1024]{2,1,0:T(8,128)(2,1)S(1)} copy-done((bf16[6,128,1024]{2,1,0:T(8,128)(2,1)S(1)}, bf16[6,128,1024]{2,1,0:T(8,128)(2,1)}, u32[]{:S(2)}) %copy-start.1) | copy-done | bytes 1572888
  1.4 0.9 %shard_map.91 = (f32[6,1280]{1,0:T(8,128)S(1)}, f32[6,1280]{1,0:T(8,128)S(1)}, f32[6,256]{1,0:T(8,128)S(1)}) custom-call(bf16[6,128,1024]{2,1,0:T(8,128)(2,1)S(1)} %copy-done.1), custom_call_target="tpu_custom_call" | custom-call | tf_op jit(solution)/shard_map/pallas_call | solution.py:472
  2.4 3.1 %collective-permute-start = (f32[6,1280]{1,0:T(8,128)S(1)}, f32[6,1280]{1,0:T(8,128)S(1)}, u32[]{:S(2)}, u32[]{:S(2)}) collective-permute-start(f32[6,1280]{1,0:T(8,128)S(1)} %get-tuple-element.20), channel_id=1, source_target_pairs={{0,4},{4,8},{8,12},{12,0},{1,5},{5,9},{9,13},{13,1},{2,6},{6,10},{... | collective-permute-start | bytes 92168 | tf_op jit(solution)/shard_map/ppermute | solution.py:501
  5.5 2.1 %collective-permute-start.1 = (f32[6,1280]{1,0:T(8,128)S(1)}, f32[6,1280]{1,0:T(8,128)S(1)}, u32[]{:S(2)}, u32[]{:S(2)}) collective-permute-start(f32[6,1280]{1,0:T(8,128)S(1)} %get-tuple-element.21), channel_id=1, source_target_pairs={{0,12},{4,0},{8,4},{12,8},{1,13},{5,1},{9,5},{13,9},{2,14},{6,2},{... | collective-permute-start | bytes 92168 | tf_op jit(solution)/shard_map/ppermute | solution.py:501
  7.5 0.9 %collective-permute-start.2 = (f32[6,256]{1,0:T(8,128)S(1)}, f32[6,256]{1,0:T(8,128)S(1)}, u32[]{:S(2)}, u32[]{:S(2)}) collective-permute-start(f32[6,256]{1,0:T(8,128)S(1)} %get-tuple-element.22.own_ref), channel_id=1, source_target_pairs={{0,8},{4,12},{8,0},{12,4},{1,9},{5,13},{9,1},{13,5},{2,10},{6,14},... | collective-permute-start | bytes 18440 | tf_op jit(solution)/shard_map/ppermute | solution.py:501
  8.5 3.6 %collective-permute-done.2.far_ref = f32[6,256]{1,0:T(8,128)S(1)} collective-permute-done((f32[6,256]{1,0:T(8,128)S(1)}, f32[6,256]{1,0:T(8,128)S(1)}, u32[]{:S(2)}, u32[]{:S(2)}) %collective-permute-start.2) | collective-permute-done | bytes 6176 | tf_op jit(solution)/shard_map/ppermute | solution.py:501
  12.1 0.0 collective-permute-done.low_ref
  12.1 0.0 copy-start.3
  12.1 0.0 copy-start.5
  12.2 2.2 %shard_map.92 = (f32[6,128,256]{2,1,0:T(8,128)S(1)}, f32[6,512]{1,0:T(8,128)S(1)}, f32[6,512]{1,0:T(8,128)S(1)}, f32[6,256]{1,0:T(8,128)S(1)}) custom-call(bf16[6,128,1024]{2,1,0:T(8,128)(2,1)S(1)} %copy-done.1, f32[6,1280]{1,0:T(8,128)S(1)} %collective-permute-done.low_ref, f32[6,1280]{1,0:T(8,128)S(1)} %collective-permute-done.1.high_ref, ...), custom_call_target="tpu_custom_call" | custom-call | flops 1207959552 | tf_op jit(solution)/shard_map/pallas_call | solution.py:472
  14.4 0.1 collective-permute-start.3
  14.5 3.8 %collective-permute-start.4 = (f32[6,512]{1,0:T(8,128)S(1)}, f32[6,512]{1,0:T(8,128)S(1)}, u32[]{:S(2)}, u32[]{:S(2)}) collective-permute-start(f32[6,512]{1,0:T(8,128)S(1)} %get-tuple-element.25), channel_id=1, source_target_pairs={{0,12},{4,0},{8,4},{12,8},{1,13},{5,1},{9,5},{13,9},{2,14},{6,2},{... | collective-permute-start | bytes 36872 | tf_op jit(solution)/shard_map/ppermute | solution.py:501
  18.2 4.5 %collective-permute-done.5.far_ref = f32[6,256]{1,0:T(8,128)S(1)} collective-permute-done((f32[6,256]{1,0:T(8,128)S(1)}, f32[6,256]{1,0:T(8,128)S(1)}, u32[]{:S(2)}, u32[]{:S(2)}) %collective-permute-start.5) | collective-permute-done | bytes 6176 | tf_op jit(solution)/shard_map/ppermute | solution.py:501
  22.8 0.0 collective-permute-done.3.low_ref
  22.8 0.0 collective-permute-done.4.high_ref
  22.8 1.1 %shard_map.94 = (bf16[192,1024]{1,0:T(8,128)(2,1)S(1)}, bf16[192,1024]{1,0:T(8,128)(2,1)S(1)}) custom-call(f32[6,128,256]{2,1,0:T(8,128)S(1)} %get-tuple-element.23.hid_ref, f32[6,512]{1,0:T(8,128)S(1)} %collective-permute-done.3.low_ref, f32[6,512]{1,0:T(8,128)S(1)} %collective-permute-done.4.high_ref, f32[6,256]{1,0:T(8,128)S(1)} %collective-permute-done.5.far_ref, ...), custom_call_target="tpu_custom_call" | custom-call | flops 603979776 | tf_op jit(solution)/shard_map/pallas_call | solution.py:472
  23.9 0.1 collective-permute-start.7
  24.0 1.1 %shard_map.97 = bf16[2,512,256]{2,1,0:T(8,128)(2,1)S(1)} custom-call(bf16[3,1024,256]{2,1,0:T(8,128)(2,1)} %bitcast.10, bf16[256,1024]{1,0:T(8,128)(2,1)} %out_ref.3), custom_call_target="tpu_custom_call" | custom-call | bytes 1048576 | tf_op jit(solution)/shard_map/pallas_call | solution.py:424
  25.2 1.7 %collective-permute-start.11 = (bf16[2,512,256]{2,1,0:T(8,128)(2,1)S(1)}, bf16[2,512,256]{2,1,0:T(8,128)(2,1)S(1)}, u32[]{:S(2)}, u32[]{:S(2)}) collective-permute-start(bf16[2,512,256]{2,1,0:T(8,128)(2,1)S(1)} %shard_map.97), channel_id=1, source_target_pairs={{0,2},{2,0},{1,3},{3,1},{4,6},{6,4},{5,7},{7,5},{8,10},{10,8},{9,1... | collective-permute-start | bytes 1572872 | tf_op jit(solution)/shard_map/ppermute | solution.py:488
  26.9 1.1 %shard_map.96 = bf16[2,512,256]{2,1,0:T(8,128)(2,1)S(1)} custom-call(bf16[3,1024,256]{2,1,0:T(8,128)(2,1)} %bitcast.11), custom_call_target="tpu_custom_call" | custom-call | bytes 1048576 | tf_op jit(solution)/shard_map/pallas_call | solution.py:424
  28.0 0.0 copy-start.2
  28.0 0.4 collective-permute-start.10
  28.5 1.1 %shard_map.93 = (bf16[192,1024]{1,0:T(8,128)(2,1)S(1)}, bf16[192,1024]{1,0:T(8,128)(2,1)S(1)}) custom-call(f32[6,128,256]{2,1,0:T(8,128)S(1)} %get-tuple-element.23.hid_ref, f32[6,512]{1,0:T(8,128)S(1)} %collective-permute-done.3.low_ref, f32[6,512]{1,0:T(8,128)S(1)} %collective-permute-done.4.high_ref, f32[6,256]{1,0:T(8,128)S(1)} %collective-permute-done.5.far_ref, ...), custom_call_target="tpu_custom_call" | custom-call | flops 603979776 | tf_op jit(solution)/shard_map/pallas_call | solution.py:472
  29.6 0.1 collective-permute-start.6
  29.7 0.0 collective-permute-done.7
  29.7 0.1 add_convert_fusion
  29.9 1.7 %collective-permute-start.8 = (bf16[192,1024]{1,0:T(8,128)(2,1)S(1)}, bf16[192,1024]{1,0:T(8,128)(2,1)S(1)}, u32[]{:S(2)}, u32[]{:S(2)}) collective-permute-start(bf16[192,1024]{1,0:T(8,128)(2,1)S(1)} %add_convert_fusion), channel_id=1, source_target_pairs={{0,2},{2,0},{1,3},{3,1},{4,6},{6,4},{5,7},{7,5},{8,10},{10,8},{9,1... | collective-permute-start | bytes 1179656 | tf_op jit(solution)/shard_map/ppermute | solution.py:488
  31.6 19.7 %collective-permute-done.10.heads_x_ref = bf16[2,512,256]{2,1,0:T(8,128)(2,1)S(1)} collective-permute-done((bf16[2,512,256]{2,1,0:T(8,128)(2,1)S(1)}, bf16[2,512,256]{2,1,0:T(8,128)(2,1)S(1)}, u32[]{:S(2)}, u32[]{:S(2)}) %collective-permute-start.10) | collective-permute-done | bytes 524320 | tf_op jit(solution)/shard_map/ppermute | solution.py:488
  51.3 1.7 %collective-permute-start.12 = (bf16[2,512,256]{2,1,0:T(8,128)(2,1)S(1)}, bf16[2,512,256]{2,1,0:T(8,128)(2,1)S(1)}, u32[]{:S(2)}, u32[]{:S(2)}) collective-permute-start(bf16[2,512,256]{2,1,0:T(8,128)(2,1)S(1)} %collective-permute-done.10.heads_x_ref), channel_id=1, source_target_pairs={{0,16},{16,0},{1,17},{17,1},{2,18},{18,2},{3,19},{19,3},{4,20},{20... | collective-permute-start | bytes 1572872 | tf_op jit(solution)/shard_map/ppermute | solution.py:492
  53.0 6.3 %collective-permute-done.8.far_ref = bf16[192,1024]{1,0:T(8,128)(2,1)S(1)} collective-permute-done((bf16[192,1024]{1,0:T(8,128)(2,1)S(1)}, bf16[192,1024]{1,0:T(8,128)(2,1)S(1)}, u32[]{:S(2)}, u32[]{:S(2)}) %collective-permute-start.8) | collective-permute-done | bytes 393248 | tf_op jit(solution)/shard_map/ppermute | solution.py:488
  59.2 0.2 shard_map.95.mine_ref
  59.4 0.1 collective-permute-start.9
  59.5 0.0 collective-permute-done.11
  59.6 1.7 %collective-permute-start.13 = (bf16[512,256]{1,0:T(8,128)(2,1)S(1)}, bf16[512,256]{1,0:T(8,128)(2,1)S(1)}, u32[]{:S(2)}, u32[]{:S(2)}) collective-permute-start(bf16[512,256]{1,0:T(8,128)(2,1)S(1)} %get-tuple-element.36.values_x_ref), channel_id=1, source_target_pairs={{0,16},{16,0},{1,17},{17,1},{2,18},{18,2},{3,19},{19,3},{4,20},{20... | collective-permute-start | bytes 786440 | tf_op jit(solution)/shard_map/ppermute | solution.py:492
  61.3 0.0 collective-permute-start.14
  61.3 8.5 %collective-permute-done.13.values_y_ref = bf16[512,256]{1,0:T(8,128)(2,1)S(1)} collective-permute-done((bf16[512,256]{1,0:T(8,128)(2,1)S(1)}, bf16[512,256]{1,0:T(8,128)(2,1)S(1)}, u32[]{:S(2)}, u32[]{:S(2)}) %collective-permute-start.13) | collective-permute-done | bytes 262176 | tf_op jit(solution)/shard_map/ppermute | solution.py:492
  69.9 0.0 collective-permute-done.12.heads_y_ref
  69.9 0.0 collective-permute-done.9.theirs_ref
  69.9 4.5 %shard_map.98 = (bf16[384,256]{1,0:T(8,128)(2,1)S(1)}, f32[384,256]{1,0:T(8,128)S(1)}, bf16[384,256]{1,0:T(8,128)(2,1)S(1)}, f32[384,256]{1,0:T(8,128)S(1)}) custom-call(bf16[192,1024]{1,0:T(8,128)(2,1)S(1)} %shard_map.95.mine_ref, bf16[192,1024]{1,0:T(8,128)(2,1)S(1)} %collective-permute-done.9.theirs_ref, f32[1,1024]{1,0:T(1,128)S(1)} %bitcast.17, ...), custom_call_target="tpu_custom_call" | custom-call | flops 1207959552 | tf_op jit(solution)/shard_map/pallas_call | solution.py:472
  74.4 0.1 collective-permute-start.15
  74.5 0.5 collective-permute-start.17
  75.0 0.9 %collective-permute-done.15 = bf16[384,256]{1,0:T(8,128)(2,1)S(1)} collective-permute-done((bf16[384,256]{1,0:T(8,128)(2,1)S(1)}, bf16[384,256]{1,0:T(8,128)(2,1)S(1)}, u32[]{:S(2)}, u32[]{:S(2)}) %collective-permute-start.15) | collective-permute-done | bytes 196640 | tf_op jit(solution)/shard_map/ppermute | solution.py:484
  75.9 0.1 add_convert_fusion.1
  76.0 1.7 %collective-permute-start.16 = (bf16[384,256]{1,0:T(8,128)(2,1)S(1)}, bf16[384,256]{1,0:T(8,128)(2,1)S(1)}, u32[]{:S(2)}, u32[]{:S(2)}) collective-permute-start(bf16[384,256]{1,0:T(8,128)(2,1)S(1)} %add_convert_fusion.1), channel_id=1, source_target_pairs={{0,2},{2,0},{1,3},{3,1},{4,6},{6,4},{5,7},{7,5},{8,10},{10,8},{9,1... | collective-permute-start | bytes 589832 | tf_op jit(solution)/shard_map/ppermute | solution.py:488
  77.7 0.0 collective-permute-done.17.got_ref
  77.7 0.8 place_near.1.near_ref
  78.5 4.5 %collective-permute-done.16.value_ref = bf16[384,256]{1,0:T(8,128)(2,1)S(1)} collective-permute-done((bf16[384,256]{1,0:T(8,128)(2,1)S(1)}, bf16[384,256]{1,0:T(8,128)(2,1)S(1)}, u32[]{:S(2)}, u32[]{:S(2)}) %collective-permute-start.16) | collective-permute-done | bytes 196640 | tf_op jit(solution)/shard_map/ppermute | solution.py:488
  83.0 0.7 place_far.1
  (21 shorter events, 0.1 us)
Async XLA Ops:
  0.0 1.4 %copy-start.1 = (bf16[6,128,1024]{2,1,0:T(8,128)(2,1)S(1)}, bf16[6,128,1024]{2,1,0:T(8,128)(2,1)}, u32[]{:S(2)}) copy-start(bf16[6,128,1024]{2,1,0:T(8,128)(2,1)} %latent_ref.1) | copy-start | bytes 4718596
  1.4 10.7 %copy-start.7 = (bf16[3,1024,256]{2,1,0:T(8,128)(2,1)S(1)}, bf16[3,1024,256]{2,1,0:T(8,128)(2,1)}, u32[]{:S(2)}) copy-start(bf16[3,1024,256]{2,1,0:T(8,128)(2,1)} %weight_ref.1) | copy-start | bytes 4718596
  1.4 10.7 %copy-start.8 = (f32[1024]{0:T(1024)S(1)}, f32[1024]{0:T(1024)}, u32[]{:S(2)}) copy-start(f32[1024]{0:T(1024)} %param.10) | copy-start | bytes 12292
  1.4 10.7 %copy-start.9 = (f32[256]{0:T(256)S(1)}, f32[256]{0:T(256)}, u32[]{:S(2)}) copy-start(f32[256]{0:T(256)} %param.12) | copy-start | bytes 3076
  2.4 9.7 %collective-permute-start = (f32[6,1280]{1,0:T(8,128)S(1)}, f32[6,1280]{1,0:T(8,128)S(1)}, u32[]{:S(2)}, u32[]{:S(2)}) collective-permute-start(f32[6,1280]{1,0:T(8,128)S(1)} %get-tuple-element.20), channel_id=1, source_target_pairs={{0,4},{4,8},{8,12},{12,0},{1,5},{5,9},{9,13},{13,1},{2,6},{6,10},{... | collective-permute-start | bytes 92168 | tf_op jit(solution)/shard_map/ppermute | solution.py:501
  5.5 6.6 %collective-permute-start.1 = (f32[6,1280]{1,0:T(8,128)S(1)}, f32[6,1280]{1,0:T(8,128)S(1)}, u32[]{:S(2)}, u32[]{:S(2)}) collective-permute-start(f32[6,1280]{1,0:T(8,128)S(1)} %get-tuple-element.21), channel_id=1, source_target_pairs={{0,12},{4,0},{8,4},{12,8},{1,13},{5,1},{9,5},{13,9},{2,14},{6,2},{... | collective-permute-start | bytes 92168 | tf_op jit(solution)/shard_map/ppermute | solution.py:501
  7.5 4.5 %collective-permute-start.2 = (f32[6,256]{1,0:T(8,128)S(1)}, f32[6,256]{1,0:T(8,128)S(1)}, u32[]{:S(2)}, u32[]{:S(2)}) collective-permute-start(f32[6,256]{1,0:T(8,128)S(1)} %get-tuple-element.22.own_ref), channel_id=1, source_target_pairs={{0,8},{4,12},{8,0},{12,4},{1,9},{5,13},{9,1},{13,5},{2,10},{6,14},... | collective-permute-start | bytes 18440 | tf_op jit(solution)/shard_map/ppermute | solution.py:501
  12.1 10.7 %copy-start.3 = (bf16[3,256,1024]{2,1,0:T(8,128)(2,1)S(1)}, bf16[3,256,1024]{2,1,0:T(8,128)(2,1)}, u32[]{:S(2)}) copy-start(bf16[3,256,1024]{2,1,0:T(8,128)(2,1)} %param.14) | copy-start | bytes 4718596
  12.1 10.7 %copy-start.5 = (f32[256]{0:T(256)S(1)}, f32[256]{0:T(256)}, u32[]{:S(2)}) copy-start(f32[256]{0:T(256)} %param.13) | copy-start | bytes 3076
  14.4 8.4 %collective-permute-start.3 = (f32[6,512]{1,0:T(8,128)S(1)}, f32[6,512]{1,0:T(8,128)S(1)}, u32[]{:S(2)}, u32[]{:S(2)}) collective-permute-start(f32[6,512]{1,0:T(8,128)S(1)} %get-tuple-element.24), channel_id=1, source_target_pairs={{0,4},{4,8},{8,12},{12,0},{1,5},{5,9},{9,13},{13,1},{2,6},{6,10},{... | collective-permute-start | bytes 36872 | tf_op jit(solution)/shard_map/ppermute | solution.py:501
  14.5 8.3 %collective-permute-start.4 = (f32[6,512]{1,0:T(8,128)S(1)}, f32[6,512]{1,0:T(8,128)S(1)}, u32[]{:S(2)}, u32[]{:S(2)}) collective-permute-start(f32[6,512]{1,0:T(8,128)S(1)} %get-tuple-element.25), channel_id=1, source_target_pairs={{0,12},{4,0},{8,4},{12,8},{1,13},{5,1},{9,5},{13,9},{2,14},{6,2},{... | collective-permute-start | bytes 36872 | tf_op jit(solution)/shard_map/ppermute | solution.py:501
  18.2 4.5 %collective-permute-start.5 = (f32[6,256]{1,0:T(8,128)S(1)}, f32[6,256]{1,0:T(8,128)S(1)}, u32[]{:S(2)}, u32[]{:S(2)}) collective-permute-start(f32[6,256]{1,0:T(8,128)S(1)} %get-tuple-element.26.own_ref), channel_id=1, source_target_pairs={{0,8},{4,12},{8,0},{12,4},{1,9},{5,13},{9,1},{13,5},{2,10},{6,14},... | collective-permute-start | bytes 18440 | tf_op jit(solution)/shard_map/ppermute | solution.py:501
  23.9 5.8 %collective-permute-start.7 = (bf16[192,1024]{1,0:T(8,128)(2,1)S(1)}, bf16[192,1024]{1,0:T(8,128)(2,1)S(1)}, u32[]{:S(2)}, u32[]{:S(2)}) collective-permute-start(bf16[192,1024]{1,0:T(8,128)(2,1)S(1)} %get-tuple-element.29), channel_id=1, source_target_pairs={{0,1},{1,0},{2,3},{3,2},{4,5},{5,4},{6,7},{7,6},{8,9},{9,8},{10,11... | collective-permute-start | bytes 1179656 | tf_op jit(solution)/shard_map/ppermute | solution.py:484
  25.2 34.3 %collective-permute-start.11 = (bf16[2,512,256]{2,1,0:T(8,128)(2,1)S(1)}, bf16[2,512,256]{2,1,0:T(8,128)(2,1)S(1)}, u32[]{:S(2)}, u32[]{:S(2)}) collective-permute-start(bf16[2,512,256]{2,1,0:T(8,128)(2,1)S(1)} %shard_map.97), channel_id=1, source_target_pairs={{0,2},{2,0},{1,3},{3,1},{4,6},{6,4},{5,7},{7,5},{8,10},{10,8},{9,1... | collective-permute-start | bytes 1572872 | tf_op jit(solution)/shard_map/ppermute | solution.py:488
  28.0 31.2 %copy-start.2 = (bf16[6,128,1024]{2,1,0:T(8,128)(2,1)S(1)}, bf16[6,128,1024]{2,1,0:T(8,128)(2,1)}, u32[]{:S(2)}) copy-start(bf16[6,128,1024]{2,1,0:T(8,128)(2,1)} %latent_ref.1) | copy-start | bytes 4718596
  28.0 23.2 %collective-permute-start.10 = (bf16[2,512,256]{2,1,0:T(8,128)(2,1)S(1)}, bf16[2,512,256]{2,1,0:T(8,128)(2,1)S(1)}, u32[]{:S(2)}, u32[]{:S(2)}) collective-permute-start(bf16[2,512,256]{2,1,0:T(8,128)(2,1)S(1)} %shard_map.96), channel_id=1, source_target_pairs={{0,2},{2,0},{1,3},{3,1},{4,6},{6,4},{5,7},{7,5},{8,10},{10,8},{9,1... | collective-permute-start | bytes 1572872 | tf_op jit(solution)/shard_map/ppermute | solution.py:488
  29.6 23.3 %collective-permute-start.6 = (bf16[192,1024]{1,0:T(8,128)(2,1)S(1)}, bf16[192,1024]{1,0:T(8,128)(2,1)S(1)}, u32[]{:S(2)}, u32[]{:S(2)}) collective-permute-start(bf16[192,1024]{1,0:T(8,128)(2,1)S(1)} %get-tuple-element.28), channel_id=1, source_target_pairs={{0,1},{1,0},{2,3},{3,2},{4,5},{5,4},{6,7},{7,6},{8,9},{9,8},{10,11... | collective-permute-start | bytes 1179656 | tf_op jit(solution)/shard_map/ppermute | solution.py:484
  29.9 29.4 %collective-permute-start.8 = (bf16[192,1024]{1,0:T(8,128)(2,1)S(1)}, bf16[192,1024]{1,0:T(8,128)(2,1)S(1)}, u32[]{:S(2)}, u32[]{:S(2)}) collective-permute-start(bf16[192,1024]{1,0:T(8,128)(2,1)S(1)} %add_convert_fusion), channel_id=1, source_target_pairs={{0,2},{2,0},{1,3},{3,1},{4,6},{6,4},{5,7},{7,5},{8,10},{10,8},{9,1... | collective-permute-start | bytes 1179656 | tf_op jit(solution)/shard_map/ppermute | solution.py:488
  51.3 18.6 %collective-permute-start.12 = (bf16[2,512,256]{2,1,0:T(8,128)(2,1)S(1)}, bf16[2,512,256]{2,1,0:T(8,128)(2,1)S(1)}, u32[]{:S(2)}, u32[]{:S(2)}) collective-permute-start(bf16[2,512,256]{2,1,0:T(8,128)(2,1)S(1)} %collective-permute-done.10.heads_x_ref), channel_id=1, source_target_pairs={{0,16},{16,0},{1,17},{17,1},{2,18},{18,2},{3,19},{19,3},{4,20},{20... | collective-permute-start | bytes 1572872 | tf_op jit(solution)/shard_map/ppermute | solution.py:492
  59.2 10.7 %copy-start = (bf16[1024,3,256]{2,0,1:T(8,128)(2,1)S(1)}, bf16[1024,3,256]{2,0,1:T(8,128)(2,1)}, u32[]{:S(2)}) copy-start(bf16[1024,3,256]{2,0,1:T(8,128)(2,1)} %param.16) | copy-start | bytes 4718596
  59.2 10.7 %copy-start.4 = (bf16[256,1024]{1,0:T(8,128)(2,1)S(1)}, bf16[256,1024]{1,0:T(8,128)(2,1)}, u32[]{:S(2)}) copy-start(bf16[256,1024]{1,0:T(8,128)(2,1)} %out_ref.3) | copy-start | bytes 1572868
  59.2 10.7 %copy-start.6 = (f32[1024]{0:T(1024)S(1)}, f32[1024]{0:T(1024)}, u32[]{:S(2)}) copy-start(f32[1024]{0:T(1024)} %param.15) | copy-start | bytes 12292
  59.4 10.4 %collective-permute-start.9 = (bf16[192,1024]{1,0:T(8,128)(2,1)S(1)}, bf16[192,1024]{1,0:T(8,128)(2,1)S(1)}, u32[]{:S(2)}, u32[]{:S(2)}) collective-permute-start(bf16[192,1024]{1,0:T(8,128)(2,1)S(1)} %shard_map.95.mine_ref), channel_id=1, source_target_pairs={{0,1},{1,0},{2,3},{3,2},{4,5},{5,4},{6,7},{7,6},{8,9},{9,8},{10,11... | collective-permute-start | bytes 1179656 | tf_op jit(solution)/shard_map/ppermute | solution.py:484
  59.6 10.3 %collective-permute-start.13 = (bf16[512,256]{1,0:T(8,128)(2,1)S(1)}, bf16[512,256]{1,0:T(8,128)(2,1)S(1)}, u32[]{:S(2)}, u32[]{:S(2)}) collective-permute-start(bf16[512,256]{1,0:T(8,128)(2,1)S(1)} %get-tuple-element.36.values_x_ref), channel_id=1, source_target_pairs={{0,16},{16,0},{1,17},{17,1},{2,18},{18,2},{3,19},{19,3},{4,20},{20... | collective-permute-start | bytes 786440 | tf_op jit(solution)/shard_map/ppermute | solution.py:492
  61.3 8.5 %collective-permute-start.14 = (bf16[512,256]{1,0:T(8,128)(2,1)S(1)}, bf16[512,256]{1,0:T(8,128)(2,1)S(1)}, u32[]{:S(2)}, u32[]{:S(2)}) collective-permute-start(bf16[512,256]{1,0:T(8,128)(2,1)S(1)} %get-tuple-element.35.outs_x_ref), channel_id=1, source_target_pairs={{0,4},{4,0},{8,12},{12,8},{1,5},{5,1},{9,13},{13,9},{2,6},{6,2},{1... | collective-permute-start | bytes 786440 | tf_op jit(solution)/shard_map/ppermute | solution.py:496
  74.4 1.5 %collective-permute-start.15 = (bf16[384,256]{1,0:T(8,128)(2,1)S(1)}, bf16[384,256]{1,0:T(8,128)(2,1)S(1)}, u32[]{:S(2)}, u32[]{:S(2)}) collective-permute-start(bf16[384,256]{1,0:T(8,128)(2,1)S(1)} %get-tuple-element.32), channel_id=1, source_target_pairs={{0,1},{1,0},{2,3},{3,2},{4,5},{5,4},{6,7},{7,6},{8,9},{9,8},{10,11... | collective-permute-start | bytes 589832 | tf_op jit(solution)/shard_map/ppermute | solution.py:484
  74.5 3.2 %collective-permute-start.17 = (bf16[384,256]{1,0:T(8,128)(2,1)S(1)}, bf16[384,256]{1,0:T(8,128)(2,1)S(1)}, u32[]{:S(2)}, u32[]{:S(2)}) collective-permute-start(bf16[384,256]{1,0:T(8,128)(2,1)S(1)} %get-tuple-element.34), channel_id=1, source_target_pairs={{0,1},{1,0},{2,3},{3,2},{4,5},{5,4},{6,7},{7,6},{8,9},{9,8},{10,11... | collective-permute-start | bytes 589832 | tf_op jit(solution)/shard_map/ppermute | solution.py:484
  76.0 7.0 %collective-permute-start.16 = (bf16[384,256]{1,0:T(8,128)(2,1)S(1)}, bf16[384,256]{1,0:T(8,128)(2,1)S(1)}, u32[]{:S(2)}, u32[]{:S(2)}) collective-permute-start(bf16[384,256]{1,0:T(8,128)(2,1)S(1)} %add_convert_fusion.1), channel_id=1, source_target_pairs={{0,2},{2,0},{1,3},{3,1},{4,6},{6,4},{5,7},{7,5},{8,10},{10,8},{9,1... | collective-permute-start | bytes 589832 | tf_op jit(solution)/shard_map/ppermute | solution.py:488

commit v5 on v4

--- a/solution.py
+++ b/solution.py
@@ -167,6 +167,10 @@
     return jnp.dot(a, b, precision=HIGHEST, preferred_element_type=f32)
 
 
+def even_place():
+    return lax.axis_index("frame") % 2 == 0
+
+
 def group_totals(sums, squares, width):
     hot = one_hot(sums.shape[1], LANES, width, True)
     return f32_dot(sums, hot), f32_dot(squares, hot)
@@ -182,36 +186,42 @@
     return f32_dot(centre, hot), f32_dot(lax.rsqrt(spread + norm_eps), hot)
 
 
-def stats_kernel(width, lat_ref, up_ref, down_ref, own_ref, sum_ref, square_ref):
+def stats_kernel(width, lat_ref, one_ref, two_ref, own_ref, sum_ref, square_ref):
     stems, frames, channels = lat_ref.shape
+    even = even_place()
     for stem in range(stems):
         block = lat_ref[stem].astype(f32)
         sum_ref[stem : stem + 1, :] = jnp.sum(block, axis=0, keepdims=True)
         square_ref[stem : stem + 1, :] = jnp.sum(block * block, axis=0, keepdims=True)
-        down_ref[stem : stem + 1, :channels] = block[:1]
-        up_ref[stem : stem + 1, :channels] = block[frames - 1 :]
+        down, up = block[:1], block[frames - 1 :]
+        one_ref[stem : stem + 1, :channels] = jnp.where(even, up, down)
+        two_ref[stem : stem + 1, :channels] = jnp.where(even, down, up)
     sums, squares = group_totals(sum_ref[...], square_ref[...], width)
-    for ref, start in ((up_ref, channels), (down_ref, channels), (own_ref, 0)):
+    for ref, start in ((one_ref, channels), (two_ref, channels), (own_ref, 0)):
         ref[:, start : start + LANES] = sums
         ref[:, start + LANES : start + 2 * LANES] = squares
 
 
 def first_kernel(
     entries, width, frame_size,
-    lat_ref, low_ref, high_ref, far_ref, own_ref, gain_ref, weight_ref, bias_ref,
-    hid_ref, up_ref, down_ref, tot_ref, act_ref, edge_ref, sum_ref, square_ref,
+    lat_ref, got_ref, swapped_ref, far_ref, own_ref, gain_ref, weight_ref, bias_ref,
+    hid_ref, one_ref, two_ref, tot_ref, act_ref, edge_ref, sum_ref, square_ref,
 ):
     stems, frames, channels = lat_ref.shape
     shard = weight_ref.shape[2]
     place = lax.axis_index("frame")
     centre, scale = channel_scale(
-        [own_ref[...], low_ref[:, channels:], high_ref[:, channels:], far_ref[...]],
+        [own_ref[...], got_ref[:, channels:], swapped_ref[:, channels:], far_ref[...]],
         entries, channels, width,
     )
+    even = even_place()
+    first_got = even == (lax.axis_index("tensor") % 2 == 0)
+    got, swapped = got_ref[:, :channels], swapped_ref[:, :channels]
+    high, low = jnp.where(first_got, got, swapped), jnp.where(first_got, swapped, got)
     scale = scale * (0.5 * gain_ref[...])
     edge_ref[...] = jnp.zeros_like(edge_ref)
-    low = silu_of_half((low_ref[:, :channels] - centre) * scale)
-    high = silu_of_half((high_ref[:, :channels] - centre) * scale)
+    low = silu_of_half((low - centre) * scale)
+    high = silu_of_half((high - centre) * scale)
     edge_ref[0:stems, :] = jnp.where(place > 0, low, 0.0)
     edge_ref[8 : 8 + stems, :] = jnp.where(place < frame_size - 1, high, 0.0)
     edge = edge_ref[...].astype(bf16)
@@ -237,17 +247,18 @@
             hid_ref[stem] = hid
             sum_ref[stem : stem + 1, :] = jnp.sum(hid, axis=0, keepdims=True)
             square_ref[stem : stem + 1, :] = jnp.sum(hid * hid, axis=0, keepdims=True)
-            down_ref[stem : stem + 1, :shard] = hid[:1]
-            up_ref[stem : stem + 1, :shard] = hid[frames - 1 :]
+            down, up = hid[:1], hid[frames - 1 :]
+            one_ref[stem : stem + 1, :shard] = jnp.where(even, up, down)
+            two_ref[stem : stem + 1, :shard] = jnp.where(even, down, up)
     sums, squares = group_totals(sum_ref[...], square_ref[...], width)
-    for ref, start in ((up_ref, shard), (down_ref, shard), (tot_ref, 0)):
+    for ref, start in ((one_ref, shard), (two_ref, shard), (tot_ref, 0)):
         ref[:, start : start + LANES] = sums
         ref[:, start + LANES : start + 2 * LANES] = squares
 
 
 def second_kernel(
     entries, width, frame_size, other,
-    hid_ref, low_ref, high_ref, far_ref, own_ref, gain_ref, weight_ref,
+    hid_ref, one_ref, two_ref, far_ref, own_ref, gain_ref, weight_ref,
     send_ref, keep_ref, act_ref,
 ):
     stems, _, shard = hid_ref.shape
@@ -256,14 +267,15 @@
     chip, core = index // 2, index % 2
     window = 1 - chip if other else chip
     centre, scale = channel_scale(
-        [own_ref[...], low_ref[:, shard:], high_ref[:, shard:], far_ref[...]],
+        [own_ref[...], one_ref[:, shard:], two_ref[:, shard:], far_ref[...]],
         entries, shard, width,
     )
+    even = even_place()
+    one, two = one_ref[:, :shard], two_ref[:, :shard]
+    high, low = jnp.where(even, one, two), jnp.where(even, two, one)
     scale = scale * (0.5 * gain_ref[...])
-    low = jnp.where(place > 0, silu_of_half((low_ref[:, :shard] - centre) * scale), 0.0)
-    high = jnp.where(
-        place < frame_size - 1, silu_of_half((high_ref[:, :shard] - centre) * scale), 0.0
-    )
+    low = jnp.where(place > 0, silu_of_half((low - centre) * scale), 0.0)
+    high = jnp.where(place < frame_size - 1, silu_of_half((high - centre) * scale), 0.0)
     row = lax.broadcasted_iota(jnp.int32, (WINDOW, shard), 0)
     half = stems // 2
     for stem in range(stems):
@@ -496,13 +508,24 @@
     return lax.ppermute(value, "frame", [(0, 1), (1, 0), (2, 3), (3, 2)])
 
 
-def shift_frames(value, by):
-    count = lax.axis_size("frame")
-    return lax.ppermute(value, "frame", [(i, (i + by) % count) for i in range(count)])
-
-
-def exchange(up, down, own):
-    return (shift_frames(up, 1), shift_frames(down, -1), shift_frames(own, 2))
+ONE = ((0, 1), (1, 0), (2, 3), (3, 2))
+TWO = ((0, 3), (3, 0), (1, 2), (2, 1))
+FAR = ((0, 2), (2, 0), (1, 3), (3, 1))
+
+
+def trade(value, pairs):
+    return lax.ppermute(value, "frame", pairs)
+
+
+def trade_by_core(one, two):
+    count = lax.axis_size("tensor")
+    pairs = [
+        (source * count + index, goal * count + index)
+        for index in range(count)
+        for source, goal in (TWO if index % 2 else ONE)
+    ]
+    value = jnp.where(lax.axis_index("tensor") % 2 == 0, one, two)
+    return lax.ppermute(value, ("frame", "tensor"), pairs)
 
 
 def fast(
@@ -529,23 +552,27 @@
     values_y = swap_groups(values_x)
     outs_z = swap_frames(outs_x)
     wide = channels + 2 * LANES
-    up, down, own = call(
+    one, two, own = call(
         functools.partial(stats_kernel, width),
         [((stems, wide), f32), ((stems, wide), f32), ((stems, 2 * LANES), f32)],
         [((stems, channels), f32)] * 2,
         [latent],
     )
-    low, high, far = exchange(up, down, own)
+    far = trade(own, FAR)
+    got = trade_by_core(one, two)
+    swapped = swap_cores(got)
     narrow = shard + 2 * LANES
-    hid, up2, down2, own2 = call(
+    hid, one2, two2, own2 = call(
         functools.partial(first_kernel, entries, width, frame_size),
         [((stems, frames, shard), f32), ((stems, narrow), f32), ((stems, narrow), f32),
          ((stems, 2 * LANES), f32)],
         [((stems * frames, channels), bf16), ((16, channels), f32)] + [((stems, shard), f32)] * 2,
-        [latent, low, high, far, own, norm1_gain[None], conv1_weight, time_bias[None]],
+        [latent, got, swapped, far, own, norm1_gain[None], conv1_weight, time_bias[None]],
         flops=6 * stems * frames * channels * shard,
     )
-    low2, high2, far2 = exchange(up2, down2, own2)
+    far2 = trade(own2, FAR)
+    got_two = trade(two2, TWO)
+    got_one = trade(one2, ONE)
     weight2 = conv2_weight.reshape(3 * shard, channels)
 
     def second(other):
@@ -553,7 +580,7 @@
             functools.partial(second_kernel, entries, width, frame_size, other),
             [((half_rows, channels), bf16)] * 2,
             [((2 * half_rows, 3 * shard), bf16)],
-            [hid, low2, high2, far2, own2, norm2_gain[None], weight2],
+            [hid, got_one, got_two, far2, own2, norm2_gain[None], weight2],
             flops=12 * half_rows * channels * shard,
         )
 

time: 84 us -> 84.8 us (level)
    ppermute x1, starting transfers between devices: 0.01 us -> 1.05 us  [swap_frames(): return lax.ppermute(value, 'frame', [(0, 1), (1, 0), (2, 3), (3, 2)])]
    ppermute x5 -> x6, starting transfers between devices: 0.78 us -> 1.77 us  [swap_cores(): return lax.ppermute(value, 'tensor', [(0, 1), (1, 0), (2, 3), (3, 2)])]
    ppermute x2, waiting for transfers between devices: 8.54 us -> 7.66 us  [swap_groups(): return lax.ppermute(value, 'groups', [(0, 1), (1, 0)])]
    ppermute x6 -> x5, starting transfers between devices: 10 us -> 9.32 us  [the longest x4 6.21 us: trade(): return lax.ppermute(value, 'frame', pairs)]
    ppermute x6 -> x5, waiting for transfers between devices: 8.16 us -> 8.56 us  [the longest x4 6.58 us: trade(): return lax.ppermute(value, 'frame', pairs)]
  transfers between devices with their start and end apart: 18 -> 18, of which waited for: 7 -> 8; matrix products, arithmetic and copies ran while one was open for 0% -> 0% of each run, Pallas kernels for 5% -> 5%
where the time goes in v5:
time: 84.8 us; the launch traced here: 84.5 us
  waiting for transfers between devices  48.1 us (57%)
  starting transfers between devices  20.5 us (24%)
  Pallas kernels  13.9 us (16%)
  local copies, waits for them, and re-layouts  1.51 us (2%)
    ppermute x4, waiting for transfers between devices, swap_chips(): return lax.ppermute(value, 'tensor', [(0, 2), (2, 0), (1, 3), (3, 1)])  31 us
    pallas_call x6, Pallas kernels, call(): pl.pallas_call(kernel, out_shape=[jax.ShapeDtypeStruct(shape, dtype) for...  10.2 us
    ppermute x2, waiting for transfers between devices, swap_groups(): return lax.ppermute(value, 'groups', [(0, 1), (1, 0)])  7.66 us
    ppermute x4, waiting for transfers between devices, trade(): return lax.ppermute(value, 'frame', pairs)  6.58 us
    ppermute x4, starting transfers between devices, trade(): return lax.ppermute(value, 'frame', pairs)  6.21 us
    ppermute x4, starting transfers between devices, swap_chips(): return lax.ppermute(value, 'tensor', [(0, 2), (2, 0), (1, 3), (3, 1)])  5.27 us
    ppermute x1, starting transfers between devices, trade_by_core(): return lax.ppermute(value, ('frame', 'tensor'), pairs)  3.12 us
    ppermute x2, starting transfers between devices, swap_groups(): return lax.ppermute(value, 'groups', [(0, 1), (1, 0)])  3.11 us
  transfers between devices with their start and end apart: 18, of which 8 were waited for; matrix products, arithmetic and copies ran while one was open for 0% of the time, Pallas kernels for 5%

profile of v5, /device:TPU:0, one launch (start us, length us, event | category | flops | bytes accessed | tf_op | source)
XLA Modules:
  0.0 84.5 jit_solution(10662597515251470076)
XLA Ops:
  0.0 1.4 %copy-done.1 = bf16[6,128,1024]{2,1,0:T(8,128)(2,1)S(1)} copy-done((bf16[6,128,1024]{2,1,0:T(8,128)(2,1)S(1)}, bf16[6,128,1024]{2,1,0:T(8,128)(2,1)}, u32[]{:S(2)}) %copy-start.1) | copy-done | bytes 1572888
  1.4 1.0 %shard_map.91 = (f32[6,1280]{1,0:T(8,128)S(1)}, f32[6,1280]{1,0:T(8,128)S(1)}, f32[6,256]{1,0:T(8,128)S(1)}) custom-call(bf16[6,128,1024]{2,1,0:T(8,128)(2,1)S(1)} %copy-done.1), custom_call_target="tpu_custom_call" | custom-call | tf_op jit(solution)/shard_map/pallas_call | solution.py:484
  2.4 3.1 %collective-permute-start = (f32[6,1280]{1,0:T(8,128)S(1)}, f32[6,1280]{1,0:T(8,128)S(1)}, u32[]{:S(2)}, u32[]{:S(2)}) collective-permute-start(f32[6,1280]{1,0:T(8,128)S(1)} %broadcast_select_fusion), channel_id=1, source_target_pairs={{0,4},{4,0},{8,12},{12,8},{1,13},{13,1},{5,9},{9,5},{2,6},{6,2},{1... | collective-permute-start | bytes 92168 | tf_op jit(solution)/shard_map/ppermute | solution.py:528
  5.6 2.0 %collective-permute-done.got_ref = f32[6,1280]{1,0:T(8,128)S(1)} collective-permute-done((f32[6,1280]{1,0:T(8,128)S(1)}, f32[6,1280]{1,0:T(8,128)S(1)}, u32[]{:S(2)}, u32[]{:S(2)}) %collective-permute-start) | collective-permute-done | bytes 30752 | tf_op jit(solution)/shard_map/ppermute | solution.py:528
  7.5 1.0 %collective-permute-start.1 = (f32[6,1280]{1,0:T(8,128)S(1)}, f32[6,1280]{1,0:T(8,128)S(1)}, u32[]{:S(2)}, u32[]{:S(2)}) collective-permute-start(f32[6,1280]{1,0:T(8,128)S(1)} %collective-permute-done.got_ref), channel_id=1, source_target_pairs={{0,1},{1,0},{2,3},{3,2},{4,5},{5,4},{6,7},{7,6},{8,9},{9,8},{10,11... | collective-permute-start | bytes 92168 | tf_op jit(solution)/shard_map/ppermute | solution.py:496
  8.5 2.0 %collective-permute-start.2 = (f32[6,256]{1,0:T(8,128)S(1)}, f32[6,256]{1,0:T(8,128)S(1)}, u32[]{:S(2)}, u32[]{:S(2)}) collective-permute-start(f32[6,256]{1,0:T(8,128)S(1)} %get-tuple-element.22.own_ref), channel_id=1, source_target_pairs={{0,8},{8,0},{4,12},{12,4},{1,9},{9,1},{5,13},{13,5},{2,10},{10,2},... | collective-permute-start | bytes 18440 | tf_op jit(solution)/shard_map/ppermute | solution.py:517
  10.6 2.5 %collective-permute-done.2.far_ref = f32[6,256]{1,0:T(8,128)S(1)} collective-permute-done((f32[6,256]{1,0:T(8,128)S(1)}, f32[6,256]{1,0:T(8,128)S(1)}, u32[]{:S(2)}, u32[]{:S(2)}) %collective-permute-start.2) | collective-permute-done | bytes 6176 | tf_op jit(solution)/shard_map/ppermute | solution.py:517
  13.1 0.0 collective-permute-done.1.swapped_ref
  13.1 0.0 copy-start.3
  13.1 0.0 copy-start.5
  13.1 2.2 %shard_map.92 = (f32[6,128,256]{2,1,0:T(8,128)S(1)}, f32[6,512]{1,0:T(8,128)S(1)}, f32[6,512]{1,0:T(8,128)S(1)}, f32[6,256]{1,0:T(8,128)S(1)}) custom-call(bf16[6,128,1024]{2,1,0:T(8,128)(2,1)S(1)} %copy-done.1, f32[6,1280]{1,0:T(8,128)S(1)} %collective-permute-done.got_ref, f32[6,1280]{1,0:T(8,128)S(1)} %collective-permute-done.1.swapped_ref, ...), custom_call_target="tpu_custom_call" | custom-call | flops 1207959552 | tf_op jit(solution)/shard_map/pallas_call | solution.py:484
  15.4 1.2 %collective-permute-start.3 = (f32[6,512]{1,0:T(8,128)S(1)}, f32[6,512]{1,0:T(8,128)S(1)}, u32[]{:S(2)}, u32[]{:S(2)}) collective-permute-start(f32[6,512]{1,0:T(8,128)S(1)} %get-tuple-element.24), channel_id=1, source_target_pairs={{0,4},{4,0},{8,12},{12,8},{1,5},{5,1},{9,13},{13,9},{2,6},{6,2},{1... | collective-permute-start | bytes 36872 | tf_op jit(solution)/shard_map/ppermute | solution.py:517
  16.6 2.4 %collective-permute-start.4 = (f32[6,512]{1,0:T(8,128)S(1)}, f32[6,512]{1,0:T(8,128)S(1)}, u32[]{:S(2)}, u32[]{:S(2)}) collective-permute-start(f32[6,512]{1,0:T(8,128)S(1)} %get-tuple-element.25), channel_id=1, source_target_pairs={{0,12},{12,0},{4,8},{8,4},{1,13},{13,1},{5,9},{9,5},{2,14},{14,2},... | collective-permute-start | bytes 36872 | tf_op jit(solution)/shard_map/ppermute | solution.py:517
  19.0 0.5 collective-permute-start.5
  19.5 4.1 %collective-permute-done.5.far_ref = f32[6,256]{1,0:T(8,128)S(1)} collective-permute-done((f32[6,256]{1,0:T(8,128)S(1)}, f32[6,256]{1,0:T(8,128)S(1)}, u32[]{:S(2)}, u32[]{:S(2)}) %collective-permute-start.5) | collective-permute-done | bytes 6176 | tf_op jit(solution)/shard_map/ppermute | solution.py:517
  23.6 0.0 collective-permute-done.3.one_ref
  23.6 1.1 %shard_map.94 = (bf16[192,1024]{1,0:T(8,128)(2,1)S(1)}, bf16[192,1024]{1,0:T(8,128)(2,1)S(1)}) custom-call(f32[6,128,256]{2,1,0:T(8,128)S(1)} %get-tuple-element.23.hid_ref, f32[6,512]{1,0:T(8,128)S(1)} %collective-permute-done.3.one_ref, f32[6,512]{1,0:T(8,128)S(1)} %collective-permute-done.4.two_ref, f32[6,256]{1,0:T(8,128)S(1)} %collective-permute-done.5.far_ref, ...), custom_call_target="tpu_custom_call" | custom-call | flops 603979776 | tf_op jit(solution)/shard_map/pallas_call | solution.py:484
  24.7 0.1 collective-permute-start.7
  24.8 1.1 %shard_map.97 = bf16[2,512,256]{2,1,0:T(8,128)(2,1)S(1)} custom-call(bf16[3,1024,256]{2,1,0:T(8,128)(2,1)} %bitcast.10, bf16[256,1024]{1,0:T(8,128)(2,1)} %out_ref.3), custom_call_target="tpu_custom_call" | custom-call | bytes 1048576 | tf_op jit(solution)/shard_map/pallas_call | solution.py:436
  26.0 1.6 %collective-permute-start.11 = (bf16[2,512,256]{2,1,0:T(8,128)(2,1)S(1)}, bf16[2,512,256]{2,1,0:T(8,128)(2,1)S(1)}, u32[]{:S(2)}, u32[]{:S(2)}) collective-permute-start(bf16[2,512,256]{2,1,0:T(8,128)(2,1)S(1)} %shard_map.97), channel_id=1, source_target_pairs={{0,2},{2,0},{1,3},{3,1},{4,6},{6,4},{5,7},{7,5},{8,10},{10,8},{9,1... | collective-permute-start | bytes 1572872 | tf_op jit(solution)/shard_map/ppermute | solution.py:500
  27.5 1.1 %shard_map.96 = bf16[2,512,256]{2,1,0:T(8,128)(2,1)S(1)} custom-call(bf16[3,1024,256]{2,1,0:T(8,128)(2,1)} %bitcast.11), custom_call_target="tpu_custom_call" | custom-call | bytes 1048576 | tf_op jit(solution)/shard_map/pallas_call | solution.py:436
  28.7 0.0 copy-start.2
  28.7 0.6 collective-permute-start.10
  29.3 1.1 %shard_map.93 = (bf16[192,1024]{1,0:T(8,128)(2,1)S(1)}, bf16[192,1024]{1,0:T(8,128)(2,1)S(1)}) custom-call(f32[6,128,256]{2,1,0:T(8,128)S(1)} %get-tuple-element.23.hid_ref, f32[6,512]{1,0:T(8,128)S(1)} %collective-permute-done.3.one_ref, f32[6,512]{1,0:T(8,128)S(1)} %collective-permute-done.4.two_ref, f32[6,256]{1,0:T(8,128)S(1)} %collective-permute-done.5.far_ref, ...), custom_call_target="tpu_custom_call" | custom-call | flops 603979776 | tf_op jit(solution)/shard_map/pallas_call | solution.py:484
  30.4 0.1 collective-permute-start.6
  30.5 0.0 collective-permute-done.7
  30.5 0.1 add_convert_fusion
  30.7 1.6 %collective-permute-start.8 = (bf16[192,1024]{1,0:T(8,128)(2,1)S(1)}, bf16[192,1024]{1,0:T(8,128)(2,1)S(1)}, u32[]{:S(2)}, u32[]{:S(2)}) collective-permute-start(bf16[192,1024]{1,0:T(8,128)(2,1)S(1)} %add_convert_fusion), channel_id=1, source_target_pairs={{0,2},{2,0},{1,3},{3,1},{4,6},{6,4},{5,7},{7,5},{8,10},{10,8},{9,1... | collective-permute-start | bytes 1179656 | tf_op jit(solution)/shard_map/ppermute | solution.py:500
  32.2 19.9 %collective-permute-done.10.heads_x_ref = bf16[2,512,256]{2,1,0:T(8,128)(2,1)S(1)} collective-permute-done((bf16[2,512,256]{2,1,0:T(8,128)(2,1)S(1)}, bf16[2,512,256]{2,1,0:T(8,128)(2,1)S(1)}, u32[]{:S(2)}, u32[]{:S(2)}) %collective-permute-start.10) | collective-permute-done | bytes 524320 | tf_op jit(solution)/shard_map/ppermute | solution.py:500
  52.1 1.5 %collective-permute-start.12 = (bf16[2,512,256]{2,1,0:T(8,128)(2,1)S(1)}, bf16[2,512,256]{2,1,0:T(8,128)(2,1)S(1)}, u32[]{:S(2)}, u32[]{:S(2)}) collective-permute-start(bf16[2,512,256]{2,1,0:T(8,128)(2,1)S(1)} %collective-permute-done.10.heads_x_ref), channel_id=1, source_target_pairs={{0,16},{16,0},{1,17},{17,1},{2,18},{18,2},{3,19},{19,3},{4,20},{20... | collective-permute-start | bytes 1572872 | tf_op jit(solution)/shard_map/ppermute | solution.py:504
  53.6 6.4 %collective-permute-done.8.far_ref = bf16[192,1024]{1,0:T(8,128)(2,1)S(1)} collective-permute-done((bf16[192,1024]{1,0:T(8,128)(2,1)S(1)}, bf16[192,1024]{1,0:T(8,128)(2,1)S(1)}, u32[]{:S(2)}, u32[]{:S(2)}) %collective-permute-start.8) | collective-permute-done | bytes 393248 | tf_op jit(solution)/shard_map/ppermute | solution.py:500
  60.0 0.2 shard_map.95.mine_ref
  60.2 0.1 collective-permute-start.9
  60.4 1.6 %collective-permute-start.13 = (bf16[512,256]{1,0:T(8,128)(2,1)S(1)}, bf16[512,256]{1,0:T(8,128)(2,1)S(1)}, u32[]{:S(2)}, u32[]{:S(2)}) collective-permute-start(bf16[512,256]{1,0:T(8,128)(2,1)S(1)} %get-tuple-element.36.values_x_ref), channel_id=1, source_target_pairs={{0,16},{16,0},{1,17},{17,1},{2,18},{18,2},{3,19},{19,3},{4,20},{20... | collective-permute-start | bytes 786440 | tf_op jit(solution)/shard_map/ppermute | solution.py:504
  62.0 1.0 %collective-permute-start.14 = (bf16[512,256]{1,0:T(8,128)(2,1)S(1)}, bf16[512,256]{1,0:T(8,128)(2,1)S(1)}, u32[]{:S(2)}, u32[]{:S(2)}) collective-permute-start(bf16[512,256]{1,0:T(8,128)(2,1)S(1)} %get-tuple-element.35.outs_x_ref), channel_id=1, source_target_pairs={{0,4},{4,0},{8,12},{12,8},{1,5},{5,1},{9,13},{13,9},{2,6},{6,2},{1... | collective-permute-start | bytes 786440 | tf_op jit(solution)/shard_map/ppermute | solution.py:508
  63.0 7.7 %collective-permute-done.13.values_y_ref = bf16[512,256]{1,0:T(8,128)(2,1)S(1)} collective-permute-done((bf16[512,256]{1,0:T(8,128)(2,1)S(1)}, bf16[512,256]{1,0:T(8,128)(2,1)S(1)}, u32[]{:S(2)}, u32[]{:S(2)}) %collective-permute-start.13) | collective-permute-done | bytes 262176 | tf_op jit(solution)/shard_map/ppermute | solution.py:504
  70.7 0.0 collective-permute-done.14.outs_z_ref
  70.7 0.0 collective-permute-done.12.heads_y_ref
  70.7 0.0 collective-permute-done.9.theirs_ref
  70.7 4.5 %shard_map.98 = (bf16[384,256]{1,0:T(8,128)(2,1)S(1)}, f32[384,256]{1,0:T(8,128)S(1)}, bf16[384,256]{1,0:T(8,128)(2,1)S(1)}, f32[384,256]{1,0:T(8,128)S(1)}) custom-call(bf16[192,1024]{1,0:T(8,128)(2,1)S(1)} %shard_map.95.mine_ref, bf16[192,1024]{1,0:T(8,128)(2,1)S(1)} %collective-permute-done.9.theirs_ref, f32[1,1024]{1,0:T(1,128)S(1)} %bitcast.17, ...), custom_call_target="tpu_custom_call" | custom-call | flops 1207959552 | tf_op jit(solution)/shard_map/pallas_call | solution.py:484
  75.2 0.1 collective-permute-start.15
  75.3 0.5 collective-permute-start.17
  75.8 0.9 %collective-permute-done.15 = bf16[384,256]{1,0:T(8,128)(2,1)S(1)} collective-permute-done((bf16[384,256]{1,0:T(8,128)(2,1)S(1)}, bf16[384,256]{1,0:T(8,128)(2,1)S(1)}, u32[]{:S(2)}, u32[]{:S(2)}) %collective-permute-start.15) | collective-permute-done | bytes 196640 | tf_op jit(solution)/shard_map/ppermute | solution.py:496
  76.7 0.1 add_convert_fusion.1
  76.8 1.6 %collective-permute-start.16 = (bf16[384,256]{1,0:T(8,128)(2,1)S(1)}, bf16[384,256]{1,0:T(8,128)(2,1)S(1)}, u32[]{:S(2)}, u32[]{:S(2)}) collective-permute-start(bf16[384,256]{1,0:T(8,128)(2,1)S(1)} %add_convert_fusion.1), channel_id=1, source_target_pairs={{0,2},{2,0},{1,3},{3,1},{4,6},{6,4},{5,7},{7,5},{8,10},{10,8},{9,1... | collective-permute-start | bytes 589832 | tf_op jit(solution)/shard_map/ppermute | solution.py:500
  78.4 0.8 place_near.1.near_ref
  79.1 4.7 %collective-permute-done.16.value_ref = bf16[384,256]{1,0:T(8,128)(2,1)S(1)} collective-permute-done((bf16[384,256]{1,0:T(8,128)(2,1)S(1)}, bf16[384,256]{1,0:T(8,128)(2,1)S(1)}, u32[]{:S(2)}, u32[]{:S(2)}) %collective-permute-start.16) | collective-permute-done | bytes 196640 | tf_op jit(solution)/shard_map/ppermute | solution.py:500
  83.8 0.7 place_far.1
  (22 shorter events, 0.1 us)
Async XLA Ops:
  0.0 13.1 %copy-start.8 = (f32[1024]{0:T(1024)S(1)}, f32[1024]{0:T(1024)}, u32[]{:S(2)}) copy-start(f32[1024]{0:T(1024)} %param.10) | copy-start | bytes 12292
  0.0 13.1 %copy-start.9 = (f32[256]{0:T(256)S(1)}, f32[256]{0:T(256)}, u32[]{:S(2)}) copy-start(f32[256]{0:T(256)} %param.12) | copy-start | bytes 3076
  0.0 1.4 %copy-start.1 = (bf16[6,128,1024]{2,1,0:T(8,128)(2,1)S(1)}, bf16[6,128,1024]{2,1,0:T(8,128)(2,1)}, u32[]{:S(2)}) copy-start(bf16[6,128,1024]{2,1,0:T(8,128)(2,1)} %latent_ref.1) | copy-start | bytes 4718596
  1.4 11.7 %copy-start.7 = (bf16[3,1024,256]{2,1,0:T(8,128)(2,1)S(1)}, bf16[3,1024,256]{2,1,0:T(8,128)(2,1)}, u32[]{:S(2)}) copy-start(bf16[3,1024,256]{2,1,0:T(8,128)(2,1)} %weight_ref.1) | copy-start | bytes 4718596
  2.4 5.1 %collective-permute-start = (f32[6,1280]{1,0:T(8,128)S(1)}, f32[6,1280]{1,0:T(8,128)S(1)}, u32[]{:S(2)}, u32[]{:S(2)}) collective-permute-start(f32[6,1280]{1,0:T(8,128)S(1)} %broadcast_select_fusion), channel_id=1, source_target_pairs={{0,4},{4,0},{8,12},{12,8},{1,13},{13,1},{5,9},{9,5},{2,6},{6,2},{1... | collective-permute-start | bytes 92168 | tf_op jit(solution)/shard_map/ppermute | solution.py:528
  7.5 5.6 %collective-permute-start.1 = (f32[6,1280]{1,0:T(8,128)S(1)}, f32[6,1280]{1,0:T(8,128)S(1)}, u32[]{:S(2)}, u32[]{:S(2)}) collective-permute-start(f32[6,1280]{1,0:T(8,128)S(1)} %collective-permute-done.got_ref), channel_id=1, source_target_pairs={{0,1},{1,0},{2,3},{3,2},{4,5},{5,4},{6,7},{7,6},{8,9},{9,8},{10,11... | collective-permute-start | bytes 92168 | tf_op jit(solution)/shard_map/ppermute | solution.py:496
  8.5 4.6 %collective-permute-start.2 = (f32[6,256]{1,0:T(8,128)S(1)}, f32[6,256]{1,0:T(8,128)S(1)}, u32[]{:S(2)}, u32[]{:S(2)}) collective-permute-start(f32[6,256]{1,0:T(8,128)S(1)} %get-tuple-element.22.own_ref), channel_id=1, source_target_pairs={{0,8},{8,0},{4,12},{12,4},{1,9},{9,1},{5,13},{13,5},{2,10},{10,2},... | collective-permute-start | bytes 18440 | tf_op jit(solution)/shard_map/ppermute | solution.py:517
  13.1 10.5 %copy-start.3 = (bf16[3,256,1024]{2,1,0:T(8,128)(2,1)S(1)}, bf16[3,256,1024]{2,1,0:T(8,128)(2,1)}, u32[]{:S(2)}) copy-start(bf16[3,256,1024]{2,1,0:T(8,128)(2,1)} %param.14) | copy-start | bytes 4718596
  13.1 10.5 %copy-start.5 = (f32[256]{0:T(256)S(1)}, f32[256]{0:T(256)}, u32[]{:S(2)}) copy-start(f32[256]{0:T(256)} %param.13) | copy-start | bytes 3076
  15.4 8.2 %collective-permute-start.3 = (f32[6,512]{1,0:T(8,128)S(1)}, f32[6,512]{1,0:T(8,128)S(1)}, u32[]{:S(2)}, u32[]{:S(2)}) collective-permute-start(f32[6,512]{1,0:T(8,128)S(1)} %get-tuple-element.24), channel_id=1, source_target_pairs={{0,4},{4,0},{8,12},{12,8},{1,5},{5,1},{9,13},{13,9},{2,6},{6,2},{1... | collective-permute-start | bytes 36872 | tf_op jit(solution)/shard_map/ppermute | solution.py:517
  16.6 7.0 %collective-permute-start.4 = (f32[6,512]{1,0:T(8,128)S(1)}, f32[6,512]{1,0:T(8,128)S(1)}, u32[]{:S(2)}, u32[]{:S(2)}) collective-permute-start(f32[6,512]{1,0:T(8,128)S(1)} %get-tuple-element.25), channel_id=1, source_target_pairs={{0,12},{12,0},{4,8},{8,4},{1,13},{13,1},{5,9},{9,5},{2,14},{14,2},... | collective-permute-start | bytes 36872 | tf_op jit(solution)/shard_map/ppermute | solution.py:517
  19.0 4.5 %collective-permute-start.5 = (f32[6,256]{1,0:T(8,128)S(1)}, f32[6,256]{1,0:T(8,128)S(1)}, u32[]{:S(2)}, u32[]{:S(2)}) collective-permute-start(f32[6,256]{1,0:T(8,128)S(1)} %get-tuple-element.26.own_ref), channel_id=1, source_target_pairs={{0,8},{8,0},{4,12},{12,4},{1,9},{9,1},{5,13},{13,5},{2,10},{10,2},... | collective-permute-start | bytes 18440 | tf_op jit(solution)/shard_map/ppermute | solution.py:517
  24.7 5.8 %collective-permute-start.7 = (bf16[192,1024]{1,0:T(8,128)(2,1)S(1)}, bf16[192,1024]{1,0:T(8,128)(2,1)S(1)}, u32[]{:S(2)}, u32[]{:S(2)}) collective-permute-start(bf16[192,1024]{1,0:T(8,128)(2,1)S(1)} %get-tuple-element.29), channel_id=1, source_target_pairs={{0,1},{1,0},{2,3},{3,2},{4,5},{5,4},{6,7},{7,6},{8,9},{9,8},{10,11... | collective-permute-start | bytes 1179656 | tf_op jit(solution)/shard_map/ppermute | solution.py:496
  26.0 34.3 %collective-permute-start.11 = (bf16[2,512,256]{2,1,0:T(8,128)(2,1)S(1)}, bf16[2,512,256]{2,1,0:T(8,128)(2,1)S(1)}, u32[]{:S(2)}, u32[]{:S(2)}) collective-permute-start(bf16[2,512,256]{2,1,0:T(8,128)(2,1)S(1)} %shard_map.97), channel_id=1, source_target_pairs={{0,2},{2,0},{1,3},{3,1},{4,6},{6,4},{5,7},{7,5},{8,10},{10,8},{9,1... | collective-permute-start | bytes 1572872 | tf_op jit(solution)/shard_map/ppermute | solution.py:500
  28.7 31.3 %copy-start.2 = (bf16[6,128,1024]{2,1,0:T(8,128)(2,1)S(1)}, bf16[6,128,1024]{2,1,0:T(8,128)(2,1)}, u32[]{:S(2)}) copy-start(bf16[6,128,1024]{2,1,0:T(8,128)(2,1)} %latent_ref.1) | copy-start | bytes 4718596
  28.7 23.4 %collective-permute-start.10 = (bf16[2,512,256]{2,1,0:T(8,128)(2,1)S(1)}, bf16[2,512,256]{2,1,0:T(8,128)(2,1)S(1)}, u32[]{:S(2)}, u32[]{:S(2)}) collective-permute-start(bf16[2,512,256]{2,1,0:T(8,128)(2,1)S(1)} %shard_map.96), channel_id=1, source_target_pairs={{0,2},{2,0},{1,3},{3,1},{4,6},{6,4},{5,7},{7,5},{8,10},{10,8},{9,1... | collective-permute-start | bytes 1572872 | tf_op jit(solution)/shard_map/ppermute | solution.py:500
  30.4 23.2 %collective-permute-start.6 = (bf16[192,1024]{1,0:T(8,128)(2,1)S(1)}, bf16[192,1024]{1,0:T(8,128)(2,1)S(1)}, u32[]{:S(2)}, u32[]{:S(2)}) collective-permute-start(bf16[192,1024]{1,0:T(8,128)(2,1)S(1)} %get-tuple-element.28), channel_id=1, source_target_pairs={{0,1},{1,0},{2,3},{3,2},{4,5},{5,4},{6,7},{7,6},{8,9},{9,8},{10,11... | collective-permute-start | bytes 1179656 | tf_op jit(solution)/shard_map/ppermute | solution.py:496
  30.7 29.4 %collective-permute-start.8 = (bf16[192,1024]{1,0:T(8,128)(2,1)S(1)}, bf16[192,1024]{1,0:T(8,128)(2,1)S(1)}, u32[]{:S(2)}, u32[]{:S(2)}) collective-permute-start(bf16[192,1024]{1,0:T(8,128)(2,1)S(1)} %add_convert_fusion), channel_id=1, source_target_pairs={{0,2},{2,0},{1,3},{3,1},{4,6},{6,4},{5,7},{7,5},{8,10},{10,8},{9,1... | collective-permute-start | bytes 1179656 | tf_op jit(solution)/shard_map/ppermute | solution.py:500
  52.1 18.6 %collective-permute-start.12 = (bf16[2,512,256]{2,1,0:T(8,128)(2,1)S(1)}, bf16[2,512,256]{2,1,0:T(8,128)(2,1)S(1)}, u32[]{:S(2)}, u32[]{:S(2)}) collective-permute-start(bf16[2,512,256]{2,1,0:T(8,128)(2,1)S(1)} %collective-permute-done.10.heads_x_ref), channel_id=1, source_target_pairs={{0,16},{16,0},{1,17},{17,1},{2,18},{18,2},{3,19},{19,3},{4,20},{20... | collective-permute-start | bytes 1572872 | tf_op jit(solution)/shard_map/ppermute | solution.py:504
  60.0 10.7 %copy-start = (bf16[1024,3,256]{2,0,1:T(8,128)(2,1)S(1)}, bf16[1024,3,256]{2,0,1:T(8,128)(2,1)}, u32[]{:S(2)}) copy-start(bf16[1024,3,256]{2,0,1:T(8,128)(2,1)} %param.16) | copy-start | bytes 4718596
  60.0 10.7 %copy-start.4 = (bf16[256,1024]{1,0:T(8,128)(2,1)S(1)}, bf16[256,1024]{1,0:T(8,128)(2,1)}, u32[]{:S(2)}) copy-start(bf16[256,1024]{1,0:T(8,128)(2,1)} %out_ref.3) | copy-start | bytes 1572868
  60.0 10.7 %copy-start.6 = (f32[1024]{0:T(1024)S(1)}, f32[1024]{0:T(1024)}, u32[]{:S(2)}) copy-start(f32[1024]{0:T(1024)} %param.15) | copy-start | bytes 12292
  60.2 10.4 %collective-permute-start.9 = (bf16[192,1024]{1,0:T(8,128)(2,1)S(1)}, bf16[192,1024]{1,0:T(8,128)(2,1)S(1)}, u32[]{:S(2)}, u32[]{:S(2)}) collective-permute-start(bf16[192,1024]{1,0:T(8,128)(2,1)S(1)} %shard_map.95.mine_ref), channel_id=1, source_target_pairs={{0,1},{1,0},{2,3},{3,2},{4,5},{5,4},{6,7},{7,6},{8,9},{9,8},{10,11... | collective-permute-start | bytes 1179656 | tf_op jit(solution)/shard_map/ppermute | solution.py:496
  60.4 10.3 %collective-permute-start.13 = (bf16[512,256]{1,0:T(8,128)(2,1)S(1)}, bf16[512,256]{1,0:T(8,128)(2,1)S(1)}, u32[]{:S(2)}, u32[]{:S(2)}) collective-permute-start(bf16[512,256]{1,0:T(8,128)(2,1)S(1)} %get-tuple-element.36.values_x_ref), channel_id=1, source_target_pairs={{0,16},{16,0},{1,17},{17,1},{2,18},{18,2},{3,19},{19,3},{4,20},{20... | collective-permute-start | bytes 786440 | tf_op jit(solution)/shard_map/ppermute | solution.py:504
  62.0 8.7 %collective-permute-start.14 = (bf16[512,256]{1,0:T(8,128)(2,1)S(1)}, bf16[512,256]{1,0:T(8,128)(2,1)S(1)}, u32[]{:S(2)}, u32[]{:S(2)}) collective-permute-start(bf16[512,256]{1,0:T(8,128)(2,1)S(1)} %get-tuple-element.35.outs_x_ref), channel_id=1, source_target_pairs={{0,4},{4,0},{8,12},{12,8},{1,5},{5,1},{9,13},{13,9},{2,6},{6,2},{1... | collective-permute-start | bytes 786440 | tf_op jit(solution)/shard_map/ppermute | solution.py:508
  75.2 1.5 %collective-permute-start.15 = (bf16[384,256]{1,0:T(8,128)(2,1)S(1)}, bf16[384,256]{1,0:T(8,128)(2,1)S(1)}, u32[]{:S(2)}, u32[]{:S(2)}) collective-permute-start(bf16[384,256]{1,0:T(8,128)(2,1)S(1)} %get-tuple-element.32), channel_id=1, source_target_pairs={{0,1},{1,0},{2,3},{3,2},{4,5},{5,4},{6,7},{7,6},{8,9},{9,8},{10,11... | collective-permute-start | bytes 589832 | tf_op jit(solution)/shard_map/ppermute | solution.py:496
  75.3 3.0 %collective-permute-start.17 = (bf16[384,256]{1,0:T(8,128)(2,1)S(1)}, bf16[384,256]{1,0:T(8,128)(2,1)S(1)}, u32[]{:S(2)}, u32[]{:S(2)}) collective-permute-start(bf16[384,256]{1,0:T(8,128)(2,1)S(1)} %get-tuple-element.34), channel_id=1, source_target_pairs={{0,1},{1,0},{2,3},{3,2},{4,5},{5,4},{6,7},{7,6},{8,9},{9,8},{10,11... | collective-permute-start | bytes 589832 | tf_op jit(solution)/shard_map/ppermute | solution.py:496
  76.8 7.0 %collective-permute-start.16 = (bf16[384,256]{1,0:T(8,128)(2,1)S(1)}, bf16[384,256]{1,0:T(8,128)(2,1)S(1)}, u32[]{:S(2)}, u32[]{:S(2)}) collective-permute-start(bf16[384,256]{1,0:T(8,128)(2,1)S(1)} %add_convert_fusion.1), channel_id=1, source_target_pairs={{0,2},{2,0},{1,3},{3,1},{4,6},{6,4},{5,7},{7,5},{8,10},{10,8},{9,1... | collective-permute-start | bytes 589832 | tf_op jit(solution)/shard_map/ppermute | solution.py:500

commit v6 on v5

--- a/solution.py
+++ b/solution.py
@@ -14,6 +14,7 @@
 WINDOW = 64
 LANES = 128
 PIECES = 4
+CHUNK = 2
 
 norm_eps = 1e-05
 rms_eps = 1e-06
@@ -186,100 +187,110 @@
     return f32_dot(centre, hot), f32_dot(lax.rsqrt(spread + norm_eps), hot)
 
 
-def stats_kernel(width, lat_ref, one_ref, two_ref, own_ref, sum_ref, square_ref):
+def stats_kernel(width, lat_ref, near_ref, own_ref, sum_ref, square_ref):
     stems, frames, channels = lat_ref.shape
-    even = even_place()
+    upward = even_place() == (lax.axis_index("tensor") % 2 == 0)
     for stem in range(stems):
         block = lat_ref[stem].astype(f32)
         sum_ref[stem : stem + 1, :] = jnp.sum(block, axis=0, keepdims=True)
         square_ref[stem : stem + 1, :] = jnp.sum(block * block, axis=0, keepdims=True)
-        down, up = block[:1], block[frames - 1 :]
-        one_ref[stem : stem + 1, :channels] = jnp.where(even, up, down)
-        two_ref[stem : stem + 1, :channels] = jnp.where(even, down, up)
+        edge = jnp.where(upward, block[frames - 1 :], block[:1])
+        near_ref[stem : stem + 1, :channels] = edge
     sums, squares = group_totals(sum_ref[...], square_ref[...], width)
-    for ref, start in ((one_ref, channels), (two_ref, channels), (own_ref, 0)):
+    for ref, start in ((near_ref, channels), (own_ref, 0)):
         ref[:, start : start + LANES] = sums
         ref[:, start + LANES : start + 2 * LANES] = squares
 
 
+def pick(value):
+    half = value.shape[0] // 2
+    return jnp.where(lax.axis_index("tensor") % 2 == 0, value[:half], value[half:])
+
+
+def both_dots(rows, near, away):
+    parts = [jnp.dot(rows, weight, preferred_element_type=f32) for weight in (near, away)]
+    return jnp.concatenate(parts, axis=1)
+
+
 def first_kernel(
     entries, width, frame_size,
-    lat_ref, got_ref, swapped_ref, far_ref, own_ref, gain_ref, weight_ref, bias_ref,
+    lat_ref, got_ref, swapped_ref, far_ref, own_ref, gain_ref, weight_ref, partner_ref,
+    bias_ref, bias_far_ref,
     hid_ref, one_ref, two_ref, tot_ref, act_ref, edge_ref, sum_ref, square_ref,
 ):
-    stems, frames, channels = lat_ref.shape
-    shard = weight_ref.shape[2]
+    frames, channels = lat_ref.shape[1:]
+    stems, _, span = hid_ref.shape
     place = lax.axis_index("frame")
+    core = lax.axis_index("tensor") % 2
     centre, scale = channel_scale(
         [own_ref[...], got_ref[:, channels:], swapped_ref[:, channels:], far_ref[...]],
         entries, channels, width,
     )
     even = even_place()
-    first_got = even == (lax.axis_index("tensor") % 2 == 0)
+    first_got = even == (core == 0)
     got, swapped = got_ref[:, :channels], swapped_ref[:, :channels]
     high, low = jnp.where(first_got, got, swapped), jnp.where(first_got, swapped, got)
     scale = scale * (0.5 * gain_ref[...])
+    low, high = pick(silu_of_half((low - centre) * scale)), pick(silu_of_half((high - centre) * scale))
+    centre, scale = pick(centre), pick(scale)
     edge_ref[...] = jnp.zeros_like(edge_ref)
-    low = silu_of_half((low - centre) * scale)
-    high = silu_of_half((high - centre) * scale)
     edge_ref[0:stems, :] = jnp.where(place > 0, low, 0.0)
     edge_ref[8 : 8 + stems, :] = jnp.where(place < frame_size - 1, high, 0.0)
     edge = edge_ref[...].astype(bf16)
-    edge_low = jnp.dot(edge, weight_ref[0], preferred_element_type=f32)
-    edge_high = jnp.dot(edge, weight_ref[2], preferred_element_type=f32)
-    row = lax.broadcasted_iota(jnp.int32, (frames, shard), 0)
-    bias = bias_ref[...]
-    step = stems // 2
-    for first in range(0, stems, step):
-        for stem in range(first, first + step):
-            block = lat_ref[stem].astype(f32)
-            block = (block - centre[stem : stem + 1]) * scale[stem : stem + 1]
-            act_ref[stem * frames : (stem + 1) * frames, :] = silu_of_half(block).astype(bf16)
-        rows = act_ref[first * frames : (first + step) * frames, :]
-        taps = [jnp.dot(rows, weight_ref[tap], preferred_element_type=f32) for tap in range(3)]
-        for stem in range(first, first + step):
-            lo = (stem - first) * frames
-            before = pltpu.roll(taps[0][lo : lo + frames], 1, 0)
-            after = pltpu.roll(taps[2][lo : lo + frames], frames - 1, 0)
-            before = jnp.where(row == 0, edge_low[stem : stem + 1], before)
-            after = jnp.where(row == frames - 1, edge_high[8 + stem : 9 + stem], after)
-            hid = taps[1][lo : lo + frames] + before + after + bias
-            hid_ref[stem] = hid
-            sum_ref[stem : stem + 1, :] = jnp.sum(hid, axis=0, keepdims=True)
-            square_ref[stem : stem + 1, :] = jnp.sum(hid * hid, axis=0, keepdims=True)
-            down, up = hid[:1], hid[frames - 1 :]
-            one_ref[stem : stem + 1, :shard] = jnp.where(even, up, down)
-            two_ref[stem : stem + 1, :shard] = jnp.where(even, down, up)
+    edge_low = both_dots(edge, weight_ref[0], partner_ref[0])
+    edge_high = both_dots(edge, weight_ref[2], partner_ref[2])
+    row = lax.broadcasted_iota(jnp.int32, (frames, span), 0)
+    bias = jnp.concatenate([bias_ref[...], bias_far_ref[...]], axis=1)
+    for stem in range(stems):
+        if stem % CHUNK == 0:
+            first, last = stem, min(stem + CHUNK, stems)
+            for part in range(first, last):
+                block = lat_ref[core * stems + part].astype(f32)
+                block = (block - centre[part : part + 1]) * scale[part : part + 1]
+                act_ref[part * frames : (part + 1) * frames, :] = silu_of_half(block).astype(bf16)
+            rows = act_ref[first * frames : last * frames, :]
+            taps = [both_dots(rows, weight_ref[tap], partner_ref[tap]) for tap in range(3)]
+        lo = (stem - first) * frames
+        before = pltpu.roll(taps[0][lo : lo + frames], 1, 0)
+        after = pltpu.roll(taps[2][lo : lo + frames], frames - 1, 0)
+        before = jnp.where(row == 0, edge_low[stem : stem + 1], before)
+        after = jnp.where(row == frames - 1, edge_high[8 + stem : 9 + stem], after)
+        hid = taps[1][lo : lo + frames] + before + after + bias
+        hid_ref[stem] = hid
+        sum_ref[stem : stem + 1, :] = jnp.sum(hid, axis=0, keepdims=True)
+        square_ref[stem : stem + 1, :] = jnp.sum(hid * hid, axis=0, keepdims=True)
+        down, up = hid[:1], hid[frames - 1 :]
+        one_ref[stem : stem + 1, :span] = jnp.where(even, up, down)
+        two_ref[stem : stem + 1, :span] = jnp.where(even, down, up)
     sums, squares = group_totals(sum_ref[...], square_ref[...], width)
-    for ref, start in ((one_ref, shard), (two_ref, shard), (tot_ref, 0)):
+    for ref, start in ((one_ref, span), (two_ref, span), (tot_ref, 0)):
         ref[:, start : start + LANES] = sums
         ref[:, start + LANES : start + 2 * LANES] = squares
 
 
 def second_kernel(
     entries, width, frame_size, other,
-    hid_ref, one_ref, two_ref, far_ref, own_ref, gain_ref, weight_ref,
-    send_ref, keep_ref, act_ref,
+    hid_ref, one_ref, two_ref, far_ref, own_ref, gain_ref, weight_ref, partner_ref,
+    total_ref, act_ref,
 ):
-    stems, _, shard = hid_ref.shape
+    stems, _, span = hid_ref.shape
+    shard = span // 2
     place = lax.axis_index("frame")
-    index = lax.axis_index("tensor")
-    chip, core = index // 2, index % 2
+    chip = lax.axis_index("tensor") // 2
     window = 1 - chip if other else chip
     centre, scale = channel_scale(
-        [own_ref[...], one_ref[:, shard:], two_ref[:, shard:], far_ref[...]],
-        entries, shard, width,
+        [own_ref[...], one_ref[:, span:], two_ref[:, span:], far_ref[...]],
+        entries, span, width,
     )
     even = even_place()
-    one, two = one_ref[:, :shard], two_ref[:, :shard]
+    one, two = one_ref[:, :span], two_ref[:, :span]
     high, low = jnp.where(even, one, two), jnp.where(even, two, one)
     scale = scale * (0.5 * gain_ref[...])
     low = jnp.where(place > 0, silu_of_half((low - centre) * scale), 0.0)
     high = jnp.where(place < frame_size - 1, silu_of_half((high - centre) * scale), 0.0)
-    row = lax.broadcasted_iota(jnp.int32, (WINDOW, shard), 0)
-    half = stems // 2
+    row = lax.broadcasted_iota(jnp.int32, (WINDOW, span), 0)
+    start = pl.multiple_of(window * WINDOW, WINDOW)
     for stem in range(stems):
-        start = pl.multiple_of(window * WINDOW, WINDOW)
         mean, factor = centre[stem : stem + 1], scale[stem : stem + 1]
         act = silu_of_half((hid_ref[stem, pl.ds(start, WINDOW), :] - mean) * factor)
         inner = silu_of_half((hid_ref[stem, WINDOW - 8 : WINDOW + 8, :] - mean) * factor)
@@ -287,15 +298,16 @@
         after = jnp.where(window == 0, inner[8:9], high[stem : stem + 1])
         before = jnp.where(row == 0, before, pltpu.roll(act, 1, 0))
         after = jnp.where(row == WINDOW - 1, after, pltpu.roll(act, WINDOW - 1, 0))
-        mine = core if stem < half else 1 - core
-        base = jnp.where(mine == 0, half * WINDOW, 0) + (stem % half) * WINDOW
-        at = pl.ds(pl.multiple_of(base, WINDOW), WINDOW)
-        act_ref[at, 0:shard] = before.astype(bf16)
-        act_ref[at, shard : 2 * shard] = act.astype(bf16)
-        act_ref[at, 2 * shard : 3 * shard] = after.astype(bf16)
-    total = jnp.dot(act_ref[...], weight_ref[...], preferred_element_type=f32)
-    send_ref[...] = total[: half * WINDOW].astype(bf16)
-    keep_ref[...] = total[half * WINDOW :].astype(bf16)
+        at = slice(stem * WINDOW, (stem + 1) * WINDOW)
+        for tap, value in enumerate((before, act, after)):
+            value = value.astype(bf16)
+            act_ref[at, tap * shard : (tap + 1) * shard] = value[:, :shard]
+            act_ref[at, (3 + tap) * shard : (4 + tap) * shard] = value[:, shard:]
+    total = jnp.dot(act_ref[:, : 3 * shard], weight_ref[...], preferred_element_type=f32)
+    total = total + jnp.dot(
+        act_ref[:, 3 * shard :], partner_ref[...], preferred_element_type=f32
+    )
+    total_ref[...] = total.astype(total_ref.dtype)
 
 
 def split2(value):
@@ -303,42 +315,67 @@
     return high, (value - high.astype(f32)).astype(bf16)
 
 
+def normed_rows(res, gain_ref):
+    mean_sq = jnp.mean(res * res, axis=1, keepdims=True)
+    return (res * lax.rsqrt(mean_sq + rms_eps) * gain_ref[...]).astype(bf16)
+
+
+def projector(normed_ref, qkv_ref, first_x_ref, first_y_ref, q_x_ref, q_z_ref, v_refs=()):
+    depth = normed_ref.shape[1] // 2
+    group, parity = lax.axis_index("groups"), lax.axis_index("frame") % 2
+
+    def half(place):
+        return normed_ref[:, pl.ds(pl.multiple_of(place * depth, depth), depth)]
+
+    def project(side, which):
+        if side == 0:
+            return jnp.dot(normed_ref[...], qkv_ref[which], preferred_element_type=f32)
+        if which == 0:
+            place, near, away = parity, q_x_ref[...], q_z_ref[...]
+        elif which == 1:
+            place, near, away = group, first_x_ref[:depth, :], first_y_ref[:depth, :]
+        else:
+            place, near, away = group, v_refs[0][...], v_refs[1][...]
+        value = jnp.dot(half(place), near, preferred_element_type=f32)
+        return value + jnp.dot(half(1 - place), away, preferred_element_type=f32)
+
+    return project
+
+
+def project_kernel(
+    mine_ref, gain_ref, qkv_ref, first_x_ref, first_y_ref, q_x_ref, q_z_ref,
+    queries_ref, keys_ref, normed_ref,
+):
+    shard = qkv_ref.shape[2]
+    normed_ref[...] = normed_rows(mine_ref[...].astype(f32), gain_ref)
+    project = projector(normed_ref, qkv_ref, first_x_ref, first_y_ref, q_x_ref, q_z_ref)
+    for side in range(2):
+        at = slice(side * shard, (side + 1) * shard)
+        queries_ref[:, at] = project(side, 0)
+        keys_ref[:, at] = project(side, 1)
+
+
 def attention_kernel(
-    mine_ref, theirs_ref, gain_ref, qkv_ref, out_ref,
-    heads_x_ref, values_x_ref, outs_x_ref, heads_y_ref, values_y_ref, outs_z_ref,
-    send_far_ref, keep_far_ref, send_near_ref, keep_near_ref,
-    res_ref, normed_ref, context_ref,
+    theirs_ref, gain_ref, qkv_ref, first_x_ref, first_y_ref, q_x_ref, q_z_ref, v_x_ref, v_y_ref,
+    queries_ref, keys_ref, mine_ref,
+    context_ref, normed_ref,
 ):
-    rows, channels = mine_ref.shape
+    rows = theirs_ref.shape[0]
     shard = qkv_ref.shape[2]
-    depth = channels // 2
-    part = shard // 2
-    group = lax.axis_index("groups")
-    index = lax.axis_index("tensor")
-    chip, core = index // 2, index % 2
-    for first, ref in ((0, mine_ref), (rows, theirs_ref)):
-        res = ref[...].astype(f32)
-        res_ref[first : first + rows, :] = res
-        mean_sq = jnp.mean(res * res, axis=1, keepdims=True)
-        normed_ref[first : first + rows, :] = (
-            res * lax.rsqrt(mean_sq + rms_eps) * gain_ref[...]
-        ).astype(bf16)
-    normed = normed_ref[...]
+    normed_ref[:rows, :] = mine_ref[...]
+    normed_ref[rows:, :] = normed_rows(theirs_ref[...].astype(f32), gain_ref)
+    weights = qkv_ref, first_x_ref, first_y_ref, q_x_ref, q_z_ref
+    project = projector(normed_ref.at[pl.ds(rows, rows), :], *weights)
+    project_all = projector(normed_ref, *weights, (v_x_ref, v_y_ref))
     lane = lax.broadcasted_iota(jnp.int32, (2 * rows, LANES), 1)
     nt = (((1,), (1,)), ((), ()))
-    near_at = pl.ds(pl.multiple_of(group * depth, depth), depth)
-    away_at = pl.ds(pl.multiple_of((1 - group) * depth, depth), depth)
-
-    def project(side, which):
-        if side == 0:
-            return jnp.dot(normed, qkv_ref[which], preferred_element_type=f32)
-        from_x = heads_x_ref[which] if which < 2 else values_x_ref[...]
-        from_y = heads_y_ref[which] if which < 2 else values_y_ref[...]
-        near = jnp.dot(normed_ref[:, near_at], from_x, preferred_element_type=f32)
-        return near + jnp.dot(normed_ref[:, away_at], from_y, preferred_element_type=f32)
-
     for side in range(2):
-        queries, keys, values = [project(side, which) for which in range(3)]
+        span = slice(side * shard, (side + 1) * shard)
+        queries, keys = [
+            jnp.concatenate([ref[:, span], project(side, which)], axis=0)
+            for which, ref in enumerate((queries_ref, keys_ref))
+        ]
+        values = project_all(side, 2)
         queries = queries * (1.0 / math.sqrt(HEAD_DIM))
         for tile in range(shard // LANES):
             at = slice(tile * LANES, (tile + 1) * LANES)
@@ -370,17 +407,29 @@
             )
             base = side * shard + tile * LANES
             context_ref[:, base : base + LANES] = (mixed[:, :LANES] / mixed[:, LANES:]).astype(bf16)
-    context = context_ref[:, :shard]
-    parity = lax.axis_index("frame") % 2
-    from_x = context_ref[:, pl.ds(pl.multiple_of(shard + parity * part, part), part)]
-    from_z = context_ref[:, pl.ds(pl.multiple_of(shard + (1 - parity) * part, part), part)]
+
+
+def output_kernel(
+    context_ref, mine_ref, theirs_ref, out_ref, first_x_ref, first_y_ref, out_z_ref,
+    send_far_ref, keep_far_ref, send_near_ref, keep_near_ref,
+    out_far_ref,
+):
+    rows, channels = mine_ref.shape
+    shard = out_ref.shape[0]
+    index = lax.axis_index("tensor")
+    chip, core = index // 2, index % 2
+    depth = channels // 2
+    group, parity = lax.axis_index("groups"), lax.axis_index("frame") % 2
+    out_far_ref[2 * group + parity] = first_x_ref[depth:, :]
+    out_far_ref[2 * (1 - group) + parity] = first_y_ref[depth:, :]
+    out_far_ref[2 * group + 1 - parity] = out_z_ref[0]
+    out_far_ref[2 * (1 - group) + 1 - parity] = out_z_ref[1]
 
     def term(block):
         at = pl.ds(pl.multiple_of(block * shard, shard), shard)
-        rows_at = pl.ds(pl.multiple_of(block * part, part), part)
-        value = jnp.dot(context, out_ref[:, at], preferred_element_type=f32)
-        value = value + jnp.dot(from_x, outs_x_ref[rows_at, :], preferred_element_type=f32)
-        return value + jnp.dot(from_z, outs_z_ref[rows_at, :], preferred_element_type=f32)
+        value = jnp.dot(context_ref[:, :shard], out_ref[:, at], preferred_element_type=f32)
+        far = jnp.dot(context_ref[:, shard:], out_far_ref[block], preferred_element_type=f32)
+        return value + far
 
     sides = ((1 - chip, send_far_ref, keep_far_ref), (chip, send_near_ref, keep_near_ref))
     for goal, send_ref, keep_ref in sides:
@@ -389,7 +438,9 @@
         send_ref[rows:, :] = value[:rows]
         block = 2 * goal + core
         at = pl.ds(pl.multiple_of(block * shard, shard), shard)
-        keep_ref[...] = term(block) + res_ref[:, at]
+        value = term(block)
+        keep_ref[:rows, :] = value[:rows] + mine_ref[:, at].astype(f32)
+        keep_ref[rows:, :] = value[rows:] + theirs_ref[:, at].astype(f32)
 
 
 def run_copies(pairs, sems):
@@ -403,56 +454,56 @@
         copy.wait()
 
 
-def pack_heads_kernel(qkv_ref, send_ref, sems):
-    depth = send_ref.shape[1]
+def row_pieces(place, depth):
     step = depth // PIECES
-    start = lax.axis_index("groups") * depth
+    for piece in range(PIECES):
+        start = pl.multiple_of(place * depth + piece * step, step)
+        yield pl.ds(start, step), pl.ds(piece * step, step)
+
+
+def pack_first_kernel(qkv_ref, out_ref, send_ref, sems):
+    depth, shard = qkv_ref.shape[1] // 2, qkv_ref.shape[2]
+    group, parity = lax.axis_index("groups"), lax.axis_index("frame") % 2
     pairs = []
-    for which in range(2):
-        for piece in range(PIECES):
-            rows = pl.ds(pl.multiple_of(start + piece * step, step), step)
-            goal = send_ref.at[which, pl.ds(piece * step, step), :]
-            pairs.append((qkv_ref.at[which, rows, :], goal))
+    for which, place, base in ((1, group, 0), (0, parity, depth + shard)):
+        for rows, goal in row_pieces(place, depth):
+            pairs.append((qkv_ref.at[which, rows, :], send_ref.at[pl.ds(base + goal.start, goal.size), :]))
+    block = pl.ds(pl.multiple_of((2 * group + parity) * shard, shard), shard)
+    for piece in range(2):
+        rows = pl.ds(piece * shard // 2, shard // 2)
+        goal = pl.ds(depth + piece * shard // 2, shard // 2)
+        pairs.append((out_ref.at[rows, block], send_ref.at[goal, :]))
     run_copies(pairs, sems)
 
 
-def pack_rest_kernel(qkv_ref, out_ref, send_ref, sems):
-    depth, shard = send_ref.shape[1:]
-    part = shard // 2
-    step = depth // PIECES
-    start = lax.axis_index("groups") * depth
-    pairs = []
-    for piece in range(PIECES):
-        rows = pl.ds(pl.multiple_of(start + piece * step, step), step)
-        pairs.append((qkv_ref.at[2, rows, :], send_ref.at[0, pl.ds(piece * step, step), :]))
-    rows = pl.ds(pl.multiple_of(lax.axis_index("frame") % 2 * part, part), part)
-    for block in range(depth // part):
-        goal = send_ref.at[1, pl.ds(block * part, part), :]
-        pairs.append((out_ref.at[rows, pl.ds(block * shard, shard)], goal))
+def pack_rest_kernel(qkv_ref, values_ref, sems):
+    pairs = [
+        (qkv_ref.at[2, rows, :], values_ref.at[goal, :])
+        for rows, goal in row_pieces(lax.axis_index("groups"), values_ref.shape[0])
+    ]
     run_copies(pairs, sems)
 
 
-def pack(kernel, shape, copies, args):
+def pack(kernel, shapes, copies, args):
     return pl.pallas_call(
         kernel,
-        out_shape=jax.ShapeDtypeStruct(shape, bf16),
+        out_shape=[jax.ShapeDtypeStruct(shape, bf16) for shape in shapes],
         in_specs=[pl.BlockSpec(memory_space=pltpu.HBM)] * len(args),
-        out_specs=pl.BlockSpec(memory_space=VMEM),
+        out_specs=[pl.BlockSpec(memory_space=VMEM)] * len(shapes),
         scratch_shapes=[pltpu.SemaphoreType.DMA((copies,))],
         compiler_params=pltpu.CompilerParams(vmem_limit_bytes=4 * 2**20),
         cost_estimate=pl.CostEstimate(flops=0, bytes_accessed=2**20, transcendentals=0),
     )(*[pltpu.with_memory_space_constraint(arg, pltpu.HBM) for arg in args])
 
 
-def residual_kernel(latent_ref, keep_ref, got_ref, far_ref, out_ref):
+def residual_kernel(latent_ref, keep_ref, far_ref, out_ref):
     stems = latent_ref.shape[0]
     index = lax.axis_index("tensor")
     chip, core = index // 2, index % 2
     start = pl.multiple_of(chip * WINDOW, WINDOW)
     for stem in range(stems // 2):
         rows = slice(stem * WINDOW, (stem + 1) * WINDOW)
-        total = keep_ref[rows, :].astype(f32) + got_ref[rows, :].astype(f32)
-        total = total + far_ref[rows, :].astype(f32)
+        total = keep_ref[rows, :] + far_ref[rows, :].astype(f32)
         latent = latent_ref[core * (stems // 2) + stem, pl.ds(start, WINDOW), :]
         out_ref[rows, :] = (latent.astype(f32) + total).astype(bf16)
 
@@ -504,10 +555,6 @@
     return lax.ppermute(value, "groups", [(0, 1), (1, 0)])
 
 
-def swap_frames(value):
-    return lax.ppermute(value, "frame", [(0, 1), (1, 0), (2, 3), (3, 2)])
-
-
 ONE = ((0, 1), (1, 0), (2, 3), (3, 2))
 TWO = ((0, 3), (3, 0), (1, 2), (2, 1))
 FAR = ((0, 2), (2, 0), (1, 3), (3, 1))
@@ -517,14 +564,13 @@
     return lax.ppermute(value, "frame", pairs)
 
 
-def trade_by_core(one, two):
+def trade_by_core(value):
     count = lax.axis_size("tensor")
     pairs = [
         (source * count + index, goal * count + index)
         for index in range(count)
         for source, goal in (TWO if index % 2 else ONE)
     ]
-    value = jnp.where(lax.axis_index("tensor") % 2 == 0, one, two)
     return lax.ppermute(value, ("frame", "tensor"), pairs)
 
 
@@ -539,70 +585,84 @@
     entries = frames * frame_size * width
     half_rows = stems // 2 * WINDOW
     qkv = jnp.transpose(qkv_weight, (1, 0, 2))
-    depth, part = channels // 2, shard // 2
-    heads = pack(pack_heads_kernel, (2, depth, shard), 2 * PIECES, [qkv])
-    rest = pack(
-        pack_rest_kernel, (2, depth, shard), PIECES + depth // part,
+    depth = channels // 2
+    (first,) = pack(
+        pack_first_kernel, [(2 * depth + shard, shard)], 2 * PIECES + 2,
         [qkv, out_weight],
     )
-    heads_x = swap_chips(heads)
-    rest_x = swap_chips(rest)
-    heads_y = swap_groups(heads_x)
-    values_x, outs_x = rest_x[0], rest_x[1]
-    values_y = swap_groups(values_x)
-    outs_z = swap_frames(outs_x)
+    (values,) = pack(pack_rest_kernel, [(depth, shard)], PIECES, [qkv])
+    first_x = swap_chips(first)
+    v_x = swap_chips(values)
+    first_x, q_x = first_x[: depth + shard], first_x[depth + shard :]
+    first_y = swap_groups(first_x)
+    q_z = trade(q_x, ONE)
+    v_y = swap_groups(v_x)
+    out_z = trade(jnp.stack([first_x[depth:], first_y[depth:]]), ONE)
+    weight1 = swap_cores(conv1_weight)
+    weight2 = swap_cores(conv2_weight).reshape(3 * shard, channels)
+    bias_far = swap_cores(time_bias)
+    gain_far = swap_cores(norm2_gain)
+    gain2 = jnp.concatenate([norm2_gain, gain_far])[None]
     wide = channels + 2 * LANES
-    one, two, own = call(
+    near, own = call(
         functools.partial(stats_kernel, width),
-        [((stems, wide), f32), ((stems, wide), f32), ((stems, 2 * LANES), f32)],
+        [((stems, wide), f32), ((stems, 2 * LANES), f32)],
         [((stems, channels), f32)] * 2,
         [latent],
     )
     far = trade(own, FAR)
-    got = trade_by_core(one, two)
+    got = trade_by_core(near)
     swapped = swap_cores(got)
-    narrow = shard + 2 * LANES
+    half, span = stems // 2, 2 * shard
+    narrow = span + 2 * LANES
     hid, one2, two2, own2 = call(
         functools.partial(first_kernel, entries, width, frame_size),
-        [((stems, frames, shard), f32), ((stems, narrow), f32), ((stems, narrow), f32),
-         ((stems, 2 * LANES), f32)],
-        [((stems * frames, channels), bf16), ((16, channels), f32)] + [((stems, shard), f32)] * 2,
-        [latent, got, swapped, far, own, norm1_gain[None], conv1_weight, time_bias[None]],
-        flops=6 * stems * frames * channels * shard,
+        [((half, frames, span), f32), ((half, narrow), f32), ((half, narrow), f32),
+         ((half, 2 * LANES), f32)],
+        [((half * frames, channels), bf16), ((16, channels), f32)] + [((half, span), f32)] * 2,
+        [latent, got, swapped, far, own, norm1_gain[None], conv1_weight, weight1,
+         time_bias[None], bias_far[None]],
+        flops=6 * stems * frames * channels * shard, limit=24,
     )
     far2 = trade(own2, FAR)
     got_two = trade(two2, TWO)
     got_one = trade(one2, ONE)
-    weight2 = conv2_weight.reshape(3 * shard, channels)
 
     def second(other):
         return call(
             functools.partial(second_kernel, entries, width, frame_size, other),
-            [((half_rows, channels), bf16)] * 2,
-            [((2 * half_rows, 3 * shard), bf16)],
-            [hid, got_one, got_two, far2, own2, norm2_gain[None], weight2],
+            [((half_rows, channels), bf16 if other else f32)],
+            [((half_rows, 6 * shard), bf16)],
+            [hid, got_one, got_two, far2, own2, gain2,
+             conv2_weight.reshape(3 * shard, channels), weight2],
             flops=12 * half_rows * channels * shard,
-        )
-
-    send, keep = second(True)
-    got = swap_cores(send)
-    summed = (got.astype(f32) + keep.astype(f32)).astype(bf16)
-    summed = swap_chips(summed)
-    send_own, keep_own = second(False)
-    got_own = swap_cores(send_own)
+        )[0]
+
+    summed = swap_chips(second(True))
     mine = call(
         residual_kernel, [((half_rows, channels), bf16)], [],
-        [latent, keep_own, got_own, summed],
+        [latent, second(False), summed],
     )[0]
     theirs = swap_cores(mine)
+    weights = [attn_gain[None], qkv, first_x, first_y, q_x, q_z]
+    projected = call(
+        project_kernel,
+        [((half_rows, 2 * shard), f32)] * 2 + [((half_rows, channels), bf16)], [],
+        [mine, *weights],
+        flops=8 * half_rows * channels * shard,
+    )
+    context = call(
+        attention_kernel, [((2 * half_rows, 2 * shard), bf16)],
+        [((2 * half_rows, channels), bf16)],
+        [theirs, *weights, v_x, v_y, *projected],
+        flops=24 * half_rows * channels * shard, limit=24,
+    )[0]
     send_far, keep_far, send_near, keep_near = call(
-        attention_kernel,
+        output_kernel,
         [((2 * half_rows, shard), bf16), ((2 * half_rows, shard), f32)] * 2,
-        [((2 * half_rows, channels), f32), ((2 * half_rows, channels), bf16),
-         ((2 * half_rows, 2 * shard), bf16)],
-        [mine, theirs, attn_gain[None], qkv, out_weight, heads_x, values_x, outs_x,
-         heads_y, values_y, outs_z],
-        flops=24 * half_rows * channels * shard, limit=24,
+        [((4, shard, shard), bf16)],
+        [context, mine, theirs, out_weight, first_x, first_y, out_z],
+        flops=8 * half_rows * channels * shard,
     )
     got_far = swap_cores(send_far)
     got_near = swap_cores(send_near)

time: 84.8 us -> 60.2 us (0.71)
  waiting for transfers between devices: 48.1 us -> 27.6 us
  starting transfers between devices: 20.5 us -> 18 us
  local copies, waits for them, and re-layouts: 1.51 us -> 0.11 us
    ppermute x4, waiting for transfers between devices: 31 us -> 10.3 us  [swap_chips(): return lax.ppermute(value, 'tensor', [(0, 2), (2, 0), (1, 3), (3, 1)])]
    ppermute x2, waiting for transfers between devices: 7.66 us -> 5.87 us  [swap_groups(): return lax.ppermute(value, 'groups', [(0, 1), (1, 0)])]
    ppermute x1, starting transfers between devices: 3.12 us -> 1.64 us  [trade_by_core(): return lax.ppermute(value, ('frame', 'tensor'), pairs)]
    unnamed x20 -> x18, local copies, waits for them, and re-layouts: 1.48 us -> 0.05 us
    ppermute x6 -> x8, waiting for transfers between devices: 0.94 us -> 2.09 us  [swap_cores(): return lax.ppermute(value, 'tensor', [(0, 1), (1, 0), (2, 3), (3, 2)])]
    ppermute x1 -> x0, starting transfers between devices: 1.05 us -> none  [swap_frames(): return lax.ppermute(value, 'frame', [(0, 1), (1, 0), (2, 3), (3, 2)])]
    ppermute x2, starting transfers between devices: 3.11 us -> 2.09 us  [swap_groups(): return lax.ppermute(value, 'groups', [(0, 1), (1, 0)])]
    ppermute x4 -> x6, starting transfers between devices: 6.21 us -> 6.85 us  [trade(): return lax.ppermute(value, 'frame', pairs)]
  transfers between devices with their start and end apart: 18 -> 21, of which waited for: 8 -> 12; matrix products, arithmetic and copies ran while one was open for 0% -> 0% of each run, Pallas kernels for 5% -> 21%
where the time goes in v6:
time: 60.2 us; the launch traced here: 60 us
  waiting for transfers between devices  27.6 us (46%)
  starting transfers between devices  18 us (30%)
  Pallas kernels  14 us (23%)
    pallas_call x8, Pallas kernels, call(): pl.pallas_call(kernel, out_shape=[jax.ShapeDtypeStruct(shape, dtype) for...  10.3 us
    ppermute x4, waiting for transfers between devices, swap_chips(): return lax.ppermute(value, 'tensor', [(0, 2), (2, 0), (1, 3), (3, 1)])  10.3 us
    ppermute x6, waiting for transfers between devices, trade(): return lax.ppermute(value, 'frame', pairs)  6.92 us
    ppermute x6, starting transfers between devices, trade(): return lax.ppermute(value, 'frame', pairs)  6.85 us
    ppermute x2, waiting for transfers between devices, swap_groups(): return lax.ppermute(value, 'groups', [(0, 1), (1, 0)])  5.87 us
    ppermute x4, starting transfers between devices, swap_chips(): return lax.ppermute(value, 'tensor', [(0, 2), (2, 0), (1, 3), (3, 1)])  5.74 us
    ppermute x1, waiting for transfers between devices, trade_by_core(): return lax.ppermute(value, ('frame', 'tensor'), pairs)  2.43 us
    pallas_call x2, Pallas kernels, pack(): pl.pallas_call(kernel, out_shape=[jax.ShapeDtypeStruct(shape, bf16) for s...  2.18 us
  transfers between devices with their start and end apart: 21, of which 12 were waited for; matrix products, arithmetic and copies ran while one was open for 0% of the time, Pallas kernels for 21%

profile of v6, /device:TPU:0, one launch (start us, length us, event | category | flops | bytes accessed | tf_op | source)
XLA Modules:
  0.0 60.0 jit_solution(15176315063997579219)
XLA Ops:
  0.0 0.5 collective-permute-start.3
  0.5 0.1 collective-permute-start.9
  0.6 1.2 %shard_map.96 = bf16[1280,256]{1,0:T(8,128)(2,1)S(1)} custom-call(bf16[3,1024,256]{2,1,0:T(8,128)(2,1)} %bitcast.12, bf16[256,1024]{1,0:T(8,128)(2,1)} %out_ref.3), custom_call_target="tpu_custom_call" | custom-call | bytes 1048576 | tf_op jit(solution)/shard_map/pallas_call | solution.py:488
  1.8 0.0 copy-start.8
  1.8 0.0 copy-start.4
  1.8 0.0 copy-start.6
  1.8 3.0 %collective-permute-start.12 = (bf16[1280,256]{1,0:T(8,128)(2,1)S(1)}, bf16[1280,256]{1,0:T(8,128)(2,1)S(1)}, u32[]{:S(2)}, u32[]{:S(2)}) collective-permute-start(bf16[1280,256]{1,0:T(8,128)(2,1)S(1)} %shard_map.96), channel_id=1, source_target_pairs={{0,2},{2,0},{1,3},{3,1},{4,6},{6,4},{5,7},{7,5},{8,10},{10,8},{9,1... | collective-permute-start | bytes 1966088 | tf_op jit(solution)/shard_map/ppermute | solution.py:551
  4.8 0.9 %shard_map.91 = (f32[6,1280]{1,0:T(8,128)S(1)}, f32[6,256]{1,0:T(8,128)S(1)}) custom-call(bf16[6,128,1024]{2,1,0:T(8,128)(2,1)S(1)} %copy-done.1), custom_call_target="tpu_custom_call" | custom-call | tf_op jit(solution)/shard_map/pallas_call | solution.py:535
  5.8 1.6 %collective-permute-start = (f32[6,1280]{1,0:T(8,128)S(1)}, f32[6,1280]{1,0:T(8,128)S(1)}, u32[]{:S(2)}, u32[]{:S(2)}) collective-permute-start(f32[6,1280]{1,0:T(8,128)S(1)} %get-tuple-element.18), channel_id=1, source_target_pairs={{0,4},{4,0},{8,12},{12,8},{1,13},{13,1},{5,9},{9,5},{2,6},{6,2},{1... | collective-permute-start | bytes 92168 | tf_op jit(solution)/shard_map/ppermute | solution.py:574
  7.4 2.4 %collective-permute-done.got_ref = f32[6,1280]{1,0:T(8,128)S(1)} collective-permute-done((f32[6,1280]{1,0:T(8,128)S(1)}, f32[6,1280]{1,0:T(8,128)S(1)}, u32[]{:S(2)}, u32[]{:S(2)}) %collective-permute-start) | collective-permute-done | bytes 30752 | tf_op jit(solution)/shard_map/ppermute | solution.py:574
  9.8 0.5 collective-permute-start.1
  10.3 0.0 collective-permute-start.4
  10.3 1.1 %collective-permute-done.4 = f32[256]{0:T(256)S(1)} collective-permute-done((f32[256]{0:T(256)S(1)}, f32[256]{0:T(256)S(1)}, u32[]{:S(2)}, u32[]{:S(2)}) %collective-permute-start.4) | collective-permute-done | bytes 1056 | tf_op jit(solution)/shard_map/ppermute | solution.py:547
  11.5 2.3 %collective-permute-start.2 = (f32[6,256]{1,0:T(8,128)S(1)}, f32[6,256]{1,0:T(8,128)S(1)}, u32[]{:S(2)}, u32[]{:S(2)}) collective-permute-start(f32[6,256]{1,0:T(8,128)S(1)} %get-tuple-element.19.own_ref), channel_id=1, source_target_pairs={{0,8},{8,0},{4,12},{12,4},{1,9},{9,1},{5,13},{13,5},{2,10},{10,2},... | collective-permute-start | bytes 18440 | tf_op jit(solution)/shard_map/ppermute | solution.py:564
  13.7 1.0 %shard_map.97 = bf16[512,256]{1,0:T(8,128)(2,1)S(1)} custom-call(bf16[3,1024,256]{2,1,0:T(8,128)(2,1)} %bitcast.13), custom_call_target="tpu_custom_call" | custom-call | bytes 1048576 | tf_op jit(solution)/shard_map/pallas_call | solution.py:488
  14.7 1.3 %collective-permute-done.2.far_ref = f32[6,256]{1,0:T(8,128)S(1)} collective-permute-done((f32[6,256]{1,0:T(8,128)S(1)}, f32[6,256]{1,0:T(8,128)S(1)}, u32[]{:S(2)}, u32[]{:S(2)}) %collective-permute-start.2) | collective-permute-done | bytes 6176 | tf_op jit(solution)/shard_map/ppermute | solution.py:564
  16.0 0.6 %collective-permute-start.15 = (bf16[512,256]{1,0:T(8,128)(2,1)S(1)}, bf16[512,256]{1,0:T(8,128)(2,1)S(1)}, u32[]{:S(2)}, u32[]{:S(2)}) collective-permute-start(bf16[512,256]{1,0:T(8,128)(2,1)S(1)} %shard_map.97), channel_id=1, source_target_pairs={{0,2},{2,0},{1,3},{3,1},{4,6},{6,4},{5,7},{7,5},{8,10},{10,8},{9,1... | collective-permute-start | bytes 786440 | tf_op jit(solution)/shard_map/ppermute | solution.py:551
  16.7 2.5 %shard_map.92 = (f32[3,128,512]{2,1,0:T(8,128)S(1)}, f32[3,768]{1,0:T(4,128)S(1)}, f32[3,768]{1,0:T(4,128)S(1)}, f32[3,256]{1,0:T(4,128)S(1)}) custom-call(bf16[6,128,1024]{2,1,0:T(8,128)(2,1)S(1)} %copy-done.1, f32[6,1280]{1,0:T(8,128)S(1)} %collective-permute-done.got_ref, f32[6,1280]{1,0:T(8,128)S(1)} %collective-permute-done.1.swapped_ref, ...), custom_call_target="tpu_custom_call" | custom-call | flops 1207959552 | tf_op jit(solution)/shard_map/pallas_call | solution.py:535
  19.2 2.3 %collective-permute-start.7 = (f32[3,256]{1,0:T(4,128)S(1)}, f32[3,256]{1,0:T(4,128)S(1)}, u32[]{:S(2)}, u32[]{:S(2)}) collective-permute-start(f32[3,256]{1,0:T(4,128)S(1)} %get-tuple-element.23.own_ref), channel_id=1, source_target_pairs={{0,8},{8,0},{4,12},{12,4},{1,9},{9,1},{5,13},{13,5},{2,10},{10,2},... | collective-permute-start | bytes 9224 | tf_op jit(solution)/shard_map/ppermute | solution.py:564
  21.5 1.8 %collective-permute-start.5 = (f32[3,768]{1,0:T(4,128)S(1)}, f32[3,768]{1,0:T(4,128)S(1)}, u32[]{:S(2)}, u32[]{:S(2)}) collective-permute-start(f32[3,768]{1,0:T(4,128)S(1)} %get-tuple-element.21), channel_id=1, source_target_pairs={{0,4},{4,0},{8,12},{12,8},{1,5},{5,1},{9,13},{13,9},{2,6},{6,2},{1... | collective-permute-start | bytes 27656 | tf_op jit(solution)/shard_map/ppermute | solution.py:564
  23.3 0.3 collective-permute-start.6
  23.6 0.1 collective-permute-done.7.far_ref
  23.7 1.5 %collective-permute-done.5.one_ref = f32[3,768]{1,0:T(4,128)S(1)} collective-permute-done((f32[3,768]{1,0:T(4,128)S(1)}, f32[3,768]{1,0:T(4,128)S(1)}, u32[]{:S(2)}, u32[]{:S(2)}) %collective-permute-start.5) | collective-permute-done | bytes 9248 | tf_op jit(solution)/shard_map/ppermute | solution.py:564
  25.2 3.6 %collective-permute-done.6.two_ref = f32[3,768]{1,0:T(4,128)S(1)} collective-permute-done((f32[3,768]{1,0:T(4,128)S(1)}, f32[3,768]{1,0:T(4,128)S(1)}, u32[]{:S(2)}, u32[]{:S(2)}) %collective-permute-start.6) | collective-permute-done | bytes 9248 | tf_op jit(solution)/shard_map/ppermute | solution.py:564
  28.8 1.1 %shard_map.94 = bf16[192,1024]{1,0:T(8,128)(2,1)S(1)} custom-call(f32[3,128,512]{2,1,0:T(8,128)S(1)} %get-tuple-element.20.hid_ref, f32[3,768]{1,0:T(4,128)S(1)} %collective-permute-done.5.one_ref, f32[3,768]{1,0:T(4,128)S(1)} %collective-permute-done.6.two_ref, f32[3,256]{1,0:T(4,128)S(1)} %collective-permute-done.7.far_ref, ...), custom_call_target="tpu_custom_call" | custom-call | flops 603979776 | tf_op jit(solution)/shard_map/pallas_call | solution.py:535
  29.9 1.6 %collective-permute-start.10 = (bf16[192,1024]{1,0:T(8,128)(2,1)S(1)}, bf16[192,1024]{1,0:T(8,128)(2,1)S(1)}, u32[]{:S(2)}, u32[]{:S(2)}) collective-permute-start(bf16[192,1024]{1,0:T(8,128)(2,1)S(1)} %shard_map.94), channel_id=1, source_target_pairs={{0,2},{2,0},{1,3},{3,1},{4,6},{6,4},{5,7},{7,5},{8,10},{10,8},{9,1... | collective-permute-start | bytes 1179656 | tf_op jit(solution)/shard_map/ppermute | solution.py:551
  31.5 1.6 %collective-permute-start.13 = (bf16[768,256]{1,0:T(8,128)(2,1)S(1)}, bf16[768,256]{1,0:T(8,128)(2,1)S(1)}, u32[]{:S(2)}, u32[]{:S(2)}) collective-permute-start(bf16[768,256]{1,0:T(8,128)(2,1)S(1)} %slice.17.first_x_ref), channel_id=1, source_target_pairs={{0,16},{16,0},{1,17},{17,1},{2,18},{18,2},{3,19},{19,3},{4,20},{20... | collective-permute-start | bytes 1179656 | tf_op jit(solution)/shard_map/ppermute | solution.py:555
  33.1 0.5 collective-permute-start.16
  33.6 0.1 collective-permute-start.14
  33.7 1.0 %shard_map.93.keep_ref = f32[192,1024]{1,0:T(8,128)S(1)} custom-call(f32[3,128,512]{2,1,0:T(8,128)S(1)} %get-tuple-element.20.hid_ref, f32[3,768]{1,0:T(4,128)S(1)} %collective-permute-done.5.one_ref, f32[3,768]{1,0:T(4,128)S(1)} %collective-permute-done.6.two_ref, f32[3,256]{1,0:T(4,128)S(1)} %collective-permute-done.7.far_ref, ...), custom_call_target="tpu_custom_call" | custom-call | flops 603979776 | tf_op jit(solution)/shard_map/pallas_call | solution.py:535
  34.8 0.0 copy-start
  34.8 4.6 %collective-permute-done.10.far_ref = bf16[192,1024]{1,0:T(8,128)(2,1)S(1)} collective-permute-done((bf16[192,1024]{1,0:T(8,128)(2,1)S(1)}, bf16[192,1024]{1,0:T(8,128)(2,1)S(1)}, u32[]{:S(2)}, u32[]{:S(2)}) %collective-permute-start.10) | collective-permute-done | bytes 393248 | tf_op jit(solution)/shard_map/ppermute | solution.py:551
  39.4 0.1 shard_map.95.mine_ref
  39.6 0.1 collective-permute-start.11
  39.7 3.9 %collective-permute-done.13.first_y_ref = bf16[768,256]{1,0:T(8,128)(2,1)S(1)} collective-permute-done((bf16[768,256]{1,0:T(8,128)(2,1)S(1)}, bf16[768,256]{1,0:T(8,128)(2,1)S(1)}, u32[]{:S(2)}, u32[]{:S(2)}) %collective-permute-start.13) | collective-permute-done | bytes 393248 | tf_op jit(solution)/shard_map/ppermute | solution.py:555
  43.6 0.1 collective-permute-start.17
  43.7 0.7 %shard_map.98 = (f32[192,512]{1,0:T(8,128)S(1)}, f32[192,512]{1,0:T(8,128)S(1)}, bf16[192,1024]{1,0:T(8,128)(2,1)S(1)}) custom-call(bf16[192,1024]{1,0:T(8,128)(2,1)S(1)} %shard_map.95.mine_ref, f32[1,1024]{1,0:T(1,128)S(1)} %bitcast.22, bf16[3,1024,256]{2,1,0:T(8,128)(2,1)S(1)} %bitcast.14, bf16[768,256]{1,0:T(8,128)(2,1)S(1)} %slice.17.first_x_ref, ...), custom_call_target="tpu_custom_call" | custom-call | flops 402653184 | tf_op jit(solution)/shard_map/pallas_call | solution.py:535
  44.4 2.0 %collective-permute-done.16.v_y_ref = bf16[512,256]{1,0:T(8,128)(2,1)S(1)} collective-permute-done((bf16[512,256]{1,0:T(8,128)(2,1)S(1)}, bf16[512,256]{1,0:T(8,128)(2,1)S(1)}, u32[]{:S(2)}, u32[]{:S(2)}) %collective-permute-start.16) | collective-permute-done | bytes 262176 | tf_op jit(solution)/shard_map/ppermute | solution.py:555
  46.4 3.3 %shard_map.99.context_ref = bf16[384,512]{1,0:T(8,128)(2,1)S(1)} custom-call(bf16[192,1024]{1,0:T(8,128)(2,1)S(1)} %collective-permute-done.11.theirs_ref, f32[1,1024]{1,0:T(1,128)S(1)} %bitcast.23, bf16[3,1024,256]{2,1,0:T(8,128)(2,1)S(1)} %bitcast.15, bf16[768,256]{1,0:T(8,128)(2,1)S(1)} %slice.17.first_x_ref, ...), custom_call_target="tpu_custom_call" | custom-call | flops 1207959552 | tf_op jit(solution)/shard_map/pallas_call | solution.py:535
  49.6 0.4 collective-permute-done.17.out_z_ref
  50.1 0.6 %shard_map.100 = (bf16[384,256]{1,0:T(8,128)(2,1)S(1)}, f32[384,256]{1,0:T(8,128)S(1)}, bf16[384,256]{1,0:T(8,128)(2,1)S(1)}, f32[384,256]{1,0:T(8,128)S(1)}) custom-call(bf16[384,512]{1,0:T(8,128)(2,1)S(1)} %shard_map.99.context_ref, bf16[192,1024]{1,0:T(8,128)(2,1)S(1)} %shard_map.95.mine_ref, bf16[192,1024]{1,0:T(8,128)(2,1)S(1)} %collective-permute-done.11.theirs_ref, ...), custom_call_target="tpu_custom_call" | custom-call | flops 402653184 | tf_op jit(solution)/shard_map/pallas_call | solution.py:535
  50.7 0.1 collective-permute-start.18
  50.8 0.5 collective-permute-start.20
  51.3 0.9 %collective-permute-done.18 = bf16[384,256]{1,0:T(8,128)(2,1)S(1)} collective-permute-done((bf16[384,256]{1,0:T(8,128)(2,1)S(1)}, bf16[384,256]{1,0:T(8,128)(2,1)S(1)}, u32[]{:S(2)}, u32[]{:S(2)}) %collective-permute-start.18) | collective-permute-done | bytes 196640 | tf_op jit(solution)/shard_map/ppermute | solution.py:547
  52.3 0.6 collective-permute-start.19
  52.9 0.8 %place_near.1.near_ref = bf16[6,128,256]{2,1,0:T(8,128)(2,1)} custom-call(f32[384,256]{1,0:T(8,128)S(1)} %get-tuple-element.29.keep_ref, bf16[384,256]{1,0:T(8,128)(2,1)S(1)} %collective-permute-done.20.got_ref), custom_call_target="tpu_custom_call" | custom-call | tf_op jit(solution)/shard_map/place_near/pallas_call | solution.py:675
  53.6 5.6 %collective-permute-done.19.value_ref = bf16[384,256]{1,0:T(8,128)(2,1)S(1)} collective-permute-done((bf16[384,256]{1,0:T(8,128)(2,1)S(1)}, bf16[384,256]{1,0:T(8,128)(2,1)S(1)}, u32[]{:S(2)}, u32[]{:S(2)}) %collective-permute-start.19) | collective-permute-done | bytes 196640 | tf_op jit(solution)/shard_map/ppermute | solution.py:551
  59.3 0.7 %place_far.1 = bf16[6,128,256]{2,1,0:T(8,128)(2,1)} custom-call(bf16[384,256]{1,0:T(8,128)(2,1)S(1)} %collective-permute-done.19.value_ref, bf16[6,128,256]{2,1,0:T(8,128)(2,1)} %place_near.1.near_ref), custom_call_target="tpu_custom_call", output_to_operand_aliasing={{}: (1, {})} | custom-call | tf_op jit(solution)/shard_map/place_far/pallas_call | solution.py:680
  (31 shorter events, 0.2 us)
Async XLA Ops:
  0.0 4.8 %copy-start.1 = (bf16[6,128,1024]{2,1,0:T(8,128)(2,1)S(1)}, bf16[6,128,1024]{2,1,0:T(8,128)(2,1)}, u32[]{:S(2)}) copy-start(bf16[6,128,1024]{2,1,0:T(8,128)(2,1)} %latent_ref.1) | copy-start | bytes 4718596
  0.0 16.6 %collective-permute-start.3 = (bf16[3,1024,256]{2,1,0:T(8,128)(2,1)}, bf16[3,1024,256]{2,1,0:T(8,128)(2,1)S(1)}, u32[]{:S(2)}, u32[]{:S(2)}) collective-permute-start(bf16[3,1024,256]{2,1,0:T(8,128)(2,1)} %weight_ref.1), channel_id=1, source_target_pairs={{0,1},{1,0},{2,3},{3,2},{4,5},{5,4},{6,7},{7,6},{8,9},{9,8},{10,11... | collective-permute-start | bytes 4718600 | tf_op jit(solution)/shard_map/ppermute | solution.py:547
  0.5 22.8 %collective-permute-start.9 = (bf16[3,256,1024]{2,1,0:T(8,128)(2,1)}, bf16[3,256,1024]{2,1,0:T(8,128)(2,1)S(1)}, u32[]{:S(2)}, u32[]{:S(2)}) collective-permute-start(bf16[3,256,1024]{2,1,0:T(8,128)(2,1)} %param.14), channel_id=1, source_target_pairs={{0,1},{1,0},{2,3},{3,2},{4,5},{5,4},{6,7},{7,6},{8,9},{9,8},{10,11... | collective-permute-start | bytes 4718600 | tf_op jit(solution)/shard_map/ppermute | solution.py:547
  0.6 9.8 %copy-start.7 = (f32[256]{0:T(256)S(1)}, f32[256]{0:T(256)}, u32[]{:S(2)}) copy-start(f32[256]{0:T(256)} %param.12) | copy-start | bytes 3076
  1.8 14.3 %copy-start.8 = (f32[256]{0:T(256)S(1)}, f32[256]{0:T(256)}, u32[]{:S(2)}) copy-start(f32[256]{0:T(256)} %param.13) | copy-start | bytes 3076
  1.8 14.9 %copy-start.4 = (bf16[3,1024,256]{2,1,0:T(8,128)(2,1)S(1)}, bf16[3,1024,256]{2,1,0:T(8,128)(2,1)}, u32[]{:S(2)}) copy-start(bf16[3,1024,256]{2,1,0:T(8,128)(2,1)} %weight_ref.1) | copy-start | bytes 4718596
  1.8 14.9 %copy-start.6 = (f32[1024]{0:T(1024)S(1)}, f32[1024]{0:T(1024)}, u32[]{:S(2)}) copy-start(f32[1024]{0:T(1024)} %param.10) | copy-start | bytes 12292
  1.8 29.7 %collective-permute-start.12 = (bf16[1280,256]{1,0:T(8,128)(2,1)S(1)}, bf16[1280,256]{1,0:T(8,128)(2,1)S(1)}, u32[]{:S(2)}, u32[]{:S(2)}) collective-permute-start(bf16[1280,256]{1,0:T(8,128)(2,1)S(1)} %shard_map.96), channel_id=1, source_target_pairs={{0,2},{2,0},{1,3},{3,1},{4,6},{6,4},{5,7},{7,5},{8,10},{10,8},{9,1... | collective-permute-start | bytes 1966088 | tf_op jit(solution)/shard_map/ppermute | solution.py:551
  5.8 4.1 %collective-permute-start = (f32[6,1280]{1,0:T(8,128)S(1)}, f32[6,1280]{1,0:T(8,128)S(1)}, u32[]{:S(2)}, u32[]{:S(2)}) collective-permute-start(f32[6,1280]{1,0:T(8,128)S(1)} %get-tuple-element.18), channel_id=1, source_target_pairs={{0,4},{4,0},{8,12},{12,8},{1,13},{13,1},{5,9},{9,5},{2,6},{6,2},{1... | collective-permute-start | bytes 92168 | tf_op jit(solution)/shard_map/ppermute | solution.py:574
  9.8 6.2 %collective-permute-start.1 = (f32[6,1280]{1,0:T(8,128)S(1)}, f32[6,1280]{1,0:T(8,128)S(1)}, u32[]{:S(2)}, u32[]{:S(2)}) collective-permute-start(f32[6,1280]{1,0:T(8,128)S(1)} %collective-permute-done.got_ref), channel_id=1, source_target_pairs={{0,1},{1,0},{2,3},{3,2},{4,5},{5,4},{6,7},{7,6},{8,9},{9,8},{10,11... | collective-permute-start | bytes 92168 | tf_op jit(solution)/shard_map/ppermute | solution.py:547
  10.3 1.2 %collective-permute-start.4 = (f32[256]{0:T(256)S(1)}, f32[256]{0:T(256)S(1)}, u32[]{:S(2)}, u32[]{:S(2)}) collective-permute-start(f32[256]{0:T(256)S(1)} %copy-done.7), channel_id=1, source_target_pairs={{0,1},{1,0},{2,3},{3,2},{4,5},{5,4},{6,7},{7,6},{8,9},{9,8},{10,11... | collective-permute-start | bytes 3080 | tf_op jit(solution)/shard_map/ppermute | solution.py:547
  11.5 4.5 %collective-permute-start.2 = (f32[6,256]{1,0:T(8,128)S(1)}, f32[6,256]{1,0:T(8,128)S(1)}, u32[]{:S(2)}, u32[]{:S(2)}) collective-permute-start(f32[6,256]{1,0:T(8,128)S(1)} %get-tuple-element.19.own_ref), channel_id=1, source_target_pairs={{0,8},{8,0},{4,12},{12,4},{1,9},{9,1},{5,13},{13,5},{2,10},{10,2},... | collective-permute-start | bytes 18440 | tf_op jit(solution)/shard_map/ppermute | solution.py:564
  16.0 5.5 %collective-permute-start.8 = (f32[256]{0:T(256)S(1)}, f32[256]{0:T(256)S(1)}, u32[]{:S(2)}, u32[]{:S(2)}) collective-permute-start(f32[256]{0:T(256)S(1)} %copy-done.8), channel_id=1, source_target_pairs={{0,1},{1,0},{2,3},{3,2},{4,5},{5,4},{6,7},{7,6},{8,9},{9,8},{10,11... | collective-permute-start | bytes 3080 | tf_op jit(solution)/shard_map/ppermute | solution.py:547
  16.0 17.1 %collective-permute-start.15 = (bf16[512,256]{1,0:T(8,128)(2,1)S(1)}, bf16[512,256]{1,0:T(8,128)(2,1)S(1)}, u32[]{:S(2)}, u32[]{:S(2)}) collective-permute-start(bf16[512,256]{1,0:T(8,128)(2,1)S(1)} %shard_map.97), channel_id=1, source_target_pairs={{0,2},{2,0},{1,3},{3,1},{4,6},{6,4},{5,7},{7,5},{8,10},{10,8},{9,1... | collective-permute-start | bytes 786440 | tf_op jit(solution)/shard_map/ppermute | solution.py:551
  16.7 12.2 %copy-start.2 = (bf16[3,256,1024]{2,1,0:T(8,128)(2,1)S(1)}, bf16[3,256,1024]{2,1,0:T(8,128)(2,1)}, u32[]{:S(2)}) copy-start(bf16[3,256,1024]{2,1,0:T(8,128)(2,1)} %param.14) | copy-start | bytes 4718596
  19.2 4.6 %collective-permute-start.7 = (f32[3,256]{1,0:T(4,128)S(1)}, f32[3,256]{1,0:T(4,128)S(1)}, u32[]{:S(2)}, u32[]{:S(2)}) collective-permute-start(f32[3,256]{1,0:T(4,128)S(1)} %get-tuple-element.23.own_ref), channel_id=1, source_target_pairs={{0,8},{8,0},{4,12},{12,4},{1,9},{9,1},{5,13},{13,5},{2,10},{10,2},... | collective-permute-start | bytes 9224 | tf_op jit(solution)/shard_map/ppermute | solution.py:564
  21.5 3.7 %collective-permute-start.5 = (f32[3,768]{1,0:T(4,128)S(1)}, f32[3,768]{1,0:T(4,128)S(1)}, u32[]{:S(2)}, u32[]{:S(2)}) collective-permute-start(f32[3,768]{1,0:T(4,128)S(1)} %get-tuple-element.21), channel_id=1, source_target_pairs={{0,4},{4,0},{8,12},{12,8},{1,5},{5,1},{9,13},{13,9},{2,6},{6,2},{1... | collective-permute-start | bytes 27656 | tf_op jit(solution)/shard_map/ppermute | solution.py:564
  23.3 5.5 %collective-permute-start.6 = (f32[3,768]{1,0:T(4,128)S(1)}, f32[3,768]{1,0:T(4,128)S(1)}, u32[]{:S(2)}, u32[]{:S(2)}) collective-permute-start(f32[3,768]{1,0:T(4,128)S(1)} %get-tuple-element.22), channel_id=1, source_target_pairs={{0,12},{12,0},{4,8},{8,4},{1,13},{13,1},{5,9},{9,5},{2,14},{14,2},... | collective-permute-start | bytes 27656 | tf_op jit(solution)/shard_map/ppermute | solution.py:564
  29.9 9.5 %collective-permute-start.10 = (bf16[192,1024]{1,0:T(8,128)(2,1)S(1)}, bf16[192,1024]{1,0:T(8,128)(2,1)S(1)}, u32[]{:S(2)}, u32[]{:S(2)}) collective-permute-start(bf16[192,1024]{1,0:T(8,128)(2,1)S(1)} %shard_map.94), channel_id=1, source_target_pairs={{0,2},{2,0},{1,3},{3,1},{4,6},{6,4},{5,7},{7,5},{8,10},{10,8},{9,1... | collective-permute-start | bytes 1179656 | tf_op jit(solution)/shard_map/ppermute | solution.py:551
  31.5 12.0 %collective-permute-start.13 = (bf16[768,256]{1,0:T(8,128)(2,1)S(1)}, bf16[768,256]{1,0:T(8,128)(2,1)S(1)}, u32[]{:S(2)}, u32[]{:S(2)}) collective-permute-start(bf16[768,256]{1,0:T(8,128)(2,1)S(1)} %slice.17.first_x_ref), channel_id=1, source_target_pairs={{0,16},{16,0},{1,17},{17,1},{2,18},{18,2},{3,19},{19,3},{4,20},{20... | collective-permute-start | bytes 1179656 | tf_op jit(solution)/shard_map/ppermute | solution.py:555
  33.1 13.3 %collective-permute-start.16 = (bf16[512,256]{1,0:T(8,128)(2,1)S(1)}, bf16[512,256]{1,0:T(8,128)(2,1)S(1)}, u32[]{:S(2)}, u32[]{:S(2)}) collective-permute-start(bf16[512,256]{1,0:T(8,128)(2,1)S(1)} %collective-permute-done.15.v_x_ref), channel_id=1, source_target_pairs={{0,16},{16,0},{1,17},{17,1},{2,18},{18,2},{3,19},{19,3},{4,20},{20... | collective-permute-start | bytes 786440 | tf_op jit(solution)/shard_map/ppermute | solution.py:555
  33.6 10.1 %collective-permute-start.14 = (bf16[512,256]{1,0:T(8,128)(2,1)S(1)}, bf16[512,256]{1,0:T(8,128)(2,1)S(1)}, u32[]{:S(2)}, u32[]{:S(2)}) collective-permute-start(bf16[512,256]{1,0:T(8,128)(2,1)S(1)} %slice.18.q_x_ref), channel_id=1, source_target_pairs={{0,4},{4,0},{8,12},{12,8},{1,5},{5,1},{9,13},{13,9},{2,6},{6,2},{1... | collective-permute-start | bytes 786440 | tf_op jit(solution)/shard_map/ppermute | solution.py:564
  34.8 8.9 %copy-start = (bf16[1024,3,256]{2,0,1:T(8,128)(2,1)S(1)}, bf16[1024,3,256]{2,0,1:T(8,128)(2,1)}, u32[]{:S(2)}) copy-start(bf16[1024,3,256]{2,0,1:T(8,128)(2,1)} %param.16) | copy-start | bytes 4718596
  34.8 8.9 %copy-start.5 = (f32[1024]{0:T(1024)S(1)}, f32[1024]{0:T(1024)}, u32[]{:S(2)}) copy-start(f32[1024]{0:T(1024)} %param.15) | copy-start | bytes 12292
  39.6 6.8 %collective-permute-start.11 = (bf16[192,1024]{1,0:T(8,128)(2,1)S(1)}, bf16[192,1024]{1,0:T(8,128)(2,1)S(1)}, u32[]{:S(2)}, u32[]{:S(2)}) collective-permute-start(bf16[192,1024]{1,0:T(8,128)(2,1)S(1)} %shard_map.95.mine_ref), channel_id=1, source_target_pairs={{0,1},{1,0},{2,3},{3,2},{4,5},{5,4},{6,7},{7,6},{8,9},{9,8},{10,11... | collective-permute-start | bytes 1179656 | tf_op jit(solution)/shard_map/ppermute | solution.py:547
  43.6 6.4 %collective-permute-start.17 = (bf16[2,256,256]{2,1,0:T(8,128)(2,1)S(1)}, bf16[2,256,256]{2,1,0:T(8,128)(2,1)S(1)}, u32[]{:S(2)}, u32[]{:S(2)}) collective-permute-start(bf16[2,256,256]{2,1,0:T(8,128)(2,1)S(1)} %pad_maximum_fusion), channel_id=1, source_target_pairs={{0,4},{4,0},{8,12},{12,8},{1,5},{5,1},{9,13},{13,9},{2,6},{6,2},{1... | collective-permute-start | bytes 786440 | tf_op jit(solution)/shard_map/ppermute | solution.py:564
  46.4 3.7 %copy-start.3 = (bf16[256,1024]{1,0:T(8,128)(2,1)S(1)}, bf16[256,1024]{1,0:T(8,128)(2,1)}, u32[]{:S(2)}) copy-start(bf16[256,1024]{1,0:T(8,128)(2,1)} %out_ref.3) | copy-start | bytes 1572868
  50.7 1.5 %collective-permute-start.18 = (bf16[384,256]{1,0:T(8,128)(2,1)S(1)}, bf16[384,256]{1,0:T(8,128)(2,1)S(1)}, u32[]{:S(2)}, u32[]{:S(2)}) collective-permute-start(bf16[384,256]{1,0:T(8,128)(2,1)S(1)} %get-tuple-element.28), channel_id=1, source_target_pairs={{0,1},{1,0},{2,3},{3,2},{4,5},{5,4},{6,7},{7,6},{8,9},{9,8},{10,11... | collective-permute-start | bytes 589832 | tf_op jit(solution)/shard_map/ppermute | solution.py:547
  50.8 2.1 %collective-permute-start.20 = (bf16[384,256]{1,0:T(8,128)(2,1)S(1)}, bf16[384,256]{1,0:T(8,128)(2,1)S(1)}, u32[]{:S(2)}, u32[]{:S(2)}) collective-permute-start(bf16[384,256]{1,0:T(8,128)(2,1)S(1)} %get-tuple-element.30), channel_id=1, source_target_pairs={{0,1},{1,0},{2,3},{3,2},{4,5},{5,4},{6,7},{7,6},{8,9},{9,8},{10,11... | collective-permute-start | bytes 589832 | tf_op jit(solution)/shard_map/ppermute | solution.py:547
  52.3 7.0 %collective-permute-start.19 = (bf16[384,256]{1,0:T(8,128)(2,1)S(1)}, bf16[384,256]{1,0:T(8,128)(2,1)S(1)}, u32[]{:S(2)}, u32[]{:S(2)}) collective-permute-start(bf16[384,256]{1,0:T(8,128)(2,1)S(1)} %add_convert_fusion), channel_id=1, source_target_pairs={{0,2},{2,0},{1,3},{3,1},{4,6},{6,4},{5,7},{7,5},{8,10},{10,8},{9,1... | collective-permute-start | bytes 589832 | tf_op jit(solution)/shard_map/ppermute | solution.py:551

commit v7 on v6

--- a/solution.py
+++ b/solution.py
@@ -9,6 +9,7 @@
 from jax.sharding import PartitionSpec as P
 
 
+TENSOR, FRAME, SONGS = "tensor", "frame", "groups"
 GROUPS = 32
 HEAD_DIM = 64
 WINDOW = 64
@@ -106,30 +107,30 @@
     out_weight,
 ):
     stem_count, frame_count, channels = latent.shape
-    tensor_size = lax.axis_size("tensor")
+    tensor_size = lax.axis_size(TENSOR)
     shard_width = channels // tensor_size
     row_count = stem_count * frame_count
-    group_entries = frame_count * lax.axis_size("frame") * (channels // GROUPS)
+    group_entries = frame_count * lax.axis_size(FRAME) * (channels // GROUPS)
     latent_f = latent.astype(jnp.float32)
     sums_one, squares_one = group_sums(latent_f, GROUPS)
-    sums_one, squares_one = lax.psum((sums_one, squares_one), "frame")
+    sums_one, squares_one = lax.psum((sums_one, squares_one), FRAME)
     act_one = jax.nn.silu(
         apply_group(latent_f, sums_one, squares_one, group_entries, norm1_gain)
     ).astype(jnp.bfloat16)
-    padded_one = extended(act_one, (("frame", 1),), 1)
+    padded_one = extended(act_one, ((FRAME, 1),), 1)
     hid_one = conv_padded(padded_one, conv1_weight, frame_count)
     hid_one = hid_one + time_bias
     local_groups = GROUPS // tensor_size
     sums_two, squares_two = group_sums(hid_one, local_groups)
-    sums_two, squares_two = lax.psum((sums_two, squares_two), "frame")
+    sums_two, squares_two = lax.psum((sums_two, squares_two), FRAME)
     act_two = jax.nn.silu(
         apply_group(hid_one, sums_two, squares_two, group_entries, norm2_gain)
     ).astype(jnp.bfloat16)
-    padded_two = extended(act_two, (("frame", 1),), 1)
+    padded_two = extended(act_two, ((FRAME, 1),), 1)
     conv_term = conv_padded(padded_two, conv2_weight, frame_count)
-    own_start = lax.axis_index("tensor") * shard_width
+    own_start = lax.axis_index(TENSOR) * shard_width
     qkv_flat = qkv_weight.reshape(channels, 3 * shard_width)
-    conv_total = lax.psum(conv_term.astype(jnp.bfloat16), "tensor").astype(jnp.float32)
+    conv_total = lax.psum(conv_term.astype(jnp.bfloat16), TENSOR).astype(jnp.float32)
     residual = (latent_f + conv_total).astype(jnp.bfloat16)
     res_f = residual.astype(jnp.float32)
     mean_sq = jnp.mean(res_f * res_f, axis=2, keepdims=True)
@@ -146,7 +147,7 @@
         stem_count, frame_count, channels
     )
     attn_share = lax.psum_scatter(
-        out_term.astype(jnp.bfloat16), "tensor", scatter_dimension=2, tiled=True
+        out_term.astype(jnp.bfloat16), TENSOR, scatter_dimension=2, tiled=True
     ).astype(jnp.float32)
     velocity = (res_own + attn_share).astype(jnp.bfloat16)
     return velocity
@@ -169,7 +170,7 @@
 
 
 def even_place():
-    return lax.axis_index("frame") % 2 == 0
+    return lax.axis_index(FRAME) % 2 == 0
 
 
 def group_totals(sums, squares, width):
@@ -189,7 +190,7 @@
 
 def stats_kernel(width, lat_ref, near_ref, own_ref, sum_ref, square_ref):
     stems, frames, channels = lat_ref.shape
-    upward = even_place() == (lax.axis_index("tensor") % 2 == 0)
+    upward = even_place() == (lax.axis_index(TENSOR) % 2 == 0)
     for stem in range(stems):
         block = lat_ref[stem].astype(f32)
         sum_ref[stem : stem + 1, :] = jnp.sum(block, axis=0, keepdims=True)
@@ -204,7 +205,7 @@
 
 def pick(value):
     half = value.shape[0] // 2
-    return jnp.where(lax.axis_index("tensor") % 2 == 0, value[:half], value[half:])
+    return jnp.where(lax.axis_index(TENSOR) % 2 == 0, value[:half], value[half:])
 
 
 def both_dots(rows, near, away):
@@ -220,8 +221,8 @@
 ):
     frames, channels = lat_ref.shape[1:]
     stems, _, span = hid_ref.shape
-    place = lax.axis_index("frame")
-    core = lax.axis_index("tensor") % 2
+    place = lax.axis_index(FRAME)
+    core = lax.axis_index(TENSOR) % 2
     centre, scale = channel_scale(
         [own_ref[...], got_ref[:, channels:], swapped_ref[:, channels:], far_ref[...]],
         entries, channels, width,
@@ -275,8 +276,8 @@
 ):
     stems, _, span = hid_ref.shape
     shard = span // 2
-    place = lax.axis_index("frame")
-    chip = lax.axis_index("tensor") // 2
+    place = lax.axis_index(FRAME)
+    chip = lax.axis_index(TENSOR) // 2
     window = 1 - chip if other else chip
     centre, scale = channel_scale(
         [own_ref[...], one_ref[:, span:], two_ref[:, span:], far_ref[...]],
@@ -322,7 +323,7 @@
 
 def projector(normed_ref, qkv_ref, first_x_ref, first_y_ref, q_x_ref, q_z_ref, v_refs=()):
     depth = normed_ref.shape[1] // 2
-    group, parity = lax.axis_index("groups"), lax.axis_index("frame") % 2
+    group, parity = lax.axis_index(SONGS), lax.axis_index(FRAME) % 2
 
     def half(place):
         return normed_ref[:, pl.ds(pl.multiple_of(place * depth, depth), depth)]
@@ -416,10 +417,10 @@
 ):
     rows, channels = mine_ref.shape
     shard = out_ref.shape[0]
-    index = lax.axis_index("tensor")
+    index = lax.axis_index(TENSOR)
     chip, core = index // 2, index % 2
     depth = channels // 2
-    group, parity = lax.axis_index("groups"), lax.axis_index("frame") % 2
+    group, parity = lax.axis_index(SONGS), lax.axis_index(FRAME) % 2
     out_far_ref[2 * group + parity] = first_x_ref[depth:, :]
     out_far_ref[2 * (1 - group) + parity] = first_y_ref[depth:, :]
     out_far_ref[2 * group + 1 - parity] = out_z_ref[0]
@@ -463,7 +464,7 @@
 
 def pack_first_kernel(qkv_ref, out_ref, send_ref, sems):
     depth, shard = qkv_ref.shape[1] // 2, qkv_ref.shape[2]
-    group, parity = lax.axis_index("groups"), lax.axis_index("frame") % 2
+    group, parity = lax.axis_index(SONGS), lax.axis_index(FRAME) % 2
     pairs = []
     for which, place, base in ((1, group, 0), (0, parity, depth + shard)):
         for rows, goal in row_pieces(place, depth):
@@ -479,7 +480,7 @@
 def pack_rest_kernel(qkv_ref, values_ref, sems):
     pairs = [
         (qkv_ref.at[2, rows, :], values_ref.at[goal, :])
-        for rows, goal in row_pieces(lax.axis_index("groups"), values_ref.shape[0])
+        for rows, goal in row_pieces(lax.axis_index(SONGS), values_ref.shape[0])
     ]
     run_copies(pairs, sems)
 
@@ -498,7 +499,7 @@
 
 def residual_kernel(latent_ref, keep_ref, far_ref, out_ref):
     stems = latent_ref.shape[0]
-    index = lax.axis_index("tensor")
+    index = lax.axis_index(TENSOR)
     chip, core = index // 2, index % 2
     start = pl.multiple_of(chip * WINDOW, WINDOW)
     for stem in range(stems // 2):
@@ -510,7 +511,7 @@
 
 def place(value_ref, out_ref, window, sems):
     stems = out_ref.shape[0]
-    core = lax.axis_index("tensor") % 2
+    core = lax.axis_index(TENSOR) % 2
     half = stems // 2
     at = pl.ds(pl.multiple_of(window * WINDOW, WINDOW), WINDOW)
     pairs = []
@@ -523,12 +524,12 @@
 
 def place_near_kernel(keep_ref, got_ref, out_ref, value_ref, sems):
     value_ref[...] = (keep_ref[...] + got_ref[...].astype(f32)).astype(bf16)
-    place(value_ref, out_ref, lax.axis_index("tensor") // 2, sems)
+    place(value_ref, out_ref, lax.axis_index(TENSOR) // 2, sems)
 
 
 def place_far_kernel(value_ref, near_ref, out_ref, sems):
     del near_ref
-    place(value_ref, out_ref, 1 - lax.axis_index("tensor") // 2, sems)
+    place(value_ref, out_ref, 1 - lax.axis_index(TENSOR) // 2, sems)
 
 
 def call(kernel, outs, scratch, args, flops=0, moved=0, limit=16):
@@ -544,15 +545,15 @@
 
 
 def swap_cores(value):
-    return lax.ppermute(value, "tensor", [(0, 1), (1, 0), (2, 3), (3, 2)])
+    return lax.ppermute(value, TENSOR, [(0, 1), (1, 0), (2, 3), (3, 2)])
 
 
 def swap_chips(value):
-    return lax.ppermute(value, "tensor", [(0, 2), (2, 0), (1, 3), (3, 1)])
+    return lax.ppermute(value, TENSOR, [(0, 2), (2, 0), (1, 3), (3, 1)])
 
 
 def swap_groups(value):
-    return lax.ppermute(value, "groups", [(0, 1), (1, 0)])
+    return lax.ppermute(value, SONGS, [(0, 1), (1, 0)])
 
 
 ONE = ((0, 1), (1, 0), (2, 3), (3, 2))
@@ -561,17 +562,17 @@
 
 
 def trade(value, pairs):
-    return lax.ppermute(value, "frame", pairs)
+    return lax.ppermute(value, FRAME, pairs)
 
 
 def trade_by_core(value):
-    count = lax.axis_size("tensor")
+    count = lax.axis_size(TENSOR)
     pairs = [
         (source * count + index, goal * count + index)
         for index in range(count)
         for source, goal in (TWO if index % 2 else ONE)
     ]
-    return lax.ppermute(value, ("frame", "tensor"), pairs)
+    return lax.ppermute(value, (FRAME, TENSOR), pairs)
 
 
 def fast(
@@ -579,7 +580,7 @@
     attn_gain, qkv_weight, out_weight,
 ):
     stems, frames, channels = latent.shape
-    frame_size = lax.axis_size("frame")
+    frame_size = lax.axis_size(FRAME)
     shard = conv1_weight.shape[2]
     width = channels // GROUPS
     entries = frames * frame_size * width
@@ -687,12 +688,12 @@
 def local(*args):
     latent = args[0]
     stems, frames, channels = latent.shape
-    tensor_size, frame_size = lax.axis_size("tensor"), lax.axis_size("frame")
+    tensor_size, frame_size = lax.axis_size(TENSOR), lax.axis_size(FRAME)
     shard = channels // tensor_size
     suits = (
         tensor_size == 4
         and frame_size == 4
-        and lax.axis_size("groups") == 2
+        and lax.axis_size(SONGS) == 2
         and frames == 2 * WINDOW
         and stems % 2 == 0
         and stems <= 8
@@ -708,16 +709,16 @@
         local,
         mesh=mesh,
         in_specs=(
-            P(None, ("groups", "frame"), None),
+            P(None, (SONGS, FRAME), None),
             P(),
-            P(None, None, "tensor"),
-            P("tensor"),
-            P("tensor"),
-            P(None, "tensor", None),
+            P(None, None, TENSOR),
+            P(TENSOR),
+            P(TENSOR),
+            P(None, TENSOR, None),
             P(),
-            P(None, None, "tensor"),
-            P("tensor", None),
+            P(None, None, TENSOR),
+            P(TENSOR, None),
         ),
-        out_specs=P(None, ("groups", "frame"), "tensor"),
+        out_specs=P(None, (SONGS, FRAME), TENSOR),
         check_vma=False,
     )

time: 60.2 us -> 60.2 us (level)
  no operation moved by 1% of the time
where the time goes in v7:
time: 60.2 us; the launch traced here: 60 us
  waiting for transfers between devices  27.6 us (46%)
  starting transfers between devices  18 us (30%)
  Pallas kernels  14 us (23%)
    pallas_call x8, Pallas kernels, call(): pl.pallas_call(kernel, out_shape=[jax.ShapeDtypeStruct(shape, dtype) for...  10.3 us
    ppermute x4, waiting for transfers between devices, swap_chips(): return lax.ppermute(value, TENSOR, [(0, 2), (2, 0), (1, 3), (3, 1)])  10.3 us
    ppermute x6, waiting for transfers between devices, trade(): return lax.ppermute(value, FRAME, pairs)  6.92 us
    ppermute x6, starting transfers between devices, trade(): return lax.ppermute(value, FRAME, pairs)  6.85 us
    ppermute x2, waiting for transfers between devices, swap_groups(): return lax.ppermute(value, SONGS, [(0, 1), (1, 0)])  5.87 us
    ppermute x4, starting transfers between devices, swap_chips(): return lax.ppermute(value, TENSOR, [(0, 2), (2, 0), (1, 3), (3, 1)])  5.74 us
    ppermute x1, waiting for transfers between devices, trade_by_core(): return lax.ppermute(value, (FRAME, TENSOR), pairs)  2.43 us
    pallas_call x2, Pallas kernels, pack(): pl.pallas_call(kernel, out_shape=[jax.ShapeDtypeStruct(shape, bf16) for s...  2.18 us
  transfers between devices with their start and end apart: 21, of which 12 were waited for; matrix products, arithmetic and copies ran while one was open for 0% of the time, Pallas kernels for 21%

profile of v7, /device:TPU:0, one launch (start us, length us, event | category | flops | bytes accessed | tf_op | source)
XLA Modules:
  0.0 60.0 jit_solution(15176315063997579219)
XLA Ops:
  0.0 0.5 collective-permute-start.3
  0.5 0.1 collective-permute-start.9
  0.6 1.2 %shard_map.96 = bf16[1280,256]{1,0:T(8,128)(2,1)S(1)} custom-call(bf16[3,1024,256]{2,1,0:T(8,128)(2,1)} %bitcast.12, bf16[256,1024]{1,0:T(8,128)(2,1)} %out_ref.3), custom_call_target="tpu_custom_call" | custom-call | bytes 1048576 | tf_op jit(solution)/shard_map/pallas_call | solution.py:489
  1.8 0.0 copy-start.8
  1.8 0.0 copy-start.4
  1.8 0.0 copy-start.6
  1.8 3.0 %collective-permute-start.12 = (bf16[1280,256]{1,0:T(8,128)(2,1)S(1)}, bf16[1280,256]{1,0:T(8,128)(2,1)S(1)}, u32[]{:S(2)}, u32[]{:S(2)}) collective-permute-start(bf16[1280,256]{1,0:T(8,128)(2,1)S(1)} %shard_map.96), channel_id=1, source_target_pairs={{0,2},{2,0},{1,3},{3,1},{4,6},{6,4},{5,7},{7,5},{8,10},{10,8},{9,1... | collective-permute-start | bytes 1966088 | tf_op jit(solution)/shard_map/ppermute | solution.py:552
  4.8 0.9 %shard_map.91 = (f32[6,1280]{1,0:T(8,128)S(1)}, f32[6,256]{1,0:T(8,128)S(1)}) custom-call(bf16[6,128,1024]{2,1,0:T(8,128)(2,1)S(1)} %copy-done.1), custom_call_target="tpu_custom_call" | custom-call | tf_op jit(solution)/shard_map/pallas_call | solution.py:536
  5.8 1.6 %collective-permute-start = (f32[6,1280]{1,0:T(8,128)S(1)}, f32[6,1280]{1,0:T(8,128)S(1)}, u32[]{:S(2)}, u32[]{:S(2)}) collective-permute-start(f32[6,1280]{1,0:T(8,128)S(1)} %get-tuple-element.18), channel_id=1, source_target_pairs={{0,4},{4,0},{8,12},{12,8},{1,13},{13,1},{5,9},{9,5},{2,6},{6,2},{1... | collective-permute-start | bytes 92168 | tf_op jit(solution)/shard_map/ppermute | solution.py:575
  7.4 2.4 %collective-permute-done.got_ref = f32[6,1280]{1,0:T(8,128)S(1)} collective-permute-done((f32[6,1280]{1,0:T(8,128)S(1)}, f32[6,1280]{1,0:T(8,128)S(1)}, u32[]{:S(2)}, u32[]{:S(2)}) %collective-permute-start) | collective-permute-done | bytes 30752 | tf_op jit(solution)/shard_map/ppermute | solution.py:575
  9.8 0.5 collective-permute-start.1
  10.3 0.0 collective-permute-start.4
  10.3 1.1 %collective-permute-done.4 = f32[256]{0:T(256)S(1)} collective-permute-done((f32[256]{0:T(256)S(1)}, f32[256]{0:T(256)S(1)}, u32[]{:S(2)}, u32[]{:S(2)}) %collective-permute-start.4) | collective-permute-done | bytes 1056 | tf_op jit(solution)/shard_map/ppermute | solution.py:548
  11.5 2.3 %collective-permute-start.2 = (f32[6,256]{1,0:T(8,128)S(1)}, f32[6,256]{1,0:T(8,128)S(1)}, u32[]{:S(2)}, u32[]{:S(2)}) collective-permute-start(f32[6,256]{1,0:T(8,128)S(1)} %get-tuple-element.19.own_ref), channel_id=1, source_target_pairs={{0,8},{8,0},{4,12},{12,4},{1,9},{9,1},{5,13},{13,5},{2,10},{10,2},... | collective-permute-start | bytes 18440 | tf_op jit(solution)/shard_map/ppermute | solution.py:565
  13.7 1.0 %shard_map.97 = bf16[512,256]{1,0:T(8,128)(2,1)S(1)} custom-call(bf16[3,1024,256]{2,1,0:T(8,128)(2,1)} %bitcast.13), custom_call_target="tpu_custom_call" | custom-call | bytes 1048576 | tf_op jit(solution)/shard_map/pallas_call | solution.py:489
  14.7 1.3 %collective-permute-done.2.far_ref = f32[6,256]{1,0:T(8,128)S(1)} collective-permute-done((f32[6,256]{1,0:T(8,128)S(1)}, f32[6,256]{1,0:T(8,128)S(1)}, u32[]{:S(2)}, u32[]{:S(2)}) %collective-permute-start.2) | collective-permute-done | bytes 6176 | tf_op jit(solution)/shard_map/ppermute | solution.py:565
  16.0 0.6 %collective-permute-start.15 = (bf16[512,256]{1,0:T(8,128)(2,1)S(1)}, bf16[512,256]{1,0:T(8,128)(2,1)S(1)}, u32[]{:S(2)}, u32[]{:S(2)}) collective-permute-start(bf16[512,256]{1,0:T(8,128)(2,1)S(1)} %shard_map.97), channel_id=1, source_target_pairs={{0,2},{2,0},{1,3},{3,1},{4,6},{6,4},{5,7},{7,5},{8,10},{10,8},{9,1... | collective-permute-start | bytes 786440 | tf_op jit(solution)/shard_map/ppermute | solution.py:552
  16.7 2.5 %shard_map.92 = (f32[3,128,512]{2,1,0:T(8,128)S(1)}, f32[3,768]{1,0:T(4,128)S(1)}, f32[3,768]{1,0:T(4,128)S(1)}, f32[3,256]{1,0:T(4,128)S(1)}) custom-call(bf16[6,128,1024]{2,1,0:T(8,128)(2,1)S(1)} %copy-done.1, f32[6,1280]{1,0:T(8,128)S(1)} %collective-permute-done.got_ref, f32[6,1280]{1,0:T(8,128)S(1)} %collective-permute-done.1.swapped_ref, ...), custom_call_target="tpu_custom_call" | custom-call | flops 1207959552 | tf_op jit(solution)/shard_map/pallas_call | solution.py:536
  19.2 2.3 %collective-permute-start.7 = (f32[3,256]{1,0:T(4,128)S(1)}, f32[3,256]{1,0:T(4,128)S(1)}, u32[]{:S(2)}, u32[]{:S(2)}) collective-permute-start(f32[3,256]{1,0:T(4,128)S(1)} %get-tuple-element.23.own_ref), channel_id=1, source_target_pairs={{0,8},{8,0},{4,12},{12,4},{1,9},{9,1},{5,13},{13,5},{2,10},{10,2},... | collective-permute-start | bytes 9224 | tf_op jit(solution)/shard_map/ppermute | solution.py:565
  21.5 1.8 %collective-permute-start.5 = (f32[3,768]{1,0:T(4,128)S(1)}, f32[3,768]{1,0:T(4,128)S(1)}, u32[]{:S(2)}, u32[]{:S(2)}) collective-permute-start(f32[3,768]{1,0:T(4,128)S(1)} %get-tuple-element.21), channel_id=1, source_target_pairs={{0,4},{4,0},{8,12},{12,8},{1,5},{5,1},{9,13},{13,9},{2,6},{6,2},{1... | collective-permute-start | bytes 27656 | tf_op jit(solution)/shard_map/ppermute | solution.py:565
  23.3 0.3 collective-permute-start.6
  23.6 0.1 collective-permute-done.7.far_ref
  23.7 1.5 %collective-permute-done.5.one_ref = f32[3,768]{1,0:T(4,128)S(1)} collective-permute-done((f32[3,768]{1,0:T(4,128)S(1)}, f32[3,768]{1,0:T(4,128)S(1)}, u32[]{:S(2)}, u32[]{:S(2)}) %collective-permute-start.5) | collective-permute-done | bytes 9248 | tf_op jit(solution)/shard_map/ppermute | solution.py:565
  25.2 3.6 %collective-permute-done.6.two_ref = f32[3,768]{1,0:T(4,128)S(1)} collective-permute-done((f32[3,768]{1,0:T(4,128)S(1)}, f32[3,768]{1,0:T(4,128)S(1)}, u32[]{:S(2)}, u32[]{:S(2)}) %collective-permute-start.6) | collective-permute-done | bytes 9248 | tf_op jit(solution)/shard_map/ppermute | solution.py:565
  28.8 1.1 %shard_map.94 = bf16[192,1024]{1,0:T(8,128)(2,1)S(1)} custom-call(f32[3,128,512]{2,1,0:T(8,128)S(1)} %get-tuple-element.20.hid_ref, f32[3,768]{1,0:T(4,128)S(1)} %collective-permute-done.5.one_ref, f32[3,768]{1,0:T(4,128)S(1)} %collective-permute-done.6.two_ref, f32[3,256]{1,0:T(4,128)S(1)} %collective-permute-done.7.far_ref, ...), custom_call_target="tpu_custom_call" | custom-call | flops 603979776 | tf_op jit(solution)/shard_map/pallas_call | solution.py:536
  29.9 1.6 %collective-permute-start.10 = (bf16[192,1024]{1,0:T(8,128)(2,1)S(1)}, bf16[192,1024]{1,0:T(8,128)(2,1)S(1)}, u32[]{:S(2)}, u32[]{:S(2)}) collective-permute-start(bf16[192,1024]{1,0:T(8,128)(2,1)S(1)} %shard_map.94), channel_id=1, source_target_pairs={{0,2},{2,0},{1,3},{3,1},{4,6},{6,4},{5,7},{7,5},{8,10},{10,8},{9,1... | collective-permute-start | bytes 1179656 | tf_op jit(solution)/shard_map/ppermute | solution.py:552
  31.5 1.6 %collective-permute-start.13 = (bf16[768,256]{1,0:T(8,128)(2,1)S(1)}, bf16[768,256]{1,0:T(8,128)(2,1)S(1)}, u32[]{:S(2)}, u32[]{:S(2)}) collective-permute-start(bf16[768,256]{1,0:T(8,128)(2,1)S(1)} %slice.17.first_x_ref), channel_id=1, source_target_pairs={{0,16},{16,0},{1,17},{17,1},{2,18},{18,2},{3,19},{19,3},{4,20},{20... | collective-permute-start | bytes 1179656 | tf_op jit(solution)/shard_map/ppermute | solution.py:556
  33.1 0.5 collective-permute-start.16
  33.6 0.1 collective-permute-start.14
  33.7 1.0 %shard_map.93.keep_ref = f32[192,1024]{1,0:T(8,128)S(1)} custom-call(f32[3,128,512]{2,1,0:T(8,128)S(1)} %get-tuple-element.20.hid_ref, f32[3,768]{1,0:T(4,128)S(1)} %collective-permute-done.5.one_ref, f32[3,768]{1,0:T(4,128)S(1)} %collective-permute-done.6.two_ref, f32[3,256]{1,0:T(4,128)S(1)} %collective-permute-done.7.far_ref, ...), custom_call_target="tpu_custom_call" | custom-call | flops 603979776 | tf_op jit(solution)/shard_map/pallas_call | solution.py:536
  34.8 0.0 copy-start
  34.8 4.6 %collective-permute-done.10.far_ref = bf16[192,1024]{1,0:T(8,128)(2,1)S(1)} collective-permute-done((bf16[192,1024]{1,0:T(8,128)(2,1)S(1)}, bf16[192,1024]{1,0:T(8,128)(2,1)S(1)}, u32[]{:S(2)}, u32[]{:S(2)}) %collective-permute-start.10) | collective-permute-done | bytes 393248 | tf_op jit(solution)/shard_map/ppermute | solution.py:552
  39.4 0.1 shard_map.95.mine_ref
  39.6 0.1 collective-permute-start.11
  39.7 3.9 %collective-permute-done.13.first_y_ref = bf16[768,256]{1,0:T(8,128)(2,1)S(1)} collective-permute-done((bf16[768,256]{1,0:T(8,128)(2,1)S(1)}, bf16[768,256]{1,0:T(8,128)(2,1)S(1)}, u32[]{:S(2)}, u32[]{:S(2)}) %collective-permute-start.13) | collective-permute-done | bytes 393248 | tf_op jit(solution)/shard_map/ppermute | solution.py:556
  43.6 0.1 collective-permute-start.17
  43.7 0.7 %shard_map.98 = (f32[192,512]{1,0:T(8,128)S(1)}, f32[192,512]{1,0:T(8,128)S(1)}, bf16[192,1024]{1,0:T(8,128)(2,1)S(1)}) custom-call(bf16[192,1024]{1,0:T(8,128)(2,1)S(1)} %shard_map.95.mine_ref, f32[1,1024]{1,0:T(1,128)S(1)} %bitcast.22, bf16[3,1024,256]{2,1,0:T(8,128)(2,1)S(1)} %bitcast.14, bf16[768,256]{1,0:T(8,128)(2,1)S(1)} %slice.17.first_x_ref, ...), custom_call_target="tpu_custom_call" | custom-call | flops 402653184 | tf_op jit(solution)/shard_map/pallas_call | solution.py:536
  44.4 2.0 %collective-permute-done.16.v_y_ref = bf16[512,256]{1,0:T(8,128)(2,1)S(1)} collective-permute-done((bf16[512,256]{1,0:T(8,128)(2,1)S(1)}, bf16[512,256]{1,0:T(8,128)(2,1)S(1)}, u32[]{:S(2)}, u32[]{:S(2)}) %collective-permute-start.16) | collective-permute-done | bytes 262176 | tf_op jit(solution)/shard_map/ppermute | solution.py:556
  46.4 3.3 %shard_map.99.context_ref = bf16[384,512]{1,0:T(8,128)(2,1)S(1)} custom-call(bf16[192,1024]{1,0:T(8,128)(2,1)S(1)} %collective-permute-done.11.theirs_ref, f32[1,1024]{1,0:T(1,128)S(1)} %bitcast.23, bf16[3,1024,256]{2,1,0:T(8,128)(2,1)S(1)} %bitcast.15, bf16[768,256]{1,0:T(8,128)(2,1)S(1)} %slice.17.first_x_ref, ...), custom_call_target="tpu_custom_call" | custom-call | flops 1207959552 | tf_op jit(solution)/shard_map/pallas_call | solution.py:536
  49.6 0.4 collective-permute-done.17.out_z_ref
  50.1 0.6 %shard_map.100 = (bf16[384,256]{1,0:T(8,128)(2,1)S(1)}, f32[384,256]{1,0:T(8,128)S(1)}, bf16[384,256]{1,0:T(8,128)(2,1)S(1)}, f32[384,256]{1,0:T(8,128)S(1)}) custom-call(bf16[384,512]{1,0:T(8,128)(2,1)S(1)} %shard_map.99.context_ref, bf16[192,1024]{1,0:T(8,128)(2,1)S(1)} %shard_map.95.mine_ref, bf16[192,1024]{1,0:T(8,128)(2,1)S(1)} %collective-permute-done.11.theirs_ref, ...), custom_call_target="tpu_custom_call" | custom-call | flops 402653184 | tf_op jit(solution)/shard_map/pallas_call | solution.py:536
  50.7 0.1 collective-permute-start.18
  50.8 0.5 collective-permute-start.20
  51.3 0.9 %collective-permute-done.18 = bf16[384,256]{1,0:T(8,128)(2,1)S(1)} collective-permute-done((bf16[384,256]{1,0:T(8,128)(2,1)S(1)}, bf16[384,256]{1,0:T(8,128)(2,1)S(1)}, u32[]{:S(2)}, u32[]{:S(2)}) %collective-permute-start.18) | collective-permute-done | bytes 196640 | tf_op jit(solution)/shard_map/ppermute | solution.py:548
  52.3 0.6 collective-permute-start.19
  52.9 0.8 %place_near.1.near_ref = bf16[6,128,256]{2,1,0:T(8,128)(2,1)} custom-call(f32[384,256]{1,0:T(8,128)S(1)} %get-tuple-element.29.keep_ref, bf16[384,256]{1,0:T(8,128)(2,1)S(1)} %collective-permute-done.20.got_ref), custom_call_target="tpu_custom_call" | custom-call | tf_op jit(solution)/shard_map/place_near/pallas_call | solution.py:676
  53.6 5.6 %collective-permute-done.19.value_ref = bf16[384,256]{1,0:T(8,128)(2,1)S(1)} collective-permute-done((bf16[384,256]{1,0:T(8,128)(2,1)S(1)}, bf16[384,256]{1,0:T(8,128)(2,1)S(1)}, u32[]{:S(2)}, u32[]{:S(2)}) %collective-permute-start.19) | collective-permute-done | bytes 196640 | tf_op jit(solution)/shard_map/ppermute | solution.py:552
  59.3 0.7 %place_far.1 = bf16[6,128,256]{2,1,0:T(8,128)(2,1)} custom-call(bf16[384,256]{1,0:T(8,128)(2,1)S(1)} %collective-permute-done.19.value_ref, bf16[6,128,256]{2,1,0:T(8,128)(2,1)} %place_near.1.near_ref), custom_call_target="tpu_custom_call", output_to_operand_aliasing={{}: (1, {})} | custom-call | tf_op jit(solution)/shard_map/place_far/pallas_call | solution.py:681
  (31 shorter events, 0.2 us)
Async XLA Ops:
  0.0 4.8 %copy-start.1 = (bf16[6,128,1024]{2,1,0:T(8,128)(2,1)S(1)}, bf16[6,128,1024]{2,1,0:T(8,128)(2,1)}, u32[]{:S(2)}) copy-start(bf16[6,128,1024]{2,1,0:T(8,128)(2,1)} %latent_ref.1) | copy-start | bytes 4718596
  0.0 16.6 %collective-permute-start.3 = (bf16[3,1024,256]{2,1,0:T(8,128)(2,1)}, bf16[3,1024,256]{2,1,0:T(8,128)(2,1)S(1)}, u32[]{:S(2)}, u32[]{:S(2)}) collective-permute-start(bf16[3,1024,256]{2,1,0:T(8,128)(2,1)} %weight_ref.1), channel_id=1, source_target_pairs={{0,1},{1,0},{2,3},{3,2},{4,5},{5,4},{6,7},{7,6},{8,9},{9,8},{10,11... | collective-permute-start | bytes 4718600 | tf_op jit(solution)/shard_map/ppermute | solution.py:548
  0.5 22.8 %collective-permute-start.9 = (bf16[3,256,1024]{2,1,0:T(8,128)(2,1)}, bf16[3,256,1024]{2,1,0:T(8,128)(2,1)S(1)}, u32[]{:S(2)}, u32[]{:S(2)}) collective-permute-start(bf16[3,256,1024]{2,1,0:T(8,128)(2,1)} %param.14), channel_id=1, source_target_pairs={{0,1},{1,0},{2,3},{3,2},{4,5},{5,4},{6,7},{7,6},{8,9},{9,8},{10,11... | collective-permute-start | bytes 4718600 | tf_op jit(solution)/shard_map/ppermute | solution.py:548
  0.6 9.8 %copy-start.7 = (f32[256]{0:T(256)S(1)}, f32[256]{0:T(256)}, u32[]{:S(2)}) copy-start(f32[256]{0:T(256)} %param.12) | copy-start | bytes 3076
  1.8 14.3 %copy-start.8 = (f32[256]{0:T(256)S(1)}, f32[256]{0:T(256)}, u32[]{:S(2)}) copy-start(f32[256]{0:T(256)} %param.13) | copy-start | bytes 3076
  1.8 14.9 %copy-start.4 = (bf16[3,1024,256]{2,1,0:T(8,128)(2,1)S(1)}, bf16[3,1024,256]{2,1,0:T(8,128)(2,1)}, u32[]{:S(2)}) copy-start(bf16[3,1024,256]{2,1,0:T(8,128)(2,1)} %weight_ref.1) | copy-start | bytes 4718596
  1.8 14.9 %copy-start.6 = (f32[1024]{0:T(1024)S(1)}, f32[1024]{0:T(1024)}, u32[]{:S(2)}) copy-start(f32[1024]{0:T(1024)} %param.10) | copy-start | bytes 12292
  1.8 29.7 %collective-permute-start.12 = (bf16[1280,256]{1,0:T(8,128)(2,1)S(1)}, bf16[1280,256]{1,0:T(8,128)(2,1)S(1)}, u32[]{:S(2)}, u32[]{:S(2)}) collective-permute-start(bf16[1280,256]{1,0:T(8,128)(2,1)S(1)} %shard_map.96), channel_id=1, source_target_pairs={{0,2},{2,0},{1,3},{3,1},{4,6},{6,4},{5,7},{7,5},{8,10},{10,8},{9,1... | collective-permute-start | bytes 1966088 | tf_op jit(solution)/shard_map/ppermute | solution.py:552
  5.8 4.1 %collective-permute-start = (f32[6,1280]{1,0:T(8,128)S(1)}, f32[6,1280]{1,0:T(8,128)S(1)}, u32[]{:S(2)}, u32[]{:S(2)}) collective-permute-start(f32[6,1280]{1,0:T(8,128)S(1)} %get-tuple-element.18), channel_id=1, source_target_pairs={{0,4},{4,0},{8,12},{12,8},{1,13},{13,1},{5,9},{9,5},{2,6},{6,2},{1... | collective-permute-start | bytes 92168 | tf_op jit(solution)/shard_map/ppermute | solution.py:575
  9.8 6.2 %collective-permute-start.1 = (f32[6,1280]{1,0:T(8,128)S(1)}, f32[6,1280]{1,0:T(8,128)S(1)}, u32[]{:S(2)}, u32[]{:S(2)}) collective-permute-start(f32[6,1280]{1,0:T(8,128)S(1)} %collective-permute-done.got_ref), channel_id=1, source_target_pairs={{0,1},{1,0},{2,3},{3,2},{4,5},{5,4},{6,7},{7,6},{8,9},{9,8},{10,11... | collective-permute-start | bytes 92168 | tf_op jit(solution)/shard_map/ppermute | solution.py:548
  10.3 1.2 %collective-permute-start.4 = (f32[256]{0:T(256)S(1)}, f32[256]{0:T(256)S(1)}, u32[]{:S(2)}, u32[]{:S(2)}) collective-permute-start(f32[256]{0:T(256)S(1)} %copy-done.7), channel_id=1, source_target_pairs={{0,1},{1,0},{2,3},{3,2},{4,5},{5,4},{6,7},{7,6},{8,9},{9,8},{10,11... | collective-permute-start | bytes 3080 | tf_op jit(solution)/shard_map/ppermute | solution.py:548
  11.5 4.5 %collective-permute-start.2 = (f32[6,256]{1,0:T(8,128)S(1)}, f32[6,256]{1,0:T(8,128)S(1)}, u32[]{:S(2)}, u32[]{:S(2)}) collective-permute-start(f32[6,256]{1,0:T(8,128)S(1)} %get-tuple-element.19.own_ref), channel_id=1, source_target_pairs={{0,8},{8,0},{4,12},{12,4},{1,9},{9,1},{5,13},{13,5},{2,10},{10,2},... | collective-permute-start | bytes 18440 | tf_op jit(solution)/shard_map/ppermute | solution.py:565
  16.0 5.5 %collective-permute-start.8 = (f32[256]{0:T(256)S(1)}, f32[256]{0:T(256)S(1)}, u32[]{:S(2)}, u32[]{:S(2)}) collective-permute-start(f32[256]{0:T(256)S(1)} %copy-done.8), channel_id=1, source_target_pairs={{0,1},{1,0},{2,3},{3,2},{4,5},{5,4},{6,7},{7,6},{8,9},{9,8},{10,11... | collective-permute-start | bytes 3080 | tf_op jit(solution)/shard_map/ppermute | solution.py:548
  16.0 17.1 %collective-permute-start.15 = (bf16[512,256]{1,0:T(8,128)(2,1)S(1)}, bf16[512,256]{1,0:T(8,128)(2,1)S(1)}, u32[]{:S(2)}, u32[]{:S(2)}) collective-permute-start(bf16[512,256]{1,0:T(8,128)(2,1)S(1)} %shard_map.97), channel_id=1, source_target_pairs={{0,2},{2,0},{1,3},{3,1},{4,6},{6,4},{5,7},{7,5},{8,10},{10,8},{9,1... | collective-permute-start | bytes 786440 | tf_op jit(solution)/shard_map/ppermute | solution.py:552
  16.7 12.2 %copy-start.2 = (bf16[3,256,1024]{2,1,0:T(8,128)(2,1)S(1)}, bf16[3,256,1024]{2,1,0:T(8,128)(2,1)}, u32[]{:S(2)}) copy-start(bf16[3,256,1024]{2,1,0:T(8,128)(2,1)} %param.14) | copy-start | bytes 4718596
  19.2 4.6 %collective-permute-start.7 = (f32[3,256]{1,0:T(4,128)S(1)}, f32[3,256]{1,0:T(4,128)S(1)}, u32[]{:S(2)}, u32[]{:S(2)}) collective-permute-start(f32[3,256]{1,0:T(4,128)S(1)} %get-tuple-element.23.own_ref), channel_id=1, source_target_pairs={{0,8},{8,0},{4,12},{12,4},{1,9},{9,1},{5,13},{13,5},{2,10},{10,2},... | collective-permute-start | bytes 9224 | tf_op jit(solution)/shard_map/ppermute | solution.py:565
  21.5 3.7 %collective-permute-start.5 = (f32[3,768]{1,0:T(4,128)S(1)}, f32[3,768]{1,0:T(4,128)S(1)}, u32[]{:S(2)}, u32[]{:S(2)}) collective-permute-start(f32[3,768]{1,0:T(4,128)S(1)} %get-tuple-element.21), channel_id=1, source_target_pairs={{0,4},{4,0},{8,12},{12,8},{1,5},{5,1},{9,13},{13,9},{2,6},{6,2},{1... | collective-permute-start | bytes 27656 | tf_op jit(solution)/shard_map/ppermute | solution.py:565
  23.3 5.5 %collective-permute-start.6 = (f32[3,768]{1,0:T(4,128)S(1)}, f32[3,768]{1,0:T(4,128)S(1)}, u32[]{:S(2)}, u32[]{:S(2)}) collective-permute-start(f32[3,768]{1,0:T(4,128)S(1)} %get-tuple-element.22), channel_id=1, source_target_pairs={{0,12},{12,0},{4,8},{8,4},{1,13},{13,1},{5,9},{9,5},{2,14},{14,2},... | collective-permute-start | bytes 27656 | tf_op jit(solution)/shard_map/ppermute | solution.py:565
  29.9 9.5 %collective-permute-start.10 = (bf16[192,1024]{1,0:T(8,128)(2,1)S(1)}, bf16[192,1024]{1,0:T(8,128)(2,1)S(1)}, u32[]{:S(2)}, u32[]{:S(2)}) collective-permute-start(bf16[192,1024]{1,0:T(8,128)(2,1)S(1)} %shard_map.94), channel_id=1, source_target_pairs={{0,2},{2,0},{1,3},{3,1},{4,6},{6,4},{5,7},{7,5},{8,10},{10,8},{9,1... | collective-permute-start | bytes 1179656 | tf_op jit(solution)/shard_map/ppermute | solution.py:552
  31.5 12.0 %collective-permute-start.13 = (bf16[768,256]{1,0:T(8,128)(2,1)S(1)}, bf16[768,256]{1,0:T(8,128)(2,1)S(1)}, u32[]{:S(2)}, u32[]{:S(2)}) collective-permute-start(bf16[768,256]{1,0:T(8,128)(2,1)S(1)} %slice.17.first_x_ref), channel_id=1, source_target_pairs={{0,16},{16,0},{1,17},{17,1},{2,18},{18,2},{3,19},{19,3},{4,20},{20... | collective-permute-start | bytes 1179656 | tf_op jit(solution)/shard_map/ppermute | solution.py:556
  33.1 13.3 %collective-permute-start.16 = (bf16[512,256]{1,0:T(8,128)(2,1)S(1)}, bf16[512,256]{1,0:T(8,128)(2,1)S(1)}, u32[]{:S(2)}, u32[]{:S(2)}) collective-permute-start(bf16[512,256]{1,0:T(8,128)(2,1)S(1)} %collective-permute-done.15.v_x_ref), channel_id=1, source_target_pairs={{0,16},{16,0},{1,17},{17,1},{2,18},{18,2},{3,19},{19,3},{4,20},{20... | collective-permute-start | bytes 786440 | tf_op jit(solution)/shard_map/ppermute | solution.py:556
  33.6 10.1 %collective-permute-start.14 = (bf16[512,256]{1,0:T(8,128)(2,1)S(1)}, bf16[512,256]{1,0:T(8,128)(2,1)S(1)}, u32[]{:S(2)}, u32[]{:S(2)}) collective-permute-start(bf16[512,256]{1,0:T(8,128)(2,1)S(1)} %slice.18.q_x_ref), channel_id=1, source_target_pairs={{0,4},{4,0},{8,12},{12,8},{1,5},{5,1},{9,13},{13,9},{2,6},{6,2},{1... | collective-permute-start | bytes 786440 | tf_op jit(solution)/shard_map/ppermute | solution.py:565
  34.8 8.9 %copy-start = (bf16[1024,3,256]{2,0,1:T(8,128)(2,1)S(1)}, bf16[1024,3,256]{2,0,1:T(8,128)(2,1)}, u32[]{:S(2)}) copy-start(bf16[1024,3,256]{2,0,1:T(8,128)(2,1)} %param.16) | copy-start | bytes 4718596
  34.8 8.9 %copy-start.5 = (f32[1024]{0:T(1024)S(1)}, f32[1024]{0:T(1024)}, u32[]{:S(2)}) copy-start(f32[1024]{0:T(1024)} %param.15) | copy-start | bytes 12292
  39.6 6.8 %collective-permute-start.11 = (bf16[192,1024]{1,0:T(8,128)(2,1)S(1)}, bf16[192,1024]{1,0:T(8,128)(2,1)S(1)}, u32[]{:S(2)}, u32[]{:S(2)}) collective-permute-start(bf16[192,1024]{1,0:T(8,128)(2,1)S(1)} %shard_map.95.mine_ref), channel_id=1, source_target_pairs={{0,1},{1,0},{2,3},{3,2},{4,5},{5,4},{6,7},{7,6},{8,9},{9,8},{10,11... | collective-permute-start | bytes 1179656 | tf_op jit(solution)/shard_map/ppermute | solution.py:548
  43.6 6.4 %collective-permute-start.17 = (bf16[2,256,256]{2,1,0:T(8,128)(2,1)S(1)}, bf16[2,256,256]{2,1,0:T(8,128)(2,1)S(1)}, u32[]{:S(2)}, u32[]{:S(2)}) collective-permute-start(bf16[2,256,256]{2,1,0:T(8,128)(2,1)S(1)} %pad_maximum_fusion), channel_id=1, source_target_pairs={{0,4},{4,0},{8,12},{12,8},{1,5},{5,1},{9,13},{13,9},{2,6},{6,2},{1... | collective-permute-start | bytes 786440 | tf_op jit(solution)/shard_map/ppermute | solution.py:565
  46.4 3.7 %copy-start.3 = (bf16[256,1024]{1,0:T(8,128)(2,1)S(1)}, bf16[256,1024]{1,0:T(8,128)(2,1)}, u32[]{:S(2)}) copy-start(bf16[256,1024]{1,0:T(8,128)(2,1)} %out_ref.3) | copy-start | bytes 1572868
  50.7 1.5 %collective-permute-start.18 = (bf16[384,256]{1,0:T(8,128)(2,1)S(1)}, bf16[384,256]{1,0:T(8,128)(2,1)S(1)}, u32[]{:S(2)}, u32[]{:S(2)}) collective-permute-start(bf16[384,256]{1,0:T(8,128)(2,1)S(1)} %get-tuple-element.28), channel_id=1, source_target_pairs={{0,1},{1,0},{2,3},{3,2},{4,5},{5,4},{6,7},{7,6},{8,9},{9,8},{10,11... | collective-permute-start | bytes 589832 | tf_op jit(solution)/shard_map/ppermute | solution.py:548
  50.8 2.1 %collective-permute-start.20 = (bf16[384,256]{1,0:T(8,128)(2,1)S(1)}, bf16[384,256]{1,0:T(8,128)(2,1)S(1)}, u32[]{:S(2)}, u32[]{:S(2)}) collective-permute-start(bf16[384,256]{1,0:T(8,128)(2,1)S(1)} %get-tuple-element.30), channel_id=1, source_target_pairs={{0,1},{1,0},{2,3},{3,2},{4,5},{5,4},{6,7},{7,6},{8,9},{9,8},{10,11... | collective-permute-start | bytes 589832 | tf_op jit(solution)/shard_map/ppermute | solution.py:548
  52.3 7.0 %collective-permute-start.19 = (bf16[384,256]{1,0:T(8,128)(2,1)S(1)}, bf16[384,256]{1,0:T(8,128)(2,1)S(1)}, u32[]{:S(2)}, u32[]{:S(2)}) collective-permute-start(bf16[384,256]{1,0:T(8,128)(2,1)S(1)} %add_convert_fusion), channel_id=1, source_target_pairs={{0,2},{2,0},{1,3},{3,1},{4,6},{6,4},{5,7},{7,5},{8,10},{10,8},{9,1... | collective-permute-start | bytes 589832 | tf_op jit(solution)/shard_map/ppermute | solution.py:552

commit v8 on v7

--- a/solution.py
+++ b/solution.py
@@ -321,7 +321,7 @@
     return (res * lax.rsqrt(mean_sq + rms_eps) * gain_ref[...]).astype(bf16)
 
 
-def projector(normed_ref, qkv_ref, first_x_ref, first_y_ref, q_x_ref, q_z_ref, v_refs=()):
+def projector(normed_ref, qkv_ref, k_x_ref, k_y_ref, q_x_ref, q_z_ref, v_refs=()):
     depth = normed_ref.shape[1] // 2
     group, parity = lax.axis_index(SONGS), lax.axis_index(FRAME) % 2
 
@@ -334,7 +334,7 @@
         if which == 0:
             place, near, away = parity, q_x_ref[...], q_z_ref[...]
         elif which == 1:
-            place, near, away = group, first_x_ref[:depth, :], first_y_ref[:depth, :]
+            place, near, away = group, k_x_ref[...], k_y_ref[...]
         else:
             place, near, away = group, v_refs[0][...], v_refs[1][...]
         value = jnp.dot(half(place), near, preferred_element_type=f32)
@@ -344,12 +344,12 @@
 
 
 def project_kernel(
-    mine_ref, gain_ref, qkv_ref, first_x_ref, first_y_ref, q_x_ref, q_z_ref,
+    mine_ref, gain_ref, qkv_ref, k_x_ref, k_y_ref, q_x_ref, q_z_ref,
     queries_ref, keys_ref, normed_ref,
 ):
     shard = qkv_ref.shape[2]
     normed_ref[...] = normed_rows(mine_ref[...].astype(f32), gain_ref)
-    project = projector(normed_ref, qkv_ref, first_x_ref, first_y_ref, q_x_ref, q_z_ref)
+    project = projector(normed_ref, qkv_ref, k_x_ref, k_y_ref, q_x_ref, q_z_ref)
     for side in range(2):
         at = slice(side * shard, (side + 1) * shard)
         queries_ref[:, at] = project(side, 0)
@@ -357,7 +357,7 @@
 
 
 def attention_kernel(
-    theirs_ref, gain_ref, qkv_ref, first_x_ref, first_y_ref, q_x_ref, q_z_ref, v_x_ref, v_y_ref,
+    theirs_ref, gain_ref, qkv_ref, k_x_ref, k_y_ref, q_x_ref, q_z_ref, v_x_ref, v_y_ref,
     queries_ref, keys_ref, mine_ref,
     context_ref, normed_ref,
 ):
@@ -365,7 +365,7 @@
     shard = qkv_ref.shape[2]
     normed_ref[:rows, :] = mine_ref[...]
     normed_ref[rows:, :] = normed_rows(theirs_ref[...].astype(f32), gain_ref)
-    weights = qkv_ref, first_x_ref, first_y_ref, q_x_ref, q_z_ref
+    weights = qkv_ref, k_x_ref, k_y_ref, q_x_ref, q_z_ref
     project = projector(normed_ref.at[pl.ds(rows, rows), :], *weights)
     project_all = projector(normed_ref, *weights, (v_x_ref, v_y_ref))
     lane = lax.broadcasted_iota(jnp.int32, (2 * rows, LANES), 1)
@@ -411,18 +411,16 @@
 
 
 def output_kernel(
-    context_ref, mine_ref, theirs_ref, out_ref, first_x_ref, first_y_ref, out_z_ref,
-    send_far_ref, keep_far_ref, send_near_ref, keep_near_ref,
-    out_far_ref,
+    away, context_ref, mine_ref, theirs_ref, out_ref, out_x_ref, out_y_ref, out_z_ref,
+    send_ref, keep_ref, out_far_ref,
 ):
-    rows, channels = mine_ref.shape
+    rows = mine_ref.shape[0]
     shard = out_ref.shape[0]
     index = lax.axis_index(TENSOR)
     chip, core = index // 2, index % 2
-    depth = channels // 2
     group, parity = lax.axis_index(SONGS), lax.axis_index(FRAME) % 2
-    out_far_ref[2 * group + parity] = first_x_ref[depth:, :]
-    out_far_ref[2 * (1 - group) + parity] = first_y_ref[depth:, :]
+    out_far_ref[2 * group + parity] = out_x_ref[...]
+    out_far_ref[2 * (1 - group) + parity] = out_y_ref[...]
     out_far_ref[2 * group + 1 - parity] = out_z_ref[0]
     out_far_ref[2 * (1 - group) + 1 - parity] = out_z_ref[1]
 
@@ -432,16 +430,15 @@
         far = jnp.dot(context_ref[:, shard:], out_far_ref[block], preferred_element_type=f32)
         return value + far
 
-    sides = ((1 - chip, send_far_ref, keep_far_ref), (chip, send_near_ref, keep_near_ref))
-    for goal, send_ref, keep_ref in sides:
-        value = term(2 * goal + 1 - core).astype(bf16)
-        send_ref[:rows, :] = value[rows:]
-        send_ref[rows:, :] = value[:rows]
-        block = 2 * goal + core
-        at = pl.ds(pl.multiple_of(block * shard, shard), shard)
-        value = term(block)
-        keep_ref[:rows, :] = value[:rows] + mine_ref[:, at].astype(f32)
-        keep_ref[rows:, :] = value[rows:] + theirs_ref[:, at].astype(f32)
+    goal = 1 - chip if away else chip
+    value = term(2 * goal + 1 - core).astype(bf16)
+    send_ref[:rows, :] = value[rows:]
+    send_ref[rows:, :] = value[:rows]
+    block = 2 * goal + core
+    at = pl.ds(pl.multiple_of(block * shard, shard), shard)
+    value = term(block)
+    keep_ref[:rows, :] = value[:rows] + mine_ref[:, at].astype(f32)
+    keep_ref[rows:, :] = value[rows:] + theirs_ref[:, at].astype(f32)
 
 
 def run_copies(pairs, sems):
@@ -465,10 +462,9 @@
 def pack_first_kernel(qkv_ref, out_ref, send_ref, sems):
     depth, shard = qkv_ref.shape[1] // 2, qkv_ref.shape[2]
     group, parity = lax.axis_index(SONGS), lax.axis_index(FRAME) % 2
-    pairs = []
-    for which, place, base in ((1, group, 0), (0, parity, depth + shard)):
-        for rows, goal in row_pieces(place, depth):
-            pairs.append((qkv_ref.at[which, rows, :], send_ref.at[pl.ds(base + goal.start, goal.size), :]))
+    pairs = [
+        (qkv_ref.at[1, rows, :], send_ref.at[goal, :]) for rows, goal in row_pieces(group, depth)
+    ]
     block = pl.ds(pl.multiple_of((2 * group + parity) * shard, shard), shard)
     for piece in range(2):
         rows = pl.ds(piece * shard // 2, shard // 2)
@@ -477,11 +473,13 @@
     run_copies(pairs, sems)
 
 
-def pack_rest_kernel(qkv_ref, values_ref, sems):
-    pairs = [
-        (qkv_ref.at[2, rows, :], values_ref.at[goal, :])
-        for rows, goal in row_pieces(lax.axis_index(SONGS), values_ref.shape[0])
-    ]
+def pack_rest_kernel(qkv_ref, send_ref, sems):
+    depth = send_ref.shape[1]
+    group, parity = lax.axis_index(SONGS), lax.axis_index(FRAME) % 2
+    pairs = []
+    for slot, which, place in ((0, 0, parity), (1, 2, group)):
+        for rows, goal in row_pieces(place, depth):
+            pairs.append((qkv_ref.at[which, rows, :], send_ref.at[slot, goal, :]))
     run_copies(pairs, sems)
 
 
@@ -587,18 +585,17 @@
     half_rows = stems // 2 * WINDOW
     qkv = jnp.transpose(qkv_weight, (1, 0, 2))
     depth = channels // 2
-    (first,) = pack(
-        pack_first_kernel, [(2 * depth + shard, shard)], 2 * PIECES + 2,
-        [qkv, out_weight],
-    )
-    (values,) = pack(pack_rest_kernel, [(depth, shard)], PIECES, [qkv])
+    (first,) = pack(pack_first_kernel, [(depth + shard, shard)], PIECES + 2, [qkv, out_weight])
+    (rest,) = pack(pack_rest_kernel, [(2, depth, shard)], 2 * PIECES, [qkv])
     first_x = swap_chips(first)
-    v_x = swap_chips(values)
-    first_x, q_x = first_x[: depth + shard], first_x[depth + shard :]
-    first_y = swap_groups(first_x)
+    rest_x = swap_chips(rest)
+    k_x, out_x = first_x[:depth], first_x[depth:]
+    q_x, v_x = rest_x[0], rest_x[1]
+    out_y = swap_groups(out_x)
+    k_y = swap_groups(k_x)
     q_z = trade(q_x, ONE)
     v_y = swap_groups(v_x)
-    out_z = trade(jnp.stack([first_x[depth:], first_y[depth:]]), ONE)
+    out_z = trade(jnp.stack([out_x, out_y]), ONE)
     weight1 = swap_cores(conv1_weight)
     weight2 = swap_cores(conv2_weight).reshape(3 * shard, channels)
     bias_far = swap_cores(time_bias)
@@ -645,7 +642,7 @@
         [latent, second(False), summed],
     )[0]
     theirs = swap_cores(mine)
-    weights = [attn_gain[None], qkv, first_x, first_y, q_x, q_z]
+    weights = [attn_gain[None], qkv, k_x, k_y, q_x, q_z]
     projected = call(
         project_kernel,
         [((half_rows, 2 * shard), f32)] * 2 + [((half_rows, channels), bf16)], [],
@@ -658,13 +655,18 @@
         [theirs, *weights, v_x, v_y, *projected],
         flops=24 * half_rows * channels * shard, limit=24,
     )[0]
-    send_far, keep_far, send_near, keep_near = call(
-        output_kernel,
-        [((2 * half_rows, shard), bf16), ((2 * half_rows, shard), f32)] * 2,
-        [((4, shard, shard), bf16)],
-        [context, mine, theirs, out_weight, first_x, first_y, out_z],
-        flops=8 * half_rows * channels * shard,
-    )
+
+    def output(away):
+        return call(
+            functools.partial(output_kernel, away),
+            [((2 * half_rows, shard), bf16), ((2 * half_rows, shard), f32)],
+            [((4, shard, shard), bf16)],
+            [context, mine, theirs, out_weight, out_x, out_y, out_z],
+            flops=4 * half_rows * channels * shard,
+        )
+
+    send_far, keep_far = output(True)
+    send_near, keep_near = output(False)
     got_far = swap_cores(send_far)
     got_near = swap_cores(send_near)
     away = (keep_far + got_far.astype(f32)).astype(bf16)

time: 60.2 us -> 68.6 us (1.14)
  starting transfers between devices: 18 us -> 22.9 us
  waiting for transfers between devices: 27.6 us -> 29.3 us
  local copies, waits for them, and re-layouts: 0.11 us -> 1.53 us
    ppermute x4, waiting for transfers between devices: 10.3 us -> 15.7 us  [swap_chips(): return lax.ppermute(value, TENSOR, [(0, 2), (2, 0), (1, 3), (3, 1)])]
    ppermute x2 -> x3, waiting for transfers between devices: 5.87 us -> 0.57 us  [swap_groups(): return lax.ppermute(value, SONGS, [(0, 1), (1, 0)])]
    ppermute x6, waiting for transfers between devices: 6.92 us -> 10.6 us  [trade(): return lax.ppermute(value, FRAME, pairs)]
    ppermute x6, starting transfers between devices: 6.85 us -> 9.03 us  [trade(): return lax.ppermute(value, FRAME, pairs)]
    ppermute x8, waiting for transfers between devices: 2.09 us -> 0.45 us  [swap_cores(): return lax.ppermute(value, TENSOR, [(0, 1), (1, 0), (2, 3), (3, 2)])]
    ppermute x2 -> x3, starting transfers between devices: 2.09 us -> 3.68 us  [swap_groups(): return lax.ppermute(value, SONGS, [(0, 1), (1, 0)])]
    ppermute x1, starting transfers between devices: 1.64 us -> 3.12 us  [trade_by_core(): return lax.ppermute(value, (FRAME, TENSOR), pairs)]
    unnamed x18 -> x20, local copies, waits for them, and re-layouts: 0.05 us -> 1.46 us
  transfers between devices with their start and end apart: 21 -> 22, of which waited for: 12 -> 9; matrix products, arithmetic and copies ran while one was open for 0% -> 0% of each run, Pallas kernels for 21% -> 19%
where the time goes in v8:
time: 68.6 us; the launch traced here: 68.4 us
  waiting for transfers between devices  29.3 us (43%)
  starting transfers between devices  22.9 us (33%)
  Pallas kernels  14.4 us (21%)
  local copies, waits for them, and re-layouts  1.53 us (2%)
    ppermute x4, waiting for transfers between devices, swap_chips(): return lax.ppermute(value, TENSOR, [(0, 2), (2, 0), (1, 3), (3, 1)])  15.7 us
    pallas_call x9, Pallas kernels, call(): pl.pallas_call(kernel, out_shape=[jax.ShapeDtypeStruct(shape, dtype) for...  10.6 us
    ppermute x6, waiting for transfers between devices, trade(): return lax.ppermute(value, FRAME, pairs)  10.6 us
    ppermute x6, starting transfers between devices, trade(): return lax.ppermute(value, FRAME, pairs)  9.03 us
    ppermute x4, starting transfers between devices, swap_chips(): return lax.ppermute(value, TENSOR, [(0, 2), (2, 0), (1, 3), (3, 1)])  4.37 us
    ppermute x3, starting transfers between devices, swap_groups(): return lax.ppermute(value, SONGS, [(0, 1), (1, 0)])  3.68 us
    ppermute x1, starting transfers between devices, trade_by_core(): return lax.ppermute(value, (FRAME, TENSOR), pairs)  3.12 us
    ppermute x8, starting transfers between devices, swap_cores(): return lax.ppermute(value, TENSOR, [(0, 1), (1, 0), (2, 3), (3, 2)])  2.67 us
  transfers between devices with their start and end apart: 22, of which 9 were waited for; matrix products, arithmetic and copies ran while one was open for 0% of the time, Pallas kernels for 19%

profile of v8, /device:TPU:0, one launch (start us, length us, event | category | flops | bytes accessed | tf_op | source)
XLA Modules:
  0.0 68.4 jit_solution(5056153710342669803)
XLA Ops:
  0.0 0.5 collective-permute-start.3
  0.5 0.0 collective-permute-start.9
  0.5 1.4 %copy-done.1 = bf16[6,128,1024]{2,1,0:T(8,128)(2,1)S(1)} copy-done((bf16[6,128,1024]{2,1,0:T(8,128)(2,1)S(1)}, bf16[6,128,1024]{2,1,0:T(8,128)(2,1)}, u32[]{:S(2)}) %copy-start.1) | copy-done | bytes 1572888
  1.9 0.9 %shard_map.91 = (f32[6,1280]{1,0:T(8,128)S(1)}, f32[6,256]{1,0:T(8,128)S(1)}) custom-call(bf16[6,128,1024]{2,1,0:T(8,128)(2,1)S(1)} %copy-done.1), custom_call_target="tpu_custom_call" | custom-call | tf_op jit(solution)/shard_map/pallas_call | solution.py:534
  2.9 3.1 %collective-permute-start = (f32[6,1280]{1,0:T(8,128)S(1)}, f32[6,1280]{1,0:T(8,128)S(1)}, u32[]{:S(2)}, u32[]{:S(2)}) collective-permute-start(f32[6,1280]{1,0:T(8,128)S(1)} %get-tuple-element.18), channel_id=1, source_target_pairs={{0,4},{4,0},{8,12},{12,8},{1,13},{13,1},{5,9},{9,5},{2,6},{6,2},{1... | collective-permute-start | bytes 92168 | tf_op jit(solution)/shard_map/ppermute | solution.py:573
  6.0 2.0 %collective-permute-done.got_ref = f32[6,1280]{1,0:T(8,128)S(1)} collective-permute-done((f32[6,1280]{1,0:T(8,128)S(1)}, f32[6,1280]{1,0:T(8,128)S(1)}, u32[]{:S(2)}, u32[]{:S(2)}) %collective-permute-start) | collective-permute-done | bytes 30752 | tf_op jit(solution)/shard_map/ppermute | solution.py:573
  8.0 1.2 %collective-permute-start.1 = (f32[6,1280]{1,0:T(8,128)S(1)}, f32[6,1280]{1,0:T(8,128)S(1)}, u32[]{:S(2)}, u32[]{:S(2)}) collective-permute-start(f32[6,1280]{1,0:T(8,128)S(1)} %collective-permute-done.got_ref), channel_id=1, source_target_pairs={{0,1},{1,0},{2,3},{3,2},{4,5},{5,4},{6,7},{7,6},{8,9},{9,8},{10,11... | collective-permute-start | bytes 92168 | tf_op jit(solution)/shard_map/ppermute | solution.py:546
  9.1 1.9 %collective-permute-start.2 = (f32[6,256]{1,0:T(8,128)S(1)}, f32[6,256]{1,0:T(8,128)S(1)}, u32[]{:S(2)}, u32[]{:S(2)}) collective-permute-start(f32[6,256]{1,0:T(8,128)S(1)} %get-tuple-element.19.own_ref), channel_id=1, source_target_pairs={{0,8},{8,0},{4,12},{12,4},{1,9},{9,1},{5,13},{13,5},{2,10},{10,2},... | collective-permute-start | bytes 18440 | tf_op jit(solution)/shard_map/ppermute | solution.py:563
  11.0 0.2 collective-permute-start.4
  11.2 1.2 %shard_map.96 = bf16[768,256]{1,0:T(8,128)(2,1)S(1)} custom-call(bf16[3,1024,256]{2,1,0:T(8,128)(2,1)} %bitcast.15, bf16[256,1024]{1,0:T(8,128)(2,1)} %out_ref.5), custom_call_target="tpu_custom_call" | custom-call | bytes 1048576 | tf_op jit(solution)/shard_map/pallas_call | solution.py:487
  12.4 0.0 copy-start.9
  12.5 1.6 %collective-permute-start.12 = (bf16[768,256]{1,0:T(8,128)(2,1)S(1)}, bf16[768,256]{1,0:T(8,128)(2,1)S(1)}, u32[]{:S(2)}, u32[]{:S(2)}) collective-permute-start(bf16[768,256]{1,0:T(8,128)(2,1)S(1)} %shard_map.96), channel_id=1, source_target_pairs={{0,2},{2,0},{1,3},{3,1},{4,6},{6,4},{5,7},{7,5},{8,10},{10,8},{9,1... | collective-permute-start | bytes 1179656 | tf_op jit(solution)/shard_map/ppermute | solution.py:550
  14.0 1.1 %shard_map.97 = bf16[2,512,256]{2,1,0:T(8,128)(2,1)S(1)} custom-call(bf16[3,1024,256]{2,1,0:T(8,128)(2,1)} %bitcast.16), custom_call_target="tpu_custom_call" | custom-call | bytes 1048576 | tf_op jit(solution)/shard_map/pallas_call | solution.py:487
  15.2 0.1 collective-permute-start.8
  15.3 0.7 collective-permute-start.14
  15.9 0.0 copy-start.3
  15.9 2.6 %shard_map.92 = (f32[3,128,512]{2,1,0:T(8,128)S(1)}, f32[3,768]{1,0:T(4,128)S(1)}, f32[3,768]{1,0:T(4,128)S(1)}, f32[3,256]{1,0:T(4,128)S(1)}) custom-call(bf16[6,128,1024]{2,1,0:T(8,128)(2,1)S(1)} %copy-done.2, f32[6,1280]{1,0:T(8,128)S(1)} %collective-permute-done.got_ref, f32[6,1280]{1,0:T(8,128)S(1)} %collective-permute-done.1.swapped_ref, ...), custom_call_target="tpu_custom_call" | custom-call | flops 1207959552 | tf_op jit(solution)/shard_map/pallas_call | solution.py:534
  18.5 1.3 %collective-permute-start.7 = (f32[3,256]{1,0:T(4,128)S(1)}, f32[3,256]{1,0:T(4,128)S(1)}, u32[]{:S(2)}, u32[]{:S(2)}) collective-permute-start(f32[3,256]{1,0:T(4,128)S(1)} %get-tuple-element.23.own_ref), channel_id=1, source_target_pairs={{0,8},{8,0},{4,12},{12,4},{1,9},{9,1},{5,13},{13,5},{2,10},{10,2},... | collective-permute-start | bytes 9224 | tf_op jit(solution)/shard_map/ppermute | solution.py:563
  19.8 2.2 %collective-permute-start.5 = (f32[3,768]{1,0:T(4,128)S(1)}, f32[3,768]{1,0:T(4,128)S(1)}, u32[]{:S(2)}, u32[]{:S(2)}) collective-permute-start(f32[3,768]{1,0:T(4,128)S(1)} %get-tuple-element.21), channel_id=1, source_target_pairs={{0,4},{4,0},{8,12},{12,8},{1,5},{5,1},{9,13},{13,9},{2,6},{6,2},{1... | collective-permute-start | bytes 27656 | tf_op jit(solution)/shard_map/ppermute | solution.py:563
  22.0 1.2 %collective-permute-start.6 = (f32[3,768]{1,0:T(4,128)S(1)}, f32[3,768]{1,0:T(4,128)S(1)}, u32[]{:S(2)}, u32[]{:S(2)}) collective-permute-start(f32[3,768]{1,0:T(4,128)S(1)} %get-tuple-element.22), channel_id=1, source_target_pairs={{0,12},{12,0},{4,8},{8,4},{1,13},{13,1},{5,9},{9,5},{2,14},{14,2},... | collective-permute-start | bytes 27656 | tf_op jit(solution)/shard_map/ppermute | solution.py:563
  23.3 0.4 collective-permute-done.5.one_ref
  23.7 3.8 %collective-permute-done.6.two_ref = f32[3,768]{1,0:T(4,128)S(1)} collective-permute-done((f32[3,768]{1,0:T(4,128)S(1)}, f32[3,768]{1,0:T(4,128)S(1)}, u32[]{:S(2)}, u32[]{:S(2)}) %collective-permute-start.6) | collective-permute-done | bytes 9248 | tf_op jit(solution)/shard_map/ppermute | solution.py:563
  27.5 1.1 %shard_map.94 = bf16[192,1024]{1,0:T(8,128)(2,1)S(1)} custom-call(f32[3,128,512]{2,1,0:T(8,128)S(1)} %get-tuple-element.20.hid_ref, f32[3,768]{1,0:T(4,128)S(1)} %collective-permute-done.5.one_ref, f32[3,768]{1,0:T(4,128)S(1)} %collective-permute-done.6.two_ref, f32[3,256]{1,0:T(4,128)S(1)} %collective-permute-done.7.far_ref, ...), custom_call_target="tpu_custom_call" | custom-call | flops 603979776 | tf_op jit(solution)/shard_map/pallas_call | solution.py:534
  28.6 0.6 collective-permute-start.10
  29.2 1.6 %collective-permute-start.13 = (bf16[512,256]{1,0:T(8,128)(2,1)S(1)}, bf16[512,256]{1,0:T(8,128)(2,1)S(1)}, u32[]{:S(2)}, u32[]{:S(2)}) collective-permute-start(bf16[512,256]{1,0:T(8,128)(2,1)S(1)} %slice.16.k_x_ref), channel_id=1, source_target_pairs={{0,16},{16,0},{1,17},{17,1},{2,18},{18,2},{3,19},{19,3},{4,20},{20... | collective-permute-start | bytes 786440 | tf_op jit(solution)/shard_map/ppermute | solution.py:554
  30.8 0.6 collective-permute-start.17
  31.4 1.1 %shard_map.93.keep_ref = f32[192,1024]{1,0:T(8,128)S(1)} custom-call(f32[3,128,512]{2,1,0:T(8,128)S(1)} %get-tuple-element.20.hid_ref, f32[3,768]{1,0:T(4,128)S(1)} %collective-permute-done.5.one_ref, f32[3,768]{1,0:T(4,128)S(1)} %collective-permute-done.6.two_ref, f32[3,256]{1,0:T(4,128)S(1)} %collective-permute-done.7.far_ref, ...), custom_call_target="tpu_custom_call" | custom-call | flops 603979776 | tf_op jit(solution)/shard_map/pallas_call | solution.py:534
  32.5 11.0 %collective-permute-done.10.far_ref = bf16[192,1024]{1,0:T(8,128)(2,1)S(1)} collective-permute-done((bf16[192,1024]{1,0:T(8,128)(2,1)S(1)}, bf16[192,1024]{1,0:T(8,128)(2,1)S(1)}, u32[]{:S(2)}, u32[]{:S(2)}) %collective-permute-start.10) | collective-permute-done | bytes 393248 | tf_op jit(solution)/shard_map/ppermute | solution.py:550
  43.5 0.1 shard_map.95.mine_ref
  43.6 0.1 collective-permute-start.11
  43.8 2.3 %collective-permute-start.15 = (bf16[512,256]{1,0:T(8,128)(2,1)S(1)}, bf16[512,256]{1,0:T(8,128)(2,1)S(1)}, u32[]{:S(2)}, u32[]{:S(2)}) collective-permute-start(bf16[512,256]{1,0:T(8,128)(2,1)S(1)} %get-tuple-element.32.q_x_ref), channel_id=1, source_target_pairs={{0,4},{4,0},{8,12},{12,8},{1,5},{5,1},{9,13},{13,9},{2,6},{6,2},{1... | collective-permute-start | bytes 786440 | tf_op jit(solution)/shard_map/ppermute | solution.py:563
  46.1 1.5 %collective-permute-start.16 = (bf16[512,256]{1,0:T(8,128)(2,1)S(1)}, bf16[512,256]{1,0:T(8,128)(2,1)S(1)}, u32[]{:S(2)}, u32[]{:S(2)}) collective-permute-start(bf16[512,256]{1,0:T(8,128)(2,1)S(1)} %get-tuple-element.31.v_x_ref), channel_id=1, source_target_pairs={{0,16},{16,0},{1,17},{17,1},{2,18},{18,2},{3,19},{19,3},{4,20},{20... | collective-permute-start | bytes 786440 | tf_op jit(solution)/shard_map/ppermute | solution.py:554
  47.6 0.1 collective-permute-start.18
  47.8 5.5 %collective-permute-done.15.q_z_ref = bf16[512,256]{1,0:T(8,128)(2,1)S(1)} collective-permute-done((bf16[512,256]{1,0:T(8,128)(2,1)S(1)}, bf16[512,256]{1,0:T(8,128)(2,1)S(1)}, u32[]{:S(2)}, u32[]{:S(2)}) %collective-permute-start.15) | collective-permute-done | bytes 262176 | tf_op jit(solution)/shard_map/ppermute | solution.py:563
  53.2 0.7 shard_map.98
  53.9 0.6 collective-permute-done.16.v_y_ref
  54.5 3.3 %shard_map.99.context_ref = bf16[384,512]{1,0:T(8,128)(2,1)S(1)} custom-call(bf16[192,1024]{1,0:T(8,128)(2,1)S(1)} %collective-permute-done.11.theirs_ref, f32[1,1024]{1,0:T(1,128)S(1)} %bitcast.27, bf16[3,1024,256]{2,1,0:T(8,128)(2,1)S(1)} %bitcast.18, bf16[512,256]{1,0:T(8,128)(2,1)S(1)} %slice.16.k_x_ref, ...), custom_call_target="tpu_custom_call" | custom-call | flops 1207959552 | tf_op jit(solution)/shard_map/pallas_call | solution.py:534
  57.8 0.9 %collective-permute-done.18.out_z_ref = bf16[2,256,256]{2,1,0:T(8,128)(2,1)S(1)} collective-permute-done((bf16[2,256,256]{2,1,0:T(8,128)(2,1)S(1)}, bf16[2,256,256]{2,1,0:T(8,128)(2,1)S(1)}, u32[]{:S(2)}, u32[]{:S(2)}) %collective-permute-start.18) | collective-permute-done | bytes 262176 | tf_op jit(solution)/shard_map/ppermute | solution.py:563
  58.6 0.4 shard_map.100
  59.1 0.1 collective-permute-start.19
  59.2 0.4 shard_map.101
  59.6 0.6 collective-permute-start.21
  60.2 0.4 collective-permute-done.19
  60.6 0.1 add_convert_fusion
  60.6 1.6 %collective-permute-start.20 = (bf16[384,256]{1,0:T(8,128)(2,1)S(1)}, bf16[384,256]{1,0:T(8,128)(2,1)S(1)}, u32[]{:S(2)}, u32[]{:S(2)}) collective-permute-start(bf16[384,256]{1,0:T(8,128)(2,1)S(1)} %add_convert_fusion), channel_id=1, source_target_pairs={{0,2},{2,0},{1,3},{3,1},{4,6},{6,4},{5,7},{7,5},{8,10},{10,8},{9,1... | collective-permute-start | bytes 589832 | tf_op jit(solution)/shard_map/ppermute | solution.py:550
  62.2 0.8 %place_near.1.near_ref = bf16[6,128,256]{2,1,0:T(8,128)(2,1)} custom-call(f32[384,256]{1,0:T(8,128)S(1)} %get-tuple-element.29.keep_ref, bf16[384,256]{1,0:T(8,128)(2,1)S(1)} %collective-permute-done.21.got_ref), custom_call_target="tpu_custom_call" | custom-call | tf_op jit(solution)/shard_map/place_near/pallas_call | solution.py:678
  63.0 4.7 %collective-permute-done.20.value_ref = bf16[384,256]{1,0:T(8,128)(2,1)S(1)} collective-permute-done((bf16[384,256]{1,0:T(8,128)(2,1)S(1)}, bf16[384,256]{1,0:T(8,128)(2,1)S(1)}, u32[]{:S(2)}, u32[]{:S(2)}) %collective-permute-start.20) | collective-permute-done | bytes 196640 | tf_op jit(solution)/shard_map/ppermute | solution.py:550
  67.7 0.7 %place_far.1 = bf16[6,128,256]{2,1,0:T(8,128)(2,1)} custom-call(bf16[384,256]{1,0:T(8,128)(2,1)S(1)} %collective-permute-done.20.value_ref, bf16[6,128,256]{2,1,0:T(8,128)(2,1)} %place_near.1.near_ref), custom_call_target="tpu_custom_call", output_to_operand_aliasing={{}: (1, {})} | custom-call | tf_op jit(solution)/shard_map/place_far/pallas_call | solution.py:683
  (35 shorter events, 0.2 us)
Async XLA Ops:
  0.0 15.9 %collective-permute-start.3 = (bf16[3,1024,256]{2,1,0:T(8,128)(2,1)}, bf16[3,1024,256]{2,1,0:T(8,128)(2,1)S(1)}, u32[]{:S(2)}, u32[]{:S(2)}) collective-permute-start(bf16[3,1024,256]{2,1,0:T(8,128)(2,1)} %weight_ref.1), channel_id=1, source_target_pairs={{0,1},{1,0},{2,3},{3,2},{4,5},{5,4},{6,7},{7,6},{8,9},{9,8},{10,11... | collective-permute-start | bytes 4718600 | tf_op jit(solution)/shard_map/ppermute | solution.py:546
  0.5 21.5 %collective-permute-start.9 = (bf16[3,256,1024]{2,1,0:T(8,128)(2,1)}, bf16[3,256,1024]{2,1,0:T(8,128)(2,1)S(1)}, u32[]{:S(2)}, u32[]{:S(2)}) collective-permute-start(bf16[3,256,1024]{2,1,0:T(8,128)(2,1)} %param.14), channel_id=1, source_target_pairs={{0,1},{1,0},{2,3},{3,2},{4,5},{5,4},{6,7},{7,6},{8,9},{9,8},{10,11... | collective-permute-start | bytes 4718600 | tf_op jit(solution)/shard_map/ppermute | solution.py:546
  0.5 1.4 %copy-start.1 = (bf16[6,128,1024]{2,1,0:T(8,128)(2,1)S(1)}, bf16[6,128,1024]{2,1,0:T(8,128)(2,1)}, u32[]{:S(2)}) copy-start(bf16[6,128,1024]{2,1,0:T(8,128)(2,1)} %latent_ref.1) | copy-start | bytes 4718596
  1.9 9.1 %copy-start.8 = (f32[256]{0:T(256)S(1)}, f32[256]{0:T(256)}, u32[]{:S(2)}) copy-start(f32[256]{0:T(256)} %param.12) | copy-start | bytes 3076
  2.9 5.1 %collective-permute-start = (f32[6,1280]{1,0:T(8,128)S(1)}, f32[6,1280]{1,0:T(8,128)S(1)}, u32[]{:S(2)}, u32[]{:S(2)}) collective-permute-start(f32[6,1280]{1,0:T(8,128)S(1)} %get-tuple-element.18), channel_id=1, source_target_pairs={{0,4},{4,0},{8,12},{12,8},{1,13},{13,1},{5,9},{9,5},{2,6},{6,2},{1... | collective-permute-start | bytes 92168 | tf_op jit(solution)/shard_map/ppermute | solution.py:573
  8.0 7.3 %collective-permute-start.1 = (f32[6,1280]{1,0:T(8,128)S(1)}, f32[6,1280]{1,0:T(8,128)S(1)}, u32[]{:S(2)}, u32[]{:S(2)}) collective-permute-start(f32[6,1280]{1,0:T(8,128)S(1)} %collective-permute-done.got_ref), channel_id=1, source_target_pairs={{0,1},{1,0},{2,3},{3,2},{4,5},{5,4},{6,7},{7,6},{8,9},{9,8},{10,11... | collective-permute-start | bytes 92168 | tf_op jit(solution)/shard_map/ppermute | solution.py:546
  9.1 6.0 %collective-permute-start.2 = (f32[6,256]{1,0:T(8,128)S(1)}, f32[6,256]{1,0:T(8,128)S(1)}, u32[]{:S(2)}, u32[]{:S(2)}) collective-permute-start(f32[6,256]{1,0:T(8,128)S(1)} %get-tuple-element.19.own_ref), channel_id=1, source_target_pairs={{0,8},{8,0},{4,12},{12,4},{1,9},{9,1},{5,13},{13,5},{2,10},{10,2},... | collective-permute-start | bytes 18440 | tf_op jit(solution)/shard_map/ppermute | solution.py:563
  11.0 1.4 %collective-permute-start.4 = (f32[256]{0:T(256)S(1)}, f32[256]{0:T(256)S(1)}, u32[]{:S(2)}, u32[]{:S(2)}) collective-permute-start(f32[256]{0:T(256)S(1)} %copy-done.8), channel_id=1, source_target_pairs={{0,1},{1,0},{2,3},{3,2},{4,5},{5,4},{6,7},{7,6},{8,9},{9,8},{10,11... | collective-permute-start | bytes 3080 | tf_op jit(solution)/shard_map/ppermute | solution.py:546
  11.2 4.7 %copy-start.5 = (bf16[3,1024,256]{2,1,0:T(8,128)(2,1)S(1)}, bf16[3,1024,256]{2,1,0:T(8,128)(2,1)}, u32[]{:S(2)}) copy-start(bf16[3,1024,256]{2,1,0:T(8,128)(2,1)} %weight_ref.1) | copy-start | bytes 4718596
  12.4 2.8 %copy-start.9 = (f32[256]{0:T(256)S(1)}, f32[256]{0:T(256)}, u32[]{:S(2)}) copy-start(f32[256]{0:T(256)} %param.13) | copy-start | bytes 3076
  12.4 3.5 %copy-start.2 = (bf16[6,128,1024]{2,1,0:T(8,128)(2,1)S(1)}, bf16[6,128,1024]{2,1,0:T(8,128)(2,1)}, u32[]{:S(2)}) copy-start(bf16[6,128,1024]{2,1,0:T(8,128)(2,1)} %latent_ref.1) | copy-start | bytes 4718596
  12.4 3.5 %copy-start.7 = (f32[1024]{0:T(1024)S(1)}, f32[1024]{0:T(1024)}, u32[]{:S(2)}) copy-start(f32[1024]{0:T(1024)} %param.10) | copy-start | bytes 12292
  12.5 16.7 %collective-permute-start.12 = (bf16[768,256]{1,0:T(8,128)(2,1)S(1)}, bf16[768,256]{1,0:T(8,128)(2,1)S(1)}, u32[]{:S(2)}, u32[]{:S(2)}) collective-permute-start(bf16[768,256]{1,0:T(8,128)(2,1)S(1)} %shard_map.96), channel_id=1, source_target_pairs={{0,2},{2,0},{1,3},{3,1},{4,6},{6,4},{5,7},{7,5},{8,10},{10,8},{9,1... | collective-permute-start | bytes 1179656 | tf_op jit(solution)/shard_map/ppermute | solution.py:550
  15.2 4.6 %collective-permute-start.8 = (f32[256]{0:T(256)S(1)}, f32[256]{0:T(256)S(1)}, u32[]{:S(2)}, u32[]{:S(2)}) collective-permute-start(f32[256]{0:T(256)S(1)} %copy-done.9), channel_id=1, source_target_pairs={{0,1},{1,0},{2,3},{3,2},{4,5},{5,4},{6,7},{7,6},{8,9},{9,8},{10,11... | collective-permute-start | bytes 3080 | tf_op jit(solution)/shard_map/ppermute | solution.py:546
  15.3 28.5 %collective-permute-start.14 = (bf16[2,512,256]{2,1,0:T(8,128)(2,1)S(1)}, bf16[2,512,256]{2,1,0:T(8,128)(2,1)S(1)}, u32[]{:S(2)}, u32[]{:S(2)}) collective-permute-start(bf16[2,512,256]{2,1,0:T(8,128)(2,1)S(1)} %shard_map.97), channel_id=1, source_target_pairs={{0,2},{2,0},{1,3},{3,1},{4,6},{6,4},{5,7},{7,5},{8,10},{10,8},{9,1... | collective-permute-start | bytes 1572872 | tf_op jit(solution)/shard_map/ppermute | solution.py:550
  15.9 11.6 %copy-start.3 = (bf16[3,256,1024]{2,1,0:T(8,128)(2,1)S(1)}, bf16[3,256,1024]{2,1,0:T(8,128)(2,1)}, u32[]{:S(2)}) copy-start(bf16[3,256,1024]{2,1,0:T(8,128)(2,1)} %param.14) | copy-start | bytes 4718596
  18.5 4.7 %collective-permute-start.7 = (f32[3,256]{1,0:T(4,128)S(1)}, f32[3,256]{1,0:T(4,128)S(1)}, u32[]{:S(2)}, u32[]{:S(2)}) collective-permute-start(f32[3,256]{1,0:T(4,128)S(1)} %get-tuple-element.23.own_ref), channel_id=1, source_target_pairs={{0,8},{8,0},{4,12},{12,4},{1,9},{9,1},{5,13},{13,5},{2,10},{10,2},... | collective-permute-start | bytes 9224 | tf_op jit(solution)/shard_map/ppermute | solution.py:563
  19.8 3.9 %collective-permute-start.5 = (f32[3,768]{1,0:T(4,128)S(1)}, f32[3,768]{1,0:T(4,128)S(1)}, u32[]{:S(2)}, u32[]{:S(2)}) collective-permute-start(f32[3,768]{1,0:T(4,128)S(1)} %get-tuple-element.21), channel_id=1, source_target_pairs={{0,4},{4,0},{8,12},{12,8},{1,5},{5,1},{9,13},{13,9},{2,6},{6,2},{1... | collective-permute-start | bytes 27656 | tf_op jit(solution)/shard_map/ppermute | solution.py:563
  22.0 5.5 %collective-permute-start.6 = (f32[3,768]{1,0:T(4,128)S(1)}, f32[3,768]{1,0:T(4,128)S(1)}, u32[]{:S(2)}, u32[]{:S(2)}) collective-permute-start(f32[3,768]{1,0:T(4,128)S(1)} %get-tuple-element.22), channel_id=1, source_target_pairs={{0,12},{12,0},{4,8},{8,4},{1,13},{13,1},{5,9},{9,5},{2,14},{14,2},... | collective-permute-start | bytes 27656 | tf_op jit(solution)/shard_map/ppermute | solution.py:563
  28.6 14.9 %collective-permute-start.10 = (bf16[192,1024]{1,0:T(8,128)(2,1)S(1)}, bf16[192,1024]{1,0:T(8,128)(2,1)S(1)}, u32[]{:S(2)}, u32[]{:S(2)}) collective-permute-start(bf16[192,1024]{1,0:T(8,128)(2,1)S(1)} %shard_map.94), channel_id=1, source_target_pairs={{0,2},{2,0},{1,3},{3,1},{4,6},{6,4},{5,7},{7,5},{8,10},{10,8},{9,1... | collective-permute-start | bytes 1179656 | tf_op jit(solution)/shard_map/ppermute | solution.py:550
  29.2 18.6 %collective-permute-start.13 = (bf16[512,256]{1,0:T(8,128)(2,1)S(1)}, bf16[512,256]{1,0:T(8,128)(2,1)S(1)}, u32[]{:S(2)}, u32[]{:S(2)}) collective-permute-start(bf16[512,256]{1,0:T(8,128)(2,1)S(1)} %slice.16.k_x_ref), channel_id=1, source_target_pairs={{0,16},{16,0},{1,17},{17,1},{2,18},{18,2},{3,19},{19,3},{4,20},{20... | collective-permute-start | bytes 786440 | tf_op jit(solution)/shard_map/ppermute | solution.py:554
  30.8 16.8 %collective-permute-start.17 = (bf16[256,256]{1,0:T(8,128)(2,1)S(1)}, bf16[256,256]{1,0:T(8,128)(2,1)S(1)}, u32[]{:S(2)}, u32[]{:S(2)}) collective-permute-start(bf16[256,256]{1,0:T(8,128)(2,1)S(1)} %get-tuple-element.34.out_x_ref), channel_id=1, source_target_pairs={{0,16},{16,0},{1,17},{17,1},{2,18},{18,2},{3,19},{19,3},{4,20},{20... | collective-permute-start | bytes 393224 | tf_op jit(solution)/shard_map/ppermute | solution.py:554
  43.6 9.6 %copy-start = (bf16[1024,3,256]{2,0,1:T(8,128)(2,1)S(1)}, bf16[1024,3,256]{2,0,1:T(8,128)(2,1)}, u32[]{:S(2)}) copy-start(bf16[1024,3,256]{2,0,1:T(8,128)(2,1)} %param.16) | copy-start | bytes 4718596
  43.6 9.6 %copy-start.6 = (f32[1024]{0:T(1024)S(1)}, f32[1024]{0:T(1024)}, u32[]{:S(2)}) copy-start(f32[1024]{0:T(1024)} %param.15) | copy-start | bytes 12292
  43.6 10.8 %collective-permute-start.11 = (bf16[192,1024]{1,0:T(8,128)(2,1)S(1)}, bf16[192,1024]{1,0:T(8,128)(2,1)S(1)}, u32[]{:S(2)}, u32[]{:S(2)}) collective-permute-start(bf16[192,1024]{1,0:T(8,128)(2,1)S(1)} %shard_map.95.mine_ref), channel_id=1, source_target_pairs={{0,1},{1,0},{2,3},{3,2},{4,5},{5,4},{6,7},{7,6},{8,9},{9,8},{10,11... | collective-permute-start | bytes 1179656 | tf_op jit(solution)/shard_map/ppermute | solution.py:546
  43.8 9.4 %collective-permute-start.15 = (bf16[512,256]{1,0:T(8,128)(2,1)S(1)}, bf16[512,256]{1,0:T(8,128)(2,1)S(1)}, u32[]{:S(2)}, u32[]{:S(2)}) collective-permute-start(bf16[512,256]{1,0:T(8,128)(2,1)S(1)} %get-tuple-element.32.q_x_ref), channel_id=1, source_target_pairs={{0,4},{4,0},{8,12},{12,8},{1,5},{5,1},{9,13},{13,9},{2,6},{6,2},{1... | collective-permute-start | bytes 786440 | tf_op jit(solution)/shard_map/ppermute | solution.py:563
  46.1 8.4 %collective-permute-start.16 = (bf16[512,256]{1,0:T(8,128)(2,1)S(1)}, bf16[512,256]{1,0:T(8,128)(2,1)S(1)}, u32[]{:S(2)}, u32[]{:S(2)}) collective-permute-start(bf16[512,256]{1,0:T(8,128)(2,1)S(1)} %get-tuple-element.31.v_x_ref), channel_id=1, source_target_pairs={{0,16},{16,0},{1,17},{17,1},{2,18},{18,2},{3,19},{19,3},{4,20},{20... | collective-permute-start | bytes 786440 | tf_op jit(solution)/shard_map/ppermute | solution.py:554
  47.6 11.0 %collective-permute-start.18 = (bf16[2,256,256]{2,1,0:T(8,128)(2,1)S(1)}, bf16[2,256,256]{2,1,0:T(8,128)(2,1)S(1)}, u32[]{:S(2)}, u32[]{:S(2)}) collective-permute-start(bf16[2,256,256]{2,1,0:T(8,128)(2,1)S(1)} %pad_maximum_fusion), channel_id=1, source_target_pairs={{0,4},{4,0},{8,12},{12,8},{1,5},{5,1},{9,13},{13,9},{2,6},{6,2},{1... | collective-permute-start | bytes 786440 | tf_op jit(solution)/shard_map/ppermute | solution.py:563
  54.5 4.2 %copy-start.4 = (bf16[256,1024]{1,0:T(8,128)(2,1)S(1)}, bf16[256,1024]{1,0:T(8,128)(2,1)}, u32[]{:S(2)}) copy-start(bf16[256,1024]{1,0:T(8,128)(2,1)} %out_ref.5) | copy-start | bytes 1572868
  59.1 1.5 %collective-permute-start.19 = (bf16[384,256]{1,0:T(8,128)(2,1)S(1)}, bf16[384,256]{1,0:T(8,128)(2,1)S(1)}, u32[]{:S(2)}, u32[]{:S(2)}) collective-permute-start(bf16[384,256]{1,0:T(8,128)(2,1)S(1)} %get-tuple-element.28), channel_id=1, source_target_pairs={{0,1},{1,0},{2,3},{3,2},{4,5},{5,4},{6,7},{7,6},{8,9},{9,8},{10,11... | collective-permute-start | bytes 589832 | tf_op jit(solution)/shard_map/ppermute | solution.py:546
  59.6 2.6 %collective-permute-start.21 = (bf16[384,256]{1,0:T(8,128)(2,1)S(1)}, bf16[384,256]{1,0:T(8,128)(2,1)S(1)}, u32[]{:S(2)}, u32[]{:S(2)}) collective-permute-start(bf16[384,256]{1,0:T(8,128)(2,1)S(1)} %get-tuple-element.30), channel_id=1, source_target_pairs={{0,1},{1,0},{2,3},{3,2},{4,5},{5,4},{6,7},{7,6},{8,9},{9,8},{10,11... | collective-permute-start | bytes 589832 | tf_op jit(solution)/shard_map/ppermute | solution.py:546
  60.6 7.0 %collective-permute-start.20 = (bf16[384,256]{1,0:T(8,128)(2,1)S(1)}, bf16[384,256]{1,0:T(8,128)(2,1)S(1)}, u32[]{:S(2)}, u32[]{:S(2)}) collective-permute-start(bf16[384,256]{1,0:T(8,128)(2,1)S(1)} %add_convert_fusion), channel_id=1, source_target_pairs={{0,2},{2,0},{1,3},{3,1},{4,6},{6,4},{5,7},{7,5},{8,10},{10,8},{9,1... | collective-permute-start | bytes 589832 | tf_op jit(solution)/shard_map/ppermute | solution.py:550

commit v9 on v8

--- a/solution.py
+++ b/solution.py
@@ -344,16 +344,15 @@
 
 
 def project_kernel(
-    mine_ref, gain_ref, qkv_ref, k_x_ref, k_y_ref, q_x_ref, q_z_ref,
+    mine_ref, gain_ref, qkv_ref, k_x_ref, k_y_ref,
     queries_ref, keys_ref, normed_ref,
 ):
     shard = qkv_ref.shape[2]
     normed_ref[...] = normed_rows(mine_ref[...].astype(f32), gain_ref)
-    project = projector(normed_ref, qkv_ref, k_x_ref, k_y_ref, q_x_ref, q_z_ref)
+    project = projector(normed_ref, qkv_ref, k_x_ref, k_y_ref, None, None)
+    queries_ref[...] = project(0, 0)
     for side in range(2):
-        at = slice(side * shard, (side + 1) * shard)
-        queries_ref[:, at] = project(side, 0)
-        keys_ref[:, at] = project(side, 1)
+        keys_ref[:, side * shard : (side + 1) * shard] = project(side, 1)
 
 
 def attention_kernel(
@@ -372,12 +371,13 @@
     nt = (((1,), (1,)), ((), ()))
     for side in range(2):
         span = slice(side * shard, (side + 1) * shard)
-        queries, keys = [
-            jnp.concatenate([ref[:, span], project(side, which)], axis=0)
-            for which, ref in enumerate((queries_ref, keys_ref))
-        ]
+        if side == 0:
+            queries = jnp.concatenate([queries_ref[...], project(0, 0)], axis=0)
+        else:
+            queries = project_all(1, 0)
+        keys = jnp.concatenate([keys_ref[:, span], project(side, 1)], axis=0)
         values = project_all(side, 2)
-        queries = queries * (1.0 / math.sqrt(HEAD_DIM))
+        queries = queries * (math.log2(math.e) / math.sqrt(HEAD_DIM))
         for tile in range(shard // LANES):
             at = slice(tile * LANES, (tile + 1) * LANES)
             q_high, q_low = split2(queries[:, at])
@@ -395,7 +395,7 @@
                 ]
                 right = jnp.concatenate(right, axis=1)
                 scores = lax.dot_general(left, right, nt, preferred_element_type=f32)
-                scores = jnp.exp(scores - jnp.max(scores, axis=1, keepdims=True))
+                scores = jnp.exp2(scores - jnp.max(scores, axis=1, keepdims=True))
                 terms.append(scores.astype(bf16))
                 mixing.append(
                     jnp.concatenate(
@@ -410,33 +410,45 @@
             context_ref[:, base : base + LANES] = (mixed[:, :LANES] / mixed[:, LANES:]).astype(bf16)
 
 
-def output_kernel(
-    away, context_ref, mine_ref, theirs_ref, out_ref, out_x_ref, out_y_ref, out_z_ref,
-    send_ref, keep_ref, out_far_ref,
+def out_far_weights(goal_ref, out_x_ref, out_y_ref, out_z_ref):
+    group, parity = lax.axis_index(SONGS), lax.axis_index(FRAME) % 2
+    goal_ref[2 * group + parity] = out_x_ref[...]
+    goal_ref[2 * (1 - group) + parity] = out_y_ref[...]
+    goal_ref[2 * group + 1 - parity] = out_z_ref[0]
+    goal_ref[2 * (1 - group) + 1 - parity] = out_z_ref[1]
+
+
+def out_term(context_ref, out_ref, far_ref, block):
+    shard = out_ref.shape[0]
+    at = pl.ds(pl.multiple_of(block * shard, shard), shard)
+    value = jnp.dot(context_ref[:, :shard], out_ref[:, at], preferred_element_type=f32)
+    return value + jnp.dot(context_ref[:, shard:], far_ref[block], preferred_element_type=f32)
+
+
+def output_send_kernel(
+    away, context_ref, out_ref, out_x_ref, out_y_ref, out_z_ref, send_ref, far_ref
 ):
-    rows = mine_ref.shape[0]
-    shard = out_ref.shape[0]
+    rows = send_ref.shape[0] // 2
     index = lax.axis_index(TENSOR)
     chip, core = index // 2, index % 2
-    group, parity = lax.axis_index(SONGS), lax.axis_index(FRAME) % 2
-    out_far_ref[2 * group + parity] = out_x_ref[...]
-    out_far_ref[2 * (1 - group) + parity] = out_y_ref[...]
-    out_far_ref[2 * group + 1 - parity] = out_z_ref[0]
-    out_far_ref[2 * (1 - group) + 1 - parity] = out_z_ref[1]
-
-    def term(block):
-        at = pl.ds(pl.multiple_of(block * shard, shard), shard)
-        value = jnp.dot(context_ref[:, :shard], out_ref[:, at], preferred_element_type=f32)
-        far = jnp.dot(context_ref[:, shard:], out_far_ref[block], preferred_element_type=f32)
-        return value + far
-
+    out_far_weights(far_ref, out_x_ref, out_y_ref, out_z_ref)
     goal = 1 - chip if away else chip
-    value = term(2 * goal + 1 - core).astype(bf16)
+    value = out_term(context_ref, out_ref, far_ref, 2 * goal + 1 - core).astype(bf16)
     send_ref[:rows, :] = value[rows:]
     send_ref[rows:, :] = value[:rows]
-    block = 2 * goal + core
+
+
+def output_keep_kernel(
+    away, context_ref, out_ref, out_x_ref, out_y_ref, out_z_ref, mine_ref, theirs_ref,
+    keep_ref, far_ref,
+):
+    rows, shard = mine_ref.shape[0], out_ref.shape[0]
+    index = lax.axis_index(TENSOR)
+    chip, core = index // 2, index % 2
+    out_far_weights(far_ref, out_x_ref, out_y_ref, out_z_ref)
+    block = 2 * (1 - chip if away else chip) + core
     at = pl.ds(pl.multiple_of(block * shard, shard), shard)
-    value = term(block)
+    value = out_term(context_ref, out_ref, far_ref, block)
     keep_ref[:rows, :] = value[:rows] + mine_ref[:, at].astype(f32)
     keep_ref[rows:, :] = value[rows:] + theirs_ref[:, at].astype(f32)
 
@@ -645,9 +657,10 @@
     weights = [attn_gain[None], qkv, k_x, k_y, q_x, q_z]
     projected = call(
         project_kernel,
-        [((half_rows, 2 * shard), f32)] * 2 + [((half_rows, channels), bf16)], [],
-        [mine, *weights],
-        flops=8 * half_rows * channels * shard,
+        [((half_rows, shard), f32), ((half_rows, 2 * shard), f32), ((half_rows, channels), bf16)],
+        [],
+        [mine, *weights[:4]],
+        flops=6 * half_rows * channels * shard,
     )
     context = call(
         attention_kernel, [((2 * half_rows, 2 * shard), bf16)],
@@ -655,18 +668,19 @@
         [theirs, *weights, v_x, v_y, *projected],
         flops=24 * half_rows * channels * shard, limit=24,
     )[0]
-
-    def output(away):
+    inputs = [context, out_weight, out_x, out_y, out_z]
+    whole, scratch = (2 * half_rows, shard), [((4, shard, shard), bf16)]
+    flops = 2 * half_rows * channels * shard
+
+    def output(away, kept):
         return call(
-            functools.partial(output_kernel, away),
-            [((2 * half_rows, shard), bf16), ((2 * half_rows, shard), f32)],
-            [((4, shard, shard), bf16)],
-            [context, mine, theirs, out_weight, out_x, out_y, out_z],
-            flops=4 * half_rows * channels * shard,
-        )
-
-    send_far, keep_far = output(True)
-    send_near, keep_near = output(False)
+            functools.partial(output_keep_kernel if kept else output_send_kernel, away),
+            [(whole, f32 if kept else bf16)], scratch,
+            inputs + [mine, theirs] if kept else inputs, flops=flops,
+        )[0]
+
+    send_far, keep_far = output(True, False), output(True, True)
+    send_near, keep_near = output(False, False), output(False, True)
     got_far = swap_cores(send_far)
     got_near = swap_cores(send_near)
     away = (keep_far + got_far.astype(f32)).astype(bf16)

time: 68.6 us -> 68.5 us (level)
  waiting for transfers between devices: 29.3 us -> 28.6 us
    ppermute x6, waiting for transfers between devices: 10.6 us -> 9.78 us  [trade(): return lax.ppermute(value, FRAME, pairs)]
    ppermute x3, waiting for transfers between devices: 0.57 us -> 1.26 us  [swap_groups(): return lax.ppermute(value, SONGS, [(0, 1), (1, 0)])]
    pallas_call x9 -> x11, Pallas kernels: 10.6 us -> 11.1 us  [call(): pl.pallas_call(kernel, out_shape=[jax.ShapeDtypeStruct(shape, dtype) for...]
  transfers between devices with their start and end apart: 22 -> 22, of which waited for: 9 -> 9; matrix products, arithmetic and copies ran while one was open for 0% -> 0% of each run, Pallas kernels for 19% -> 20%
where the time goes in v9:
time: 68.5 us; the launch traced here: 68.3 us
  waiting for transfers between devices  28.6 us (42%)
  starting transfers between devices  22.9 us (33%)
  Pallas kernels  14.9 us (22%)
  local copies, waits for them, and re-layouts  1.53 us (2%)
    ppermute x4, waiting for transfers between devices, swap_chips(): return lax.ppermute(value, TENSOR, [(0, 2), (2, 0), (1, 3), (3, 1)])  15.4 us
    pallas_call x11, Pallas kernels, call(): pl.pallas_call(kernel, out_shape=[jax.ShapeDtypeStruct(shape, dtype) for...  11.1 us
    ppermute x6, waiting for transfers between devices, trade(): return lax.ppermute(value, FRAME, pairs)  9.78 us
    ppermute x6, starting transfers between devices, trade(): return lax.ppermute(value, FRAME, pairs)  9.03 us
    ppermute x4, starting transfers between devices, swap_chips(): return lax.ppermute(value, TENSOR, [(0, 2), (2, 0), (1, 3), (3, 1)])  4.37 us
    ppermute x3, starting transfers between devices, swap_groups(): return lax.ppermute(value, SONGS, [(0, 1), (1, 0)])  3.68 us
    ppermute x1, starting transfers between devices, trade_by_core(): return lax.ppermute(value, (FRAME, TENSOR), pairs)  3.12 us
    ppermute x8, starting transfers between devices, swap_cores(): return lax.ppermute(value, TENSOR, [(0, 1), (1, 0), (2, 3), (3, 2)])  2.67 us
  transfers between devices with their start and end apart: 22, of which 9 were waited for; matrix products, arithmetic and copies ran while one was open for 0% of the time, Pallas kernels for 20%

profile of v9, /device:TPU:0, one launch (start us, length us, event | category | flops | bytes accessed | tf_op | source)
XLA Modules:
  0.0 68.3 jit_solution(8574282391021059706)
XLA Ops:
  0.0 0.5 collective-permute-start.3
  0.5 0.0 collective-permute-start.9
  0.5 1.4 %copy-done.1 = bf16[6,128,1024]{2,1,0:T(8,128)(2,1)S(1)} copy-done((bf16[6,128,1024]{2,1,0:T(8,128)(2,1)S(1)}, bf16[6,128,1024]{2,1,0:T(8,128)(2,1)}, u32[]{:S(2)}) %copy-start.1) | copy-done | bytes 1572888
  1.9 0.9 %shard_map.91 = (f32[6,1280]{1,0:T(8,128)S(1)}, f32[6,256]{1,0:T(8,128)S(1)}) custom-call(bf16[6,128,1024]{2,1,0:T(8,128)(2,1)S(1)} %copy-done.1), custom_call_target="tpu_custom_call" | custom-call | tf_op jit(solution)/shard_map/pallas_call | solution.py:546
  2.9 3.1 %collective-permute-start = (f32[6,1280]{1,0:T(8,128)S(1)}, f32[6,1280]{1,0:T(8,128)S(1)}, u32[]{:S(2)}, u32[]{:S(2)}) collective-permute-start(f32[6,1280]{1,0:T(8,128)S(1)} %get-tuple-element.14), channel_id=1, source_target_pairs={{0,4},{4,0},{8,12},{12,8},{1,13},{13,1},{5,9},{9,5},{2,6},{6,2},{1... | collective-permute-start | bytes 92168 | tf_op jit(solution)/shard_map/ppermute | solution.py:585
  6.0 2.0 %collective-permute-done.got_ref = f32[6,1280]{1,0:T(8,128)S(1)} collective-permute-done((f32[6,1280]{1,0:T(8,128)S(1)}, f32[6,1280]{1,0:T(8,128)S(1)}, u32[]{:S(2)}, u32[]{:S(2)}) %collective-permute-start) | collective-permute-done | bytes 30752 | tf_op jit(solution)/shard_map/ppermute | solution.py:585
  8.0 1.2 %collective-permute-start.1 = (f32[6,1280]{1,0:T(8,128)S(1)}, f32[6,1280]{1,0:T(8,128)S(1)}, u32[]{:S(2)}, u32[]{:S(2)}) collective-permute-start(f32[6,1280]{1,0:T(8,128)S(1)} %collective-permute-done.got_ref), channel_id=1, source_target_pairs={{0,1},{1,0},{2,3},{3,2},{4,5},{5,4},{6,7},{7,6},{8,9},{9,8},{10,11... | collective-permute-start | bytes 92168 | tf_op jit(solution)/shard_map/ppermute | solution.py:558
  9.1 1.9 %collective-permute-start.2 = (f32[6,256]{1,0:T(8,128)S(1)}, f32[6,256]{1,0:T(8,128)S(1)}, u32[]{:S(2)}, u32[]{:S(2)}) collective-permute-start(f32[6,256]{1,0:T(8,128)S(1)} %get-tuple-element.15.own_ref), channel_id=1, source_target_pairs={{0,8},{8,0},{4,12},{12,4},{1,9},{9,1},{5,13},{13,5},{2,10},{10,2},... | collective-permute-start | bytes 18440 | tf_op jit(solution)/shard_map/ppermute | solution.py:575
  11.0 0.2 collective-permute-start.4
  11.2 1.2 %shard_map.96 = bf16[768,256]{1,0:T(8,128)(2,1)S(1)} custom-call(bf16[3,1024,256]{2,1,0:T(8,128)(2,1)} %bitcast.15, bf16[256,1024]{1,0:T(8,128)(2,1)} %out_ref.9), custom_call_target="tpu_custom_call" | custom-call | bytes 1048576 | tf_op jit(solution)/shard_map/pallas_call | solution.py:499
  12.4 0.0 copy-start.9
  12.5 1.6 %collective-permute-start.12 = (bf16[768,256]{1,0:T(8,128)(2,1)S(1)}, bf16[768,256]{1,0:T(8,128)(2,1)S(1)}, u32[]{:S(2)}, u32[]{:S(2)}) collective-permute-start(bf16[768,256]{1,0:T(8,128)(2,1)S(1)} %shard_map.96), channel_id=1, source_target_pairs={{0,2},{2,0},{1,3},{3,1},{4,6},{6,4},{5,7},{7,5},{8,10},{10,8},{9,1... | collective-permute-start | bytes 1179656 | tf_op jit(solution)/shard_map/ppermute | solution.py:562
  14.0 1.1 %shard_map.97 = bf16[2,512,256]{2,1,0:T(8,128)(2,1)S(1)} custom-call(bf16[3,1024,256]{2,1,0:T(8,128)(2,1)} %bitcast.16), custom_call_target="tpu_custom_call" | custom-call | bytes 1048576 | tf_op jit(solution)/shard_map/pallas_call | solution.py:499
  15.2 0.1 collective-permute-start.8
  15.3 0.7 collective-permute-start.14
  15.9 2.6 %shard_map.92 = (f32[3,128,512]{2,1,0:T(8,128)S(1)}, f32[3,768]{1,0:T(4,128)S(1)}, f32[3,768]{1,0:T(4,128)S(1)}, f32[3,256]{1,0:T(4,128)S(1)}) custom-call(bf16[6,128,1024]{2,1,0:T(8,128)(2,1)S(1)} %copy-done.2, f32[6,1280]{1,0:T(8,128)S(1)} %collective-permute-done.got_ref, f32[6,1280]{1,0:T(8,128)S(1)} %collective-permute-done.1.swapped_ref, ...), custom_call_target="tpu_custom_call" | custom-call | flops 1207959552 | tf_op jit(solution)/shard_map/pallas_call | solution.py:546
  18.5 1.3 %collective-permute-start.7 = (f32[3,256]{1,0:T(4,128)S(1)}, f32[3,256]{1,0:T(4,128)S(1)}, u32[]{:S(2)}, u32[]{:S(2)}) collective-permute-start(f32[3,256]{1,0:T(4,128)S(1)} %get-tuple-element.19.own_ref), channel_id=1, source_target_pairs={{0,8},{8,0},{4,12},{12,4},{1,9},{9,1},{5,13},{13,5},{2,10},{10,2},... | collective-permute-start | bytes 9224 | tf_op jit(solution)/shard_map/ppermute | solution.py:575
  19.8 2.2 %collective-permute-start.5 = (f32[3,768]{1,0:T(4,128)S(1)}, f32[3,768]{1,0:T(4,128)S(1)}, u32[]{:S(2)}, u32[]{:S(2)}) collective-permute-start(f32[3,768]{1,0:T(4,128)S(1)} %get-tuple-element.17), channel_id=1, source_target_pairs={{0,4},{4,0},{8,12},{12,8},{1,5},{5,1},{9,13},{13,9},{2,6},{6,2},{1... | collective-permute-start | bytes 27656 | tf_op jit(solution)/shard_map/ppermute | solution.py:575
  22.0 1.2 %collective-permute-start.6 = (f32[3,768]{1,0:T(4,128)S(1)}, f32[3,768]{1,0:T(4,128)S(1)}, u32[]{:S(2)}, u32[]{:S(2)}) collective-permute-start(f32[3,768]{1,0:T(4,128)S(1)} %get-tuple-element.18), channel_id=1, source_target_pairs={{0,12},{12,0},{4,8},{8,4},{1,13},{13,1},{5,9},{9,5},{2,14},{14,2},... | collective-permute-start | bytes 27656 | tf_op jit(solution)/shard_map/ppermute | solution.py:575
  23.3 0.4 collective-permute-done.5.one_ref
  23.7 3.8 %collective-permute-done.6.two_ref = f32[3,768]{1,0:T(4,128)S(1)} collective-permute-done((f32[3,768]{1,0:T(4,128)S(1)}, f32[3,768]{1,0:T(4,128)S(1)}, u32[]{:S(2)}, u32[]{:S(2)}) %collective-permute-start.6) | collective-permute-done | bytes 9248 | tf_op jit(solution)/shard_map/ppermute | solution.py:575
  27.5 1.1 %shard_map.94 = bf16[192,1024]{1,0:T(8,128)(2,1)S(1)} custom-call(f32[3,128,512]{2,1,0:T(8,128)S(1)} %get-tuple-element.16.hid_ref, f32[3,768]{1,0:T(4,128)S(1)} %collective-permute-done.5.one_ref, f32[3,768]{1,0:T(4,128)S(1)} %collective-permute-done.6.two_ref, f32[3,256]{1,0:T(4,128)S(1)} %collective-permute-done.7.far_ref, ...), custom_call_target="tpu_custom_call" | custom-call | flops 603979776 | tf_op jit(solution)/shard_map/pallas_call | solution.py:546
  28.6 0.6 collective-permute-start.10
  29.2 1.6 %collective-permute-start.13 = (bf16[512,256]{1,0:T(8,128)(2,1)S(1)}, bf16[512,256]{1,0:T(8,128)(2,1)S(1)}, u32[]{:S(2)}, u32[]{:S(2)}) collective-permute-start(bf16[512,256]{1,0:T(8,128)(2,1)S(1)} %slice.16.k_x_ref), channel_id=1, source_target_pairs={{0,16},{16,0},{1,17},{17,1},{2,18},{18,2},{3,19},{19,3},{4,20},{20... | collective-permute-start | bytes 786440 | tf_op jit(solution)/shard_map/ppermute | solution.py:566
  30.8 0.6 collective-permute-start.17
  31.4 1.1 %shard_map.93.keep_ref = f32[192,1024]{1,0:T(8,128)S(1)} custom-call(f32[3,128,512]{2,1,0:T(8,128)S(1)} %get-tuple-element.16.hid_ref, f32[3,768]{1,0:T(4,128)S(1)} %collective-permute-done.5.one_ref, f32[3,768]{1,0:T(4,128)S(1)} %collective-permute-done.6.two_ref, f32[3,256]{1,0:T(4,128)S(1)} %collective-permute-done.7.far_ref, ...), custom_call_target="tpu_custom_call" | custom-call | flops 603979776 | tf_op jit(solution)/shard_map/pallas_call | solution.py:546
  32.5 11.0 %collective-permute-done.10.far_ref = bf16[192,1024]{1,0:T(8,128)(2,1)S(1)} collective-permute-done((bf16[192,1024]{1,0:T(8,128)(2,1)S(1)}, bf16[192,1024]{1,0:T(8,128)(2,1)S(1)}, u32[]{:S(2)}, u32[]{:S(2)}) %collective-permute-start.10) | collective-permute-done | bytes 393248 | tf_op jit(solution)/shard_map/ppermute | solution.py:562
  43.5 0.1 shard_map.95.mine_ref
  43.6 0.1 collective-permute-start.11
  43.8 2.3 %collective-permute-start.15 = (bf16[512,256]{1,0:T(8,128)(2,1)S(1)}, bf16[512,256]{1,0:T(8,128)(2,1)S(1)}, u32[]{:S(2)}, u32[]{:S(2)}) collective-permute-start(bf16[512,256]{1,0:T(8,128)(2,1)S(1)} %get-tuple-element.24.q_x_ref), channel_id=1, source_target_pairs={{0,4},{4,0},{8,12},{12,8},{1,5},{5,1},{9,13},{13,9},{2,6},{6,2},{1... | collective-permute-start | bytes 786440 | tf_op jit(solution)/shard_map/ppermute | solution.py:575
  46.1 1.5 %collective-permute-start.16 = (bf16[512,256]{1,0:T(8,128)(2,1)S(1)}, bf16[512,256]{1,0:T(8,128)(2,1)S(1)}, u32[]{:S(2)}, u32[]{:S(2)}) collective-permute-start(bf16[512,256]{1,0:T(8,128)(2,1)S(1)} %get-tuple-element.23.v_x_ref), channel_id=1, source_target_pairs={{0,16},{16,0},{1,17},{17,1},{2,18},{18,2},{3,19},{19,3},{4,20},{20... | collective-permute-start | bytes 786440 | tf_op jit(solution)/shard_map/ppermute | solution.py:566
  47.6 0.1 collective-permute-start.18
  47.8 0.6 shard_map.98
  48.4 4.9 %collective-permute-done.15.q_z_ref = bf16[512,256]{1,0:T(8,128)(2,1)S(1)} collective-permute-done((bf16[512,256]{1,0:T(8,128)(2,1)S(1)}, bf16[512,256]{1,0:T(8,128)(2,1)S(1)}, u32[]{:S(2)}, u32[]{:S(2)}) %collective-permute-start.15) | collective-permute-done | bytes 262176 | tf_op jit(solution)/shard_map/ppermute | solution.py:575
  53.2 1.3 %collective-permute-done.16.v_y_ref = bf16[512,256]{1,0:T(8,128)(2,1)S(1)} collective-permute-done((bf16[512,256]{1,0:T(8,128)(2,1)S(1)}, bf16[512,256]{1,0:T(8,128)(2,1)S(1)}, u32[]{:S(2)}, u32[]{:S(2)}) %collective-permute-start.16) | collective-permute-done | bytes 262176 | tf_op jit(solution)/shard_map/ppermute | solution.py:566
  54.5 3.5 %shard_map.99.context_ref = bf16[384,512]{1,0:T(8,128)(2,1)S(1)} custom-call(bf16[192,1024]{1,0:T(8,128)(2,1)S(1)} %collective-permute-done.11.theirs_ref, f32[1,1024]{1,0:T(1,128)S(1)} %bitcast.27, bf16[3,1024,256]{2,1,0:T(8,128)(2,1)S(1)} %bitcast.18, bf16[512,256]{1,0:T(8,128)(2,1)S(1)} %slice.16.k_x_ref, ...), custom_call_target="tpu_custom_call" | custom-call | flops 1207959552 | tf_op jit(solution)/shard_map/pallas_call | solution.py:546
  58.0 0.7 collective-permute-done.18.out_z_ref
  58.6 0.3 shard_map.101
  59.0 0.1 collective-permute-start.19
  59.0 0.3 shard_map.103
  59.4 0.6 collective-permute-start.21
  59.9 0.3 shard_map.100
  60.3 0.2 collective-permute-done.19
  60.5 1.6 %collective-permute-start.20 = (bf16[384,256]{1,0:T(8,128)(2,1)S(1)}, bf16[384,256]{1,0:T(8,128)(2,1)S(1)}, u32[]{:S(2)}, u32[]{:S(2)}) collective-permute-start(bf16[384,256]{1,0:T(8,128)(2,1)S(1)} %add_convert_fusion), channel_id=1, source_target_pairs={{0,2},{2,0},{1,3},{3,1},{4,6},{6,4},{5,7},{7,5},{8,10},{10,8},{9,1... | collective-permute-start | bytes 589832 | tf_op jit(solution)/shard_map/ppermute | solution.py:562
  62.1 0.3 shard_map.102.keep_ref
  62.4 0.8 %place_near.1.near_ref = bf16[6,128,256]{2,1,0:T(8,128)(2,1)} custom-call(f32[384,256]{1,0:T(8,128)S(1)} %shard_map.102.keep_ref, bf16[384,256]{1,0:T(8,128)(2,1)S(1)} %collective-permute-done.21.got_ref), custom_call_target="tpu_custom_call" | custom-call | tf_op jit(solution)/shard_map/place_near/pallas_call | solution.py:692
  63.2 4.3 %collective-permute-done.20.value_ref = bf16[384,256]{1,0:T(8,128)(2,1)S(1)} collective-permute-done((bf16[384,256]{1,0:T(8,128)(2,1)S(1)}, bf16[384,256]{1,0:T(8,128)(2,1)S(1)}, u32[]{:S(2)}, u32[]{:S(2)}) %collective-permute-start.20) | collective-permute-done | bytes 196640 | tf_op jit(solution)/shard_map/ppermute | solution.py:562
  67.5 0.7 %place_far.1 = bf16[6,128,256]{2,1,0:T(8,128)(2,1)} custom-call(bf16[384,256]{1,0:T(8,128)(2,1)S(1)} %collective-permute-done.20.value_ref, bf16[6,128,256]{2,1,0:T(8,128)(2,1)} %place_near.1.near_ref), custom_call_target="tpu_custom_call", output_to_operand_aliasing={{}: (1, {})} | custom-call | tf_op jit(solution)/shard_map/place_far/pallas_call | solution.py:697
  (37 shorter events, 0.2 us)
Async XLA Ops:
  0.0 15.9 %collective-permute-start.3 = (bf16[3,1024,256]{2,1,0:T(8,128)(2,1)}, bf16[3,1024,256]{2,1,0:T(8,128)(2,1)S(1)}, u32[]{:S(2)}, u32[]{:S(2)}) collective-permute-start(bf16[3,1024,256]{2,1,0:T(8,128)(2,1)} %weight_ref.1), channel_id=1, source_target_pairs={{0,1},{1,0},{2,3},{3,2},{4,5},{5,4},{6,7},{7,6},{8,9},{9,8},{10,11... | collective-permute-start | bytes 4718600 | tf_op jit(solution)/shard_map/ppermute | solution.py:558
  0.5 21.5 %collective-permute-start.9 = (bf16[3,256,1024]{2,1,0:T(8,128)(2,1)}, bf16[3,256,1024]{2,1,0:T(8,128)(2,1)S(1)}, u32[]{:S(2)}, u32[]{:S(2)}) collective-permute-start(bf16[3,256,1024]{2,1,0:T(8,128)(2,1)} %param.14), channel_id=1, source_target_pairs={{0,1},{1,0},{2,3},{3,2},{4,5},{5,4},{6,7},{7,6},{8,9},{9,8},{10,11... | collective-permute-start | bytes 4718600 | tf_op jit(solution)/shard_map/ppermute | solution.py:558
  0.5 1.4 %copy-start.1 = (bf16[6,128,1024]{2,1,0:T(8,128)(2,1)S(1)}, bf16[6,128,1024]{2,1,0:T(8,128)(2,1)}, u32[]{:S(2)}) copy-start(bf16[6,128,1024]{2,1,0:T(8,128)(2,1)} %latent_ref.1) | copy-start | bytes 4718596
  1.9 9.1 %copy-start.8 = (f32[256]{0:T(256)S(1)}, f32[256]{0:T(256)}, u32[]{:S(2)}) copy-start(f32[256]{0:T(256)} %param.12) | copy-start | bytes 3076
  2.9 5.1 %collective-permute-start = (f32[6,1280]{1,0:T(8,128)S(1)}, f32[6,1280]{1,0:T(8,128)S(1)}, u32[]{:S(2)}, u32[]{:S(2)}) collective-permute-start(f32[6,1280]{1,0:T(8,128)S(1)} %get-tuple-element.14), channel_id=1, source_target_pairs={{0,4},{4,0},{8,12},{12,8},{1,13},{13,1},{5,9},{9,5},{2,6},{6,2},{1... | collective-permute-start | bytes 92168 | tf_op jit(solution)/shard_map/ppermute | solution.py:585
  8.0 7.3 %collective-permute-start.1 = (f32[6,1280]{1,0:T(8,128)S(1)}, f32[6,1280]{1,0:T(8,128)S(1)}, u32[]{:S(2)}, u32[]{:S(2)}) collective-permute-start(f32[6,1280]{1,0:T(8,128)S(1)} %collective-permute-done.got_ref), channel_id=1, source_target_pairs={{0,1},{1,0},{2,3},{3,2},{4,5},{5,4},{6,7},{7,6},{8,9},{9,8},{10,11... | collective-permute-start | bytes 92168 | tf_op jit(solution)/shard_map/ppermute | solution.py:558
  9.1 6.0 %collective-permute-start.2 = (f32[6,256]{1,0:T(8,128)S(1)}, f32[6,256]{1,0:T(8,128)S(1)}, u32[]{:S(2)}, u32[]{:S(2)}) collective-permute-start(f32[6,256]{1,0:T(8,128)S(1)} %get-tuple-element.15.own_ref), channel_id=1, source_target_pairs={{0,8},{8,0},{4,12},{12,4},{1,9},{9,1},{5,13},{13,5},{2,10},{10,2},... | collective-permute-start | bytes 18440 | tf_op jit(solution)/shard_map/ppermute | solution.py:575
  11.0 1.4 %collective-permute-start.4 = (f32[256]{0:T(256)S(1)}, f32[256]{0:T(256)S(1)}, u32[]{:S(2)}, u32[]{:S(2)}) collective-permute-start(f32[256]{0:T(256)S(1)} %copy-done.8), channel_id=1, source_target_pairs={{0,1},{1,0},{2,3},{3,2},{4,5},{5,4},{6,7},{7,6},{8,9},{9,8},{10,11... | collective-permute-start | bytes 3080 | tf_op jit(solution)/shard_map/ppermute | solution.py:558
  11.2 4.7 %copy-start.5 = (bf16[3,1024,256]{2,1,0:T(8,128)(2,1)S(1)}, bf16[3,1024,256]{2,1,0:T(8,128)(2,1)}, u32[]{:S(2)}) copy-start(bf16[3,1024,256]{2,1,0:T(8,128)(2,1)} %weight_ref.1) | copy-start | bytes 4718596
  12.4 2.8 %copy-start.9 = (f32[256]{0:T(256)S(1)}, f32[256]{0:T(256)}, u32[]{:S(2)}) copy-start(f32[256]{0:T(256)} %param.13) | copy-start | bytes 3076
  12.4 3.5 %copy-start.2 = (bf16[6,128,1024]{2,1,0:T(8,128)(2,1)S(1)}, bf16[6,128,1024]{2,1,0:T(8,128)(2,1)}, u32[]{:S(2)}) copy-start(bf16[6,128,1024]{2,1,0:T(8,128)(2,1)} %latent_ref.1) | copy-start | bytes 4718596
  12.4 3.5 %copy-start.7 = (f32[1024]{0:T(1024)S(1)}, f32[1024]{0:T(1024)}, u32[]{:S(2)}) copy-start(f32[1024]{0:T(1024)} %param.10) | copy-start | bytes 12292
  12.5 16.7 %collective-permute-start.12 = (bf16[768,256]{1,0:T(8,128)(2,1)S(1)}, bf16[768,256]{1,0:T(8,128)(2,1)S(1)}, u32[]{:S(2)}, u32[]{:S(2)}) collective-permute-start(bf16[768,256]{1,0:T(8,128)(2,1)S(1)} %shard_map.96), channel_id=1, source_target_pairs={{0,2},{2,0},{1,3},{3,1},{4,6},{6,4},{5,7},{7,5},{8,10},{10,8},{9,1... | collective-permute-start | bytes 1179656 | tf_op jit(solution)/shard_map/ppermute | solution.py:562
  15.2 4.6 %collective-permute-start.8 = (f32[256]{0:T(256)S(1)}, f32[256]{0:T(256)S(1)}, u32[]{:S(2)}, u32[]{:S(2)}) collective-permute-start(f32[256]{0:T(256)S(1)} %copy-done.9), channel_id=1, source_target_pairs={{0,1},{1,0},{2,3},{3,2},{4,5},{5,4},{6,7},{7,6},{8,9},{9,8},{10,11... | collective-permute-start | bytes 3080 | tf_op jit(solution)/shard_map/ppermute | solution.py:558
  15.3 28.5 %collective-permute-start.14 = (bf16[2,512,256]{2,1,0:T(8,128)(2,1)S(1)}, bf16[2,512,256]{2,1,0:T(8,128)(2,1)S(1)}, u32[]{:S(2)}, u32[]{:S(2)}) collective-permute-start(bf16[2,512,256]{2,1,0:T(8,128)(2,1)S(1)} %shard_map.97), channel_id=1, source_target_pairs={{0,2},{2,0},{1,3},{3,1},{4,6},{6,4},{5,7},{7,5},{8,10},{10,8},{9,1... | collective-permute-start | bytes 1572872 | tf_op jit(solution)/shard_map/ppermute | solution.py:562
  15.9 11.6 %copy-start.4 = (bf16[3,256,1024]{2,1,0:T(8,128)(2,1)S(1)}, bf16[3,256,1024]{2,1,0:T(8,128)(2,1)}, u32[]{:S(2)}) copy-start(bf16[3,256,1024]{2,1,0:T(8,128)(2,1)} %param.14) | copy-start | bytes 4718596
  18.5 4.7 %collective-permute-start.7 = (f32[3,256]{1,0:T(4,128)S(1)}, f32[3,256]{1,0:T(4,128)S(1)}, u32[]{:S(2)}, u32[]{:S(2)}) collective-permute-start(f32[3,256]{1,0:T(4,128)S(1)} %get-tuple-element.19.own_ref), channel_id=1, source_target_pairs={{0,8},{8,0},{4,12},{12,4},{1,9},{9,1},{5,13},{13,5},{2,10},{10,2},... | collective-permute-start | bytes 9224 | tf_op jit(solution)/shard_map/ppermute | solution.py:575
  19.8 3.9 %collective-permute-start.5 = (f32[3,768]{1,0:T(4,128)S(1)}, f32[3,768]{1,0:T(4,128)S(1)}, u32[]{:S(2)}, u32[]{:S(2)}) collective-permute-start(f32[3,768]{1,0:T(4,128)S(1)} %get-tuple-element.17), channel_id=1, source_target_pairs={{0,4},{4,0},{8,12},{12,8},{1,5},{5,1},{9,13},{13,9},{2,6},{6,2},{1... | collective-permute-start | bytes 27656 | tf_op jit(solution)/shard_map/ppermute | solution.py:575
  22.0 5.5 %collective-permute-start.6 = (f32[3,768]{1,0:T(4,128)S(1)}, f32[3,768]{1,0:T(4,128)S(1)}, u32[]{:S(2)}, u32[]{:S(2)}) collective-permute-start(f32[3,768]{1,0:T(4,128)S(1)} %get-tuple-element.18), channel_id=1, source_target_pairs={{0,12},{12,0},{4,8},{8,4},{1,13},{13,1},{5,9},{9,5},{2,14},{14,2},... | collective-permute-start | bytes 27656 | tf_op jit(solution)/shard_map/ppermute | solution.py:575
  28.6 14.9 %collective-permute-start.10 = (bf16[192,1024]{1,0:T(8,128)(2,1)S(1)}, bf16[192,1024]{1,0:T(8,128)(2,1)S(1)}, u32[]{:S(2)}, u32[]{:S(2)}) collective-permute-start(bf16[192,1024]{1,0:T(8,128)(2,1)S(1)} %shard_map.94), channel_id=1, source_target_pairs={{0,2},{2,0},{1,3},{3,1},{4,6},{6,4},{5,7},{7,5},{8,10},{10,8},{9,1... | collective-permute-start | bytes 1179656 | tf_op jit(solution)/shard_map/ppermute | solution.py:562
  29.2 18.6 %collective-permute-start.13 = (bf16[512,256]{1,0:T(8,128)(2,1)S(1)}, bf16[512,256]{1,0:T(8,128)(2,1)S(1)}, u32[]{:S(2)}, u32[]{:S(2)}) collective-permute-start(bf16[512,256]{1,0:T(8,128)(2,1)S(1)} %slice.16.k_x_ref), channel_id=1, source_target_pairs={{0,16},{16,0},{1,17},{17,1},{2,18},{18,2},{3,19},{19,3},{4,20},{20... | collective-permute-start | bytes 786440 | tf_op jit(solution)/shard_map/ppermute | solution.py:566
  30.8 16.8 %collective-permute-start.17 = (bf16[256,256]{1,0:T(8,128)(2,1)S(1)}, bf16[256,256]{1,0:T(8,128)(2,1)S(1)}, u32[]{:S(2)}, u32[]{:S(2)}) collective-permute-start(bf16[256,256]{1,0:T(8,128)(2,1)S(1)} %get-tuple-element.26.out_x_ref), channel_id=1, source_target_pairs={{0,16},{16,0},{1,17},{17,1},{2,18},{18,2},{3,19},{19,3},{4,20},{20... | collective-permute-start | bytes 393224 | tf_op jit(solution)/shard_map/ppermute | solution.py:566
  43.6 4.2 %copy-start = (bf16[1024,3,256]{2,0,1:T(8,128)(2,1)S(1)}, bf16[1024,3,256]{2,0,1:T(8,128)(2,1)}, u32[]{:S(2)}) copy-start(bf16[1024,3,256]{2,0,1:T(8,128)(2,1)} %param.16) | copy-start | bytes 4718596
  43.6 4.1 %copy-start.6 = (f32[1024]{0:T(1024)S(1)}, f32[1024]{0:T(1024)}, u32[]{:S(2)}) copy-start(f32[1024]{0:T(1024)} %param.15) | copy-start | bytes 12292
  43.6 10.8 %collective-permute-start.11 = (bf16[192,1024]{1,0:T(8,128)(2,1)S(1)}, bf16[192,1024]{1,0:T(8,128)(2,1)S(1)}, u32[]{:S(2)}, u32[]{:S(2)}) collective-permute-start(bf16[192,1024]{1,0:T(8,128)(2,1)S(1)} %shard_map.95.mine_ref), channel_id=1, source_target_pairs={{0,1},{1,0},{2,3},{3,2},{4,5},{5,4},{6,7},{7,6},{8,9},{9,8},{10,11... | collective-permute-start | bytes 1179656 | tf_op jit(solution)/shard_map/ppermute | solution.py:558
  43.8 9.4 %collective-permute-start.15 = (bf16[512,256]{1,0:T(8,128)(2,1)S(1)}, bf16[512,256]{1,0:T(8,128)(2,1)S(1)}, u32[]{:S(2)}, u32[]{:S(2)}) collective-permute-start(bf16[512,256]{1,0:T(8,128)(2,1)S(1)} %get-tuple-element.24.q_x_ref), channel_id=1, source_target_pairs={{0,4},{4,0},{8,12},{12,8},{1,5},{5,1},{9,13},{13,9},{2,6},{6,2},{1... | collective-permute-start | bytes 786440 | tf_op jit(solution)/shard_map/ppermute | solution.py:575
  46.1 8.4 %collective-permute-start.16 = (bf16[512,256]{1,0:T(8,128)(2,1)S(1)}, bf16[512,256]{1,0:T(8,128)(2,1)S(1)}, u32[]{:S(2)}, u32[]{:S(2)}) collective-permute-start(bf16[512,256]{1,0:T(8,128)(2,1)S(1)} %get-tuple-element.23.v_x_ref), channel_id=1, source_target_pairs={{0,16},{16,0},{1,17},{17,1},{2,18},{18,2},{3,19},{19,3},{4,20},{20... | collective-permute-start | bytes 786440 | tf_op jit(solution)/shard_map/ppermute | solution.py:566
  47.6 11.0 %collective-permute-start.18 = (bf16[2,256,256]{2,1,0:T(8,128)(2,1)S(1)}, bf16[2,256,256]{2,1,0:T(8,128)(2,1)S(1)}, u32[]{:S(2)}, u32[]{:S(2)}) collective-permute-start(bf16[2,256,256]{2,1,0:T(8,128)(2,1)S(1)} %pad_maximum_fusion), channel_id=1, source_target_pairs={{0,4},{4,0},{8,12},{12,8},{1,5},{5,1},{9,13},{13,9},{2,6},{6,2},{1... | collective-permute-start | bytes 786440 | tf_op jit(solution)/shard_map/ppermute | solution.py:575
  54.5 4.2 %copy-start.3 = (bf16[256,1024]{1,0:T(8,128)(2,1)S(1)}, bf16[256,1024]{1,0:T(8,128)(2,1)}, u32[]{:S(2)}) copy-start(bf16[256,1024]{1,0:T(8,128)(2,1)} %out_ref.9) | copy-start | bytes 1572868
  59.0 1.5 %collective-permute-start.19 = (bf16[384,256]{1,0:T(8,128)(2,1)S(1)}, bf16[384,256]{1,0:T(8,128)(2,1)S(1)}, u32[]{:S(2)}, u32[]{:S(2)}) collective-permute-start(bf16[384,256]{1,0:T(8,128)(2,1)S(1)} %shard_map.101), channel_id=1, source_target_pairs={{0,1},{1,0},{2,3},{3,2},{4,5},{5,4},{6,7},{7,6},{8,9},{9,8},{10,11... | collective-permute-start | bytes 589832 | tf_op jit(solution)/shard_map/ppermute | solution.py:558
  59.4 3.0 %collective-permute-start.21 = (bf16[384,256]{1,0:T(8,128)(2,1)S(1)}, bf16[384,256]{1,0:T(8,128)(2,1)S(1)}, u32[]{:S(2)}, u32[]{:S(2)}) collective-permute-start(bf16[384,256]{1,0:T(8,128)(2,1)S(1)} %shard_map.103), channel_id=1, source_target_pairs={{0,1},{1,0},{2,3},{3,2},{4,5},{5,4},{6,7},{7,6},{8,9},{9,8},{10,11... | collective-permute-start | bytes 589832 | tf_op jit(solution)/shard_map/ppermute | solution.py:558
  60.5 7.0 %collective-permute-start.20 = (bf16[384,256]{1,0:T(8,128)(2,1)S(1)}, bf16[384,256]{1,0:T(8,128)(2,1)S(1)}, u32[]{:S(2)}, u32[]{:S(2)}) collective-permute-start(bf16[384,256]{1,0:T(8,128)(2,1)S(1)} %add_convert_fusion), channel_id=1, source_target_pairs={{0,2},{2,0},{1,3},{3,1},{4,6},{6,4},{5,7},{7,5},{8,10},{10,8},{9,1... | collective-permute-start | bytes 589832 | tf_op jit(solution)/shard_map/ppermute | solution.py:562

commit v10 on v9

--- a/solution.py
+++ b/solution.py
@@ -344,15 +344,16 @@
 
 
 def project_kernel(
-    mine_ref, gain_ref, qkv_ref, k_x_ref, k_y_ref,
+    mine_ref, gain_ref, qkv_ref, k_x_ref, k_y_ref, q_x_ref, q_z_ref,
     queries_ref, keys_ref, normed_ref,
 ):
     shard = qkv_ref.shape[2]
     normed_ref[...] = normed_rows(mine_ref[...].astype(f32), gain_ref)
-    project = projector(normed_ref, qkv_ref, k_x_ref, k_y_ref, None, None)
-    queries_ref[...] = project(0, 0)
+    project = projector(normed_ref, qkv_ref, k_x_ref, k_y_ref, q_x_ref, q_z_ref)
     for side in range(2):
-        keys_ref[:, side * shard : (side + 1) * shard] = project(side, 1)
+        at = slice(side * shard, (side + 1) * shard)
+        queries_ref[:, at] = project(side, 0)
+        keys_ref[:, at] = project(side, 1)
 
 
 def attention_kernel(
@@ -371,11 +372,10 @@
     nt = (((1,), (1,)), ((), ()))
     for side in range(2):
         span = slice(side * shard, (side + 1) * shard)
-        if side == 0:
-            queries = jnp.concatenate([queries_ref[...], project(0, 0)], axis=0)
-        else:
-            queries = project_all(1, 0)
-        keys = jnp.concatenate([keys_ref[:, span], project(side, 1)], axis=0)
+        queries, keys = [
+            jnp.concatenate([ref[:, span], project(side, which)], axis=0)
+            for which, ref in enumerate((queries_ref, keys_ref))
+        ]
         values = project_all(side, 2)
         queries = queries * (math.log2(math.e) / math.sqrt(HEAD_DIM))
         for tile in range(shard // LANES):
@@ -657,10 +657,9 @@
     weights = [attn_gain[None], qkv, k_x, k_y, q_x, q_z]
     projected = call(
         project_kernel,
-        [((half_rows, shard), f32), ((half_rows, 2 * shard), f32), ((half_rows, channels), bf16)],
-        [],
-        [mine, *weights[:4]],
-        flops=6 * half_rows * channels * shard,
+        [((half_rows, 2 * shard), f32)] * 2 + [((half_rows, channels), bf16)], [],
+        [mine, *weights],
+        flops=8 * half_rows * channels * shard,
     )
     context = call(
         attention_kernel, [((2 * half_rows, 2 * shard), bf16)],

time: 68.5 us -> 68.5 us (level)
    ppermute x6, waiting for transfers between devices: 9.78 us -> 10.6 us  [trade(): return lax.ppermute(value, FRAME, pairs)]
    ppermute x3, waiting for transfers between devices: 1.26 us -> 0.57 us  [swap_groups(): return lax.ppermute(value, SONGS, [(0, 1), (1, 0)])]
where the time goes in v10:
time: 68.5 us; the launch traced here: 68.3 us
  waiting for transfers between devices  28.8 us (42%)
  starting transfers between devices  22.9 us (33%)
  Pallas kernels  14.8 us (22%)
  local copies, waits for them, and re-layouts  1.53 us (2%)
    ppermute x4, waiting for transfers between devices, swap_chips(): return lax.ppermute(value, TENSOR, [(0, 2), (2, 0), (1, 3), (3, 1)])  15.4 us
    pallas_call x11, Pallas kernels, call(): pl.pallas_call(kernel, out_shape=[jax.ShapeDtypeStruct(shape, dtype) for...  11 us
    ppermute x6, waiting for transfers between devices, trade(): return lax.ppermute(value, FRAME, pairs)  10.6 us
    ppermute x6, starting transfers between devices, trade(): return lax.ppermute(value, FRAME, pairs)  9.03 us
    ppermute x4, starting transfers between devices, swap_chips(): return lax.ppermute(value, TENSOR, [(0, 2), (2, 0), (1, 3), (3, 1)])  4.37 us
    ppermute x3, starting transfers between devices, swap_groups(): return lax.ppermute(value, SONGS, [(0, 1), (1, 0)])  3.68 us
    ppermute x1, starting transfers between devices, trade_by_core(): return lax.ppermute(value, (FRAME, TENSOR), pairs)  3.12 us
    ppermute x8, starting transfers between devices, swap_cores(): return lax.ppermute(value, TENSOR, [(0, 1), (1, 0), (2, 3), (3, 2)])  2.66 us
  transfers between devices with their start and end apart: 22, of which 9 were waited for; matrix products, arithmetic and copies ran while one was open for 0% of the time, Pallas kernels for 20%

profile of v10, /device:TPU:0, one launch (start us, length us, event | category | flops | bytes accessed | tf_op | source)
XLA Modules:
  0.0 68.3 jit_solution(16437654997634540684)
XLA Ops:
  0.0 0.5 collective-permute-start.3
  0.5 0.0 collective-permute-start.9
  0.5 1.4 %copy-done.1 = bf16[6,128,1024]{2,1,0:T(8,128)(2,1)S(1)} copy-done((bf16[6,128,1024]{2,1,0:T(8,128)(2,1)S(1)}, bf16[6,128,1024]{2,1,0:T(8,128)(2,1)}, u32[]{:S(2)}) %copy-start.1) | copy-done | bytes 1572888
  1.9 0.9 %shard_map.91 = (f32[6,1280]{1,0:T(8,128)S(1)}, f32[6,256]{1,0:T(8,128)S(1)}) custom-call(bf16[6,128,1024]{2,1,0:T(8,128)(2,1)S(1)} %copy-done.1), custom_call_target="tpu_custom_call" | custom-call | tf_op jit(solution)/shard_map/pallas_call | solution.py:546
  2.9 3.1 %collective-permute-start = (f32[6,1280]{1,0:T(8,128)S(1)}, f32[6,1280]{1,0:T(8,128)S(1)}, u32[]{:S(2)}, u32[]{:S(2)}) collective-permute-start(f32[6,1280]{1,0:T(8,128)S(1)} %get-tuple-element.14), channel_id=1, source_target_pairs={{0,4},{4,0},{8,12},{12,8},{1,13},{13,1},{5,9},{9,5},{2,6},{6,2},{1... | collective-permute-start | bytes 92168 | tf_op jit(solution)/shard_map/ppermute | solution.py:585
  6.0 2.0 %collective-permute-done.got_ref = f32[6,1280]{1,0:T(8,128)S(1)} collective-permute-done((f32[6,1280]{1,0:T(8,128)S(1)}, f32[6,1280]{1,0:T(8,128)S(1)}, u32[]{:S(2)}, u32[]{:S(2)}) %collective-permute-start) | collective-permute-done | bytes 30752 | tf_op jit(solution)/shard_map/ppermute | solution.py:585
  8.0 1.2 %collective-permute-start.1 = (f32[6,1280]{1,0:T(8,128)S(1)}, f32[6,1280]{1,0:T(8,128)S(1)}, u32[]{:S(2)}, u32[]{:S(2)}) collective-permute-start(f32[6,1280]{1,0:T(8,128)S(1)} %collective-permute-done.got_ref), channel_id=1, source_target_pairs={{0,1},{1,0},{2,3},{3,2},{4,5},{5,4},{6,7},{7,6},{8,9},{9,8},{10,11... | collective-permute-start | bytes 92168 | tf_op jit(solution)/shard_map/ppermute | solution.py:558
  9.1 1.9 %collective-permute-start.2 = (f32[6,256]{1,0:T(8,128)S(1)}, f32[6,256]{1,0:T(8,128)S(1)}, u32[]{:S(2)}, u32[]{:S(2)}) collective-permute-start(f32[6,256]{1,0:T(8,128)S(1)} %get-tuple-element.15.own_ref), channel_id=1, source_target_pairs={{0,8},{8,0},{4,12},{12,4},{1,9},{9,1},{5,13},{13,5},{2,10},{10,2},... | collective-permute-start | bytes 18440 | tf_op jit(solution)/shard_map/ppermute | solution.py:575
  11.0 0.2 collective-permute-start.4
  11.2 1.2 %shard_map.96 = bf16[768,256]{1,0:T(8,128)(2,1)S(1)} custom-call(bf16[3,1024,256]{2,1,0:T(8,128)(2,1)} %bitcast.15, bf16[256,1024]{1,0:T(8,128)(2,1)} %out_ref.9), custom_call_target="tpu_custom_call" | custom-call | bytes 1048576 | tf_op jit(solution)/shard_map/pallas_call | solution.py:499
  12.4 0.0 copy-start.9
  12.5 1.6 %collective-permute-start.12 = (bf16[768,256]{1,0:T(8,128)(2,1)S(1)}, bf16[768,256]{1,0:T(8,128)(2,1)S(1)}, u32[]{:S(2)}, u32[]{:S(2)}) collective-permute-start(bf16[768,256]{1,0:T(8,128)(2,1)S(1)} %shard_map.96), channel_id=1, source_target_pairs={{0,2},{2,0},{1,3},{3,1},{4,6},{6,4},{5,7},{7,5},{8,10},{10,8},{9,1... | collective-permute-start | bytes 1179656 | tf_op jit(solution)/shard_map/ppermute | solution.py:562
  14.0 1.1 %shard_map.97 = bf16[2,512,256]{2,1,0:T(8,128)(2,1)S(1)} custom-call(bf16[3,1024,256]{2,1,0:T(8,128)(2,1)} %bitcast.16), custom_call_target="tpu_custom_call" | custom-call | bytes 1048576 | tf_op jit(solution)/shard_map/pallas_call | solution.py:499
  15.2 0.1 collective-permute-start.8
  15.3 0.7 collective-permute-start.14
  15.9 2.6 %shard_map.92 = (f32[3,128,512]{2,1,0:T(8,128)S(1)}, f32[3,768]{1,0:T(4,128)S(1)}, f32[3,768]{1,0:T(4,128)S(1)}, f32[3,256]{1,0:T(4,128)S(1)}) custom-call(bf16[6,128,1024]{2,1,0:T(8,128)(2,1)S(1)} %copy-done.2, f32[6,1280]{1,0:T(8,128)S(1)} %collective-permute-done.got_ref, f32[6,1280]{1,0:T(8,128)S(1)} %collective-permute-done.1.swapped_ref, ...), custom_call_target="tpu_custom_call" | custom-call | flops 1207959552 | tf_op jit(solution)/shard_map/pallas_call | solution.py:546
  18.5 1.3 %collective-permute-start.7 = (f32[3,256]{1,0:T(4,128)S(1)}, f32[3,256]{1,0:T(4,128)S(1)}, u32[]{:S(2)}, u32[]{:S(2)}) collective-permute-start(f32[3,256]{1,0:T(4,128)S(1)} %get-tuple-element.19.own_ref), channel_id=1, source_target_pairs={{0,8},{8,0},{4,12},{12,4},{1,9},{9,1},{5,13},{13,5},{2,10},{10,2},... | collective-permute-start | bytes 9224 | tf_op jit(solution)/shard_map/ppermute | solution.py:575
  19.8 2.2 %collective-permute-start.5 = (f32[3,768]{1,0:T(4,128)S(1)}, f32[3,768]{1,0:T(4,128)S(1)}, u32[]{:S(2)}, u32[]{:S(2)}) collective-permute-start(f32[3,768]{1,0:T(4,128)S(1)} %get-tuple-element.17), channel_id=1, source_target_pairs={{0,4},{4,0},{8,12},{12,8},{1,5},{5,1},{9,13},{13,9},{2,6},{6,2},{1... | collective-permute-start | bytes 27656 | tf_op jit(solution)/shard_map/ppermute | solution.py:575
  22.0 1.2 %collective-permute-start.6 = (f32[3,768]{1,0:T(4,128)S(1)}, f32[3,768]{1,0:T(4,128)S(1)}, u32[]{:S(2)}, u32[]{:S(2)}) collective-permute-start(f32[3,768]{1,0:T(4,128)S(1)} %get-tuple-element.18), channel_id=1, source_target_pairs={{0,12},{12,0},{4,8},{8,4},{1,13},{13,1},{5,9},{9,5},{2,14},{14,2},... | collective-permute-start | bytes 27656 | tf_op jit(solution)/shard_map/ppermute | solution.py:575
  23.3 0.4 collective-permute-done.5.one_ref
  23.7 3.8 %collective-permute-done.6.two_ref = f32[3,768]{1,0:T(4,128)S(1)} collective-permute-done((f32[3,768]{1,0:T(4,128)S(1)}, f32[3,768]{1,0:T(4,128)S(1)}, u32[]{:S(2)}, u32[]{:S(2)}) %collective-permute-start.6) | collective-permute-done | bytes 9248 | tf_op jit(solution)/shard_map/ppermute | solution.py:575
  27.5 1.1 %shard_map.94 = bf16[192,1024]{1,0:T(8,128)(2,1)S(1)} custom-call(f32[3,128,512]{2,1,0:T(8,128)S(1)} %get-tuple-element.16.hid_ref, f32[3,768]{1,0:T(4,128)S(1)} %collective-permute-done.5.one_ref, f32[3,768]{1,0:T(4,128)S(1)} %collective-permute-done.6.two_ref, f32[3,256]{1,0:T(4,128)S(1)} %collective-permute-done.7.far_ref, ...), custom_call_target="tpu_custom_call" | custom-call | flops 603979776 | tf_op jit(solution)/shard_map/pallas_call | solution.py:546
  28.6 0.6 collective-permute-start.10
  29.2 1.6 %collective-permute-start.13 = (bf16[512,256]{1,0:T(8,128)(2,1)S(1)}, bf16[512,256]{1,0:T(8,128)(2,1)S(1)}, u32[]{:S(2)}, u32[]{:S(2)}) collective-permute-start(bf16[512,256]{1,0:T(8,128)(2,1)S(1)} %slice.16.k_x_ref), channel_id=1, source_target_pairs={{0,16},{16,0},{1,17},{17,1},{2,18},{18,2},{3,19},{19,3},{4,20},{20... | collective-permute-start | bytes 786440 | tf_op jit(solution)/shard_map/ppermute | solution.py:566
  30.8 0.6 collective-permute-start.17
  31.4 1.1 %shard_map.93.keep_ref = f32[192,1024]{1,0:T(8,128)S(1)} custom-call(f32[3,128,512]{2,1,0:T(8,128)S(1)} %get-tuple-element.16.hid_ref, f32[3,768]{1,0:T(4,128)S(1)} %collective-permute-done.5.one_ref, f32[3,768]{1,0:T(4,128)S(1)} %collective-permute-done.6.two_ref, f32[3,256]{1,0:T(4,128)S(1)} %collective-permute-done.7.far_ref, ...), custom_call_target="tpu_custom_call" | custom-call | flops 603979776 | tf_op jit(solution)/shard_map/pallas_call | solution.py:546
  32.5 11.0 %collective-permute-done.10.far_ref = bf16[192,1024]{1,0:T(8,128)(2,1)S(1)} collective-permute-done((bf16[192,1024]{1,0:T(8,128)(2,1)S(1)}, bf16[192,1024]{1,0:T(8,128)(2,1)S(1)}, u32[]{:S(2)}, u32[]{:S(2)}) %collective-permute-start.10) | collective-permute-done | bytes 393248 | tf_op jit(solution)/shard_map/ppermute | solution.py:562
  43.5 0.1 shard_map.95.mine_ref
  43.6 0.1 collective-permute-start.11
  43.8 2.3 %collective-permute-start.15 = (bf16[512,256]{1,0:T(8,128)(2,1)S(1)}, bf16[512,256]{1,0:T(8,128)(2,1)S(1)}, u32[]{:S(2)}, u32[]{:S(2)}) collective-permute-start(bf16[512,256]{1,0:T(8,128)(2,1)S(1)} %get-tuple-element.24.q_x_ref), channel_id=1, source_target_pairs={{0,4},{4,0},{8,12},{12,8},{1,5},{5,1},{9,13},{13,9},{2,6},{6,2},{1... | collective-permute-start | bytes 786440 | tf_op jit(solution)/shard_map/ppermute | solution.py:575
  46.1 1.5 %collective-permute-start.16 = (bf16[512,256]{1,0:T(8,128)(2,1)S(1)}, bf16[512,256]{1,0:T(8,128)(2,1)S(1)}, u32[]{:S(2)}, u32[]{:S(2)}) collective-permute-start(bf16[512,256]{1,0:T(8,128)(2,1)S(1)} %get-tuple-element.23.v_x_ref), channel_id=1, source_target_pairs={{0,16},{16,0},{1,17},{17,1},{2,18},{18,2},{3,19},{19,3},{4,20},{20... | collective-permute-start | bytes 786440 | tf_op jit(solution)/shard_map/ppermute | solution.py:566
  47.6 0.1 collective-permute-start.18
  47.8 5.5 %collective-permute-done.15.q_z_ref = bf16[512,256]{1,0:T(8,128)(2,1)S(1)} collective-permute-done((bf16[512,256]{1,0:T(8,128)(2,1)S(1)}, bf16[512,256]{1,0:T(8,128)(2,1)S(1)}, u32[]{:S(2)}, u32[]{:S(2)}) %collective-permute-start.15) | collective-permute-done | bytes 262176 | tf_op jit(solution)/shard_map/ppermute | solution.py:575
  53.2 0.7 %shard_map.98 = (f32[192,512]{1,0:T(8,128)S(1)}, f32[192,512]{1,0:T(8,128)S(1)}, bf16[192,1024]{1,0:T(8,128)(2,1)S(1)}) custom-call(bf16[192,1024]{1,0:T(8,128)(2,1)S(1)} %shard_map.95.mine_ref, f32[1,1024]{1,0:T(1,128)S(1)} %bitcast.26, bf16[3,1024,256]{2,1,0:T(8,128)(2,1)S(1)} %bitcast.17, bf16[512,256]{1,0:T(8,128)(2,1)S(1)} %slice.16.k_x_ref, ...), custom_call_target="tpu_custom_call" | custom-call | flops 402653184 | tf_op jit(solution)/shard_map/pallas_call | solution.py:546
  53.9 0.6 collective-permute-done.16.v_y_ref
  54.5 3.3 %shard_map.99.context_ref = bf16[384,512]{1,0:T(8,128)(2,1)S(1)} custom-call(bf16[192,1024]{1,0:T(8,128)(2,1)S(1)} %collective-permute-done.11.theirs_ref, f32[1,1024]{1,0:T(1,128)S(1)} %bitcast.27, bf16[3,1024,256]{2,1,0:T(8,128)(2,1)S(1)} %bitcast.18, bf16[512,256]{1,0:T(8,128)(2,1)S(1)} %slice.16.k_x_ref, ...), custom_call_target="tpu_custom_call" | custom-call | flops 1207959552 | tf_op jit(solution)/shard_map/pallas_call | solution.py:546
  57.8 0.9 %collective-permute-done.18.out_z_ref = bf16[2,256,256]{2,1,0:T(8,128)(2,1)S(1)} collective-permute-done((bf16[2,256,256]{2,1,0:T(8,128)(2,1)S(1)}, bf16[2,256,256]{2,1,0:T(8,128)(2,1)S(1)}, u32[]{:S(2)}, u32[]{:S(2)}) %collective-permute-start.18) | collective-permute-done | bytes 262176 | tf_op jit(solution)/shard_map/ppermute | solution.py:575
  58.6 0.3 shard_map.101
  59.0 0.1 collective-permute-start.19
  59.0 0.3 shard_map.103
  59.4 0.6 collective-permute-start.21
  59.9 0.3 shard_map.100
  60.3 0.2 collective-permute-done.19
  60.5 1.6 %collective-permute-start.20 = (bf16[384,256]{1,0:T(8,128)(2,1)S(1)}, bf16[384,256]{1,0:T(8,128)(2,1)S(1)}, u32[]{:S(2)}, u32[]{:S(2)}) collective-permute-start(bf16[384,256]{1,0:T(8,128)(2,1)S(1)} %add_convert_fusion), channel_id=1, source_target_pairs={{0,2},{2,0},{1,3},{3,1},{4,6},{6,4},{5,7},{7,5},{8,10},{10,8},{9,1... | collective-permute-start | bytes 589832 | tf_op jit(solution)/shard_map/ppermute | solution.py:562
  62.1 0.3 shard_map.102.keep_ref
  62.4 0.8 %place_near.1.near_ref = bf16[6,128,256]{2,1,0:T(8,128)(2,1)} custom-call(f32[384,256]{1,0:T(8,128)S(1)} %shard_map.102.keep_ref, bf16[384,256]{1,0:T(8,128)(2,1)S(1)} %collective-permute-done.21.got_ref), custom_call_target="tpu_custom_call" | custom-call | tf_op jit(solution)/shard_map/place_near/pallas_call | solution.py:691
  63.2 4.3 %collective-permute-done.20.value_ref = bf16[384,256]{1,0:T(8,128)(2,1)S(1)} collective-permute-done((bf16[384,256]{1,0:T(8,128)(2,1)S(1)}, bf16[384,256]{1,0:T(8,128)(2,1)S(1)}, u32[]{:S(2)}, u32[]{:S(2)}) %collective-permute-start.20) | collective-permute-done | bytes 196640 | tf_op jit(solution)/shard_map/ppermute | solution.py:562
  67.5 0.7 %place_far.1 = bf16[6,128,256]{2,1,0:T(8,128)(2,1)} custom-call(bf16[384,256]{1,0:T(8,128)(2,1)S(1)} %collective-permute-done.20.value_ref, bf16[6,128,256]{2,1,0:T(8,128)(2,1)} %place_near.1.near_ref), custom_call_target="tpu_custom_call", output_to_operand_aliasing={{}: (1, {})} | custom-call | tf_op jit(solution)/shard_map/place_far/pallas_call | solution.py:696
  (37 shorter events, 0.2 us)
Async XLA Ops:
  0.0 15.9 %collective-permute-start.3 = (bf16[3,1024,256]{2,1,0:T(8,128)(2,1)}, bf16[3,1024,256]{2,1,0:T(8,128)(2,1)S(1)}, u32[]{:S(2)}, u32[]{:S(2)}) collective-permute-start(bf16[3,1024,256]{2,1,0:T(8,128)(2,1)} %weight_ref.1), channel_id=1, source_target_pairs={{0,1},{1,0},{2,3},{3,2},{4,5},{5,4},{6,7},{7,6},{8,9},{9,8},{10,11... | collective-permute-start | bytes 4718600 | tf_op jit(solution)/shard_map/ppermute | solution.py:558
  0.5 21.5 %collective-permute-start.9 = (bf16[3,256,1024]{2,1,0:T(8,128)(2,1)}, bf16[3,256,1024]{2,1,0:T(8,128)(2,1)S(1)}, u32[]{:S(2)}, u32[]{:S(2)}) collective-permute-start(bf16[3,256,1024]{2,1,0:T(8,128)(2,1)} %param.14), channel_id=1, source_target_pairs={{0,1},{1,0},{2,3},{3,2},{4,5},{5,4},{6,7},{7,6},{8,9},{9,8},{10,11... | collective-permute-start | bytes 4718600 | tf_op jit(solution)/shard_map/ppermute | solution.py:558
  0.5 1.4 %copy-start.1 = (bf16[6,128,1024]{2,1,0:T(8,128)(2,1)S(1)}, bf16[6,128,1024]{2,1,0:T(8,128)(2,1)}, u32[]{:S(2)}) copy-start(bf16[6,128,1024]{2,1,0:T(8,128)(2,1)} %latent_ref.1) | copy-start | bytes 4718596
  1.9 9.1 %copy-start.8 = (f32[256]{0:T(256)S(1)}, f32[256]{0:T(256)}, u32[]{:S(2)}) copy-start(f32[256]{0:T(256)} %param.12) | copy-start | bytes 3076
  2.9 5.1 %collective-permute-start = (f32[6,1280]{1,0:T(8,128)S(1)}, f32[6,1280]{1,0:T(8,128)S(1)}, u32[]{:S(2)}, u32[]{:S(2)}) collective-permute-start(f32[6,1280]{1,0:T(8,128)S(1)} %get-tuple-element.14), channel_id=1, source_target_pairs={{0,4},{4,0},{8,12},{12,8},{1,13},{13,1},{5,9},{9,5},{2,6},{6,2},{1... | collective-permute-start | bytes 92168 | tf_op jit(solution)/shard_map/ppermute | solution.py:585
  8.0 7.3 %collective-permute-start.1 = (f32[6,1280]{1,0:T(8,128)S(1)}, f32[6,1280]{1,0:T(8,128)S(1)}, u32[]{:S(2)}, u32[]{:S(2)}) collective-permute-start(f32[6,1280]{1,0:T(8,128)S(1)} %collective-permute-done.got_ref), channel_id=1, source_target_pairs={{0,1},{1,0},{2,3},{3,2},{4,5},{5,4},{6,7},{7,6},{8,9},{9,8},{10,11... | collective-permute-start | bytes 92168 | tf_op jit(solution)/shard_map/ppermute | solution.py:558
  9.1 6.0 %collective-permute-start.2 = (f32[6,256]{1,0:T(8,128)S(1)}, f32[6,256]{1,0:T(8,128)S(1)}, u32[]{:S(2)}, u32[]{:S(2)}) collective-permute-start(f32[6,256]{1,0:T(8,128)S(1)} %get-tuple-element.15.own_ref), channel_id=1, source_target_pairs={{0,8},{8,0},{4,12},{12,4},{1,9},{9,1},{5,13},{13,5},{2,10},{10,2},... | collective-permute-start | bytes 18440 | tf_op jit(solution)/shard_map/ppermute | solution.py:575
  11.0 1.4 %collective-permute-start.4 = (f32[256]{0:T(256)S(1)}, f32[256]{0:T(256)S(1)}, u32[]{:S(2)}, u32[]{:S(2)}) collective-permute-start(f32[256]{0:T(256)S(1)} %copy-done.8), channel_id=1, source_target_pairs={{0,1},{1,0},{2,3},{3,2},{4,5},{5,4},{6,7},{7,6},{8,9},{9,8},{10,11... | collective-permute-start | bytes 3080 | tf_op jit(solution)/shard_map/ppermute | solution.py:558
  11.2 4.7 %copy-start.5 = (bf16[3,1024,256]{2,1,0:T(8,128)(2,1)S(1)}, bf16[3,1024,256]{2,1,0:T(8,128)(2,1)}, u32[]{:S(2)}) copy-start(bf16[3,1024,256]{2,1,0:T(8,128)(2,1)} %weight_ref.1) | copy-start | bytes 4718596
  12.4 2.8 %copy-start.9 = (f32[256]{0:T(256)S(1)}, f32[256]{0:T(256)}, u32[]{:S(2)}) copy-start(f32[256]{0:T(256)} %param.13) | copy-start | bytes 3076
  12.4 3.5 %copy-start.2 = (bf16[6,128,1024]{2,1,0:T(8,128)(2,1)S(1)}, bf16[6,128,1024]{2,1,0:T(8,128)(2,1)}, u32[]{:S(2)}) copy-start(bf16[6,128,1024]{2,1,0:T(8,128)(2,1)} %latent_ref.1) | copy-start | bytes 4718596
  12.4 3.5 %copy-start.7 = (f32[1024]{0:T(1024)S(1)}, f32[1024]{0:T(1024)}, u32[]{:S(2)}) copy-start(f32[1024]{0:T(1024)} %param.10) | copy-start | bytes 12292
  12.5 16.7 %collective-permute-start.12 = (bf16[768,256]{1,0:T(8,128)(2,1)S(1)}, bf16[768,256]{1,0:T(8,128)(2,1)S(1)}, u32[]{:S(2)}, u32[]{:S(2)}) collective-permute-start(bf16[768,256]{1,0:T(8,128)(2,1)S(1)} %shard_map.96), channel_id=1, source_target_pairs={{0,2},{2,0},{1,3},{3,1},{4,6},{6,4},{5,7},{7,5},{8,10},{10,8},{9,1... | collective-permute-start | bytes 1179656 | tf_op jit(solution)/shard_map/ppermute | solution.py:562
  15.2 4.6 %collective-permute-start.8 = (f32[256]{0:T(256)S(1)}, f32[256]{0:T(256)S(1)}, u32[]{:S(2)}, u32[]{:S(2)}) collective-permute-start(f32[256]{0:T(256)S(1)} %copy-done.9), channel_id=1, source_target_pairs={{0,1},{1,0},{2,3},{3,2},{4,5},{5,4},{6,7},{7,6},{8,9},{9,8},{10,11... | collective-permute-start | bytes 3080 | tf_op jit(solution)/shard_map/ppermute | solution.py:558
  15.3 28.5 %collective-permute-start.14 = (bf16[2,512,256]{2,1,0:T(8,128)(2,1)S(1)}, bf16[2,512,256]{2,1,0:T(8,128)(2,1)S(1)}, u32[]{:S(2)}, u32[]{:S(2)}) collective-permute-start(bf16[2,512,256]{2,1,0:T(8,128)(2,1)S(1)} %shard_map.97), channel_id=1, source_target_pairs={{0,2},{2,0},{1,3},{3,1},{4,6},{6,4},{5,7},{7,5},{8,10},{10,8},{9,1... | collective-permute-start | bytes 1572872 | tf_op jit(solution)/shard_map/ppermute | solution.py:562
  15.9 11.6 %copy-start.4 = (bf16[3,256,1024]{2,1,0:T(8,128)(2,1)S(1)}, bf16[3,256,1024]{2,1,0:T(8,128)(2,1)}, u32[]{:S(2)}) copy-start(bf16[3,256,1024]{2,1,0:T(8,128)(2,1)} %param.14) | copy-start | bytes 4718596
  18.5 4.7 %collective-permute-start.7 = (f32[3,256]{1,0:T(4,128)S(1)}, f32[3,256]{1,0:T(4,128)S(1)}, u32[]{:S(2)}, u32[]{:S(2)}) collective-permute-start(f32[3,256]{1,0:T(4,128)S(1)} %get-tuple-element.19.own_ref), channel_id=1, source_target_pairs={{0,8},{8,0},{4,12},{12,4},{1,9},{9,1},{5,13},{13,5},{2,10},{10,2},... | collective-permute-start | bytes 9224 | tf_op jit(solution)/shard_map/ppermute | solution.py:575
  19.8 3.9 %collective-permute-start.5 = (f32[3,768]{1,0:T(4,128)S(1)}, f32[3,768]{1,0:T(4,128)S(1)}, u32[]{:S(2)}, u32[]{:S(2)}) collective-permute-start(f32[3,768]{1,0:T(4,128)S(1)} %get-tuple-element.17), channel_id=1, source_target_pairs={{0,4},{4,0},{8,12},{12,8},{1,5},{5,1},{9,13},{13,9},{2,6},{6,2},{1... | collective-permute-start | bytes 27656 | tf_op jit(solution)/shard_map/ppermute | solution.py:575
  22.0 5.5 %collective-permute-start.6 = (f32[3,768]{1,0:T(4,128)S(1)}, f32[3,768]{1,0:T(4,128)S(1)}, u32[]{:S(2)}, u32[]{:S(2)}) collective-permute-start(f32[3,768]{1,0:T(4,128)S(1)} %get-tuple-element.18), channel_id=1, source_target_pairs={{0,12},{12,0},{4,8},{8,4},{1,13},{13,1},{5,9},{9,5},{2,14},{14,2},... | collective-permute-start | bytes 27656 | tf_op jit(solution)/shard_map/ppermute | solution.py:575
  28.6 14.9 %collective-permute-start.10 = (bf16[192,1024]{1,0:T(8,128)(2,1)S(1)}, bf16[192,1024]{1,0:T(8,128)(2,1)S(1)}, u32[]{:S(2)}, u32[]{:S(2)}) collective-permute-start(bf16[192,1024]{1,0:T(8,128)(2,1)S(1)} %shard_map.94), channel_id=1, source_target_pairs={{0,2},{2,0},{1,3},{3,1},{4,6},{6,4},{5,7},{7,5},{8,10},{10,8},{9,1... | collective-permute-start | bytes 1179656 | tf_op jit(solution)/shard_map/ppermute | solution.py:562
  29.2 18.6 %collective-permute-start.13 = (bf16[512,256]{1,0:T(8,128)(2,1)S(1)}, bf16[512,256]{1,0:T(8,128)(2,1)S(1)}, u32[]{:S(2)}, u32[]{:S(2)}) collective-permute-start(bf16[512,256]{1,0:T(8,128)(2,1)S(1)} %slice.16.k_x_ref), channel_id=1, source_target_pairs={{0,16},{16,0},{1,17},{17,1},{2,18},{18,2},{3,19},{19,3},{4,20},{20... | collective-permute-start | bytes 786440 | tf_op jit(solution)/shard_map/ppermute | solution.py:566
  30.8 16.8 %collective-permute-start.17 = (bf16[256,256]{1,0:T(8,128)(2,1)S(1)}, bf16[256,256]{1,0:T(8,128)(2,1)S(1)}, u32[]{:S(2)}, u32[]{:S(2)}) collective-permute-start(bf16[256,256]{1,0:T(8,128)(2,1)S(1)} %get-tuple-element.26.out_x_ref), channel_id=1, source_target_pairs={{0,16},{16,0},{1,17},{17,1},{2,18},{18,2},{3,19},{19,3},{4,20},{20... | collective-permute-start | bytes 393224 | tf_op jit(solution)/shard_map/ppermute | solution.py:566
  43.6 9.6 %copy-start = (bf16[1024,3,256]{2,0,1:T(8,128)(2,1)S(1)}, bf16[1024,3,256]{2,0,1:T(8,128)(2,1)}, u32[]{:S(2)}) copy-start(bf16[1024,3,256]{2,0,1:T(8,128)(2,1)} %param.16) | copy-start | bytes 4718596
  43.6 9.6 %copy-start.6 = (f32[1024]{0:T(1024)S(1)}, f32[1024]{0:T(1024)}, u32[]{:S(2)}) copy-start(f32[1024]{0:T(1024)} %param.15) | copy-start | bytes 12292
  43.6 10.8 %collective-permute-start.11 = (bf16[192,1024]{1,0:T(8,128)(2,1)S(1)}, bf16[192,1024]{1,0:T(8,128)(2,1)S(1)}, u32[]{:S(2)}, u32[]{:S(2)}) collective-permute-start(bf16[192,1024]{1,0:T(8,128)(2,1)S(1)} %shard_map.95.mine_ref), channel_id=1, source_target_pairs={{0,1},{1,0},{2,3},{3,2},{4,5},{5,4},{6,7},{7,6},{8,9},{9,8},{10,11... | collective-permute-start | bytes 1179656 | tf_op jit(solution)/shard_map/ppermute | solution.py:558
  43.8 9.4 %collective-permute-start.15 = (bf16[512,256]{1,0:T(8,128)(2,1)S(1)}, bf16[512,256]{1,0:T(8,128)(2,1)S(1)}, u32[]{:S(2)}, u32[]{:S(2)}) collective-permute-start(bf16[512,256]{1,0:T(8,128)(2,1)S(1)} %get-tuple-element.24.q_x_ref), channel_id=1, source_target_pairs={{0,4},{4,0},{8,12},{12,8},{1,5},{5,1},{9,13},{13,9},{2,6},{6,2},{1... | collective-permute-start | bytes 786440 | tf_op jit(solution)/shard_map/ppermute | solution.py:575
  46.1 8.4 %collective-permute-start.16 = (bf16[512,256]{1,0:T(8,128)(2,1)S(1)}, bf16[512,256]{1,0:T(8,128)(2,1)S(1)}, u32[]{:S(2)}, u32[]{:S(2)}) collective-permute-start(bf16[512,256]{1,0:T(8,128)(2,1)S(1)} %get-tuple-element.23.v_x_ref), channel_id=1, source_target_pairs={{0,16},{16,0},{1,17},{17,1},{2,18},{18,2},{3,19},{19,3},{4,20},{20... | collective-permute-start | bytes 786440 | tf_op jit(solution)/shard_map/ppermute | solution.py:566
  47.6 11.0 %collective-permute-start.18 = (bf16[2,256,256]{2,1,0:T(8,128)(2,1)S(1)}, bf16[2,256,256]{2,1,0:T(8,128)(2,1)S(1)}, u32[]{:S(2)}, u32[]{:S(2)}) collective-permute-start(bf16[2,256,256]{2,1,0:T(8,128)(2,1)S(1)} %pad_maximum_fusion), channel_id=1, source_target_pairs={{0,4},{4,0},{8,12},{12,8},{1,5},{5,1},{9,13},{13,9},{2,6},{6,2},{1... | collective-permute-start | bytes 786440 | tf_op jit(solution)/shard_map/ppermute | solution.py:575
  54.5 4.2 %copy-start.3 = (bf16[256,1024]{1,0:T(8,128)(2,1)S(1)}, bf16[256,1024]{1,0:T(8,128)(2,1)}, u32[]{:S(2)}) copy-start(bf16[256,1024]{1,0:T(8,128)(2,1)} %out_ref.9) | copy-start | bytes 1572868
  59.0 1.5 %collective-permute-start.19 = (bf16[384,256]{1,0:T(8,128)(2,1)S(1)}, bf16[384,256]{1,0:T(8,128)(2,1)S(1)}, u32[]{:S(2)}, u32[]{:S(2)}) collective-permute-start(bf16[384,256]{1,0:T(8,128)(2,1)S(1)} %shard_map.101), channel_id=1, source_target_pairs={{0,1},{1,0},{2,3},{3,2},{4,5},{5,4},{6,7},{7,6},{8,9},{9,8},{10,11... | collective-permute-start | bytes 589832 | tf_op jit(solution)/shard_map/ppermute | solution.py:558
  59.4 3.0 %collective-permute-start.21 = (bf16[384,256]{1,0:T(8,128)(2,1)S(1)}, bf16[384,256]{1,0:T(8,128)(2,1)S(1)}, u32[]{:S(2)}, u32[]{:S(2)}) collective-permute-start(bf16[384,256]{1,0:T(8,128)(2,1)S(1)} %shard_map.103), channel_id=1, source_target_pairs={{0,1},{1,0},{2,3},{3,2},{4,5},{5,4},{6,7},{7,6},{8,9},{9,8},{10,11... | collective-permute-start | bytes 589832 | tf_op jit(solution)/shard_map/ppermute | solution.py:558
  60.5 7.0 %collective-permute-start.20 = (bf16[384,256]{1,0:T(8,128)(2,1)S(1)}, bf16[384,256]{1,0:T(8,128)(2,1)S(1)}, u32[]{:S(2)}, u32[]{:S(2)}) collective-permute-start(bf16[384,256]{1,0:T(8,128)(2,1)S(1)} %add_convert_fusion), channel_id=1, source_target_pairs={{0,2},{2,0},{1,3},{3,1},{4,6},{6,4},{5,7},{7,5},{8,10},{10,8},{9,1... | collective-permute-start | bytes 589832 | tf_op jit(solution)/shard_map/ppermute | solution.py:562
